TPU v7x, 32 devices: a whole 2x2x4 slice. The times are simulated.
32 devices in a mesh: seq: 4 (over z), fsdp: 8 (over y, x, core).
Axes of the slice: x: 2, y: 2, z: 4, core: 2. Of those that a mesh axis runs over, the one named last changes fastest.
Arguments:
- block_input: bfloat16 [8, 512, 1152], P('fsdp', 'seq'), may hold values from -60 to 60
- grad_output: bfloat16 [8, 512, 1152], P('fsdp', 'seq'), may hold values from -6 to 6
- attn_norm_gain: bfloat16 [2, 1152], P(None, 'fsdp'), may hold values from 0.25 to 1.75
- attn_norm_bias: bfloat16 [2, 1152], P(None, 'fsdp'), may hold values from -3 to 3
- qkv_weight: bfloat16 [2, 1152, 3456], P(None, 'fsdp'), may hold values from -0.19939321 to 0.19939321
- qv_bias: bfloat16 [2, 2, 1152], P(None, None, 'fsdp'), may hold values from -3 to 3
- out_weight: bfloat16 [2, 1152, 1152], P(None, 'fsdp'), may hold values from -6 to 6
- out_bias: bfloat16 [2, 1152], P(None, 'fsdp'), may hold values from -3 to 3
- mlp_norm_gain: bfloat16 [2, 1152], P(None, 'fsdp'), may hold values from 0.25 to 1.75
- mlp_norm_bias: bfloat16 [2, 1152], P(None, 'fsdp'), may hold values from -3 to 3
- up_weight: bfloat16 [2, 1152, 4304], P(None, 'fsdp'), may hold values from -0.1875 to 0.1875
- up_bias: bfloat16 [2, 4304], P(None, 'fsdp'), may hold values from -3 to 3
- down_weight: bfloat16 [2, 4304, 1152], P(None, 'fsdp'), may hold values from -0.09375 to 0.09375
- down_bias: bfloat16 [2, 1152], P(None, 'fsdp'), may hold values from -3 to 3
Outputs:
- block_output: bfloat16 [8, 512, 1152], P('fsdp', 'seq')
- grad_input: float32 [8, 512, 1152], P('fsdp', 'seq')
- grad_attn_norm_gain: float32 [2, 1152], P(None, 'fsdp')
- grad_attn_norm_bias: float32 [2, 1152], P(None, 'fsdp')
- grad_qkv_weight: float32 [2, 1152, 3456], P(None, 'fsdp')
- grad_qv_bias: float32 [2, 2, 1152], P(None, None, 'fsdp')
- grad_out_weight: float32 [2, 1152, 1152], P(None, 'fsdp')
- grad_out_bias: float32 [2, 1152], P(None, 'fsdp')
- grad_mlp_norm_gain: float32 [2, 1152], P(None, 'fsdp')
- grad_mlp_norm_bias: float32 [2, 1152], P(None, 'fsdp')
- grad_up_weight: float32 [2, 1152, 4304], P(None, 'fsdp')
- grad_up_bias: float32 [2, 4304], P(None, 'fsdp')
- grad_down_weight: float32 [2, 4304, 1152], P(None, 'fsdp')
- grad_down_bias: float32 [2, 1152], P(None, 'fsdp')
All inputs are finite; a program needn't handle non-finite values.
Results may differ from a plain program's by a relative error of at most 0.018.
The roundings to bfloat16 on the way count: a program that leaves them out, or rounds other values in their place, can miss the bound.
Values may be sent and summed in bfloat16 or wider, within the bound.
No kernel may reach another device: no remote copies, remote signals or barrier semaphores. Data moves between devices by JAX's collectives and lax.ppermute only.
A program may use at most 384 MiB of HBM per device.

v0:
```python
import jax
import jax.numpy as jnp
from jax import lax
from jax.sharding import PartitionSpec as P

D = 1152
HEAD_DIM = 72
LAYERS = 2


EPSILON = 1e-06


def normalize(hidden, norm_gain, norm_offset):
    center = hidden - jnp.mean(hidden, axis=-1, keepdims=True)
    variance = jnp.mean(center * center, axis=-1, keepdims=True)
    inverse_std = lax.rsqrt(variance + EPSILON)
    normed = center * inverse_std
    return (
        normed * norm_gain.astype(jnp.float32) + norm_offset.astype(jnp.float32),
        normed,
        inverse_std,
    )


def normalize_back(upstream, normed, inverse_std, norm_gain):
    scaled = upstream * norm_gain.astype(jnp.float32)
    grad_hidden = inverse_std * (
        scaled
        - jnp.mean(scaled, axis=-1, keepdims=True)
        - normed * jnp.mean(scaled * normed, axis=-1, keepdims=True)
    )
    return (grad_hidden, jnp.sum(upstream * normed, axis=0), jnp.sum(upstream, axis=0))


def tangent_gelu(values):
    return jax.nn.gelu(values, approximate=True)


def gelu_back(values, upstream):
    return jax.vjp(tangent_gelu, values)[1](upstream)[0]


def contract_rows(left, right):
    return lax.dot_general(
        left, right, (((0,), (0,)), ((), ())), preferred_element_type=jnp.float32
    )


def contract_cols(left, right):
    return lax.dot_general(
        left, right, (((1,), (1,)), ((), ())), preferred_element_type=jnp.float32
    )


def attend_forward(query_block, key_heads, value_heads, scaling):
    scores = (
        jnp.einsum("qhd,khd->hqk", query_block, key_heads, preferred_element_type=jnp.float32)
        * scaling
    )
    row_peak = jnp.max(scores, axis=-1, keepdims=True)
    logsum = row_peak + jnp.log(jnp.sum(jnp.exp(scores - row_peak), axis=-1, keepdims=True))
    probability = jnp.exp(scores - logsum).astype(jnp.bfloat16)
    output = jnp.einsum(
        "hqk,khd->qhd", probability, value_heads, preferred_element_type=jnp.float32
    )
    return (output.astype(jnp.bfloat16), logsum[..., 0])


def attend_backward(query_block, key_heads, value_heads, grad_block, logsum_block, scaling):
    scores = (
        jnp.einsum("qhd,khd->hqk", query_block, key_heads, preferred_element_type=jnp.float32)
        * scaling
    )
    probability = jnp.exp(scores - logsum_block[..., None])
    prob_low = probability.astype(jnp.bfloat16)
    grad_value = jnp.einsum(
        "hqk,qhd->khd", prob_low, grad_block, preferred_element_type=jnp.float32
    )
    grad_prob = jnp.einsum(
        "qhd,khd->hqk", grad_block, value_heads, preferred_element_type=jnp.float32
    )
    row_inner = jnp.sum(probability * grad_prob, axis=-1, keepdims=True)
    grad_scores = (probability * (grad_prob - row_inner)).astype(jnp.bfloat16)
    grad_query = (
        jnp.einsum("hqk,khd->qhd", grad_scores, key_heads, preferred_element_type=jnp.float32)
        * scaling
    )
    grad_key = (
        jnp.einsum("hqk,qhd->khd", grad_scores, query_block, preferred_element_type=jnp.float32)
        * scaling
    )
    return (grad_query.astype(jnp.bfloat16), grad_key, grad_value)


def heads_forward(query_heads, key_flat, value_flat):
    seq_length, feature_width = query_heads.shape
    head_count = feature_width // HEAD_DIM
    block_rows = min(512, seq_length)
    block_count = seq_length // block_rows
    query_blocks = query_heads.reshape(block_count, block_rows, head_count, HEAD_DIM)
    key_heads = key_flat.reshape(seq_length, head_count, HEAD_DIM)
    value_heads = value_flat.reshape(seq_length, head_count, HEAD_DIM)
    outputs, logsums = lax.map(
        lambda query_block: attend_forward(query_block, key_heads, value_heads, HEAD_DIM ** (-0.5)),
        query_blocks,
    )
    return (outputs.reshape(seq_length, feature_width), logsums)


def heads_backward(query_heads, key_flat, value_flat, grad_flat, logsums):
    seq_length, feature_width = query_heads.shape
    head_count = feature_width // HEAD_DIM
    block_rows = min(512, seq_length)
    block_count = seq_length // block_rows
    query_blocks = query_heads.reshape(block_count, block_rows, head_count, HEAD_DIM)
    grad_blocks = grad_flat.reshape(block_count, block_rows, head_count, HEAD_DIM)
    key_heads = key_flat.reshape(seq_length, head_count, HEAD_DIM)
    value_heads = value_flat.reshape(seq_length, head_count, HEAD_DIM)

    def step(totals, inputs):
        query_block, grad_block, logsum_block = inputs
        grad_query, grad_key, grad_value = attend_backward(
            query_block, key_heads, value_heads, grad_block, logsum_block, HEAD_DIM ** (-0.5)
        )
        return ((totals[0] + grad_key, totals[1] + grad_value), grad_query)

    start = jnp.zeros((seq_length, head_count, HEAD_DIM), jnp.float32)
    (grad_keys, grad_values), grad_queries = lax.scan(
        step, (start, start), (query_blocks, grad_blocks, logsums)
    )
    return (
        grad_queries.reshape(seq_length, feature_width),
        grad_keys.astype(jnp.bfloat16).reshape(seq_length, feature_width),
        grad_values.astype(jnp.bfloat16).reshape(seq_length, feature_width),
    )


def body(
    block_input,
    grad_output,
    attn_norm_gain,
    attn_norm_bias,
    qkv_weight,
    qv_bias,
    out_weight,
    out_bias,
    mlp_norm_gain,
    mlp_norm_bias,
    up_weight,
    up_bias,
    down_weight,
    down_bias,
):
    hidden = block_input[0].astype(jnp.float32)
    stored = []
    for layer_number in range(LAYERS):
        attn_params = (
            lax.all_gather(attn_norm_gain[layer_number], "fsdp", axis=0, tiled=True),
            lax.all_gather(attn_norm_bias[layer_number], "fsdp", axis=0, tiled=True),
            lax.all_gather(qkv_weight[layer_number], "fsdp", axis=0, tiled=True),
            lax.all_gather(qv_bias[layer_number], "fsdp", axis=1, tiled=True),
            lax.all_gather(out_weight[layer_number], "fsdp", axis=0, tiled=True),
            lax.all_gather(out_bias[layer_number], "fsdp", axis=0, tiled=True),
        )
        gain_one, offset_one, proj_qkv, bias_qv, proj_out, bias_out = attn_params
        normed_in, normed_one, inverse_one = normalize(hidden, gain_one, offset_one)
        attn_in = normed_in.astype(jnp.bfloat16)
        bias_row = jnp.concatenate(
            [
                bias_qv[0].astype(jnp.float32),
                jnp.zeros((D,), jnp.float32),
                bias_qv[1].astype(jnp.float32),
            ]
        )
        projected = jnp.dot(attn_in, proj_qkv, preferred_element_type=jnp.float32) + bias_row
        queries = projected[:, :D].astype(jnp.bfloat16)
        keys_tok = projected[:, D : 2 * D].astype(jnp.bfloat16)
        values_tok = projected[:, 2 * D :].astype(jnp.bfloat16)
        query_heads, key_flat, value_flat = (
            lax.all_to_all(queries, "seq", split_axis=1, concat_axis=0, tiled=True),
            lax.all_to_all(keys_tok, "seq", split_axis=1, concat_axis=0, tiled=True),
            lax.all_to_all(values_tok, "seq", split_axis=1, concat_axis=0, tiled=True),
        )
        out_heads, logsums = heads_forward(query_heads, key_flat, value_flat)
        attended = lax.all_to_all(out_heads, "seq", split_axis=0, concat_axis=1, tiled=True)
        after_attn = (
            hidden
            + jnp.dot(attended, proj_out, preferred_element_type=jnp.float32)
            + bias_out.astype(jnp.float32)
        )
        mlp_params = (
            lax.all_gather(mlp_norm_gain[layer_number], "fsdp", axis=0, tiled=True),
            lax.all_gather(mlp_norm_bias[layer_number], "fsdp", axis=0, tiled=True),
            lax.all_gather(up_weight[layer_number], "fsdp", axis=0, tiled=True),
            lax.all_gather(up_bias[layer_number], "fsdp", axis=0, tiled=True),
            lax.all_gather(down_weight[layer_number], "fsdp", axis=0, tiled=True),
            lax.all_gather(down_bias[layer_number], "fsdp", axis=0, tiled=True),
        )
        gain_two, offset_two, proj_up, bias_up, proj_down, bias_down = mlp_params
        normed_mid, normed_two, inverse_two = normalize(after_attn, gain_two, offset_two)
        mlp_in = normed_mid.astype(jnp.bfloat16)
        pre_act = jnp.dot(mlp_in, proj_up, preferred_element_type=jnp.float32) + bias_up.astype(
            jnp.float32
        )
        activated = tangent_gelu(pre_act).astype(jnp.bfloat16)
        hidden = (
            after_attn
            + jnp.dot(activated, proj_down, preferred_element_type=jnp.float32)
            + bias_down.astype(jnp.float32)
        )
        stored.append(
            (
                attn_params,
                mlp_params,
                normed_one,
                inverse_one,
                attn_in,
                query_heads,
                key_flat,
                value_flat,
                logsums,
                attended,
                normed_two,
                inverse_two,
                mlp_in,
                pre_act,
                activated,
            )
        )
    block_output = hidden.astype(jnp.bfloat16)[None]
    grad_hidden = grad_output[0].astype(jnp.float32)
    attn_shares = [None] * LAYERS
    mlp_shares = [None] * LAYERS
    for layer_number in reversed(range(LAYERS)):
        (
            attn_params,
            mlp_params,
            normed_one,
            inverse_one,
            attn_in,
            query_heads,
            key_flat,
            value_flat,
            logsums,
            attended,
            normed_two,
            inverse_two,
            mlp_in,
            pre_act,
            activated,
        ) = stored[layer_number]
        mlp_params = (
            lax.all_gather(mlp_norm_gain[layer_number], "fsdp", axis=0, tiled=True),
            lax.all_gather(mlp_norm_bias[layer_number], "fsdp", axis=0, tiled=True),
            lax.all_gather(up_weight[layer_number], "fsdp", axis=0, tiled=True),
            lax.all_gather(up_bias[layer_number], "fsdp", axis=0, tiled=True),
            lax.all_gather(down_weight[layer_number], "fsdp", axis=0, tiled=True),
            lax.all_gather(down_bias[layer_number], "fsdp", axis=0, tiled=True),
        )
        gain_two, offset_two, proj_up, bias_up, proj_down, bias_down = mlp_params
        grad_low = grad_hidden.astype(jnp.bfloat16)
        g_down_bias = jnp.sum(grad_hidden, axis=0)
        grad_act = contract_cols(grad_low, proj_down)
        grad_pre = gelu_back(pre_act, grad_act)
        g_up_bias = jnp.sum(grad_pre, axis=0)
        grad_pre_low = grad_pre.astype(jnp.bfloat16)
        g_up = contract_rows(mlp_in, grad_pre_low)
        grad_mid = contract_cols(grad_pre_low, proj_up)
        grad_norm_two, g_gain_two, g_offset_two = normalize_back(
            grad_mid, normed_two, inverse_two, gain_two
        )
        grad_after = grad_hidden + grad_norm_two
        g_down = contract_rows(activated, grad_low)
        mlp_shares[layer_number] = (
            lax.psum_scatter(
                g_gain_two.astype(jnp.bfloat16), "fsdp", scatter_dimension=0, tiled=True
            ).astype(jnp.float32),
            lax.psum_scatter(
                g_offset_two.astype(jnp.bfloat16), "fsdp", scatter_dimension=0, tiled=True
            ).astype(jnp.float32),
            lax.psum_scatter(
                g_up.astype(jnp.bfloat16), "fsdp", scatter_dimension=0, tiled=True
            ).astype(jnp.float32),
            lax.psum_scatter(
                g_up_bias.astype(jnp.bfloat16), "fsdp", scatter_dimension=0, tiled=True
            ).astype(jnp.float32),
            lax.psum_scatter(
                g_down.astype(jnp.bfloat16), "fsdp", scatter_dimension=0, tiled=True
            ).astype(jnp.float32),
            lax.psum_scatter(
                g_down_bias.astype(jnp.bfloat16), "fsdp", scatter_dimension=0, tiled=True
            ).astype(jnp.float32),
        )
        attn_params = (
            lax.all_gather(attn_norm_gain[layer_number], "fsdp", axis=0, tiled=True),
            lax.all_gather(attn_norm_bias[layer_number], "fsdp", axis=0, tiled=True),
            lax.all_gather(qkv_weight[layer_number], "fsdp", axis=0, tiled=True),
            lax.all_gather(qv_bias[layer_number], "fsdp", axis=1, tiled=True),
            lax.all_gather(out_weight[layer_number], "fsdp", axis=0, tiled=True),
            lax.all_gather(out_bias[layer_number], "fsdp", axis=0, tiled=True),
        )
        gain_one, offset_one, proj_qkv, bias_qv, proj_out, bias_out = attn_params
        g_out_bias = jnp.sum(grad_after, axis=0)
        after_low = grad_after.astype(jnp.bfloat16)
        g_out = contract_rows(attended, after_low)
        grad_attended = contract_cols(after_low, proj_out).astype(jnp.bfloat16)
        grad_heads = lax.all_to_all(grad_attended, "seq", split_axis=1, concat_axis=0, tiled=True)
        head_grad_q, head_grad_k, head_grad_v = heads_backward(
            query_heads, key_flat, value_flat, grad_heads, logsums
        )
        grad_q, grad_k, grad_v = (
            lax.all_to_all(head_grad_q, "seq", split_axis=0, concat_axis=1, tiled=True),
            lax.all_to_all(head_grad_k, "seq", split_axis=0, concat_axis=1, tiled=True),
            lax.all_to_all(head_grad_v, "seq", split_axis=0, concat_axis=1, tiled=True),
        )
        grad_proj = jnp.concatenate([grad_q, grad_k, grad_v], axis=1)
        g_qkv = contract_rows(attn_in, grad_proj)
        g_qv_bias = jnp.stack(
            [
                jnp.sum(grad_q.astype(jnp.float32), axis=0),
                jnp.sum(grad_v.astype(jnp.float32), axis=0),
            ]
        )
        grad_in = contract_cols(grad_proj, proj_qkv)
        grad_norm_one, g_gain_one, g_offset_one = normalize_back(
            grad_in, normed_one, inverse_one, gain_one
        )
        grad_hidden = grad_after + grad_norm_one
        attn_shares[layer_number] = (
            lax.psum_scatter(
                g_gain_one.astype(jnp.bfloat16), "fsdp", scatter_dimension=0, tiled=True
            ).astype(jnp.float32),
            lax.psum_scatter(
                g_offset_one.astype(jnp.bfloat16), "fsdp", scatter_dimension=0, tiled=True
            ).astype(jnp.float32),
            lax.psum_scatter(
                g_qkv.astype(jnp.bfloat16), "fsdp", scatter_dimension=0, tiled=True
            ).astype(jnp.float32),
            lax.psum_scatter(
                g_qv_bias.astype(jnp.bfloat16), "fsdp", scatter_dimension=1, tiled=True
            ).astype(jnp.float32),
            lax.psum_scatter(
                g_out.astype(jnp.bfloat16), "fsdp", scatter_dimension=0, tiled=True
            ).astype(jnp.float32),
            lax.psum_scatter(
                g_out_bias.astype(jnp.bfloat16), "fsdp", scatter_dimension=0, tiled=True
            ).astype(jnp.float32),
        )
    attn_stack = [jnp.stack([entry[member] for entry in attn_shares]) for member in range(6)]
    mlp_stack = [jnp.stack([entry[member] for entry in mlp_shares]) for member in range(6)]
    summed = (
        lax.psum(attn_stack[0].astype(jnp.bfloat16), "seq").astype(jnp.float32),
        lax.psum(attn_stack[1].astype(jnp.bfloat16), "seq").astype(jnp.float32),
        lax.psum(attn_stack[2].astype(jnp.bfloat16), "seq").astype(jnp.float32),
        lax.psum(attn_stack[3].astype(jnp.bfloat16), "seq").astype(jnp.float32),
        lax.psum(attn_stack[4].astype(jnp.bfloat16), "seq").astype(jnp.float32),
        lax.psum(attn_stack[5].astype(jnp.bfloat16), "seq").astype(jnp.float32),
        lax.psum(mlp_stack[0].astype(jnp.bfloat16), "seq").astype(jnp.float32),
        lax.psum(mlp_stack[1].astype(jnp.bfloat16), "seq").astype(jnp.float32),
        lax.psum(mlp_stack[2].astype(jnp.bfloat16), "seq").astype(jnp.float32),
        lax.psum(mlp_stack[3].astype(jnp.bfloat16), "seq").astype(jnp.float32),
        lax.psum(mlp_stack[4].astype(jnp.bfloat16), "seq").astype(jnp.float32),
        lax.psum(mlp_stack[5].astype(jnp.bfloat16), "seq").astype(jnp.float32),
    )
    return (
        block_output,
        grad_hidden[None],
        summed[0],
        summed[1],
        summed[2],
        summed[3],
        summed[4],
        summed[5],
        summed[6],
        summed[7],
        summed[8],
        summed[9],
        summed[10],
        summed[11],
    )


def solution(mesh):
    return jax.shard_map(
        body,
        mesh=mesh,
        in_specs=(
            P("fsdp", "seq", None),
            P("fsdp", "seq", None),
            P(None, "fsdp"),
            P(None, "fsdp"),
            P(None, "fsdp", None),
            P(None, None, "fsdp"),
            P(None, "fsdp", None),
            P(None, "fsdp"),
            P(None, "fsdp"),
            P(None, "fsdp"),
            P(None, "fsdp", None),
            P(None, "fsdp"),
            P(None, "fsdp", None),
            P(None, "fsdp"),
        ),
        out_specs=(
            P("fsdp", "seq", None),
            P("fsdp", "seq", None),
            P(None, "fsdp"),
            P(None, "fsdp"),
            P(None, "fsdp", None),
            P(None, None, "fsdp"),
            P(None, "fsdp", None),
            P(None, "fsdp"),
            P(None, "fsdp"),
            P(None, "fsdp"),
            P(None, "fsdp", None),
            P(None, "fsdp"),
            P(None, "fsdp", None),
            P(None, "fsdp"),
        ),
        check_vma=False,
    )
```

profile of v0, /device:TPU:0, one launch (start us, length us, event | category | flops | bytes accessed | tf_op | source)
XLA Modules:
  0.0 1460.4 jit_solution(17177897069649028770)
XLA Ops:
  14.8 4.9 fusion.175
  28.6 26.9 %all-reduce.33 = (bf16[4304]{0:T(1024)(128)(2,1)}, bf16[1152]{0:T(1024)(128)(2,1)S(1)}, bf16[1152]{0:T(1024)(128)(2,1)S(1)}, bf16[1152]{0:T(1024)(128)(2,1)S(1)}...) all-reduce(bf16[4304]{0:T(1024)(128)(2,1)S(1)} %dynamic-update-slic, ...), channel_id=23, replica_groups=mesh['seq'=4,'fsdp'=8] {'fsdp'}, use_global_device_ids=true, to_apply=%add.12 | all-reduce | flops 21280 | bytes 85120
  55.5 12.0 all-gather.15
  67.5 9.7 all-gather.3
  77.2 18.6 %fusion.139 = (f32[1152]{0:T(1024)S(1)}, f32[1152]{0:T(1024)S(1)}) fusion(bf16[1,2,1152]{1,0,2:T(2,128)(2,1)S(1)} %all-gather.15), kind=kLoop, calls=%fused_computation.141 | loop fusion | flops 2304 | bytes 13824 | tf_op jit(solution)/shard_map/convert_element_type | solution.py:171
  95.8 18.9 %fusion.141 = (f32[1152]{0:T(1024)S(1)}, f32[1152]{0:T(1024)S(1)}) fusion(bf16[1,2,1152]{1,0,2:T(2,128)(2,1)S(1)} %all-gather.3), kind=kLoop, calls=%fused_computation.145 | loop fusion | flops 2304 | bytes 13824 | tf_op jit(solution)/shard_map/convert_element_type | solution.py:171
  115.7 4.7 fusion.41
  121.4 4.9 all-to-all-start
  127.2 9.2 all-to-all-done
  140.7 7.2 all-to-all-done.1
  148.0 14.7 %all-to-all-start.2 = ((bf16[128,4,288]{0,2,1:T(8,128)(2,1)}), bf16[128,4,288]{0,2,1:T(8,128)(2,1)S(1)}, u32[]{:S(2)}, u32[]{:S(2)}) async-start(bf16[128,4,288]{0,2,1:T(8,128)(2,1)} %bitcast.7), calls=%async_computation.2 | async-start | bytes 589824 | tf_op jit(solution)/shard_map/all_to_all | solution.py:182
  163.2 6.1 all-to-all-done.2
  174.7 3.5 all-to-all-start.3
  178.4 6.9 all-to-all-done.3
  188.0 9.2 fusion.26
  197.2 72.4 %all-gather.39.cloned.1.call-done = bf16[1,4304,1152]{2,0,1:T(2,128)(2,1)} async-done(((bf16[1,538,1152]{2,0,1:T(2,128)(2,1)}), bf16[1,4304,1152]{2,0,1:T(2,128)(2,1)}) %all-gather.39.cloned.1.call-update) | async-done | bytes 9916432 | tf_op jit(solution)/shard_map/all_gather | solution.py:197
  269.6 9.5 fusion.183
  279.3 44.6 %all-gather.41.cloned.1.call-done = bf16[1,1152,3456]{2,1,0:T(8,128)(2,1)} async-done(((bf16[1,144,3456]{2,1,0:T(8,128)(2,1)}), bf16[1,1152,3456]{2,1,0:T(8,128)(2,1)}) %all-gather.41.cloned.1.call-update) | async-done | bytes 7962640 | tf_op jit(solution)/shard_map/all_gather | solution.py:161
  324.0 4.7 fusion.38
  329.7 4.6 all-to-all-start.4
  335.2 9.1 all-to-all-done.4
  348.6 7.2 all-to-all-done.5
  359.9 6.4 all-to-all-done.6
  371.1 3.9 all-to-all-start.7
  375.1 6.5 all-to-all-done.7
  384.4 36.0 %all-gather.45.cloned.1.call-done = bf16[1,1152,4304]{2,1,0:T(8,128)(2,1)} async-done(((bf16[1,144,4304]{2,1,0:T(8,128)(2,1)}), bf16[1,1152,4304]{2,1,0:T(8,128)(2,1)}) %all-gather.45.cloned.1.call-update) | async-done | bytes 9916432 | tf_op jit(solution)/shard_map/all_gather | solution.py:195
  420.4 9.2 fusion.29
  429.6 96.1 %all-gather.47.cloned.1.call-done = bf16[1,4304,1152]{2,0,1:T(2,128)(2,1)} async-done(((bf16[1,538,1152]{2,0,1:T(2,128)(2,1)}), bf16[1,4304,1152]{2,0,1:T(2,128)(2,1)}) %all-gather.47.cloned.1.call-update) | async-done | bytes 9916432 | tf_op jit(solution)/shard_map/all_gather | solution.py:197
  525.7 11.8 fusion.185
  537.5 8.4 multiply_reduce_fusion.4
  551.2 14.6 all_to_all.280
  568.5 3.9 fusion.120
  572.4 3.7 multiply_reduce_fusion.1
  581.4 4.6 multiply_convert_fusion.1
  592.3 5.0 all-to-all-start.10
  605.8 4.1 all-to-all-start.9
  612.4 4.6 all-to-all-done.9
  617.0 6.7 multiply_reduce_fusion.6
  625.5 11.7 fusion.186
  637.2 8.3 multiply_reduce_fusion.5
  649.3 6.5 convolution_convert_fusion.4
  658.9 11.3 all_to_all.281
  674.5 4.1 all-to-all-start.15
  678.7 3.5 multiply_reduce_fusion
  688.4 5.0 all-to-all-start.14
  696.8 3.9 all-to-all-done.14
  700.7 13.3 all_to_all.282
  714.0 7.9 convolution_convert_fusion.5
  723.4 5.6 convolution_convert_fusion.2
  730.3 5.6 convolution_convert_fusion.3
  737.6 6.6 convolution_convert_fusion
  745.7 8.9 convolution_convert_fusion.1
  754.7 280.2 %fusion.170 = (bf16[544,1152]{1,0:T(8,128)(2,1)}, bf16[544,1152]{1,0:T(8,128)(2,1)}) fusion(bf16[4304,1152]{1,0:T(8,128)(2,1)} %convolution_convert_fusion, bf16[4304,1152]{1,0:T(8,128)(2,1)} %convolution_convert_fusion.1), kind=kCustom, calls=%all-reduce-scatter.2 | all-reduce-scatter fusion | flops 10027009 | bytes 22340096
  1042.2 8.3 concatenate.17
  1053.3 9.2 concatenate.16
  1073.7 23.1 %reduce-scatter.25.cloned.1.call-done = bf16[144,4304]{1,0:T(8,128)(2,1)} async-done(((bf16[1152,4304]{1,0:T(8,128)(2,1)}), bf16[144,4304]{1,0:T(8,128)(2,1)}) %reduce-scatter.25.cloned.1.call-update) | async-done | bytes 1239568 | tf_op jit(solution)/shard_map/reduce_scatter | solution.py:282
  1102.9 30.4 %reduce-scatter.31.cloned.1.call-done = bf16[144,2]{1,0:T(8,128)(2,1)} async-done(((bf16[1152,2]{1,0:T(8,128)(2,1)}), bf16[144,2]{1,0:T(8,128)(2,1)}) %reduce-scatter.31.cloned.1.call-update) | async-done | bytes 592
  1134.2 6.9 fusion.136
  1141.2 23.7 %all-reduce.32 = (bf16[1152]{0:T(1024)(128)(2,1)S(1)}, bf16[1152]{0:T(1024)(128)(2,1)S(1)}, bf16[1152]{0:T(1024)(128)(2,1)S(1)}, bf16[1152]{0:T(1024)(128)(2,1)S...) all-reduce(bf16[1152]{0:T(1024)(128)(2,1)S(1)} %dynamic-update-slic, ...), channel_id=25, replica_groups=mesh['seq'=4,'fsdp'=8] {'fsdp'}, use_global_device_ids=true, to_apply=%add.13 | all-reduce | flops 23584 | bytes 94336
  1168.6 9.5 fusion.91
  1178.9 19.4 %all-reduce.34 = (bf16[2,144]{1,0:T(2,128)(2,1)S(1)}, bf16[2,144]{1,0:T(2,128)(2,1)S(1)}, bf16[2,2,144]{2,1,0:T(2,128)(2,1)S(1)}, bf16[2,144]{1,0:T(2,128)(2,1)S...) all-reduce(bf16[2,144]{1,0:T(2,128)(2,1)S(1)} %pad_maximum_fusion.1, ...), channel_id=1, replica_groups=mesh['seq'=4,'fsdp'=8] {'seq'}, use_global_device_ids=true, to_apply=%region_26.27 | all-reduce | flops 3380 | bytes 13520 | tf_op jit(solution)/shard_map/psum | solution.py:353
  1203.0 238.7 %all-reduce.39.cloned.1.call-done = (bf16[2,538,1152]{2,1,0:T(8,128)(2,1)}, bf16[2,144,3456]{2,1,0:T(8,128)(2,1)}, bf16[2,144,1152]{2,1,0:T(8,128)(2,1)}, bf16[2,144,4304]{2,1,0:T(8,128)(2,1)}) async-done(((bf16[2,538,1152]{2,1,0:T(8,128)(2,1)}, bf16[2,144,3456]{2,1,0:T(8,128)(2,1)}, bf16[2,144,1152]{2,1,0:T(8,128)(2,1)}, bf16[2,144,4304]{2,1,0:T(8,128)(2,1)}), (bf16[2,538,1152]{2,1,0:T(8,128)(2,1)}, ...) | async-done | bytes 7612432 | tf_op jit(solution)/shard_map/psum | solution.py:363
  1441.7 3.9 convert_element_type.421
  1449.5 4.2 copy.149
  (450 shorter events, 146.3 us)
Async XLA Ops:
  7.2 108.0 %all-gather.33.cloned.1.call-start = ((), (), s32[]{:S(2)}) async-start(), calls=%async_computation.30 | async-start | bytes 8957952 | tf_op jit(solution)/shard_map/all_gather | solution.py:161
  10.3 168.1 %all-gather.35.cloned.1.call-start = ((), (), s32[]{:S(2)}) async-start(), calls=%async_computation.31 | async-start | bytes 2985984 | tf_op jit(solution)/shard_map/all_gather | solution.py:163
  11.3 176.7 %all-gather.37.cloned.1.call-start = ((), (), s32[]{:S(2)}) async-start(), calls=%async_computation.32 | async-start | bytes 11280384 | tf_op jit(solution)/shard_map/all_gather | solution.py:195
  14.8 254.8 %all-gather.39.cloned.1.call-start = ((), (), s32[]{:S(2)}) async-start(), calls=%async_computation.33 | async-start | bytes 22311936 | tf_op jit(solution)/shard_map/all_gather | solution.py:197
  19.8 304.2 %all-gather.41.cloned.1.call-start = ((), (), s32[]{:S(2)}) async-start(), calls=%async_computation.34 | async-start | bytes 8957952 | tf_op jit(solution)/shard_map/all_gather | solution.py:161
  20.5 354.6 %all-gather.43.cloned.1.call-start = ((), (), s32[]{:S(2)}) async-start(), calls=%async_computation.35 | async-start | bytes 2985984 | tf_op jit(solution)/shard_map/all_gather | solution.py:163
  21.1 399.3 %all-gather.45.cloned.1.call-start = ((), (), s32[]{:S(2)}) async-start(), calls=%async_computation.36 | async-start | bytes 11280384 | tf_op jit(solution)/shard_map/all_gather | solution.py:195
  21.8 503.9 %all-gather.47.cloned.1.call-start = ((), (), s32[]{:S(2)}) async-start(), calls=%async_computation.37 | async-start | bytes 22311936 | tf_op jit(solution)/shard_map/all_gather | solution.py:197
  22.6 92.2 %copy-start.5 = (bf16[1,128,1152]{2,1,0:T(8,128)(2,1)S(1)}, bf16[1,128,1152]{2,1,0:T(8,128)(2,1)}, u32[]{:S(2)}) copy-start(bf16[1,128,1152]{2,1,0:T(8,128)(2,1)} %param.14) | copy-start | bytes 884740
  55.5 59.7 %copy-start.41 = (f32[1152]{0:T(1024)}, f32[1152]{0:T(1024)S(1)}, u32[]{:S(2)}) copy-start(f32[1152]{0:T(1024)S(1)} %convert_element_type.473) | copy-start | bytes 13828
  55.5 59.7 %copy-start.33 = (f32[1152]{0:T(1024)}, f32[1152]{0:T(1024)S(1)}, u32[]{:S(2)}) copy-start(f32[1152]{0:T(1024)S(1)} %convert_element_type.472) | copy-start | bytes 13828
  121.4 15.0 %all-to-all-start = ((bf16[128,4,288]{0,2,1:T(8,128)(2,1)}), bf16[128,4,288]{0,2,1:T(8,128)(2,1)S(1)}, u32[]{:S(2)}, u32[]{:S(2)}) async-start(bf16[128,4,288]{0,2,1:T(8,128)(2,1)} %bitcast.3), calls=%async_computation | async-start | bytes 589824 | tf_op jit(solution)/shard_map/all_to_all | solution.py:183
  136.4 11.6 all-to-all-start.1
  148.0 21.4 %all-to-all-start.2 = ((bf16[128,4,288]{0,2,1:T(8,128)(2,1)}), bf16[128,4,288]{0,2,1:T(8,128)(2,1)S(1)}, u32[]{:S(2)}, u32[]{:S(2)}) async-start(bf16[128,4,288]{0,2,1:T(8,128)(2,1)} %bitcast.7), calls=%async_computation.2 | async-start | bytes 589824 | tf_op jit(solution)/shard_map/all_to_all | solution.py:182
  163.2 7.2 copy-start.22
  174.7 10.6 all-to-all-start.3
  178.3 9.8 copy-start.45
  178.3 145.7 %copy-start.43 = (f32[1152]{0:T(1024)}, f32[1152]{0:T(1024)S(1)}, u32[]{:S(2)}) copy-start(f32[1152]{0:T(1024)S(1)} %convert_element_type.480) | copy-start | bytes 13828
  178.3 145.7 %copy-start.35 = (f32[1152]{0:T(1024)}, f32[1152]{0:T(1024)S(1)}, u32[]{:S(2)}) copy-start(f32[1152]{0:T(1024)S(1)} %convert_element_type.479) | copy-start | bytes 13828
  187.8 9.5 copy-start.55
  188.0 9.2 copy-start.71
  279.1 44.9 %copy-start.51 = (f32[128]{0:T(128)}, f32[128]{0:T(128)S(1)}, u32[]{:S(2)}) copy-start(f32[128]{0:T(128)S(1)} %broadcast_multiply_fusion.9) | copy-start | bytes 1540
  279.3 44.7 %copy-start.67 = (f32[128]{0:T(128)}, f32[128]{0:T(128)S(1)}, u32[]{:S(2)}) copy-start(f32[128]{0:T(128)S(1)} %add_rsqrt_fusion.1) | copy-start | bytes 1540
  329.7 14.6 %all-to-all-start.4 = ((bf16[128,4,288]{0,2,1:T(8,128)(2,1)}), bf16[128,4,288]{0,2,1:T(8,128)(2,1)S(1)}, u32[]{:S(2)}, u32[]{:S(2)}) async-start(bf16[128,4,288]{0,2,1:T(8,128)(2,1)} %bitcast.16), calls=%async_computation.4 | async-start | bytes 589824 | tf_op jit(solution)/shard_map/all_to_all | solution.py:183
  344.3 11.6 all-to-all-start.5
  355.9 10.5 all-to-all-start.6
  359.9 7.5 copy-start.25
  371.1 10.6 all-to-all-start.7
  375.1 45.3 %copy-start.47 = (f32[1152]{0:T(1024)}, f32[1152]{0:T(1024)S(1)}, u32[]{:S(2)}) copy-start(f32[1152]{0:T(1024)S(1)} %convert_element_type.483) | copy-start | bytes 13828
  384.2 153.4 %copy-start.53 = (f32[128]{0:T(128)}, f32[128]{0:T(128)S(1)}, u32[]{:S(2)}) copy-start(f32[128]{0:T(128)S(1)} %broadcast_multiply_fusion.8) | copy-start | bytes 1540
  384.4 153.1 %copy-start.69 = (f32[128]{0:T(128)}, f32[128]{0:T(128)S(1)}, u32[]{:S(2)}) copy-start(f32[128]{0:T(128)S(1)} %add_rsqrt_fusion) | copy-start | bytes 1540
  384.4 141.3 %copy-start.27 = (bf16[1,128,1152]{2,1,0:T(8,128)(2,1)S(1)}, bf16[1,128,1152]{2,1,0:T(8,128)(2,1)}, u32[]{:S(2)}) copy-start(bf16[1,128,1152]{2,1,0:T(8,128)(2,1)} %param.15) | copy-start | bytes 884740
  537.5 8.5 copy-start.14
  537.5 8.5 copy-start.28
  537.5 10.0 copy-start.9
  577.9 14.4 all-to-all-start.11
  592.3 56.8 %copy-start.19 = (bf16[4,128,288]{1,2,0:T(8,128)(2,1)}, bf16[4,128,288]{1,2,0:T(8,128)(2,1)S(1)}, u32[]{:S(2)}) copy-start(bf16[4,128,288]{1,2,0:T(8,128)(2,1)S(1)} %all-to-all-done.11) | copy-start | bytes 884740
  592.3 13.5 all-to-all-start.10
  605.8 11.2 all-to-all-start.9
  609.9 458.8 %reduce-scatter.23.cloned.1.call-start = ((), (), s32[]{:S(2)}) async-start(), calls=%async_computation.27 | async-start | bytes 2985984 | tf_op jit(solution)/shard_map/reduce_scatter | solution.py:343
  612.3 456.4 %reduce-scatter.21.cloned.1.call-start = ((), (), s32[]{:S(2)}) async-start(), calls=%async_computation.26 | async-start | bytes 2985984 | tf_op jit(solution)/shard_map/reduce_scatter | solution.py:343
  624.5 20.9 %copy-start.12 = (f32[128,1152]{1,0:T(8,128)}, f32[128,1152]{1,0:T(8,128)S(1)}, u32[]{:S(2)}) copy-start(f32[128,1152]{1,0:T(8,128)S(1)} %get-tuple-element.239) | copy-start | bytes 1769476
  625.5 11.7 copy-start.56
  625.5 11.7 copy-start.72
  637.2 8.3 copy-start.16
  646.3 9.6 copy-start.11
  648.7 422.0 %reduce-scatter.19.cloned.1.call-start = ((), (), s32[]{:S(2)}) async-start(), calls=%async_computation.25 | async-start | bytes 8957952 | tf_op jit(solution)/shard_map/reduce_scatter | solution.py:337
  655.9 14.5 copy-start.38
  674.5 13.9 all-to-all-start.15
  688.4 12.3 all-to-all-start.14
  693.5 20.6 %copy-start.34 = (f32[1152]{0:T(1024)S(1)}, f32[1152]{0:T(1024)}, u32[]{:S(2)}) copy-start(f32[1152]{0:T(1024)} %copy-done.33) | copy-start | bytes 13828
  693.5 20.6 %copy-start.42 = (f32[1152]{0:T(1024)S(1)}, f32[1152]{0:T(1024)}, u32[]{:S(2)}) copy-start(f32[1152]{0:T(1024)} %copy-done.41) | copy-start | bytes 13828
  693.5 20.6 %copy-start.50 = (f32[128]{0:T(128)S(1)}, f32[128]{0:T(128)}, u32[]{:S(2)}) copy-start(f32[128]{0:T(128)} %copy-done.49) | copy-start | bytes 1540
  693.5 20.6 %copy-start.66 = (f32[128]{0:T(128)S(1)}, f32[128]{0:T(128)}, u32[]{:S(2)}) copy-start(f32[128]{0:T(128)} %copy-done.65) | copy-start | bytes 1540
  693.5 377.2 %reduce-scatter.17.cloned.1.call-start = ((), (), s32[]{:S(2)}) async-start(), calls=%async_computation.24 | async-start | bytes 8957952 | tf_op jit(solution)/shard_map/reduce_scatter | solution.py:337
  722.0 351.8 %reduce-scatter.27.cloned.1.call-start = ((), (), s32[]{:S(2)}) async-start(), calls=%async_computation.29 | async-start | bytes 11280384 | tf_op jit(solution)/shard_map/reduce_scatter | solution.py:282
  729.1 367.8 %reduce-scatter.25.cloned.1.call-start = ((), (), s32[]{:S(2)}) async-start(), calls=%async_computation.28 | async-start | bytes 11280384 | tf_op jit(solution)/shard_map/reduce_scatter | solution.py:282
  735.9 397.3 %reduce-scatter.31.cloned.1.call-start = ((), (), s32[]{:S(2)}) async-start(), calls=%async_computation.39 | async-start | bytes 331776
  1035.8 6.4 collective-permute-start.1
  1039.0 14.3 collective-permute-start
  1042.2 135.9 %reduce-scatter.29.cloned.1.call-start = ((), (), s32[]{:S(2)}) async-start(), calls=%async_computation.38 | async-start | bytes 331776
  1068.4 373.3 %all-reduce.39.cloned.1.call-start = ((), (), s32[]{:S(2)}) async-start(), calls=%async_computation.40 | async-start | bytes 15335424 | tf_op jit(solution)/shard_map/psum | solution.py:363
  1100.2 33.9 %copy-start.6 = (bf16[1,128,1152]{2,1,0:T(8,128)(2,1)S(1)}, bf16[1,128,1152]{2,1,0:T(8,128)(2,1)}, u32[]{:S(2)}) copy-start(bf16[1,128,1152]{2,1,0:T(8,128)(2,1)} %param.14) | copy-start | bytes 884740
  1134.1 7.0 copy-start.58
  (59 other events, 221.7 us)
Sparse Core Ops, SparseCore 0:
  10.4 58.0 all-gather.32
  70.4 30.2 all-gather.34
  103.1 61.3 all-gather.36
  166.8 102.7 all-gather.38
  271.4 52.5 all-gather.40
  326.3 30.2 all-gather.42
  359.0 61.3 all-gather.44
  422.8 102.7 all-gather.46
  614.8 44.1 reduce-scatter.22
  663.3 43.7 reduce-scatter.20
  710.6 80.6 reduce-scatter.18
  795.1 102.0 reduce-scatter.16
  900.8 112.9 reduce-scatter.26
  1017.7 79.1 reduce-scatter.24
  1100.3 32.8 reduce-scatter.30
  1136.2 32.8 reduce-scatter.28
  1172.7 268.8 all-reduce.38
where the time goes:
time: 1470 us; the launch traced here: 1460 us
  waiting for transfers between devices  614 us (42%)
  blocking collectives  411 us (28%)
  matrix products  182 us (12%)
  local copies, waits for them, and re-layouts  87.8 us (6%)
  other arithmetic  77.8 us (5%)
  starting transfers between devices  69.6 us (5%)
  between operations  19.1 us (1%)
    unnamed x3, blocking collectives  331 us
    psum x1, waiting for transfers between devices, body(): lax.psum(mlp_stack[4].astype(jnp.bfloat16), 'seq').astype(jnp.float32)  239 us
    all_gather x2, waiting for transfers between devices, body(): lax.all_gather(down_weight[layer_number], 'fsdp', axis=0, tiled=True)  168 us
    dot_general x8, matrix products, contract_cols(): lax.dot_general(left, right, (((1,), (1,)), ((), ())), preferred_element_...  58.3 us
    dot_general x8, matrix products, contract_rows(): lax.dot_general(left, right, (((0,), (0,)), ((), ())), preferred_element_...  45.9 us
    all_gather x2, waiting for transfers between devices, body(): lax.all_gather(qkv_weight[layer_number], 'fsdp', axis=0, tiled=True)  44.7 us
    unnamed x236, local copies, waits for them, and re-layouts  42.1 us
    convert_element_type x2, other arithmetic, body(): bias_qv[0].astype(jnp.float32)  37.5 us
  transfers between devices with their start and end apart: 32, of which 18 were waited for; matrix products, arithmetic and copies ran while one was open for 38% of the time, Pallas kernels for 0%

commit v1 on v0

v1 whole, which is shorter than its diff:
```python
import functools

import jax
import jax.numpy as jnp
from jax import lax
from jax.experimental import pallas as pl
from jax.experimental.pallas import tpu as pltpu
from jax.sharding import PartitionSpec as P

HEAD_DIM = 72
EPSILON = 1e-06
LOW = jnp.bfloat16
FULL = jnp.float32


def normalize(hidden):
    center = hidden - jnp.mean(hidden, axis=-1, keepdims=True)
    variance = jnp.mean(center * center, axis=-1, keepdims=True)
    inverse_std = lax.rsqrt(variance + EPSILON)
    return center * inverse_std, inverse_std


def normalize_back(upstream, normed, inverse_std, gain):
    scaled = upstream * gain
    grad_hidden = inverse_std * (
        scaled
        - jnp.mean(scaled, axis=-1, keepdims=True)
        - normed * jnp.mean(scaled * normed, axis=-1, keepdims=True)
    )
    return grad_hidden, jnp.sum(upstream * normed, axis=0), jnp.sum(upstream, axis=0)


def tangent_gelu(values):
    return jax.nn.gelu(values, approximate=True)


def gelu_back(values, upstream):
    return jax.vjp(tangent_gelu, values)[1](upstream)[0]


def mm(left, right):
    return jnp.dot(left, right, preferred_element_type=FULL)


def mm_rows(left, right):
    return lax.dot_general(left, right, (((0,), (0,)), ((), ())), preferred_element_type=FULL)


def mm_cols(left, right):
    return lax.dot_general(left, right, (((1,), (1,)), ((), ())), preferred_element_type=FULL)


def head_window(head, width):
    low = head * HEAD_DIM // 128 * 128
    high = min(-(-(head + 1) * HEAD_DIM // 128) * 128, width)
    return low, high


def head_mask(head, low, high):
    lane = lax.broadcasted_iota(jnp.int32, (1, high - low), 1) + low
    return (lane >= head * HEAD_DIM) & (lane < (head + 1) * HEAD_DIM)


def attend_forward_kernel(qkv_ref, o_ref, lse_ref, acc_ref):
    tokens, width = o_ref.shape
    rows = min(256, tokens)
    scaling = HEAD_DIM ** (-0.5)
    acc_ref[...] = jnp.zeros_like(acc_ref)
    for head in range(width // HEAD_DIM):
        low, high = head_window(head, width)
        mask = head_mask(head, low, high)
        keys = qkv_ref[1, :, low:high]
        values = jnp.where(mask, qkv_ref[2, :, low:high], jnp.zeros((), LOW))
        for start in range(0, tokens, rows):
            queries = jnp.where(mask, qkv_ref[0, start : start + rows, low:high], jnp.zeros((), LOW))
            scores = mm_cols(queries, keys) * scaling
            peak = jnp.max(scores, axis=-1, keepdims=True)
            total = jnp.sum(jnp.exp(scores - peak), axis=-1, keepdims=True)
            lse = peak + jnp.log(total)
            probability = jnp.exp(scores - lse).astype(LOW)
            acc_ref[start : start + rows, low:high] += mm(probability, values)
            lse_ref[start : start + rows, head : head + 1] = lse
    o_ref[...] = acc_ref[...].astype(LOW)


def attend_forward(qkv):
    _, tokens, width = qkv.shape
    heads = width // HEAD_DIM
    return pl.pallas_call(
        attend_forward_kernel,
        out_shape=(
            jax.ShapeDtypeStruct((tokens, width), LOW),
            jax.ShapeDtypeStruct((tokens, heads), FULL),
        ),
        in_specs=[pl.BlockSpec(memory_space=pltpu.VMEM)],
        out_specs=(pl.BlockSpec(memory_space=pltpu.VMEM),) * 2,
        scratch_shapes=[pltpu.VMEM((tokens, width), FULL)],
        compiler_params=pltpu.CompilerParams(vmem_limit_bytes=40 << 20),
        cost_estimate=pl.CostEstimate(
            flops=4 * heads * tokens * tokens * 128,
            transcendentals=2 * heads * tokens * tokens,
            bytes_accessed=8 * tokens * width,
        ),
        name="attend_forward",
    )(qkv)


def attend_backward_kernel(qkv_ref, do_ref, lse_ref, grad_ref, dq_ref, dk_ref, dv_ref):
    tokens, width = do_ref.shape
    rows = min(256, tokens)
    scaling = HEAD_DIM ** (-0.5)
    for ref in (dq_ref, dk_ref, dv_ref):
        ref[...] = jnp.zeros_like(ref)
    zero = jnp.zeros((), LOW)
    for head in range(width // HEAD_DIM):
        low, high = head_window(head, width)
        mask = head_mask(head, low, high)
        keys = qkv_ref[1, :, low:high]
        values = qkv_ref[2, :, low:high]
        keys_masked = jnp.where(mask, keys, zero)
        for start in range(0, tokens, rows):
            span = slice(start, start + rows)
            queries = jnp.where(mask, qkv_ref[0, span, low:high], zero)
            upstream = jnp.where(mask, do_ref[span, low:high], zero)
            scores = mm_cols(queries, keys) * scaling
            probability = jnp.exp(scores - lse_ref[span, head : head + 1])
            grad_prob = mm_cols(upstream, values)
            inner = jnp.sum(probability * grad_prob, axis=-1, keepdims=True)
            grad_scores = (probability * (grad_prob - inner)).astype(LOW)
            dv_ref[:, low:high] += mm_rows(probability.astype(LOW), upstream)
            dk_ref[:, low:high] += mm_rows(grad_scores, queries)
            dq_ref[span, low:high] += mm(grad_scores, keys_masked)
    grad_ref[0] = (dq_ref[...] * scaling).astype(LOW)
    grad_ref[1] = (dk_ref[...] * scaling).astype(LOW)
    grad_ref[2] = dv_ref[...].astype(LOW)


def attend_backward(qkv, upstream, lse):
    _, tokens, width = qkv.shape
    heads = width // HEAD_DIM
    return pl.pallas_call(
        attend_backward_kernel,
        out_shape=jax.ShapeDtypeStruct((3, tokens, width), LOW),
        in_specs=[pl.BlockSpec(memory_space=pltpu.VMEM)] * 3,
        out_specs=pl.BlockSpec(memory_space=pltpu.VMEM),
        scratch_shapes=[pltpu.VMEM((tokens, width), FULL)] * 3,
        compiler_params=pltpu.CompilerParams(vmem_limit_bytes=48 << 20),
        cost_estimate=pl.CostEstimate(
            flops=10 * heads * tokens * tokens * 128,
            transcendentals=heads * tokens * tokens,
            bytes_accessed=14 * tokens * width,
        ),
        name="attend_backward",
    )(qkv, upstream, lse)


def make_body(ranks, owners):
    pairs = ranks // 2

    def shift(value, step):
        return lax.ppermute(value, "seq", [(i, (i + step) % ranks) for i in range(ranks)])

    def swap(value):
        return lax.ppermute(value, "seq", [(i, i ^ 1) for i in range(ranks)])

    def pair_shift(value, step):
        return lax.ppermute(value, "seq", [(i, (i + 2 * step) % ranks) for i in range(ranks)])

    def gather_tokens(mine):
        return jnp.concatenate([mine] + [shift(mine, j) for j in range(1, ranks)], axis=0)

    def body(
        block_input,
        grad_output,
        attn_norm_gain,
        attn_norm_bias,
        qkv_weight,
        qv_bias,
        out_weight,
        out_bias,
        mlp_norm_gain,
        mlp_norm_bias,
        up_weight,
        up_bias,
        down_weight,
        down_bias,
    ):
        layers = qkv_weight.shape[0]
        tokens, width = block_input.shape[1:]
        slab = width // ranks
        part = qkv_weight.shape[1]
        hidden_part = down_weight.shape[1]
        half = -(-hidden_part // 32) * 16
        me = lax.axis_index("seq")
        side = me % 2
        pair = me // 2

        def rank_at(j):
            return (me + j) % ranks

        def by_fsdp(value):
            return lax.all_gather(value, "fsdp", axis=0, tiled=True)

        def qkv_share(layer):
            blocks = qkv_weight[layer].reshape(part, 3, width)
            return lax.dynamic_slice(blocks, (0, 0, me * slab), (part, 3, slab)).reshape(part, 3 * slab)

        def up_share(layer):
            blocks = jnp.pad(
                up_weight[layer].reshape(part, owners, hidden_part),
                ((0, 0), (0, 0), (0, 2 * half - hidden_part)),
            )
            return lax.dynamic_slice(blocks, (0, 0, side * half), (part, owners, half)).reshape(
                part, owners * half
            )

        def down_share(layer):
            padded = jnp.pad(down_weight[layer], ((0, 2 * half - hidden_part), (0, 0)))
            return lax.dynamic_slice(padded, (side * half, 0), (half, width))

        up_rows = -(-hidden_part // part)
        small = []
        for layer in range(layers):
            small += [
                attn_norm_gain[layer],
                attn_norm_bias[layer],
                qv_bias[layer, 0],
                qv_bias[layer, 1],
                out_bias[layer],
                mlp_norm_gain[layer],
                mlp_norm_bias[layer],
                down_bias[layer],
            ]
            padded = jnp.pad(up_bias[layer], (0, up_rows * part - hidden_part))
            small += [padded[i * part : (i + 1) * part] for i in range(up_rows)]
        per_layer = 8 + up_rows
        small = jnp.stack(small, axis=1)

        gathered = []
        for layer in range(layers):
            pieces = [out_weight[layer], qkv_share(layer)]
            if layer == 0:
                pieces.append(small)
            attn = by_fsdp(jnp.concatenate(pieces, axis=1))
            gathered.append((attn, by_fsdp(up_share(layer)), by_fsdp(down_share(layer))))
        small_all = gathered[0][0][:, width + 3 * slab :].T.astype(FULL)

        vectors = []
        for layer in range(layers):
            rows = small_all[layer * per_layer : (layer + 1) * per_layer]
            up_all = rows[8:].reshape(up_rows, owners, part).transpose(1, 0, 2).reshape(owners, up_rows * part)
            up_all = jnp.pad(up_all[:, :hidden_part], ((0, 0), (0, 2 * half - hidden_part)))
            up_half = lax.dynamic_slice(up_all, (0, side * half), (owners, half)).reshape(owners * half)
            q_mine = lax.dynamic_slice(rows[2], (me * slab,), (slab,))
            v_mine = lax.dynamic_slice(rows[3], (me * slab,), (slab,))
            vectors.append(
                dict(
                    gain_one=rows[0],
                    bias_one=rows[1],
                    bias_q=q_mine,
                    bias_v=v_mine,
                    bias_out=rows[4],
                    gain_two=rows[5],
                    bias_two=rows[6],
                    bias_down=rows[7],
                    bias_up=up_half,
                )
            )

        hidden = block_input[0].astype(FULL)
        all_input = gather_tokens(block_input[0])
        stored = []
        for layer in range(layers):
            v = vectors[layer]
            attn, proj_up, proj_down = gathered[layer]
            proj_out = attn[:, :width].reshape(ranks, slab, width)
            proj_qkv = attn[:, width : width + 3 * slab]
            normed_one, inverse_one = normalize(hidden)
            if layer == 0:
                normed_all, _ = normalize(all_input.astype(FULL))
                attn_in = (normed_all * v["gain_one"] + v["bias_one"]).astype(LOW)
            else:
                attn_in = gather_tokens((normed_one * v["gain_one"] + v["bias_one"]).astype(LOW))
            bias_row = jnp.concatenate([v["bias_q"], jnp.zeros((slab,), FULL), v["bias_v"]])
            projected = (mm(attn_in, proj_qkv) + bias_row).astype(LOW)
            qkv = jnp.stack([projected[:, i * slab : (i + 1) * slab] for i in range(3)])
            out_heads, lse = attend_forward(qkv)
            attended = jnp.zeros((ranks, tokens, slab), LOW)
            for j in range(ranks):
                piece = out_heads[j * tokens : (j + 1) * tokens]
                piece = shift(piece, -j) if j else piece
                attended = lax.dynamic_update_slice(attended, piece[None], (rank_at(j), 0, 0))
            after_attn = (
                hidden
                + lax.dot_general(
                    attended, proj_out, (((0, 2), (0, 1)), ((), ())), preferred_element_type=FULL
                )
                + v["bias_out"]
            )
            normed_two, inverse_two = normalize(after_attn)
            mlp_mine = (normed_two * v["gain_two"] + v["bias_two"]).astype(LOW)
            mlp_in = jnp.concatenate([mlp_mine, swap(mlp_mine)], axis=0)
            pre_act = mm(mlp_in, proj_up) + v["bias_up"]
            activated = tangent_gelu(pre_act).astype(LOW)
            mixed = mm(activated, proj_down)
            other = swap(mixed[tokens:].astype(LOW))
            hidden = after_attn + mixed[:tokens] + other.astype(FULL) + v["bias_down"]
            stored.append(
                (normed_one, inverse_one, attn_in, qkv, lse, attended, normed_two, inverse_two, mlp_in, pre_act, activated)
            )
        block_output = hidden.astype(LOW)[None]

        def scatter(value):
            return lax.psum_scatter(value.astype(LOW), "fsdp", scatter_dimension=0, tiled=True)

        def sum_ranks(value):
            blocks = value.reshape((ranks, value.shape[0] // ranks) + value.shape[1:])
            mine = lax.dynamic_index_in_dim(blocks, me, 0, keepdims=False).astype(FULL)
            for j in range(1, ranks):
                mine += shift(lax.dynamic_index_in_dim(blocks, rank_at(j), 0, keepdims=False), j).astype(FULL)
            return gather_ranks(mine.astype(LOW)).reshape(value.shape)

        def gather_ranks(mine):
            result = jnp.zeros((ranks,) + mine.shape, mine.dtype)
            for j in range(ranks):
                piece = shift(mine, j) if j else mine
                result = lax.dynamic_update_slice(result, piece[None], (rank_at(-j),) + (0,) * mine.ndim)
            return result

        def sum_pairs(value):
            count = value.shape[0] // pairs
            blocks = value.reshape((pairs, count) + value.shape[1:])
            mine = lax.dynamic_index_in_dim(blocks, pair, 0, keepdims=False).astype(FULL)
            for j in range(1, pairs):
                mine += pair_shift(
                    lax.dynamic_index_in_dim(blocks, (pair + j) % pairs, 0, keepdims=False), j
                ).astype(FULL)
            mine = mine.astype(LOW)
            result = jnp.zeros((pairs,) + mine.shape, LOW)
            for j in range(pairs):
                piece = pair_shift(mine, j) if j else mine
                result = lax.dynamic_update_slice(
                    result, piece[None], ((pair - j) % pairs,) + (0,) * mine.ndim
                )
            result = result.reshape(value.shape)
            other = swap(result)
            first = side == 0
            return jnp.where(first, result, other), jnp.where(first, other, result)

        grad_hidden = grad_output[0].astype(FULL)
        weight_grads = [None] * layers
        small_grads = [None] * layers
        for layer in reversed(range(layers)):
            v = vectors[layer]
            attn, proj_up, proj_down = gathered[layer]
            proj_out = attn[:, :width].reshape(ranks, slab, width)
            proj_qkv = attn[:, width : width + 3 * slab]
            normed_one, inverse_one, attn_in, qkv, lse, attended, normed_two, inverse_two, mlp_in, pre_act, activated = stored[layer]
            grad_mine = grad_hidden.astype(LOW)
            grad_low = jnp.concatenate([grad_mine, swap(grad_mine)], axis=0)
            g_down_bias = jnp.sum(grad_hidden, axis=0)
            grad_pre = gelu_back(pre_act, mm_cols(grad_low, proj_down))
            g_up_bias = jnp.sum(grad_pre, axis=0)
            grad_pre_low = grad_pre.astype(LOW)
            mixed = mm_cols(grad_pre_low, proj_up)
            grad_mid = mixed[:tokens] + swap(mixed[tokens:].astype(LOW)).astype(FULL)
            g_down = scatter(mm_rows(activated, grad_low))
            g_up = scatter(mm_rows(mlp_in, grad_pre_low))
            grad_norm_two, g_gain_two, g_bias_two = normalize_back(
                grad_mid, normed_two, inverse_two, v["gain_two"]
            )
            grad_after = grad_hidden + grad_norm_two
            g_out_bias = jnp.sum(grad_after, axis=0)
            after_low = grad_after.astype(LOW)
            grad_attended = lax.dot_general(
                proj_out, after_low, (((2,), (1,)), ((), ())), preferred_element_type=FULL
            )
            grad_attended = grad_attended.astype(LOW).transpose(0, 2, 1)
            grad_heads = jnp.concatenate(
                [lax.dynamic_index_in_dim(grad_attended, me, 0, keepdims=False)]
                + [
                    shift(lax.dynamic_index_in_dim(grad_attended, rank_at(j), 0, keepdims=False), j)
                    for j in range(1, ranks)
                ],
                axis=0,
            )
            g_out = scatter(
                lax.dot_general(
                    attended, after_low, (((1,), (0,)), ((), ())), preferred_element_type=FULL
                ).reshape(width, width)
            )
            grad_qkv = attend_backward(qkv, grad_heads, lse)
            grad_proj = jnp.concatenate([grad_qkv[i] for i in range(3)], axis=1)
            partial_in = mm_cols(grad_proj, proj_qkv)
            grad_in = partial_in[:tokens]
            for j in range(1, ranks):
                grad_in += shift(partial_in[j * tokens : (j + 1) * tokens].astype(LOW), -j).astype(FULL)
            g_qkv = scatter(mm_rows(attn_in, grad_proj))
            g_q_bias = jnp.sum(grad_qkv[0].astype(FULL), axis=0)
            g_v_bias = jnp.sum(grad_qkv[2].astype(FULL), axis=0)
            grad_norm_one, g_gain_one, g_bias_one = normalize_back(
                grad_in, normed_one, inverse_one, v["gain_one"]
            )
            grad_hidden = grad_after + grad_norm_one

            down_halves = sum_pairs(g_down)
            g_down = jnp.concatenate(down_halves, axis=0)[:hidden_part]
            up_halves = sum_pairs(g_up)
            g_up = jnp.concatenate(
                [u.reshape(part, owners, half) for u in up_halves], axis=2
            )[:, :, :hidden_part].reshape(part, owners * hidden_part)
            g_out = sum_ranks(g_out)
            g_qkv = gather_ranks(g_qkv).reshape(ranks, part, 3, slab).transpose(1, 2, 0, 3).reshape(part, 3 * width)
            weight_grads[layer] = tuple(g.astype(FULL) for g in (g_qkv, g_out, g_up, g_down))

            zeros = jnp.zeros((width,), FULL)
            q_row = lax.dynamic_update_slice(zeros, g_q_bias, (me * slab,))
            v_row = lax.dynamic_update_slice(zeros, g_v_bias, (me * slab,))
            up_row = lax.dynamic_update_slice(
                jnp.zeros((owners, 2 * half), FULL), g_up_bias.reshape(owners, half), (0, side * half)
            )
            rows = jnp.stack(
                [g_gain_one, g_bias_one, q_row, v_row, g_out_bias, g_gain_two, g_bias_two, g_down_bias]
            )
            rows = rows.reshape(8, owners, part).transpose(1, 0, 2).reshape(owners, 8 * part)
            small_grads[layer] = jnp.concatenate([rows, up_row], axis=1)

        small_sum = jnp.concatenate(small_grads, axis=1)
        small_sum = jnp.pad(small_sum, ((0, 0), (0, -small_sum.shape[1] % 128)))
        small_sum = jnp.sum(
            lax.all_to_all(small_sum, "fsdp", split_axis=0, concat_axis=0, tiled=True), axis=0
        )
        total = small_sum
        for j in range(1, ranks):
            total = total + shift(small_sum, j)
        each = 8 * part + 2 * half
        small_out = [[] for _ in range(9)]
        for layer in range(layers):
            mine = total[layer * each : (layer + 1) * each]
            rows = mine[: 8 * part].reshape(8, part)
            for i in range(8):
                small_out[i].append(rows[i])
            small_out[8].append(mine[8 * part : 8 * part + hidden_part])
        s = [jnp.stack(entry) for entry in small_out]
        w = [jnp.stack([weight_grads[layer][i] for layer in range(layers)]) for i in range(4)]
        return (
            block_output,
            grad_hidden[None],
            s[0],
            s[1],
            w[0],
            jnp.stack([s[2], s[3]], axis=1),
            w[1],
            s[4],
            s[5],
            s[6],
            w[2],
            s[8],
            w[3],
            s[7],
        )

    return body


def solution(mesh):
    row, cols, deep = P(None, "fsdp"), P("fsdp", "seq", None), P(None, "fsdp", None)
    last = P(None, None, "fsdp")
    return jax.shard_map(
        make_body(mesh.shape["seq"], mesh.shape["fsdp"]),
        mesh=mesh,
        in_specs=(cols, cols, row, row, deep, last, deep, row, row, row, deep, row, deep, row),
        out_specs=(cols, cols, row, row, deep, last, deep, row, row, row, deep, row, deep, row),
        check_vma=False,
    )
```

time: 1470 us -> 839 us (0.57)
  blocking collectives: 411 us -> 0 us
  waiting for transfers between devices: 614 us -> 444 us
  matrix products: 182 us -> 94.3 us
  starting transfers between devices: 69.6 us -> 105 us
  other arithmetic: 77.8 us -> 42.7 us
  local copies, waits for them, and re-layouts: 87.8 us -> 112 us
  Pallas kernels: 0 us -> 17 us
    unnamed x3 -> x0, blocking collectives: 331 us -> none
    psum x1 -> x0, waiting for transfers between devices: 239 us -> none  [body(): lax.psum(mlp_stack[4].astype(jnp.bfloat16), 'seq').astype(jnp.float32)]
    ppermute x0 -> x65, waiting for transfers between devices: none -> 234 us  [the longest x45 115 us: shift(): lax.ppermute(value, 'seq', [(i, (i + step) % ranks) for i in range(ranks)])]
    all_gather x8 -> x6, waiting for transfers between devices: 249 us -> 94.3 us  [by_fsdp(): return lax.all_gather(value, 'fsdp', axis=0, tiled=True)]
    ppermute x0 -> x65, starting transfers between devices: none -> 99.9 us  [the longest x45 72.1 us: shift(): lax.ppermute(value, 'seq', [(i, (i + step) % ranks) for i in range(ranks)])]
    dot_general x36 -> x24, matrix products: 182 us -> 94.3 us  [the longest x6 30.9 us: mm_cols(): lax.dot_general(left, right, (((1,), (1,)), ((), ())), preferred_element_...]
    reduce_scatter x6 -> x8, waiting for transfers between devices: 23.1 us -> 110 us  [scatter(): lax.psum_scatter(value.astype(LOW), 'fsdp', scatter_dimension=0, tiled=True)]
    all_to_all x13 -> x1, waiting for transfers between devices: 69.5 us -> 5.23 us  [body(): lax.all_to_all(small_sum, 'fsdp', split_axis=0, concat_axis=0, tiled=True)]
  transfers between devices with their start and end apart: 32 -> 80, of which waited for: 18 -> 45; matrix products, arithmetic and copies ran while one was open for 38% -> 24% of each run, Pallas kernels for 0% -> 1%
where the time goes in v1:
time: 839 us; the launch traced here: 831 us
  waiting for transfers between devices  444 us (53%)
  local copies, waits for them, and re-layouts  112 us (13%)
  starting transfers between devices  105 us (13%)
  matrix products  94.3 us (11%)
  other arithmetic  42.7 us (5%)
  Pallas kernels  17 us (2%)
  between operations  16.9 us (2%)
    ppermute x45, waiting for transfers between devices, shift(): lax.ppermute(value, 'seq', [(i, (i + step) % ranks) for i in range(ranks)])  115 us
    reduce_scatter x8, waiting for transfers between devices, scatter(): lax.psum_scatter(value.astype(LOW), 'fsdp', scatter_dimension=0, tiled=True)  110 us
    all_gather x6, waiting for transfers between devices, by_fsdp(): return lax.all_gather(value, 'fsdp', axis=0, tiled=True)  94.3 us
    ppermute x45, starting transfers between devices, shift(): lax.ppermute(value, 'seq', [(i, (i + step) % ranks) for i in range(ranks)])  72.1 us
    ppermute x8, waiting for transfers between devices, pair_shift(): lax.ppermute(value, 'seq', [(i, (i + 2 * step) % ranks) for i in range(ra...  70.8 us
    ppermute x12, waiting for transfers between devices, swap(): return lax.ppermute(value, 'seq', [(i, i ^ 1) for i in range(ranks)])  48.5 us
    dot_general x6, matrix products, mm_cols(): lax.dot_general(left, right, (((1,), (1,)), ((), ())), preferred_element_...  30.9 us
    dot_general x6, matrix products, mm_rows(): lax.dot_general(left, right, (((0,), (0,)), ((), ())), preferred_element_...  26.8 us
  transfers between devices with their start and end apart: 80, of which 45 were waited for; matrix products, arithmetic and copies ran while one was open for 24% of the time, Pallas kernels for 1%

profile of v1, /device:TPU:0, one launch (start us, length us, event | category | flops | bytes accessed | tf_op | source)
XLA Modules:
  0.0 830.8 jit_solution(2776664857330721330)
XLA Ops:
  29.7 4.4 fusion.121
  42.3 5.0 collective-permute-start.2
  54.7 17.6 %collective-permute-done.1 = bf16[128,1152]{1,0:T(8,128)(2,1)S(1)} collective-permute-done((bf16[128,1152]{1,0:T(8,128)(2,1)S(1)}, bf16[128,1152]{1,0:T(8,128)(2,1)S(1)}, u32[]{:S(2)}, u32[]{:S(2)}) %collective-permute-start.1) | collective-permute-done | bytes 294944 | tf_op jit(solution)/shard_map/ppermute | solution.py:161
  74.2 4.7 slice_reduce_fusion
  83.8 3.4 attend_forward.2
  93.2 3.5 slice.623
  106.4 4.4 collective-permute-done.6
  110.8 6.1 convolution_add_fusion.1
  116.9 28.9 %all-gather.11.cloned.1.call-done = bf16[2176,1152]{1,0:T(8,128)(2,1)} async-done(((bf16[272,1152]{1,0:T(8,128)(2,1)}), bf16[2176,1152]{1,0:T(8,128)(2,1)}) %all-gather.11.cloned.1.call-update) | async-done | bytes 5013520 | tf_op jit(solution)/shard_map/all_gather | solution.py:202
  145.7 4.9 fusion.105
  152.2 7.7 collective-permute-done.7
  160.5 3.4 collective-permute-start.10
  165.0 21.4 %all-gather.13.cloned.1.call-done = bf16[1152,2016]{1,0:T(8,128)(2,1)} async-done(((bf16[144,2016]{1,0:T(8,128)(2,1)}), bf16[1152,2016]{1,0:T(8,128)(2,1)}) %all-gather.13.cloned.1.call-update) | async-done | bytes 4644880 | tf_op jit(solution)/shard_map/all_gather | solution.py:202
  186.4 3.5 slice.640
  193.9 3.4 attend_forward.3
  198.2 3.4 collective-permute-start.11
  206.8 4.6 collective-permute-done.12
  221.2 7.7 all-gather.15.cloned.1.call-done
  228.9 5.5 convolution_add_fusion
  234.5 36.4 %all-gather.17.cloned.1.call-done = bf16[2176,1152]{1,0:T(8,128)(2,1)} async-done(((bf16[272,1152]{1,0:T(8,128)(2,1)}), bf16[2176,1152]{1,0:T(8,128)(2,1)}) %all-gather.17.cloned.1.call-update) | async-done | bytes 5013520 | tf_op jit(solution)/shard_map/all_gather | solution.py:202
  270.9 6.0 fusion.135
  276.9 4.6 fusion.65
  285.6 5.9 collective-permute-done.17
  292.3 4.8 collective-permute-done.15
  300.9 3.4 collective-permute-start.20
  307.5 5.3 collective-permute-done.19
  312.9 5.1 attend_backward.2
  322.4 3.4 fusion.132
  331.1 6.8 collective-permute-done.23
  337.8 11.3 %collective-permute-done.22 = bf16[128,1152]{1,0:T(8,128)(2,1)S(1)} collective-permute-done((bf16[128,1152]{1,0:T(8,128)(2,1)S(1)}, bf16[128,1152]{1,0:T(8,128)(2,1)S(1)}, u32[]{:S(2)}, u32[]{:S(2)}) %collective-permute-start.22) | collective-permute-done | bytes 294944 | tf_op jit(solution)/shard_map/ppermute | solution.py:161
  351.0 6.0 collective-permute-start.24
  359.6 3.7 collective-permute-done.24
  363.2 7.1 fusion.134
  370.4 4.8 fusion.62
  377.0 5.4 collective-permute-done.25
  394.8 5.1 attend_backward.3
  408.8 5.3 convolution_convert_fusion.2
  414.1 6.1 convolution_convert_fusion
  420.3 5.4 convolution_convert_fusion.3
  430.3 5.0 fusion.133
  439.4 4.3 convolution_convert_fusion.1
  447.2 7.9 collective-permute-done.30
  461.5 5.2 all-to-all-done
  466.8 6.0 collective-permute-start.34
  485.0 3.5 collective-permute-start.40
  489.6 5.1 collective-permute-done.38
  494.8 8.0 collective-permute-done.39
  504.6 4.5 collective-permute-start.49
  524.6 12.5 %collective-permute-done.50 = bf16[36,1152]{1,0:T(8,128)(2,1)S(1)} collective-permute-done((bf16[36,1152]{1,0:T(8,128)(2,1)S(1)}, bf16[36,1152]{1,0:T(8,128)(2,1)S(1)}, u32[]{:S(2)}, u32[]{:S(2)}) %collective-permute-start.50) | collective-permute-done | bytes 82976 | tf_op jit(solution)/shard_map/ppermute | solution.py:161
  537.1 8.4 %collective-permute-done.51 = bf16[36,1152]{1,0:T(8,128)(2,1)S(1)} collective-permute-done((bf16[36,1152]{1,0:T(8,128)(2,1)S(1)}, bf16[36,1152]{1,0:T(8,128)(2,1)S(1)}, u32[]{:S(2)}, u32[]{:S(2)}) %collective-permute-start.51) | collective-permute-done | bytes 82976 | tf_op jit(solution)/shard_map/ppermute | solution.py:161
  563.7 3.4 maximum_convert_fusion.2
  575.5 4.6 collective-permute-start.56
  581.3 40.9 %reduce-scatter.23.cloned.1.call-done = bf16[272,1152]{1,0:T(8,128)(2,1)} async-done(((bf16[2176,1152]{1,0:T(8,128)(2,1)}), bf16[272,1152]{1,0:T(8,128)(2,1)}) %reduce-scatter.23.cloned.1.call-update) | async-done | bytes 626704 | tf_op jit(solution)/shard_map/reduce_scatter | solution.py:314
  626.5 21.3 %collective-permute-done.62 = bf16[136,1152]{1,0:T(8,128)(2,1)S(1)} collective-permute-done((bf16[136,1152]{1,0:T(8,128)(2,1)S(1)}, bf16[136,1152]{1,0:T(8,128)(2,1)S(1)}, u32[]{:S(2)}, u32[]{:S(2)}) %collective-permute-start.62) | collective-permute-done | bytes 313376 | tf_op jit(solution)/shard_map/ppermute | solution.py:167
  649.5 11.7 %collective-permute-done.57 = bf16[72,2176]{1,0:T(8,128)(2,1)S(1)} collective-permute-done((bf16[72,2176]{1,0:T(8,128)(2,1)S(1)}, bf16[72,2176]{1,0:T(8,128)(2,1)S(1)}, u32[]{:S(2)}, u32[]{:S(2)}) %collective-permute-start.57) | collective-permute-done | bytes 313376 | tf_op jit(solution)/shard_map/ppermute | solution.py:167
  661.4 5.7 collective-permute-done.63
  668.2 13.3 %reduce-scatter.17.cloned.1.call-done = bf16[144,2176]{1,0:T(8,128)(2,1)} async-done(((bf16[1152,2176]{1,0:T(8,128)(2,1)}), bf16[144,2176]{1,0:T(8,128)(2,1)}) %reduce-scatter.17.cloned.1.call-update) | async-done | bytes 626704 | tf_op jit(solution)/shard_map/reduce_scatter | solution.py:314
  685.6 55.4 %reduce-scatter.21.cloned.1.call-done = bf16[272,1152]{1,0:T(8,128)(2,1)} async-done(((bf16[2176,1152]{1,0:T(8,128)(2,1)}), bf16[272,1152]{1,0:T(8,128)(2,1)}) %reduce-scatter.21.cloned.1.call-update) | async-done | bytes 626704 | tf_op jit(solution)/shard_map/reduce_scatter | solution.py:314
  753.2 14.3 %collective-permute-done.59 = bf16[136,1152]{1,0:T(8,128)(2,1)} collective-permute-done((bf16[136,1152]{1,0:T(8,128)(2,1)}, bf16[136,1152]{1,0:T(8,128)(2,1)}, u32[]{:S(2)}, u32[]{:S(2)}) %collective-permute-start.59) | collective-permute-done | bytes 313376 | tf_op jit(solution)/shard_map/ppermute | solution.py:167
  768.7 12.1 %collective-permute-done.54 = bf16[72,2176]{1,0:T(8,128)(2,1)S(1)} collective-permute-done((bf16[72,2176]{1,0:T(8,128)(2,1)S(1)}, bf16[72,2176]{1,0:T(8,128)(2,1)S(1)}, u32[]{:S(2)}, u32[]{:S(2)}) %collective-permute-start.54) | collective-permute-done | bytes 313376 | tf_op jit(solution)/shard_map/ppermute | solution.py:167
  781.0 5.6 collective-permute-done.60
  787.1 12.9 %collective-permute-done.55 = bf16[144,2176]{1,0:T(8,128)(2,1)S(1)} collective-permute-done((bf16[144,2176]{1,0:T(8,128)(2,1)S(1)}, bf16[144,2176]{1,0:T(8,128)(2,1)S(1)}, u32[]{:S(2)}, u32[]{:S(2)}) %collective-permute-start.55) | collective-permute-done | bytes 626720 | tf_op jit(solution)/shard_map/ppermute | solution.py:164
  809.7 3.8 collective-permute-done.61
  815.1 6.1 copy.172
  (651 shorter events, 247.2 us)
Async XLA Ops:
  7.2 65.9 %all-gather.7.cloned.1.call-start = ((), (), s32[]{:S(2)}) async-start(), calls=%async_computation.9 | async-start | bytes 5308416 | tf_op jit(solution)/shard_map/all_gather | solution.py:202
  18.7 92.1 %all-gather.9.cloned.1.call-start = ((), (), s32[]{:S(2)}) async-start(), calls=%async_computation.10 | async-start | bytes 5640192 | tf_op jit(solution)/shard_map/all_gather | solution.py:202
  29.7 116.0 %all-gather.11.cloned.1.call-start = ((), (), s32[]{:S(2)}) async-start(), calls=%async_computation.11 | async-start | bytes 5640192 | tf_op jit(solution)/shard_map/all_gather | solution.py:202
  35.3 151.1 %all-gather.13.cloned.1.call-start = ((), (), s32[]{:S(2)}) async-start(), calls=%async_computation.12 | async-start | bytes 5308416 | tf_op jit(solution)/shard_map/all_gather | solution.py:202
  38.3 190.7 %all-gather.15.cloned.1.call-start = ((), (), s32[]{:S(2)}) async-start(), calls=%async_computation.13 | async-start | bytes 5640192 | tf_op jit(solution)/shard_map/all_gather | solution.py:202
  42.2 228.7 %all-gather.17.cloned.1.call-start = ((), (), s32[]{:S(2)}) async-start(), calls=%async_computation.14 | async-start | bytes 5640192 | tf_op jit(solution)/shard_map/all_gather | solution.py:202
  42.3 12.5 %collective-permute-start.2 = (bf16[128,1152]{1,0:T(8,128)(2,1)S(1)}, bf16[128,1152]{1,0:T(8,128)(2,1)S(1)}, u32[]{:S(2)}, u32[]{:S(2)}) collective-permute-start(bf16[128,1152]{1,0:T(8,128)(2,1)S(1)} %bitcast.339), channel_id=1, source_target_pairs={{0,24},{8,0},{16,8},{24,16},{1,25},{9,1},{17,9},{25,17},{2,26},{10... | collective-permute-start | bytes 884744 | tf_op jit(solution)/shard_map/ppermute | solution.py:161
  47.3 25.1 %collective-permute-start.1 = (bf16[128,1152]{1,0:T(8,128)(2,1)S(1)}, bf16[128,1152]{1,0:T(8,128)(2,1)S(1)}, u32[]{:S(2)}, u32[]{:S(2)}) collective-permute-start(bf16[128,1152]{1,0:T(8,128)(2,1)S(1)} %bitcast.340), channel_id=1, source_target_pairs={{0,16},{8,24},{16,0},{24,8},{1,17},{9,25},{17,1},{25,9},{2,18},{10... | collective-permute-start | bytes 884744 | tf_op jit(solution)/shard_map/ppermute | solution.py:161
  47.3 25.1 %collective-permute-start = (bf16[128,1152]{1,0:T(8,128)(2,1)S(1)}, bf16[128,1152]{1,0:T(8,128)(2,1)S(1)}, u32[]{:S(2)}, u32[]{:S(2)}) collective-permute-start(bf16[128,1152]{1,0:T(8,128)(2,1)S(1)} %bitcast.341), channel_id=1, source_target_pairs={{0,8},{8,16},{16,24},{24,0},{1,9},{9,17},{17,25},{25,1},{2,10},{10... | collective-permute-start | bytes 884744 | tf_op jit(solution)/shard_map/ppermute | solution.py:161
  51.3 432.3 %reduce-scatter.11.cloned.1.call-start = ((), (), s32[]{:S(2)}) async-start(), calls=%async_computation.16 | async-start | bytes 2322432 | tf_op jit(solution)/shard_map/reduce_scatter | solution.py:314
  88.0 8.7 %collective-permute-start.3 = (bf16[128,288]{1,0:T(8,128)(2,1)S(1)}, bf16[128,288]{1,0:T(8,128)(2,1)S(1)}, u32[]{:S(2)}, u32[]{:S(2)}) collective-permute-start(bf16[128,288]{1,0:T(8,128)(2,1)S(1)} %get-tuple-element.175), channel_id=1, source_target_pairs={{0,24},{8,0},{16,8},{24,16},{1,25},{9,1},{17,9},{25,17},{2,26},{10... | collective-permute-start | bytes 221192 | tf_op jit(solution)/shard_map/ppermute | solution.py:161
  88.1 11.5 %collective-permute-start.4 = (bf16[128,288]{1,0:T(8,128)(2,1)S(1)}, bf16[128,288]{1,0:T(8,128)(2,1)S(1)}, u32[]{:S(2)}, u32[]{:S(2)}) collective-permute-start(bf16[128,288]{1,0:T(8,128)(2,1)S(1)} %get-tuple-element.174), channel_id=1, source_target_pairs={{0,16},{8,24},{16,0},{24,8},{1,17},{9,25},{17,1},{25,9},{2,18},{10... | collective-permute-start | bytes 221192 | tf_op jit(solution)/shard_map/ppermute | solution.py:161
  91.1 8.7 %collective-permute-start.5 = (bf16[128,288]{1,0:T(8,128)(2,1)S(1)}, bf16[128,288]{1,0:T(8,128)(2,1)S(1)}, u32[]{:S(2)}, u32[]{:S(2)}) collective-permute-start(bf16[128,288]{1,0:T(8,128)(2,1)S(1)} %get-tuple-element.173), channel_id=1, source_target_pairs={{0,8},{8,16},{16,24},{24,0},{1,9},{9,17},{17,25},{25,1},{2,10},{10... | collective-permute-start | bytes 221192 | tf_op jit(solution)/shard_map/ppermute | solution.py:161
  150.6 9.2 %collective-permute-start.7 = (bf16[128,1152]{1,0:T(8,128)(2,1)S(1)}, bf16[128,1152]{1,0:T(8,128)(2,1)S(1)}, u32[]{:S(2)}, u32[]{:S(2)}) collective-permute-start(bf16[128,1152]{1,0:T(8,128)(2,1)S(1)} %slice.813), channel_id=1, source_target_pairs={{0,8},{8,0},{16,24},{24,16},{1,9},{9,1},{17,25},{25,17},{2,10},{10... | collective-permute-start | bytes 884744 | tf_op jit(solution)/shard_map/ppermute | solution.py:164
  160.5 29.3 %collective-permute-start.10 = (bf16[128,1152]{1,0:T(8,128)(2,1)S(1)}, bf16[128,1152]{1,0:T(8,128)(2,1)S(1)}, u32[]{:S(2)}, u32[]{:S(2)}) collective-permute-start(bf16[128,1152]{1,0:T(8,128)(2,1)S(1)} %add_convert_fusion.3), channel_id=1, source_target_pairs={{0,24},{8,0},{16,8},{24,16},{1,25},{9,1},{17,9},{25,17},{2,26},{10... | collective-permute-start | bytes 884744 | tf_op jit(solution)/shard_map/ppermute | solution.py:161
  163.9 26.0 %collective-permute-start.9 = (bf16[128,1152]{1,0:T(8,128)(2,1)S(1)}, bf16[128,1152]{1,0:T(8,128)(2,1)S(1)}, u32[]{:S(2)}, u32[]{:S(2)}) collective-permute-start(bf16[128,1152]{1,0:T(8,128)(2,1)S(1)} %add_convert_fusion.3), channel_id=1, source_target_pairs={{0,16},{8,24},{16,0},{24,8},{1,17},{9,25},{17,1},{25,9},{2,18},{10... | collective-permute-start | bytes 884744 | tf_op jit(solution)/shard_map/ppermute | solution.py:161
  163.9 26.0 %collective-permute-start.8 = (bf16[128,1152]{1,0:T(8,128)(2,1)S(1)}, bf16[128,1152]{1,0:T(8,128)(2,1)S(1)}, u32[]{:S(2)}, u32[]{:S(2)}) collective-permute-start(bf16[128,1152]{1,0:T(8,128)(2,1)S(1)} %add_convert_fusion.3), channel_id=1, source_target_pairs={{0,8},{8,16},{16,24},{24,0},{1,9},{9,17},{17,25},{25,1},{2,10},{10... | collective-permute-start | bytes 884744 | tf_op jit(solution)/shard_map/ppermute | solution.py:161
  201.6 9.8 %collective-permute-start.12 = (bf16[128,288]{1,0:T(8,128)(2,1)}, bf16[128,288]{1,0:T(8,128)(2,1)}, u32[]{:S(2)}, u32[]{:S(2)}) collective-permute-start(bf16[128,288]{1,0:T(8,128)(2,1)} %get-tuple-element.170), channel_id=1, source_target_pairs={{0,16},{8,24},{16,0},{24,8},{1,17},{9,25},{17,1},{25,9},{2,18},{10... | collective-permute-start | bytes 221192 | tf_op jit(solution)/shard_map/ppermute | solution.py:161
  201.6 10.8 %collective-permute-start.13 = (bf16[128,288]{1,0:T(8,128)(2,1)S(1)}, bf16[128,288]{1,0:T(8,128)(2,1)}, u32[]{:S(2)}, u32[]{:S(2)}) collective-permute-start(bf16[128,288]{1,0:T(8,128)(2,1)S(1)} %get-tuple-element.169), channel_id=1, source_target_pairs={{0,8},{8,16},{16,24},{24,0},{1,9},{9,17},{17,25},{25,1},{2,10},{10... | collective-permute-start | bytes 221192 | tf_op jit(solution)/shard_map/ppermute | solution.py:161
  217.7 11.2 %collective-permute-start.14 = (bf16[128,1152]{1,0:T(8,128)(2,1)S(1)}, bf16[128,1152]{1,0:T(8,128)(2,1)S(1)}, u32[]{:S(2)}, u32[]{:S(2)}) collective-permute-start(bf16[128,1152]{1,0:T(8,128)(2,1)S(1)} %add_convert_fusion.2), channel_id=1, source_target_pairs={{0,8},{8,0},{16,24},{24,16},{1,9},{9,1},{17,25},{25,17},{2,10},{10... | collective-permute-start | bytes 884744 | tf_op jit(solution)/shard_map/ppermute | solution.py:164
  217.8 16.7 %collective-permute-start.16 = (bf16[128,1152]{1,0:T(8,128)(2,1)}, bf16[128,1152]{1,0:T(8,128)(2,1)}, u32[]{:S(2)}, u32[]{:S(2)}) collective-permute-start(bf16[128,1152]{1,0:T(8,128)(2,1)} %bitcast.51), channel_id=1, source_target_pairs={{0,8},{8,0},{16,24},{24,16},{1,9},{9,1},{17,25},{25,17},{2,10},{10... | collective-permute-start | bytes 884744 | tf_op jit(solution)/shard_map/ppermute | solution.py:164
  281.6 9.9 %collective-permute-start.17 = (bf16[128,1152]{1,0:T(8,128)(2,1)S(1)}, bf16[128,1152]{1,0:T(8,128)(2,1)S(1)}, u32[]{:S(2)}, u32[]{:S(2)}) collective-permute-start(bf16[128,1152]{1,0:T(8,128)(2,1)S(1)} %slice.811), channel_id=1, source_target_pairs={{0,8},{8,0},{16,24},{24,16},{1,9},{9,1},{17,25},{25,17},{2,10},{10... | collective-permute-start | bytes 884744 | tf_op jit(solution)/shard_map/ppermute | solution.py:164
  285.0 12.1 %collective-permute-start.15 = (bf16[128,1152]{1,0:T(8,128)(2,1)S(1)}, bf16[128,1152]{1,0:T(8,128)(2,1)S(1)}, u32[]{:S(2)}, u32[]{:S(2)}) collective-permute-start(bf16[128,1152]{1,0:T(8,128)(2,1)S(1)} %slice.812), channel_id=1, source_target_pairs={{0,8},{8,0},{16,24},{24,16},{1,9},{9,1},{17,25},{25,17},{2,10},{10... | collective-permute-start | bytes 884744 | tf_op jit(solution)/shard_map/ppermute | solution.py:164
  304.3 8.5 %collective-permute-start.19 = (bf16[128,288]{1,0:T(8,128)(2,1)S(1)}, bf16[128,288]{1,0:T(8,128)(2,1)S(1)}, u32[]{:S(2)}, u32[]{:S(2)}) collective-permute-start(bf16[128,288]{1,0:T(8,128)(2,1)S(1)} %get-tuple-element.167), channel_id=1, source_target_pairs={{0,16},{8,24},{16,0},{24,8},{1,17},{9,25},{17,1},{25,9},{2,18},{10... | collective-permute-start | bytes 221192 | tf_op jit(solution)/shard_map/ppermute | solution.py:161
  322.3 180.5 %reduce-scatter.15.cloned.1.call-start = ((), (), s32[]{:S(2)}) async-start(), calls=%async_computation.18 | async-start | bytes 2985984 | tf_op jit(solution)/shard_map/reduce_scatter | solution.py:314
  325.9 11.9 %collective-permute-start.23 = (bf16[128,1152]{1,0:T(8,128)(2,1)S(1)}, bf16[128,1152]{1,0:T(8,128)(2,1)S(1)}, u32[]{:S(2)}, u32[]{:S(2)}) collective-permute-start(bf16[128,1152]{1,0:T(8,128)(2,1)S(1)} %get-tuple-element.141), channel_id=1, source_target_pairs={{0,8},{8,16},{16,24},{24,0},{1,9},{9,17},{17,25},{25,1},{2,10},{10... | collective-permute-start | bytes 884744 | tf_op jit(solution)/shard_map/ppermute | solution.py:161
  326.2 22.9 %collective-permute-start.22 = (bf16[128,1152]{1,0:T(8,128)(2,1)S(1)}, bf16[128,1152]{1,0:T(8,128)(2,1)S(1)}, u32[]{:S(2)}, u32[]{:S(2)}) collective-permute-start(bf16[128,1152]{1,0:T(8,128)(2,1)S(1)} %get-tuple-element.142), channel_id=1, source_target_pairs={{0,16},{8,24},{16,0},{24,8},{1,17},{9,25},{17,1},{25,9},{2,18},{10... | collective-permute-start | bytes 884744 | tf_op jit(solution)/shard_map/ppermute | solution.py:161
  328.3 20.8 %collective-permute-start.21 = (bf16[128,1152]{1,0:T(8,128)(2,1)S(1)}, bf16[128,1152]{1,0:T(8,128)(2,1)S(1)}, u32[]{:S(2)}, u32[]{:S(2)}) collective-permute-start(bf16[128,1152]{1,0:T(8,128)(2,1)S(1)} %get-tuple-element.140), channel_id=1, source_target_pairs={{0,24},{8,0},{16,8},{24,16},{1,25},{9,1},{17,9},{25,17},{2,26},{10... | collective-permute-start | bytes 884744 | tf_op jit(solution)/shard_map/ppermute | solution.py:161
  351.0 12.3 %collective-permute-start.24 = (bf16[128,1152]{1,0:T(8,128)(2,1)S(1)}, bf16[128,1152]{1,0:T(8,128)(2,1)S(1)}, u32[]{:S(2)}, u32[]{:S(2)}) collective-permute-start(bf16[128,1152]{1,0:T(8,128)(2,1)S(1)} %convert_element_type.347), channel_id=1, source_target_pairs={{0,8},{8,0},{16,24},{24,16},{1,9},{9,1},{17,25},{25,17},{2,10},{10... | collective-permute-start | bytes 884744 | tf_op jit(solution)/shard_map/ppermute | solution.py:164
  359.3 155.1 %reduce-scatter.9.cloned.1.call-start = ((), (), s32[]{:S(2)}) async-start(), calls=%async_computation.15 | async-start | bytes 2322432 | tf_op jit(solution)/shard_map/reduce_scatter | solution.py:314
  404.4 145.0 %reduce-scatter.13.cloned.1.call-start = ((), (), s32[]{:S(2)}) async-start(), calls=%async_computation.17 | async-start | bytes 2985984 | tf_op jit(solution)/shard_map/reduce_scatter | solution.py:314
  407.9 166.5 %reduce-scatter.19.cloned.1.call-start = ((), (), s32[]{:S(2)}) async-start(), calls=%async_computation.20 | async-start | bytes 5640192 | tf_op jit(solution)/shard_map/reduce_scatter | solution.py:314
  414.1 208.1 %reduce-scatter.23.cloned.1.call-start = ((), (), s32[]{:S(2)}) async-start(), calls=%async_computation.22 | async-start | bytes 5640192 | tf_op jit(solution)/shard_map/reduce_scatter | solution.py:314
  420.3 261.2 %reduce-scatter.17.cloned.1.call-start = ((), (), s32[]{:S(2)}) async-start(), calls=%async_computation.19 | async-start | bytes 5640192 | tf_op jit(solution)/shard_map/reduce_scatter | solution.py:314
  425.8 315.1 %reduce-scatter.21.cloned.1.call-start = ((), (), s32[]{:S(2)}) async-start(), calls=%async_computation.21 | async-start | bytes 5640192 | tf_op jit(solution)/shard_map/reduce_scatter | solution.py:314
  435.4 11.9 %collective-permute-start.31 = (bf16[128,1152]{1,0:T(8,128)(2,1)S(1)}, bf16[128,1152]{1,0:T(8,128)(2,1)S(1)}, u32[]{:S(2)}, u32[]{:S(2)}) collective-permute-start(bf16[128,1152]{1,0:T(8,128)(2,1)S(1)} %get-tuple-element.135), channel_id=1, source_target_pairs={{0,8},{8,16},{16,24},{24,0},{1,9},{9,17},{17,25},{25,1},{2,10},{10... | collective-permute-start | bytes 884744 | tf_op jit(solution)/shard_map/ppermute | solution.py:161
  435.4 19.7 %collective-permute-start.30 = (bf16[128,1152]{1,0:T(8,128)(2,1)S(1)}, bf16[128,1152]{1,0:T(8,128)(2,1)}, u32[]{:S(2)}, u32[]{:S(2)}) collective-permute-start(bf16[128,1152]{1,0:T(8,128)(2,1)S(1)} %get-tuple-element.136), channel_id=1, source_target_pairs={{0,16},{8,24},{16,0},{24,8},{1,17},{9,25},{17,1},{25,9},{2,18},{10... | collective-permute-start | bytes 884744 | tf_op jit(solution)/shard_map/ppermute | solution.py:161
  436.4 18.8 %collective-permute-start.29 = (bf16[128,1152]{1,0:T(8,128)(2,1)S(1)}, bf16[128,1152]{1,0:T(8,128)(2,1)}, u32[]{:S(2)}, u32[]{:S(2)}) collective-permute-start(bf16[128,1152]{1,0:T(8,128)(2,1)S(1)} %get-tuple-element.134), channel_id=1, source_target_pairs={{0,24},{8,0},{16,8},{24,16},{1,25},{9,1},{17,9},{25,17},{2,26},{10... | collective-permute-start | bytes 884744 | tf_op jit(solution)/shard_map/ppermute | solution.py:161
  458.1 8.6 %all-to-all-start = ((f32[8,1,3456]{2,1,0:T(1,128)}), f32[8,1,3456]{2,1,0:T(1,128)S(1)}, u32[]{:S(2)}, u32[]{:S(2)}) async-start(f32[8,1,3456]{2,1,0:T(1,128)} %copy.168), calls=%async_computation | async-start | bytes 221184 | tf_op jit(solution)/shard_map/all_to_all | solution.py:431
  483.5 11.2 %collective-permute-start.38 = (bf16[144,864]{1,0:T(8,128)(2,1)}, bf16[144,864]{1,0:T(8,128)(2,1)S(1)}, u32[]{:S(2)}, u32[]{:S(2)}) collective-permute-start(bf16[144,864]{1,0:T(8,128)(2,1)} %reduce-scatter.11.cloned.1.call-done), channel_id=1, source_target_pairs={{0,8},{8,16},{16,24},{24,0},{1,9},{9,17},{17,25},{25,1},{2,10},{10... | collective-permute-start | bytes 746504 | tf_op jit(solution)/shard_map/ppermute | solution.py:161
  484.7 18.0 %collective-permute-start.39 = (bf16[144,864]{1,0:T(8,128)(2,1)}, bf16[144,864]{1,0:T(8,128)(2,1)S(1)}, u32[]{:S(2)}, u32[]{:S(2)}) collective-permute-start(bf16[144,864]{1,0:T(8,128)(2,1)} %reduce-scatter.11.cloned.1.call-done), channel_id=1, source_target_pairs={{0,16},{8,24},{16,0},{24,8},{1,17},{9,25},{17,1},{25,9},{2,18},{10... | collective-permute-start | bytes 746504 | tf_op jit(solution)/shard_map/ppermute | solution.py:161
  485.0 24.6 %collective-permute-start.40 = (bf16[144,864]{1,0:T(8,128)(2,1)}, bf16[144,864]{1,0:T(8,128)(2,1)S(1)}, u32[]{:S(2)}, u32[]{:S(2)}) collective-permute-start(bf16[144,864]{1,0:T(8,128)(2,1)} %reduce-scatter.11.cloned.1.call-done), channel_id=1, source_target_pairs={{0,24},{8,0},{16,8},{24,16},{1,25},{9,1},{17,9},{25,17},{2,26},{10... | collective-permute-start | bytes 746504 | tf_op jit(solution)/shard_map/ppermute | solution.py:161
  504.6 13.6 %collective-permute-start.49 = (bf16[36,1152]{1,0:T(8,128)(2,1)}, bf16[36,1152]{1,0:T(8,128)(2,1)}, u32[]{:S(2)}, u32[]{:S(2)}) collective-permute-start(bf16[36,1152]{1,0:T(8,128)(2,1)} %get-tuple-element.181), channel_id=1, source_target_pairs={{0,24},{8,0},{16,8},{24,16},{1,25},{9,1},{17,9},{25,17},{2,26},{10... | collective-permute-start | bytes 248840 | tf_op jit(solution)/shard_map/ppermute | solution.py:161
  509.1 10.6 %collective-permute-start.48 = (bf16[36,1152]{1,0:T(8,128)(2,1)}, bf16[36,1152]{1,0:T(8,128)(2,1)}, u32[]{:S(2)}, u32[]{:S(2)}) collective-permute-start(bf16[36,1152]{1,0:T(8,128)(2,1)} %get-tuple-element.182), channel_id=1, source_target_pairs={{0,16},{8,24},{16,0},{24,8},{1,17},{9,25},{17,1},{25,9},{2,18},{10... | collective-permute-start | bytes 248840 | tf_op jit(solution)/shard_map/ppermute | solution.py:161
  509.1 10.6 %collective-permute-start.47 = (bf16[36,1152]{1,0:T(8,128)(2,1)}, bf16[36,1152]{1,0:T(8,128)(2,1)}, u32[]{:S(2)}, u32[]{:S(2)}) collective-permute-start(bf16[36,1152]{1,0:T(8,128)(2,1)} %get-tuple-element.180), channel_id=1, source_target_pairs={{0,8},{8,16},{16,24},{24,0},{1,9},{9,17},{17,25},{25,1},{2,10},{10... | collective-permute-start | bytes 248840 | tf_op jit(solution)/shard_map/ppermute | solution.py:161
  514.4 34.9 %collective-permute-start.35 = (bf16[144,864]{1,0:T(8,128)(2,1)}, bf16[144,864]{1,0:T(8,128)(2,1)S(1)}, u32[]{:S(2)}, u32[]{:S(2)}) collective-permute-start(bf16[144,864]{1,0:T(8,128)(2,1)} %reduce-scatter.9.cloned.1.call-done), channel_id=1, source_target_pairs={{0,8},{8,16},{16,24},{24,0},{1,9},{9,17},{17,25},{25,1},{2,10},{10... | collective-permute-start | bytes 746504 | tf_op jit(solution)/shard_map/ppermute | solution.py:161
  517.3 32.0 %collective-permute-start.36 = (bf16[144,864]{1,0:T(8,128)(2,1)}, bf16[144,864]{1,0:T(8,128)(2,1)S(1)}, u32[]{:S(2)}, u32[]{:S(2)}) collective-permute-start(bf16[144,864]{1,0:T(8,128)(2,1)} %reduce-scatter.9.cloned.1.call-done), channel_id=1, source_target_pairs={{0,16},{8,24},{16,0},{24,8},{1,17},{9,25},{17,1},{25,9},{2,18},{10... | collective-permute-start | bytes 746504 | tf_op jit(solution)/shard_map/ppermute | solution.py:161
  518.2 39.1 %collective-permute-start.37 = (bf16[144,864]{1,0:T(8,128)(2,1)}, bf16[144,864]{1,0:T(8,128)(2,1)S(1)}, u32[]{:S(2)}, u32[]{:S(2)}) collective-permute-start(bf16[144,864]{1,0:T(8,128)(2,1)} %reduce-scatter.9.cloned.1.call-done), channel_id=1, source_target_pairs={{0,24},{8,0},{16,8},{24,16},{1,25},{9,1},{17,9},{25,17},{2,26},{10... | collective-permute-start | bytes 746504 | tf_op jit(solution)/shard_map/ppermute | solution.py:161
  520.8 16.3 %collective-permute-start.50 = (bf16[36,1152]{1,0:T(8,128)(2,1)S(1)}, bf16[36,1152]{1,0:T(8,128)(2,1)S(1)}, u32[]{:S(2)}, u32[]{:S(2)}) collective-permute-start(bf16[36,1152]{1,0:T(8,128)(2,1)S(1)} %get-tuple-element.109), channel_id=1, source_target_pairs={{0,8},{8,16},{16,24},{24,0},{1,9},{9,17},{17,25},{25,1},{2,10},{10... | collective-permute-start | bytes 248840 | tf_op jit(solution)/shard_map/ppermute | solution.py:161
  522.5 23.0 %collective-permute-start.51 = (bf16[36,1152]{1,0:T(8,128)(2,1)S(1)}, bf16[36,1152]{1,0:T(8,128)(2,1)S(1)}, u32[]{:S(2)}, u32[]{:S(2)}) collective-permute-start(bf16[36,1152]{1,0:T(8,128)(2,1)S(1)} %get-tuple-element.109), channel_id=1, source_target_pairs={{0,16},{8,24},{16,0},{24,8},{1,17},{9,25},{17,1},{25,9},{2,18},{10... | collective-permute-start | bytes 248840 | tf_op jit(solution)/shard_map/ppermute | solution.py:161
  537.1 11.3 %collective-permute-start.52 = (bf16[36,1152]{1,0:T(8,128)(2,1)S(1)}, bf16[36,1152]{1,0:T(8,128)(2,1)S(1)}, u32[]{:S(2)}, u32[]{:S(2)}) collective-permute-start(bf16[36,1152]{1,0:T(8,128)(2,1)S(1)} %get-tuple-element.109), channel_id=1, source_target_pairs={{0,24},{8,0},{16,8},{24,16},{1,25},{9,1},{17,9},{25,17},{2,26},{10... | collective-permute-start | bytes 248840 | tf_op jit(solution)/shard_map/ppermute | solution.py:161
  551.1 10.9 %collective-permute-start.43 = (bf16[36,1152]{1,0:T(8,128)(2,1)}, bf16[36,1152]{1,0:T(8,128)(2,1)}, u32[]{:S(2)}, u32[]{:S(2)}) collective-permute-start(bf16[36,1152]{1,0:T(8,128)(2,1)} %get-tuple-element.178), channel_id=1, source_target_pairs={{0,24},{8,0},{16,8},{24,16},{1,25},{9,1},{17,9},{25,17},{2,26},{10... | collective-permute-start | bytes 248840 | tf_op jit(solution)/shard_map/ppermute | solution.py:161
  575.5 50.2 %collective-permute-start.56 = (bf16[72,2176]{1,0:T(8,128)(2,1)S(1)}, bf16[72,2176]{1,0:T(8,128)(2,1)S(1)}, u32[]{:S(2)}, u32[]{:S(2)}) collective-permute-start(bf16[72,2176]{1,0:T(8,128)(2,1)S(1)} %dynamic-slice_bitcast_fusion.2), channel_id=1, source_target_pairs={{0,16},{8,24},{16,0},{24,8},{1,17},{9,25},{17,1},{25,9},{2,18},{10... | collective-permute-start | bytes 940040 | tf_op jit(solution)/shard_map/ppermute | solution.py:167
  623.3 24.6 %collective-permute-start.62 = (bf16[136,1152]{1,0:T(8,128)(2,1)S(1)}, bf16[136,1152]{1,0:T(8,128)(2,1)S(1)}, u32[]{:S(2)}, u32[]{:S(2)}) collective-permute-start(bf16[136,1152]{1,0:T(8,128)(2,1)S(1)} %dynamic-slice_bitcast_fusion), channel_id=1, source_target_pairs={{0,16},{8,24},{16,0},{24,8},{1,17},{9,25},{17,1},{25,9},{2,18},{10... | collective-permute-start | bytes 940040 | tf_op jit(solution)/shard_map/ppermute | solution.py:167
  625.9 35.4 %collective-permute-start.57 = (bf16[72,2176]{1,0:T(8,128)(2,1)S(1)}, bf16[72,2176]{1,0:T(8,128)(2,1)S(1)}, u32[]{:S(2)}, u32[]{:S(2)}) collective-permute-start(bf16[72,2176]{1,0:T(8,128)(2,1)S(1)} %get-tuple-element.105), channel_id=1, source_target_pairs={{0,16},{8,24},{16,0},{24,8},{1,17},{9,25},{17,1},{25,9},{2,18},{10... | collective-permute-start | bytes 940040 | tf_op jit(solution)/shard_map/ppermute | solution.py:167
  649.5 17.5 %collective-permute-start.63 = (bf16[136,1152]{1,0:T(8,128)(2,1)S(1)}, bf16[136,1152]{1,0:T(8,128)(2,1)S(1)}, u32[]{:S(2)}, u32[]{:S(2)}) collective-permute-start(bf16[136,1152]{1,0:T(8,128)(2,1)S(1)} %get-tuple-element.101), channel_id=1, source_target_pairs={{0,16},{8,24},{16,0},{24,8},{1,17},{9,25},{17,1},{25,9},{2,18},{10... | collective-permute-start | bytes 940040 | tf_op jit(solution)/shard_map/ppermute | solution.py:167
  661.3 83.8 %collective-permute-start.58 = (bf16[144,2176]{1,0:T(8,128)(2,1)S(1)}, bf16[144,2176]{1,0:T(8,128)(2,1)S(1)}, u32[]{:S(2)}, u32[]{:S(2)}) collective-permute-start(bf16[144,2176]{1,0:T(8,128)(2,1)S(1)} %bitcast.353), channel_id=1, source_target_pairs={{0,8},{8,0},{16,24},{24,16},{1,9},{9,1},{17,25},{25,17},{2,10},{10... | collective-permute-start | bytes 1880072 | tf_op jit(solution)/shard_map/ppermute | solution.py:164
  667.8 82.2 %collective-permute-start.64 = (bf16[272,1152]{1,0:T(8,128)(2,1)}, bf16[272,1152]{1,0:T(8,128)(2,1)}, u32[]{:S(2)}, u32[]{:S(2)}) collective-permute-start(bf16[272,1152]{1,0:T(8,128)(2,1)} %bitcast.148), channel_id=1, source_target_pairs={{0,8},{8,0},{16,24},{24,16},{1,9},{9,1},{17,25},{25,17},{2,10},{10... | collective-permute-start | bytes 1880072 | tf_op jit(solution)/shard_map/ppermute | solution.py:164
  683.2 68.3 %collective-permute-start.53 = (bf16[72,2176]{1,0:T(8,128)(2,1)}, bf16[72,2176]{1,0:T(8,128)(2,1)}, u32[]{:S(2)}, u32[]{:S(2)}) collective-permute-start(bf16[72,2176]{1,0:T(8,128)(2,1)} %dynamic-slice_bitcast_fusion.3), channel_id=1, source_target_pairs={{0,16},{8,24},{16,0},{24,8},{1,17},{9,25},{17,1},{25,9},{2,18},{10... | collective-permute-start | bytes 940040 | tf_op jit(solution)/shard_map/ppermute | solution.py:167
  742.7 24.8 %collective-permute-start.59 = (bf16[136,1152]{1,0:T(8,128)(2,1)}, bf16[136,1152]{1,0:T(8,128)(2,1)}, u32[]{:S(2)}, u32[]{:S(2)}) collective-permute-start(bf16[136,1152]{1,0:T(8,128)(2,1)} %dynamic-slice_bitcast_fusion.1), channel_id=1, source_target_pairs={{0,16},{8,24},{16,0},{24,8},{1,17},{9,25},{17,1},{25,9},{2,18},{10... | collective-permute-start | bytes 940040 | tf_op jit(solution)/shard_map/ppermute | solution.py:167
  752.6 28.2 %collective-permute-start.54 = (bf16[72,2176]{1,0:T(8,128)(2,1)S(1)}, bf16[72,2176]{1,0:T(8,128)(2,1)S(1)}, u32[]{:S(2)}, u32[]{:S(2)}) collective-permute-start(bf16[72,2176]{1,0:T(8,128)(2,1)S(1)} %get-tuple-element.103), channel_id=1, source_target_pairs={{0,16},{8,24},{16,0},{24,8},{1,17},{9,25},{17,1},{25,9},{2,18},{10... | collective-permute-start | bytes 940040 | tf_op jit(solution)/shard_map/ppermute | solution.py:167
  768.6 18.0 %collective-permute-start.60 = (bf16[136,1152]{1,0:T(8,128)(2,1)S(1)}, bf16[136,1152]{1,0:T(8,128)(2,1)S(1)}, u32[]{:S(2)}, u32[]{:S(2)}) collective-permute-start(bf16[136,1152]{1,0:T(8,128)(2,1)S(1)} %get-tuple-element.99), channel_id=1, source_target_pairs={{0,16},{8,24},{16,0},{24,8},{1,17},{9,25},{17,1},{25,9},{2,18},{10... | collective-permute-start | bytes 940040 | tf_op jit(solution)/shard_map/ppermute | solution.py:167
  780.9 19.2 %collective-permute-start.55 = (bf16[144,2176]{1,0:T(8,128)(2,1)S(1)}, bf16[144,2176]{1,0:T(8,128)(2,1)S(1)}, u32[]{:S(2)}, u32[]{:S(2)}) collective-permute-start(bf16[144,2176]{1,0:T(8,128)(2,1)S(1)} %bitcast.354), channel_id=1, source_target_pairs={{0,8},{8,0},{16,24},{24,16},{1,9},{9,1},{17,25},{25,17},{2,10},{10... | collective-permute-start | bytes 1880072 | tf_op jit(solution)/shard_map/ppermute | solution.py:164
  786.6 26.8 %collective-permute-start.61 = (bf16[272,1152]{1,0:T(8,128)(2,1)S(1)}, bf16[272,1152]{1,0:T(8,128)(2,1)}, u32[]{:S(2)}, u32[]{:S(2)}) collective-permute-start(bf16[272,1152]{1,0:T(8,128)(2,1)S(1)} %bitcast.352), channel_id=1, source_target_pairs={{0,8},{8,0},{16,24},{24,16},{1,9},{9,1},{17,25},{25,17},{2,10},{10... | collective-permute-start | bytes 1880072 | tf_op jit(solution)/shard_map/ppermute | solution.py:164
  (133 other events, 1147.5 us)
Sparse Core Ops, SparseCore 0:
  18.8 41.5 all-gather.6
  62.9 40.1 all-gather.8
  105.5 40.1 all-gather.10
  147.4 38.9 all-gather.12
  188.7 40.1 all-gather.14
  230.7 40.1 all-gather.16
  322.4 39.6 reduce-scatter.10
  366.6 43.7 reduce-scatter.14
  413.8 40.8 reduce-scatter.8
  459.0 43.7 reduce-scatter.12
  506.9 55.7 reduce-scatter.18
  566.4 55.7 reduce-scatter.22
  625.7 55.7 reduce-scatter.16
  685.2 55.7 reduce-scatter.20

commit v2 on v1

v2 whole, which is shorter than its diff:
```python
import functools
import math

import jax
import jax.numpy as jnp
from jax import lax
from jax.experimental import pallas as pl
from jax.experimental.pallas import tpu as pltpu
from jax.sharding import PartitionSpec as P

HEAD_DIM = 72
EPSILON = 1e-06
LOW = jnp.bfloat16
FULL = jnp.float32


def normalize(hidden):
    center = hidden - jnp.mean(hidden, axis=-1, keepdims=True)
    variance = jnp.mean(center * center, axis=-1, keepdims=True)
    inverse_std = lax.rsqrt(variance + EPSILON)
    return center * inverse_std, inverse_std


def normalize_back(upstream, normed, inverse_std, gain):
    scaled = upstream * gain
    grad_hidden = inverse_std * (
        scaled
        - jnp.mean(scaled, axis=-1, keepdims=True)
        - normed * jnp.mean(scaled * normed, axis=-1, keepdims=True)
    )
    return (
        grad_hidden,
        jnp.sum(upstream * normed, axis=0, keepdims=True),
        jnp.sum(upstream, axis=0, keepdims=True),
    )


def tangent_gelu(values):
    return jax.nn.gelu(values, approximate=True)


def gelu_back(values, upstream):
    return jax.vjp(tangent_gelu, values)[1](upstream)[0]


def mm(left, right):
    return jnp.dot(left, right, preferred_element_type=FULL)


def mm_rows(left, right):
    return lax.dot_general(left, right, (((0,), (0,)), ((), ())), preferred_element_type=FULL)


def mm_cols(left, right):
    return lax.dot_general(left, right, (((1,), (1,)), ((), ())), preferred_element_type=FULL)


def head_window(head, width):
    low = head * HEAD_DIM // 128 * 128
    high = min(-(-(head + 1) * HEAD_DIM // 128) * 128, width)
    return low, high


def head_mask(head, low, high):
    lane = lax.broadcasted_iota(jnp.int32, (1, high - low), 1) + low
    return (lane >= head * HEAD_DIM) & (lane < (head + 1) * HEAD_DIM)


def attend_forward_kernel(qkv_ref, o_ref, lse_ref, acc_ref):
    tokens, width = o_ref.shape
    rows = min(256, tokens)
    scaling = HEAD_DIM ** (-0.5)
    acc_ref[...] = jnp.zeros_like(acc_ref)
    for head in range(width // HEAD_DIM):
        low, high = head_window(head, width)
        mask = head_mask(head, low, high)
        keys = qkv_ref[1, :, low:high]
        values = jnp.where(mask, qkv_ref[2, :, low:high], jnp.zeros((), LOW))
        for start in range(0, tokens, rows):
            queries = jnp.where(mask, qkv_ref[0, start : start + rows, low:high], jnp.zeros((), LOW))
            scores = mm_cols(queries, keys) * scaling
            peak = jnp.max(scores, axis=-1, keepdims=True)
            total = jnp.sum(jnp.exp(scores - peak), axis=-1, keepdims=True)
            lse = peak + jnp.log(total)
            probability = jnp.exp(scores - lse).astype(LOW)
            acc_ref[start : start + rows, low:high] += mm(probability, values)
            lse_ref[start : start + rows, head : head + 1] = lse
    o_ref[...] = acc_ref[...].astype(LOW)


def attend_forward(qkv):
    _, tokens, width = qkv.shape
    heads = width // HEAD_DIM
    return pl.pallas_call(
        attend_forward_kernel,
        out_shape=(
            jax.ShapeDtypeStruct((tokens, width), LOW),
            jax.ShapeDtypeStruct((tokens, heads), FULL),
        ),
        in_specs=[pl.BlockSpec(memory_space=pltpu.VMEM)],
        out_specs=(pl.BlockSpec(memory_space=pltpu.VMEM),) * 2,
        scratch_shapes=[pltpu.VMEM((tokens, width), FULL)],
        compiler_params=pltpu.CompilerParams(vmem_limit_bytes=40 << 20),
        cost_estimate=pl.CostEstimate(
            flops=4 * heads * tokens * tokens * 128,
            transcendentals=2 * heads * tokens * tokens,
            bytes_accessed=8 * tokens * width,
        ),
        name="attend_forward",
    )(qkv)


def attend_backward_kernel(
    qkv_ref, do_ref, lse_ref, proj_ref, grad_ref, leave_ref, q_bias_ref, v_bias_ref, dq_ref, dk_ref, dv_ref
):
    tokens, width = do_ref.shape
    rows = min(256, tokens)
    scaling = HEAD_DIM ** (-0.5)
    for ref in (dq_ref, dk_ref, dv_ref):
        ref[...] = jnp.zeros_like(ref)
    zero = jnp.zeros((), LOW)
    for head in range(width // HEAD_DIM):
        low, high = head_window(head, width)
        mask = head_mask(head, low, high)
        keys = qkv_ref[1, :, low:high]
        values = qkv_ref[2, :, low:high]
        keys_masked = jnp.where(mask, keys, zero)
        for start in range(0, tokens, rows):
            span = slice(start, start + rows)
            queries = jnp.where(mask, qkv_ref[0, span, low:high], zero)
            upstream = jnp.where(mask, do_ref[span, low:high], zero)
            scores = mm_cols(queries, keys) * scaling
            probability = jnp.exp(scores - lse_ref[span, head : head + 1])
            grad_prob = mm_cols(upstream, values)
            inner = jnp.sum(probability * grad_prob, axis=-1, keepdims=True)
            grad_scores = (probability * (grad_prob - inner)).astype(LOW)
            dv_ref[:, low:high] += mm_rows(probability.astype(LOW), upstream)
            dk_ref[:, low:high] += mm_rows(grad_scores, queries)
            dq_ref[span, low:high] += mm(grad_scores, keys_masked)
    dq = (dq_ref[...] * scaling).astype(LOW)
    dv = dv_ref[...].astype(LOW)
    grad_ref[:, :width] = dq
    grad_ref[:, width : 2 * width] = (dk_ref[...] * scaling).astype(LOW)
    grad_ref[:, 2 * width :] = dv
    q_bias_ref[...] = jnp.sum(dq.astype(FULL), axis=0, keepdims=True)
    v_bias_ref[...] = jnp.sum(dv.astype(FULL), axis=0, keepdims=True)
    ranks, block, _ = leave_ref.shape
    for rank in range(ranks):
        leave_ref[rank] = mm_cols(grad_ref[rank * block : (rank + 1) * block], proj_ref[...]).astype(LOW)


def attend_backward(qkv, upstream, lse, proj, ranks):
    _, tokens, width = qkv.shape
    heads = width // HEAD_DIM
    model = proj.shape[0]
    return pl.pallas_call(
        attend_backward_kernel,
        out_shape=(
            jax.ShapeDtypeStruct((tokens, 3 * width), LOW),
            jax.ShapeDtypeStruct((ranks, tokens // ranks, model), LOW),
            jax.ShapeDtypeStruct((1, width), FULL),
            jax.ShapeDtypeStruct((1, width), FULL),
        ),
        in_specs=[pl.BlockSpec(memory_space=pltpu.VMEM)] * 4,
        out_specs=(pl.BlockSpec(memory_space=pltpu.VMEM),) * 4,
        scratch_shapes=[pltpu.VMEM((tokens, width), FULL)] * 3,
        compiler_params=pltpu.CompilerParams(vmem_limit_bytes=48 << 20),
        cost_estimate=pl.CostEstimate(flops=0, transcendentals=0, bytes_accessed=24 << 20),
        name="attend_backward",
    )(qkv, upstream, lse, proj)


def attn_share_kernel(me_ref, out_w_ref, qkv_ref, *refs, layers, with_small, ranks):
    out_ref = refs[-1]
    part, width = out_w_ref.shape
    slab = width // ranks
    out_ref[:part, :width] = out_w_ref[...]
    for rank in range(ranks):

        @pl.when(me_ref[0] == rank)
        def _():
            for i in range(3):
                source = (i * ranks + rank) * slab
                target = width + i * slab
                out_ref[:part, target : target + slab] = qkv_ref[:, source : source + slab]

    if with_small:
        out_ref[part:, :] = jnp.zeros((out_ref.shape[0] - part, out_ref.shape[1]), LOW)
        for layer in range(layers):
            target = 0
            for ref in refs[:-1]:
                count = ref.shape[-1]
                for row in range(ref.shape[0] // layers):
                    source = layer * (ref.shape[0] // layers) + row
                    out_ref[part + layer : part + layer + 1, target : target + count] = ref[source : source + 1, :]
                    target += count


def attn_share(me, out_w, qkv_w, small, layers, ranks):
    part, width = out_w.shape
    rows = part + 8 * (len(small) > 0)
    return pl.pallas_call(
        functools.partial(attn_share_kernel, layers=layers, with_small=len(small) > 0, ranks=ranks),
        out_shape=jax.ShapeDtypeStruct((rows, width + 3 * width // ranks), LOW),
        in_specs=[pl.BlockSpec(memory_space=pltpu.SMEM)]
        + [pl.BlockSpec(memory_space=pltpu.VMEM)] * (2 + len(small)),
        out_specs=pl.BlockSpec(memory_space=pltpu.VMEM),
        compiler_params=pltpu.CompilerParams(vmem_limit_bytes=24 << 20),
        cost_estimate=pl.CostEstimate(flops=1, transcendentals=0, bytes_accessed=1),
        name="attn_share",
    )(me.reshape(1), out_w, qkv_w, *small)


def share_kernel(side_ref, up_ref, down_ref, out_ref, *, owners, layer, half):
    part = up_ref.shape[0]
    hidden_part, _, width = down_ref.shape
    flank = owners // 2 * half
    out_ref[...] = jnp.zeros_like(out_ref)
    for side in range(2):

        @pl.when(side_ref[0] == side)
        def _():
            first = side * half
            count = min(half, hidden_part - first)
            out_ref[:count, :width] = down_ref[first : first + count, layer, :]
            for owner in range(owners):
                source = owner * hidden_part + first
                target = width + owner * half - (owner >= owners // 2) * flank
                row = (owner >= owners // 2) * part
                out_ref[row : row + part, target : target + count] = up_ref[:, source : source + count]


def feed_share(side, up, down, layer, owners, half):
    part, (hidden_part, _, width) = up.shape[0], down.shape
    lanes = width + -(-owners // 2 * half // 128) * 128
    return pl.pallas_call(
        functools.partial(share_kernel, owners=owners, layer=layer, half=half),
        out_shape=jax.ShapeDtypeStruct((max(2 * part, half), lanes), LOW),
        in_specs=[pl.BlockSpec(memory_space=pltpu.SMEM)] + [pl.BlockSpec(memory_space=pltpu.VMEM)] * 2,
        out_specs=pl.BlockSpec(memory_space=pltpu.VMEM),
        compiler_params=pltpu.CompilerParams(vmem_limit_bytes=24 << 20),
        cost_estimate=pl.CostEstimate(flops=1, transcendentals=0, bytes_accessed=1),
        name="feed_share",
    )(side.reshape(1), up, down)


def local_call(kernel, name, out_shape, *operands, scalars=(), scratch=()):
    moved = sum(math.prod(a.shape) * a.dtype.itemsize for a in (*operands, *jax.tree.leaves(out_shape)))
    return pl.pallas_call(
        kernel,
        out_shape=out_shape,
        in_specs=[pl.BlockSpec(memory_space=pltpu.SMEM)] * len(scalars)
        + [pl.BlockSpec(memory_space=pltpu.VMEM)] * len(operands),
        out_specs=jax.tree.map(lambda _: pl.BlockSpec(memory_space=pltpu.VMEM), out_shape),
        scratch_shapes=list(scratch),
        compiler_params=pltpu.CompilerParams(vmem_limit_bytes=48 << 20),
        cost_estimate=pl.CostEstimate(flops=20000000000, transcendentals=0, bytes_accessed=moved),
        name=name,
    )(*[s.reshape(1) for s in scalars], *operands)


def grad_kernel(*refs, owners, columns, total, split):
    core_ref, refs = (refs[0], refs[1:]) if split else (None, refs)
    count = len(columns)
    lefts, rights = refs[:count], refs[count : 2 * count]
    outs, flips = refs[2 * count : len(refs) - count], refs[len(refs) - count :]
    rows = lefts[0].shape[1] // owners
    for target, width in columns:
        gap = slice(target + width, min([t for t, _ in columns if t > target], default=total))
        if gap.stop > gap.start:
            for out in outs:
                out[..., gap] = jnp.zeros(out.shape[:-1] + (gap.stop - gap.start,), LOW)
    for left, right, flip, (target, width) in zip(lefts, rights, flips, columns, strict=True):
        flip[...] = left[...].T
        for start in range(0, width, 256):
            size = min(256, width - start)
            value = mm(flip[...], right[:, start : start + size]).astype(LOW)
            if not split:
                outs[0][:, target + start : target + start + size] = value
                continue
            for core in range(2):

                @pl.when(core_ref[0] == core)
                def _():
                    for owner in range(owners):
                        out = outs[(owner % 2 != core) * 1]
                        out[owner // 2, :, target + start : target + start + size] = value[
                            owner * rows : (owner + 1) * rows
                        ]


def weight_grad(pieces, owners, total, core=None):
    lefts, rights = [p[0] for p in pieces], [p[1] for p in pieces]
    rows = lefts[0].shape[1]
    split = core is not None
    shape = (owners // 2, rows // owners, total) if split else (rows, total)
    out = jax.ShapeDtypeStruct(shape, LOW)
    return local_call(
        functools.partial(
            grad_kernel,
            owners=owners,
            columns=[(p[2], p[1].shape[1]) for p in pieces],
            total=total,
            split=split,
        ),
        "weight_grad",
        (out, out) if split else out,
        *lefts,
        *rights,
        scalars=(core,) if split else (),
        scratch=[pltpu.VMEM((left.shape[1], left.shape[0]), LOW) for left in lefts],
    )


def feed_backward_kernel(
    mine_ref, other_ref, pre_ref, up_ref, down_ref, low_ref, grad_ref, keep_ref, leave_ref, bias_ref, acc_ref
):
    tokens = mine_ref.shape[0]
    low_ref[:tokens] = mine_ref[...]
    low_ref[tokens:] = other_ref[...]
    acc_ref[...] = jnp.zeros_like(acc_ref)
    scale = (2 / math.pi) ** 0.5
    units = pre_ref.shape[1]
    for start in range(0, units, 512):
        span = slice(start, min(start + 512, units))
        pre = pre_ref[:, span]
        square = pre * pre
        bend = jnp.tanh(scale * (pre + 0.044715 * pre * square))
        slope = 0.5 * (1 + bend) + 0.5 * pre * (1 - bend * bend) * (scale * (1 + 3 * 0.044715 * square))
        grad = mm_cols(low_ref[...], down_ref[span, :]) * slope
        bias_ref[:, span] = jnp.sum(grad, axis=0, keepdims=True)
        grad = grad.astype(LOW)
        grad_ref[:, span] = grad
        acc_ref[...] += mm_cols(grad, up_ref[:, span])
    keep_ref[...] = acc_ref[:tokens]
    leave_ref[...] = acc_ref[tokens:].astype(LOW)


def feed_backward(mine, other, pre_act, up, down):
    tokens, width = mine.shape
    units = pre_act.shape[1]
    return local_call(
        feed_backward_kernel,
        "feed_backward",
        (
            jax.ShapeDtypeStruct((2 * tokens, width), LOW),
            jax.ShapeDtypeStruct((2 * tokens, units), LOW),
            jax.ShapeDtypeStruct((tokens, width), FULL),
            jax.ShapeDtypeStruct((tokens, width), LOW),
            jax.ShapeDtypeStruct((1, units), FULL),
        ),
        mine,
        other,
        pre_act,
        up,
        down,
        scratch=[pltpu.VMEM((2 * tokens, width), FULL)],
    )


def mid_backward_kernel(
    side_ref, keep_ref, got_ref, normed_ref, inverse_ref, gain_ref, grad_ref, proj_ref, *outs
):
    after_ref, send_ref, mine_ref, other_ref, g_gain_ref, g_bias_ref, g_out_ref, g_down_ref = outs
    upstream = keep_ref[...] + got_ref[...].astype(FULL)
    grad = grad_ref[...]
    back, g_gain, g_bias = normalize_back(upstream, normed_ref[...], inverse_ref[...], gain_ref[...])
    after = grad + back
    after_ref[...] = after
    g_gain_ref[...] = g_gain
    g_bias_ref[...] = g_bias
    g_out_ref[...] = jnp.sum(after, axis=0, keepdims=True)
    g_down_ref[...] = jnp.sum(grad, axis=0, keepdims=True)
    low = after.astype(LOW)
    flank = mine_ref.shape[1]
    for side in range(2):

        @pl.when(side_ref[0] == side)
        def _():
            mine_ref[...] = low[:, side * flank : (side + 1) * flank]
            other_ref[...] = low[:, (1 - side) * flank : (2 - side) * flank]

    ranks, _, slab = send_ref.shape
    for rank in range(ranks):
        send_ref[rank] = mm_cols(low, proj_ref[rank * slab : (rank + 1) * slab, :]).astype(LOW)


def mid_backward(side, keep, got, normed, inverse, gain, grad, proj, ranks):
    tokens, width = keep.shape
    row = jax.ShapeDtypeStruct((1, width), FULL)
    half = jax.ShapeDtypeStruct((tokens, width // 2), LOW)
    return local_call(
        mid_backward_kernel,
        "mid_backward",
        (
            jax.ShapeDtypeStruct((tokens, width), FULL),
            jax.ShapeDtypeStruct((ranks, tokens, width // ranks), LOW),
            half,
            half,
            row,
            row,
            row,
            row,
        ),
        keep,
        got,
        normed,
        inverse,
        gain,
        grad,
        proj,
        scalars=(side,),
    )


def end_backward_kernel(got_ref, normed_ref, inverse_ref, gain_ref, after_ref, out_ref, low_ref, g_gain_ref, g_bias_ref):
    upstream = got_ref[0].astype(FULL)
    for rank in range(1, got_ref.shape[0]):
        upstream += got_ref[rank].astype(FULL)
    back, g_gain, g_bias = normalize_back(upstream, normed_ref[...], inverse_ref[...], gain_ref[...])
    total = after_ref[...] + back
    out_ref[...] = total
    low_ref[...] = total.astype(LOW)
    g_gain_ref[...] = g_gain
    g_bias_ref[...] = g_bias


def end_backward(got, normed, inverse, gain, after):
    tokens, width = after.shape
    row = jax.ShapeDtypeStruct((1, width), FULL)
    return local_call(
        end_backward_kernel,
        "end_backward",
        (
            jax.ShapeDtypeStruct((tokens, width), FULL),
            jax.ShapeDtypeStruct((tokens, width), LOW),
            row,
            row,
        ),
        got,
        normed,
        inverse,
        gain,
        after,
    )


def meet_kernel(chip_ref, keep_ref, got_ref, *outs):
    step = pl.program_id(0)
    for j, out in enumerate(outs):

        @pl.when(step == j)
        def _():
            out[...] = (keep_ref[0].astype(FULL) + got_ref[0].astype(FULL)).astype(LOW)


def meet_cores(chip, keep, got):
    chips, rows, columns = keep.shape
    block = pl.BlockSpec((1, rows, columns), lambda j, chip_ref: (chip_ref[0] ^ j, 0, 0))
    return pl.pallas_call(
        meet_kernel,
        grid_spec=pltpu.PrefetchScalarGridSpec(
            num_scalar_prefetch=1,
            grid=(chips,),
            in_specs=[block, block],
            out_specs=[pl.BlockSpec((rows, columns), lambda j, chip_ref: (0, 0))] * chips,
        ),
        out_shape=[jax.ShapeDtypeStruct((rows, columns), LOW)] * chips,
        compiler_params=pltpu.CompilerParams(vmem_limit_bytes=24 << 20),
        cost_estimate=pl.CostEstimate(flops=0, transcendentals=0, bytes_accessed=6 * chips * rows * columns),
        name="meet_cores",
    )(chip.reshape(1), keep, got)


def add_kernel(*refs):
    total = refs[0][...].astype(FULL)
    for ref in refs[1:-1]:
        total += ref[...].astype(FULL)
    refs[-1][...] = total.astype(LOW)


def add_all(*values):
    return local_call(add_kernel, "add_all", jax.ShapeDtypeStruct(values[0].shape, LOW), *values)


def up_kernel(side_ref, own_ref, across_ref, *refs, owners, half):
    out_ref = refs[-1]
    hidden_part = out_ref.shape[2] // owners
    for mine in range(2):

        @pl.when(side_ref[0] == mine)
        def _():
            for side in range(2):
                ref = own_ref if side == mine else across_ref
                first = side * half
                count = min(half, hidden_part - first)
                for owner in range(owners):
                    target = owner * hidden_part + first
                    source = owner * half
                    out_ref[0, :, target : target + count] = ref[:, source : source + count].astype(FULL)


def mixed_kernel(me_ref, sums_ref, others_ref, *refs, ranks, layers_seen, offset):
    shares, (qkv_out, out_out) = refs[:ranks], refs[-2:]
    width = out_out.shape[2]
    slab, flank, pairs = width // ranks, width // 2, ranks // 2
    for me in range(ranks):

        @pl.when(me_ref[0] == me)
        def _():
            side, pair = me % 2, me // 2
            for j in range(pairs):
                for flip in range(2):
                    rank = (pair - j) % pairs * 2 + (side ^ flip)
                    ref = shares[2 * j + flip]
                    for i in range(3):
                        target = (i * ranks + rank) * slab
                        qkv_out[0, :, target : target + slab] = ref[:, i * slab : (i + 1) * slab].astype(FULL)
            for flip, ref in enumerate((sums_ref, others_ref)):
                target = (side ^ flip) * flank
                out_out[0, :, target : target + flank] = ref[:, offset : offset + flank].astype(FULL)


def write_layer(kernel, name, layer, layers, shapes, earlier, scalar, *values):
    return pl.pallas_call(
        kernel,
        grid=(1,),
        out_shape=tuple(jax.ShapeDtypeStruct((layers,) + s, FULL) for s in shapes),
        in_specs=[pl.BlockSpec(memory_space=pltpu.SMEM)]
        + [pl.BlockSpec(v.shape, lambda i: (0, 0)) for v in values]
        + [pl.BlockSpec(memory_space=pl.ANY)] * len(earlier),
        out_specs=tuple(pl.BlockSpec((1,) + s, lambda i: (layer, 0, 0)) for s in shapes),
        input_output_aliases={1 + len(values) + i: i for i in range(len(earlier))},
        compiler_params=pltpu.CompilerParams(vmem_limit_bytes=40 << 20),
        cost_estimate=pl.CostEstimate(flops=0, transcendentals=0, bytes_accessed=8 << 20),
        name=name,
    )(scalar.reshape(1), *values, *earlier)


def down_kernel(side_ref, *refs):
    out_ref = refs[-1]
    half = refs[0].shape[0]
    hidden_part = out_ref.shape[0]
    for mine in range(2):

        @pl.when(side_ref[0] == mine)
        def _():
            for layer in range(len(refs) // 2):
                for side in range(2):
                    ref = refs[2 * layer + (side != mine)]
                    first = side * half
                    count = min(half, hidden_part - first)
                    out_ref[first : first + count, layer, :] = ref[:count].astype(FULL)


def pack_kernel(side_ref, *refs, owners, layers, half):
    out_ref = refs[-1]
    each = len(refs) // layers
    out_ref[...] = jnp.zeros_like(out_ref)
    target = 0
    for layer in range(layers):
        rows = refs[layer * each : (layer + 1) * each]
        for ref in rows[:-1]:
            part = ref.shape[1] // owners
            for owner in range(owners):
                out_ref[owner : owner + 1, target : target + part] = ref[:, owner * part : (owner + 1) * part]
            target += part
        for side in range(2):

            @pl.when(side_ref[0] == side)
            def _():
                for owner in range(owners):
                    first = target + side * half
                    out_ref[owner : owner + 1, first : first + half] = rows[-1][
                        :, owner * half : (owner + 1) * half
                    ]

        target += 2 * half


def unpack_kernel(first_ref, second_ref, *outs, layers, half):
    values = first_ref[...] + second_ref[...]
    part = outs[0].shape[1]
    target = 0
    for layer in range(layers):
        for out in outs[:-1]:
            out[layer : layer + 1, :] = values[:, target : target + part]
            target += part
        out = outs[-1]
        out[layer : layer + 1, :] = values[:, target : target + out.shape[1]]
        target += 2 * half


class Order:
    def __init__(self):
        self.last = ()

    def enter(self, *values):
        if not self.last:
            return values
        return lax.optimization_barrier(tuple(values) + self.last)[: len(values)]

    def leave(self, *values):
        self.last = tuple(values)


class Chain:
    def __init__(self, steps):
        self.steps = steps
        self.result = None
        self.step()

    def step(self):
        try:
            next(self.steps)
        except StopIteration as stop:
            self.result = stop.value


def make_body(ranks, owners):
    pairs, chips = ranks // 2, owners // 2

    def shift(value, step):
        return lax.ppermute(value, "seq", [(i, (i + step) % ranks) for i in range(ranks)])

    def swap(value):
        return lax.ppermute(value, "seq", [(i, i ^ 1) for i in range(ranks)])

    def pair_shift(value, step):
        return lax.ppermute(value, "seq", [(i, (i + 2 * step) % ranks) for i in range(ranks)])

    def owner_xor(value, bits):
        return lax.ppermute(value, "fsdp", [(i, i ^ bits) for i in range(owners)])

    def exchange(blocks):
        return lax.all_to_all(blocks, "seq", split_axis=0, concat_axis=0, tiled=True)

    def body(
        block_input,
        grad_output,
        attn_norm_gain,
        attn_norm_bias,
        qkv_weight,
        qv_bias,
        out_weight,
        out_bias,
        mlp_norm_gain,
        mlp_norm_bias,
        up_weight,
        up_bias,
        down_weight,
        down_bias,
    ):
        layers = qkv_weight.shape[0]
        tokens, width = block_input.shape[1:]
        slab, flank = width // ranks, width // 2
        part = qkv_weight.shape[1]
        hidden_part = down_weight.shape[1]
        half = -(-hidden_part // 32) * 16
        me = lax.axis_index("seq")
        owner = lax.axis_index("fsdp")
        core, chip = owner % 2, owner // 2
        side, pair = me % 2, me // 2

        def at(value, index, axis=0):
            return lax.dynamic_index_in_dim(value, index, axis, keepdims=False)

        def put(value, block, *index):
            return lax.dynamic_update_slice(
                value, block.reshape((1,) * len(index) + block.shape), index + (0,) * block.ndim
            )

        def rank_at(j):
            return (me + j) % ranks

        order = Order()

        def owner_steps(keep, send):
            got = owner_xor(send, 1)
            yield
            (got,) = order.enter(got)
            mine, *sends = meet_cores(chip, keep, got)
            order.leave(*sends)
            got = [owner_xor(send, 2 * j) for j, send in enumerate(sends, 1)]
            yield
            return add_all(mine, *order.enter(*got))

        def queue_steps(value):
            value = lax.psum_scatter(value, "fsdp", scatter_dimension=0, tiled=True)
            yield
            return order.enter(value)[0]

        def pair_steps(value):
            order.leave(value)
            got = [pair_shift(value, j) for j in range(1, pairs)]
            yield
            own = add_all(value, *order.enter(*got))
            order.leave(own)
            across = swap(own)
            yield
            return own, order.enter(across)[0]

        def mixed_steps(value):
            order.leave(value)
            share = value[:, : 3 * slab]
            got = [pair_shift(value, j) for j in range(1, pairs)]
            across = [swap(share)]
            yield
            got = order.enter(*got)
            total = add_all(*[v[:, offset:] for v in (value, *got)])
            sends = [g[:, : 3 * slab] for g in got]
            sends[0] = jnp.concatenate([got[0][:, :offset], total], axis=1)
            order.leave(*sends)
            across += [swap(send) for send in sends]
            yield
            across = list(order.enter(*across))
            shares = [share, across[0]]
            for piece, flipped in zip(got, across[1:], strict=True):
                shares += [piece, flipped]
            return sends[0], across[1], *shares

        def written(steps, stage, write):
            value = yield from steps
            value = yield from stage(value)
            value = write(*value)
            order.leave(*value)
            return value

        columns = width + 3 * slab
        offset = -(-3 * slab // 128) * 128

        def gather_tokens(mine):
            return [mine] + [shift(mine, j) for j in range(1, ranks)]

        def in_order(blocks):
            result = jnp.zeros((ranks,) + blocks[0].shape, LOW)
            for j, block in enumerate(blocks):
                result = put(result, block, rank_at(-j))
            return result.reshape(ranks * tokens, width)

        all_input = gather_tokens(block_input[0])
        small = (
            attn_norm_gain,
            attn_norm_bias,
            qv_bias.reshape(2 * layers, part),
            out_bias,
            mlp_norm_gain,
            mlp_norm_bias,
            down_bias,
            up_bias,
        )
        down_turned = down_weight.transpose(1, 0, 2)
        attn_shares, feed_shares = [], []
        for layer in range(layers):
            share = attn_share(
                me, out_weight[layer], *order.enter(qkv_weight[layer]), small if layer == 0 else (), layers, ranks
            )
            order.leave(share)
            attn_shares.append(lax.all_gather(share, "fsdp", axis=0))
            share = feed_share(side, *order.enter(up_weight[layer]), down_turned, layer, owners, half)
            order.leave(share)
            feed_shares.append(lax.all_gather(share, "fsdp", axis=0))
        small_all, *all_input = order.enter(attn_shares[0][:, part:], *all_input)
        rows_all = small_all[:, :layers, : 8 * part].reshape(owners, layers, 8, part)
        rows_all = rows_all.transpose(1, 2, 0, 3).reshape(layers, 8, width).astype(FULL)
        up_all = small_all[:, :layers, 8 * part : 8 * part + hidden_part].astype(FULL)
        up_all = jnp.pad(up_all, ((0, 0), (0, 0), (0, 2 * half - hidden_part)))

        vectors = []
        for layer in range(layers):
            rows = rows_all[layer]
            vectors.append(
                dict(
                    gain_one=rows[0],
                    bias_one=rows[1],
                    bias_q=lax.dynamic_slice(rows[2], (me * slab,), (slab,)),
                    bias_v=lax.dynamic_slice(rows[3], (me * slab,), (slab,)),
                    bias_out=rows[4],
                    gain_two=rows[5],
                    bias_two=rows[6],
                    bias_down=rows[7],
                    bias_up=lax.dynamic_slice(
                        up_all[:, layer], (0, side * half), (owners, half)
                    ).reshape(owners * half),
                )
            )

        hidden = block_input[0].astype(FULL)
        stored = []
        for layer in range(layers):
            v = vectors[layer]
            normed_one, inverse_one = normalize(hidden)
            if layer == 0:
                normed_all, _ = normalize(in_order(all_input).astype(FULL))
                attn_in = (normed_all * v["gain_one"] + v["bias_one"]).astype(LOW)
            else:
                attn_mine = (normed_one * v["gain_one"] + v["bias_one"]).astype(LOW)
                order.leave(attn_mine)
                attn_in = in_order(order.enter(*gather_tokens(attn_mine)))
            attn = order.enter(attn_shares[layer])[0][:, :part].reshape(width, columns)
            proj_out, proj_qkv = lax.optimization_barrier((attn[:, :width], attn[:, width:]))
            bias_row = jnp.concatenate([v["bias_q"], jnp.zeros((slab,), FULL), v["bias_v"]])
            projected = (mm(attn_in, proj_qkv) + bias_row).astype(LOW)
            qkv = jnp.stack([projected[:, i * slab : (i + 1) * slab] for i in range(3)])
            out_heads, lse = attend_forward(qkv)
            out_heads = out_heads.reshape(ranks, tokens, slab)
            order.leave(out_heads)
            (attended,) = order.enter(exchange(out_heads))
            after_attn = (
                hidden
                + lax.dot_general(
                    attended,
                    proj_out.reshape(ranks, slab, width),
                    (((0, 2), (0, 1)), ((), ())),
                    preferred_element_type=FULL,
                )
                + v["bias_out"]
            )
            normed_two, inverse_two = normalize(after_attn)
            mlp_mine = (normed_two * v["gain_two"] + v["bias_two"]).astype(LOW)
            order.leave(mlp_mine)
            attended_other = swap(order.enter(attended)[0])
            mlp_other, attended_other, feed = order.enter(swap(mlp_mine), attended_other, feed_shares[layer])
            attended_pair = jnp.concatenate([attended, attended_other], axis=1)
            proj_up = jnp.concatenate(
                [feed[:, i * part : (i + 1) * part, width : width + owners // 2 * half] for i in range(2)], axis=2
            ).reshape(width, owners * half)
            proj_down = feed[:, :half, :width].reshape(owners * half, width)
            proj_up, proj_down = lax.optimization_barrier((proj_up, proj_down))
            mlp_in = jnp.concatenate([mlp_mine, mlp_other], axis=0)
            pre_act = mm(mlp_in, proj_up) + v["bias_up"]
            activated = tangent_gelu(pre_act).astype(LOW)
            mixed = mm(activated, proj_down)
            leaving = mixed[tokens:].astype(LOW)
            order.leave(leaving)
            other = swap(leaving)
            if layer < layers - 1:
                (other,) = order.enter(other)
            hidden = after_attn + mixed[:tokens] + other.astype(FULL) + v["bias_down"]
            stored.append(
                (
                    (proj_qkv, proj_out, proj_up, proj_down),
                    (normed_one, inverse_one, attn_in, qkv, lse, attended_pair),
                    (normed_two, inverse_two, mlp_in, pre_act, activated),
                )
            )
        block_output = hidden.astype(LOW)[None]

        def writer(key, kernel, layer, scalar, *shapes):
            def write(*values):
                outs[key] = write_layer(
                    kernel, "write_" + key, layer, layers, shapes, outs[key], scalar, *values
                )
                return outs[key]

            return write

        def held(*values):
            return values

        def sum_rows(value):
            return jnp.sum(value, axis=0, keepdims=True)

        grad_hidden, grad_mine = grad_output[0].astype(FULL), grad_output[0]
        small_grads = [None] * layers
        downs = [None] * layers
        outs = dict(up=(), mixed=())
        before = None
        for layer in reversed(range(layers)):
            v = vectors[layer]
            proj_qkv, proj_out, proj_up, proj_down = stored[layer][0]
            normed_one, inverse_one, attn_in, qkv, lse, attended_pair = stored[layer][1]
            normed_two, inverse_two, mlp_in, pre_act, activated = stored[layer][2]
            grad_other = swap(grad_mine)
            if before:
                before["down"].step()
            (grad_other,) = order.enter(grad_other)
            grad_low, grad_pre_low, mixed, leaving, g_up_bias = feed_backward(
                grad_mine, grad_other, pre_act, proj_up, proj_down
            )
            order.leave(leaving)
            other = swap(leaving)
            g_down = weight_grad([(activated, order.enter(grad_low)[0], 0)], owners, width)
            order.leave(g_down)
            down_chain = Chain(written(queue_steps(g_down), pair_steps, held))
            keep, send = weight_grad([(mlp_in, order.enter(grad_pre_low)[0], 0)], owners, half * owners, core)
            order.leave(send)
            up_chain = Chain(
                written(
                    owner_steps(keep, send),
                    pair_steps,
                    writer(
                        "up",
                        functools.partial(up_kernel, owners=owners, half=half),
                        layer,
                        side,
                        (part, owners * hidden_part),
                    ),
                )
            )
            (other,) = order.enter(other)
            order.leave(other)
            if before:
                before["up"].step()
            grad_after, sends, after_mine, after_send, g_gain_two, g_bias_two, g_out_bias, g_down_bias = mid_backward(
                side,
                mixed,
                *order.enter(other),
                normed_two,
                inverse_two,
                v["gain_two"].reshape(1, width),
                grad_hidden,
                proj_out,
                ranks,
            )
            order.leave(sends)
            grad_heads = exchange(sends)
            after_other = swap(after_send)
            up_chain.step()
            grad_heads, after_other = order.enter(grad_heads, after_other)
            order.leave(grad_heads)
            if before:
                before["down"].step()
            grad_proj, leaving, g_q_bias, g_v_bias = attend_backward(
                qkv, order.enter(grad_heads)[0].reshape(ranks * tokens, slab), lse, proj_qkv, ranks
            )
            order.leave(leaving)
            arrived = exchange(leaving)
            if before:
                before["mixed"].step()
            (grad_proj,) = order.enter(grad_proj)
            after_pair = jnp.concatenate([after_mine, after_other], axis=0)
            attended_flat = attended_pair.transpose(1, 0, 2).reshape(2 * tokens, width)
            g_mixed = weight_grad(
                [(attn_in, grad_proj, 0), (attended_flat, after_pair, offset)],
                owners,
                offset + flank,
                core if before else None,
            )
            order.leave(*(g_mixed if before else (g_mixed,)))
            mixed_chain = Chain(
                written(
                    owner_steps(*g_mixed) if before else queue_steps(g_mixed),
                    mixed_steps,
                    writer(
                        "mixed",
                        functools.partial(mixed_kernel, ranks=ranks, layers_seen=layers, offset=offset),
                        layer,
                        me,
                        (part, 3 * width),
                        (part, width),
                    ),
                )
            )
            if before:
                mixed_chain.step()
            (arrived,) = order.enter(arrived)
            grad_hidden, grad_mine, g_gain_one, g_bias_one = end_backward(
                arrived, normed_one, inverse_one, v["gain_one"].reshape(1, width), grad_after
            )
            order.leave(grad_mine)
            up_chain.step()
            if before:
                before["up"].step()
                before["down"].step()
                before["mixed"].step()
                down_chain.step()
            last, before = before, dict(up=up_chain, down=down_chain, mixed=mixed_chain)
            downs[layer] = down_chain

            zeros = jnp.zeros((1, width), FULL)
            small_grads[layer] = (
                g_gain_one,
                g_bias_one,
                lax.dynamic_update_slice(zeros, g_q_bias, (0, me * slab)),
                lax.dynamic_update_slice(zeros, g_v_bias, (0, me * slab)),
                g_out_bias,
                g_gain_two,
                g_bias_two,
                g_down_bias,
                g_up_bias,
            )

        each = 8 * part + 2 * half
        small_sum = local_call(
            functools.partial(pack_kernel, owners=owners, layers=layers, half=half),
            "pack_small",
            jax.ShapeDtypeStruct((owners, -(-layers * each // 128) * 128), FULL),
            *order.enter(*[row for grads in small_grads for row in grads]),
            scalars=(side,),
        )
        order.leave(small_sum)
        small_sum = lax.all_to_all(small_sum, "fsdp", split_axis=0, concat_axis=0, tiled=True)
        before["up"].step()
        last["mixed"].step()
        before["mixed"].step()
        before["down"].step()
        small_sum = sum_rows(order.enter(small_sum)[0])
        order.leave(small_sum)
        total = small_sum
        for j in range(1, pairs):
            total = total + pair_shift(small_sum, j)
        before["up"].step()
        before["mixed"].step()
        (total,) = order.enter(total)
        order.leave(total)
        total_other = swap(total)
        before["down"].step()
        down_out = local_call(
            down_kernel,
            "write_down",
            jax.ShapeDtypeStruct((hidden_part, layers, width), FULL),
            *order.enter(*[piece for chain in downs for piece in chain.result]),
            scalars=(side,),
        )
        order.leave(down_out)
        s = local_call(
            functools.partial(unpack_kernel, layers=layers, half=half),
            "unpack_small",
            tuple(jax.ShapeDtypeStruct((layers, n), FULL) for n in [part] * 8 + [hidden_part]),
            *order.enter(total, total_other),
        )
        order.leave(*s)
        before["mixed"].step()
        return (
            block_output,
            grad_hidden[None],
            s[0],
            s[1],
            outs["mixed"][0],
            jnp.stack([s[2], s[3]], axis=1),
            outs["mixed"][1],
            s[4],
            s[5],
            s[6],
            outs["up"][0],
            s[8],
            down_out.transpose(1, 0, 2),
            s[7],
        )

    return body


def solution(mesh):
    row, cols, deep = P(None, "fsdp"), P("fsdp", "seq", None), P(None, "fsdp", None)
    last = P(None, None, "fsdp")
    return jax.shard_map(
        make_body(mesh.shape["seq"], mesh.shape["fsdp"]),
        mesh=mesh,
        in_specs=(cols, cols, row, row, deep, last, deep, row, row, row, deep, row, deep, row),
        out_specs=(cols, cols, row, row, deep, last, deep, row, row, row, deep, row, deep, row),
        check_vma=False,
    )
```

time: 839 us -> 639 us (0.76)
  waiting for transfers between devices: 444 us -> 215 us
  Pallas kernels: 17 us -> 122 us
  matrix products: 94.3 us -> 18.9 us
  local copies, waits for them, and re-layouts: 112 us -> 135 us
  starting transfers between devices: 105 us -> 91.3 us
  other arithmetic: 42.7 us -> 30 us
    ppermute x45 -> x6, waiting for transfers between devices: 115 us -> 3.91 us  [shift(): lax.ppermute(value, 'seq', [(i, (i + step) % ranks) for i in range(ranks)])]
    reduce_scatter x8 -> x3, waiting for transfers between devices: 110 us -> 0.02 us  [queue_steps(): value = lax.psum_scatter(value, 'fsdp', scatter_dimension=0, tiled=True)]
    pallas_call x2 -> x37, Pallas kernels: 10.1 us -> 115 us  [the longest x24 75.6 us: local_call(): pl.pallas_call(kernel, out_shape=out_shape, in_specs=[pl.BlockSpec(memory...]
    dot_general x18 -> x2, matrix products: 69.7 us -> 4.54 us  [body(): lax.dot_general(attended, proj_out.reshape(ranks, slab, width), (((0, 2),...]
    ppermute x45 -> x6, starting transfers between devices: 72.1 us -> 12.6 us  [shift(): lax.ppermute(value, 'seq', [(i, (i + step) % ranks) for i in range(ranks)])]
    unnamed x238 -> x304, local copies, waits for them, and re-layouts: 16.5 us -> 67.9 us
    all_gather x6 -> x4, waiting for transfers between devices: 94.3 us -> 59.5 us  [the longest x2 29.8 us: body(): attn_shares.append(lax.all_gather(share, 'fsdp', axis=0))]
    all_to_all x0 -> x6, waiting for transfers between devices: none -> 33.4 us  [exchange(): lax.all_to_all(blocks, 'seq', split_axis=0, concat_axis=0, tiled=True)]
  transfers between devices with their start and end apart: 80 -> 60, of which waited for: 45 -> 22; matrix products, arithmetic and copies ran while one was open for 24% -> 18% of each run, Pallas kernels for 1% -> 17%
where the time goes in v2:
time: 639 us; the launch traced here: 628 us
  waiting for transfers between devices  215 us (34%)
  local copies, waits for them, and re-layouts  135 us (21%)
  Pallas kernels  122 us (19%)
  starting transfers between devices  91.3 us (14%)
  other arithmetic  30 us (5%)
  matrix products  18.9 us (3%)
  between operations  16 us (3%)
    pallas_call x24, Pallas kernels, local_call(): pl.pallas_call(kernel, out_shape=out_shape, in_specs=[pl.BlockSpec(memory...  75.6 us
    ppermute x21, waiting for transfers between devices, swap(): return lax.ppermute(value, 'seq', [(i, i ^ 1) for i in range(ranks)])  73.1 us
    unnamed x304, local copies, waits for them, and re-layouts  67.9 us
    ppermute x7, waiting for transfers between devices, pair_shift(): lax.ppermute(value, 'seq', [(i, (i + 2 * step) % ranks) for i in range(ra...  39.4 us
    all_to_all x6, waiting for transfers between devices, exchange(): lax.all_to_all(blocks, 'seq', split_axis=0, concat_axis=0, tiled=True)  33.4 us
    all_to_all x6, starting transfers between devices, exchange(): lax.all_to_all(blocks, 'seq', split_axis=0, concat_axis=0, tiled=True)  31.7 us
    all_gather x2, waiting for transfers between devices, body(): attn_shares.append(lax.all_gather(share, 'fsdp', axis=0))  29.8 us
    all_gather x2, waiting for transfers between devices, body(): feed_shares.append(lax.all_gather(share, 'fsdp', axis=0))  29.7 us
  transfers between devices with their start and end apart: 60, of which 22 were waited for; matrix products, arithmetic and copies ran while one was open for 18% of the time, Pallas kernels for 17%

profile of v2, /device:TPU:0, one launch (start us, length us, event | category | flops | bytes accessed | tf_op | source)
XLA Modules:
  0.0 628.3 jit_solution(1795480220778364329)
XLA Ops:
  12.2 3.4 slice_bitcast_fusion
  26.6 3.1 collective-permute-start
  33.8 21.2 %all-gather.9.cloned.1.call-done = bf16[1216,2016]{1,0:T(8,128)(2,1)} async-done(((bf16[152,2016]{1,0:T(8,128)(2,1)}), bf16[1216,2016]{1,0:T(8,128)(2,1)}) %all-gather.9.cloned.1.call-update) | async-done | bytes 4902928 | tf_op jit(solution)/shard_map/all_gather | solution.py:759
  56.0 2.7 slice.222
  70.2 3.4 attend_forward.2
  76.2 5.0 all-to-all-start
  82.6 8.6 %all-to-all-done = bf16[4,128,288]{1,2,0:T(8,128)(2,1)S(1)} async-done(((bf16[4,128,288]{1,2,0:T(8,128)(2,1)}), bf16[4,128,288]{1,2,0:T(8,128)(2,1)S(1)}, u32[]{:S(2)}, u32[]{:S(2)}) %all-to-all-start) | async-done | bytes 294944 | tf_op jit(solution)/shard_map/all_to_all | solution.py:636
  99.6 5.6 collective-permute-done.3
  105.2 3.4 collective-permute-done.4
  108.6 12.8 %all-gather.11.cloned.1.call-done = bf16[2304,2304]{1,0:T(8,128)(2,1)} async-done(((bf16[288,2304]{1,0:T(8,128)(2,1)}), bf16[2304,2304]{1,0:T(8,128)(2,1)}) %all-gather.11.cloned.1.call-update) | async-done | bytes 10616848 | tf_op jit(solution)/shard_map/all_gather | solution.py:762
  121.4 2.8 slice.235
  124.2 4.8 fusion.47
  130.6 4.7 fusion.15
  138.6 7.7 %collective-permute-done.5 = bf16[128,1152]{1,0:T(8,128)(2,1)S(1)} collective-permute-done((bf16[128,1152]{1,0:T(8,128)(2,1)S(1)}, bf16[128,1152]{1,0:T(8,128)(2,1)S(1)}, u32[]{:S(2)}, u32[]{:S(2)}) %collective-permute-start.5) | collective-permute-done | bytes 294944 | tf_op jit(solution)/shard_map/ppermute | solution.py:627
  153.6 8.6 %all-gather.13.cloned.1.call-done = bf16[1152,2016]{1,0:T(8,128)(2,1)} async-done(((bf16[144,2016]{1,0:T(8,128)(2,1)}), bf16[1152,2016]{1,0:T(8,128)(2,1)}) %all-gather.13.cloned.1.call-update) | async-done | bytes 4644880 | tf_op jit(solution)/shard_map/all_gather | solution.py:759
  162.2 3.5 slice.291.proj_ref
  167.4 3.9 collective-permute-done.7
  176.8 3.4 attend_forward.3
  182.8 8.8 %all-to-all-start.1 = ((bf16[4,128,288]{1,2,0:T(8,128)(2,1)}), bf16[4,128,288]{1,2,0:T(8,128)(2,1)S(1)}, u32[]{:S(2)}, u32[]{:S(2)}) async-start(bf16[4,128,288]{1,2,0:T(8,128)(2,1)} %copy.71), calls=%async_computation.1 | async-start | bytes 589824 | tf_op jit(solution)/shard_map/all_to_all | solution.py:636
  195.5 4.4 all-to-all-done.1
  199.9 2.7 fusion.50
  204.4 2.8 collective-permute-start.9
  211.5 16.9 %all-gather.15.cloned.1.call-done = bf16[2304,2304]{1,0:T(8,128)(2,1)} async-done(((bf16[288,2304]{1,0:T(8,128)(2,1)}), bf16[2304,2304]{1,0:T(8,128)(2,1)}) %all-gather.15.cloned.1.call-update) | async-done | bytes 10616848 | tf_op jit(solution)/shard_map/all_gather | solution.py:762
  228.4 3.0 fusion.46
  231.4 5.1 slice.255
  238.1 3.4 fusion.23
  245.3 8.2 %feed_backward.2 = (bf16[256,1152]{1,0:T(8,128)(2,1)S(1)}, bf16[256,2176]{1,0:T(8,128)(2,1)S(1)}, f32[128,1152]{1,0:T(8,128)S(1)}, bf16[128,1152]{1,0:T(8,128)(2,1)S(1)}, f32[1,2176]{1,0:T(1,128)S(1)}) custom-call(bf16[128,1152]{1,0:T(8,128)(2,1)S(1)} %bitcast.161, bf16[128,1152]{1,0:T(8,128)(2,1)} %collective-permute-done.12.other_ref, ...), custom_call_target="tpu_custom_call" | custom-call | flops 20000000000 | bytes 15442432 | tf_op jit(solution)/shard_map/feed_backward/pallas_call | solution.py:249
  256.7 4.0 weight_grad.6
  268.1 6.0 weight_grad.7
  284.2 2.7 mid_backward.2
  293.5 4.2 all-to-all-start.2
  312.3 4.0 meet_cores.3
  324.7 7.3 %attend_backward.2 = (bf16[512,864]{1,0:T(8,128)(2,1)S(1)}, bf16[4,128,1152]{2,1,0:T(8,128)(2,1)S(1)}, f32[1,288]{1,0:T(1,128)S(1)}, f32[1,288]{1,0:T(1,128)S(1)}) custom-call(bf16[3,512,288]{2,1,0:T(8,128)(2,1)S(1)} %copy-done.13, bf16[512,288]{1,0:T(8,128)(2,1)S(1)} %bitcast.154, f32[512,4]{1,0:T(8,128)S(1)} %copy-done.39, bf16[1152,864]{1,0:T(8,128)(2,1)S(1)} %copy-done.5), custom_call_target="tpu_custom_call" | custom-call | bytes 25165824 | tf_op jit(solution)/shard_map/attend_backward/pallas_call | solution.py:156
  335.1 5.2 all-to-all-start.3
  343.9 3.7 weight_grad.8
  347.6 20.3 %all-to-all-done.3.got_ref = bf16[4,128,1152]{2,1,0:T(8,128)(2,1)} async-done(((bf16[4,128,1152]{2,1,0:T(8,128)(2,1)}), bf16[4,128,1152]{2,1,0:T(8,128)(2,1)}, u32[]{:S(2)}, u32[]{:S(2)}) %all-to-all-start.3) | async-done | bytes 1179680 | tf_op jit(solution)/shard_map/all_to_all | solution.py:636
  369.0 2.7 end_backward.2
  378.1 4.2 collective-permute-done.16.other_ref
  384.0 9.0 %feed_backward.3 = (bf16[256,1152]{1,0:T(8,128)(2,1)S(1)}, bf16[256,2176]{1,0:T(8,128)(2,1)S(1)}, f32[128,1152]{1,0:T(8,128)S(1)}, bf16[128,1152]{1,0:T(8,128)(2,1)}, f32[1,2176]{1,0:T(1,128)S(1)}) custom-call(bf16[128,1152]{1,0:T(8,128)(2,1)} %get-tuple-element.255.mine_ref, bf16[128,1152]{1,0:T(8,128)(2,1)S(1)} %collective-permute-done.16.other_ref, ...), custom_call_target="tpu_custom_call" | custom-call | flops 20000000000 | bytes 15442432 | tf_op jit(solution)/shard_map/feed_backward/pallas_call | solution.py:249
  395.8 3.9 weight_grad.9
  400.9 6.2 weight_grad.10
  408.6 3.0 collective-permute-done.20.got_ref
  411.7 8.2 %collective-permute-done.21.refs_1_ = bf16[144,2176]{1,0:T(8,128)(2,1)} collective-permute-done((bf16[144,2176]{1,0:T(8,128)(2,1)}, bf16[144,2176]{1,0:T(8,128)(2,1)}, u32[]{:S(2)}, u32[]{:S(2)}) %collective-permute-start.21) | collective-permute-done | bytes 626720 | tf_op jit(solution)/shard_map/ppermute | solution.py:630
  422.2 2.7 mid_backward.3
  429.6 4.1 all-to-all-start.4
  439.9 4.0 meet_cores.4
  455.0 7.3 %attend_backward.3 = (bf16[512,864]{1,0:T(8,128)(2,1)S(1)}, bf16[4,128,1152]{2,1,0:T(8,128)(2,1)S(1)}, f32[1,288]{1,0:T(1,128)S(1)}, f32[1,288]{1,0:T(1,128)S(1)}) custom-call(bf16[3,512,288]{2,1,0:T(8,128)(2,1)S(1)} %copy-done.11, bf16[512,288]{1,0:T(8,128)(2,1)S(1)} %bitcast.155, f32[512,4]{1,0:T(8,128)S(1)} %copy-done.37, bf16[1152,864]{1,0:T(8,128)(2,1)S(1)} %copy-done.3), custom_call_target="tpu_custom_call" | custom-call | bytes 25165824 | tf_op jit(solution)/shard_map/attend_backward/pallas_call | solution.py:156
  464.2 4.4 all-to-all-start.5
  471.0 6.3 weight_grad.11
  478.2 2.9 collective-permute-start.26
  485.8 2.7 add_all.12.refs_0_
  488.4 3.2 write_up.2.refs_0_
  491.6 21.0 %collective-permute-done.27.refs_3_ = bf16[272,1152]{1,0:T(8,128)(2,1)S(1)} collective-permute-done((bf16[272,1152]{1,0:T(8,128)(2,1)}, bf16[272,1152]{1,0:T(8,128)(2,1)S(1)}, u32[]{:S(2)}, u32[]{:S(2)}) %collective-permute-start.27) | collective-permute-done | bytes 626720 | tf_op jit(solution)/shard_map/ppermute | solution.py:627
  513.0 3.3 collective-permute-start.38
  525.8 2.7 end_backward.3
  529.8 3.4 all-to-all-start.6
  533.2 7.1 %collective-permute-done.38.refs_1_ = bf16[144,2176]{1,0:T(8,128)(2,1)} collective-permute-done((bf16[144,2176]{1,0:T(8,128)(2,1)}, bf16[144,2176]{1,0:T(8,128)(2,1)}, u32[]{:S(2)}, u32[]{:S(2)}) %collective-permute-start.38) | collective-permute-done | bytes 626720 | tf_op jit(solution)/shard_map/ppermute | solution.py:630
  542.8 2.9 write_mixed.2
  545.6 5.8 collective-permute-done.35.refs_3_
  555.6 23.8 %collective-permute-done.32.refs_1_ = bf16[272,1152]{1,0:T(8,128)(2,1)} collective-permute-done((bf16[272,1152]{1,0:T(8,128)(2,1)}, bf16[272,1152]{1,0:T(8,128)(2,1)}, u32[]{:S(2)}, u32[]{:S(2)}) %collective-permute-start.32) | collective-permute-done | bytes 626720 | tf_op jit(solution)/shard_map/ppermute | solution.py:630
  581.9 10.5 %collective-permute-done.41.across_ref = bf16[144,2176]{1,0:T(8,128)(2,1)S(1)} collective-permute-done((bf16[144,2176]{1,0:T(8,128)(2,1)S(1)}, bf16[144,2176]{1,0:T(8,128)(2,1)S(1)}, u32[]{:S(2)}, u32[]{:S(2)}) %collective-permute-start.41) | collective-permute-done | bytes 626720 | tf_op jit(solution)/shard_map/ppermute | solution.py:627
  596.8 14.8 %collective-permute-done.43.refs_1_ = bf16[272,1152]{1,0:T(8,128)(2,1)S(1)} collective-permute-done((bf16[272,1152]{1,0:T(8,128)(2,1)S(1)}, bf16[272,1152]{1,0:T(8,128)(2,1)S(1)}, u32[]{:S(2)}, u32[]{:S(2)}) %collective-permute-start.43) | collective-permute-done | bytes 626720 | tf_op jit(solution)/shard_map/ppermute | solution.py:627
  611.5 3.5 write_down.1
  615.1 3.0 collective-permute-done.42.second_ref
  (530 shorter events, 214.5 us)
Async XLA Ops:
  7.2 47.9 %all-gather.9.cloned.1.call-start = ((), (), s32[]{:S(2)}) async-start(), calls=%async_computation.13 | async-start | bytes 5603328 | tf_op jit(solution)/shard_map/all_gather | solution.py:759
  12.1 109.2 %all-gather.11.cloned.1.call-start = ((), (), s32[]{:S(2)}) async-start(), calls=%async_computation.14 | async-start | bytes 11943936 | tf_op jit(solution)/shard_map/all_gather | solution.py:762
  20.0 142.2 %all-gather.13.cloned.1.call-start = ((), (), s32[]{:S(2)}) async-start(), calls=%async_computation.15 | async-start | bytes 5308416 | tf_op jit(solution)/shard_map/all_gather | solution.py:759
  22.1 206.3 %all-gather.15.cloned.1.call-start = ((), (), s32[]{:S(2)}) async-start(), calls=%async_computation.16 | async-start | bytes 11943936 | tf_op jit(solution)/shard_map/all_gather | solution.py:762
  26.6 34.2 %collective-permute-start = (bf16[128,1152]{1,0:T(8,128)(2,1)}, bf16[128,1152]{1,0:T(8,128)(2,1)S(1)}, u32[]{:S(2)}, u32[]{:S(2)}) collective-permute-start(bf16[128,1152]{1,0:T(8,128)(2,1)} %bitcast), channel_id=1, source_target_pairs={{0,8},{8,16},{16,24},{24,0},{1,9},{9,17},{17,25},{25,1},{2,10},{10... | collective-permute-start | bytes 884744 | tf_op jit(solution)/shard_map/ppermute | solution.py:624
  29.6 31.1 %collective-permute-start.1 = (bf16[128,1152]{1,0:T(8,128)(2,1)}, bf16[128,1152]{1,0:T(8,128)(2,1)S(1)}, u32[]{:S(2)}, u32[]{:S(2)}) collective-permute-start(bf16[128,1152]{1,0:T(8,128)(2,1)} %bitcast), channel_id=1, source_target_pairs={{0,16},{8,24},{16,0},{24,8},{1,17},{9,25},{17,1},{25,9},{2,18},{10... | collective-permute-start | bytes 884744 | tf_op jit(solution)/shard_map/ppermute | solution.py:624
  32.3 28.5 %collective-permute-start.2 = (bf16[128,1152]{1,0:T(8,128)(2,1)}, bf16[128,1152]{1,0:T(8,128)(2,1)}, u32[]{:S(2)}, u32[]{:S(2)}) collective-permute-start(bf16[128,1152]{1,0:T(8,128)(2,1)} %bitcast), channel_id=1, source_target_pairs={{0,24},{8,0},{16,8},{24,16},{1,25},{9,1},{17,9},{25,17},{2,26},{10... | collective-permute-start | bytes 884744 | tf_op jit(solution)/shard_map/ppermute | solution.py:624
  76.2 15.0 %all-to-all-start = ((bf16[4,128,288]{1,2,0:T(8,128)(2,1)}), bf16[4,128,288]{1,2,0:T(8,128)(2,1)S(1)}, u32[]{:S(2)}, u32[]{:S(2)}) async-start(bf16[4,128,288]{1,2,0:T(8,128)(2,1)} %copy.69), calls=%async_computation | async-start | bytes 589824 | tf_op jit(solution)/shard_map/all_to_all | solution.py:636
  93.1 31.1 %copy-start.120 = (f32[128,1152]{1,0:T(8,128)}, f32[128,1152]{1,0:T(8,128)S(1)}, u32[]{:S(2)}) copy-start(f32[128,1152]{1,0:T(8,128)S(1)} %get-tuple-element.492) | copy-start | bytes 1769476
  94.9 10.3 %collective-permute-start.3 = (bf16[128,1152]{1,0:T(8,128)(2,1)}, bf16[128,1152]{1,0:T(8,128)(2,1)}, u32[]{:S(2)}, u32[]{:S(2)}) collective-permute-start(bf16[128,1152]{1,0:T(8,128)(2,1)} %get-tuple-element.452), channel_id=1, source_target_pairs={{0,8},{8,0},{16,24},{24,16},{1,9},{9,1},{17,25},{25,17},{2,10},{10... | collective-permute-start | bytes 884744 | tf_op jit(solution)/shard_map/ppermute | solution.py:627
  94.9 13.6 %collective-permute-start.4 = (bf16[4,128,288]{1,2,0:T(8,128)(2,1)S(1)}, bf16[4,128,288]{1,2,0:T(8,128)(2,1)}, u32[]{:S(2)}, u32[]{:S(2)}) collective-permute-start(bf16[4,128,288]{1,2,0:T(8,128)(2,1)S(1)} %all-to-all-done), channel_id=1, source_target_pairs={{0,8},{8,0},{16,24},{24,16},{1,9},{9,1},{17,25},{25,17},{2,10},{10... | collective-permute-start | bytes 884744 | tf_op jit(solution)/shard_map/ppermute | solution.py:627
  137.1 9.2 %collective-permute-start.5 = (bf16[128,1152]{1,0:T(8,128)(2,1)S(1)}, bf16[128,1152]{1,0:T(8,128)(2,1)S(1)}, u32[]{:S(2)}, u32[]{:S(2)}) collective-permute-start(bf16[128,1152]{1,0:T(8,128)(2,1)S(1)} %slice.353), channel_id=1, source_target_pairs={{0,8},{8,0},{16,24},{24,16},{1,9},{9,1},{17,25},{25,17},{2,10},{10... | collective-permute-start | bytes 884744 | tf_op jit(solution)/shard_map/ppermute | solution.py:627
  148.3 19.1 %collective-permute-start.6 = (bf16[128,1152]{1,0:T(8,128)(2,1)S(1)}, bf16[128,1152]{1,0:T(8,128)(2,1)}, u32[]{:S(2)}, u32[]{:S(2)}) collective-permute-start(bf16[128,1152]{1,0:T(8,128)(2,1)S(1)} %get-tuple-element.215), channel_id=1, source_target_pairs={{0,8},{8,16},{16,24},{24,0},{1,9},{9,17},{17,25},{25,1},{2,10},{10... | collective-permute-start | bytes 884744 | tf_op jit(solution)/shard_map/ppermute | solution.py:624
  149.8 21.6 %collective-permute-start.7 = (bf16[128,1152]{1,0:T(8,128)(2,1)S(1)}, bf16[128,1152]{1,0:T(8,128)(2,1)}, u32[]{:S(2)}, u32[]{:S(2)}) collective-permute-start(bf16[128,1152]{1,0:T(8,128)(2,1)S(1)} %get-tuple-element.215), channel_id=1, source_target_pairs={{0,16},{8,24},{16,0},{24,8},{1,17},{9,25},{17,1},{25,9},{2,18},{10... | collective-permute-start | bytes 884744 | tf_op jit(solution)/shard_map/ppermute | solution.py:624
  152.2 19.2 %collective-permute-start.8 = (bf16[128,1152]{1,0:T(8,128)(2,1)S(1)}, bf16[128,1152]{1,0:T(8,128)(2,1)}, u32[]{:S(2)}, u32[]{:S(2)}) collective-permute-start(bf16[128,1152]{1,0:T(8,128)(2,1)S(1)} %get-tuple-element.215), channel_id=1, source_target_pairs={{0,24},{8,0},{16,8},{24,16},{1,25},{9,1},{17,9},{25,17},{2,26},{10... | collective-permute-start | bytes 884744 | tf_op jit(solution)/shard_map/ppermute | solution.py:624
  176.8 23.1 %copy-start.138 = (f32[1152]{0:T(1024)S(1)}, f32[1152]{0:T(1024)}, u32[]{:S(2)}) copy-start(f32[1152]{0:T(1024)} %get-tuple-element.437) | copy-start | bytes 13828
  182.8 17.0 %all-to-all-start.1 = ((bf16[4,128,288]{1,2,0:T(8,128)(2,1)}), bf16[4,128,288]{1,2,0:T(8,128)(2,1)S(1)}, u32[]{:S(2)}, u32[]{:S(2)}) async-start(bf16[4,128,288]{1,2,0:T(8,128)(2,1)} %copy.71), calls=%async_computation.1 | async-start | bytes 589824 | tf_op jit(solution)/shard_map/all_to_all | solution.py:636
  191.6 185.4 %reduce-scatter.4.cloned.1.call-start = ((), (), s32[]{:S(2)}) async-start(), calls=%async_computation.10 | async-start | bytes 5640192 | tf_op jit(solution)/shard_map/reduce_scatter | solution.py:689
  191.8 53.2 %collective-permute-start.12 = (bf16[128,1152]{1,0:T(8,128)(2,1)S(1)}, bf16[128,1152]{1,0:T(8,128)(2,1)}, u32[]{:S(2)}, u32[]{:S(2)}) collective-permute-start(bf16[128,1152]{1,0:T(8,128)(2,1)S(1)} %bitcast.160), channel_id=1, source_target_pairs={{0,8},{8,0},{16,24},{24,16},{1,9},{9,1},{17,25},{25,17},{2,10},{10... | collective-permute-start | bytes 884744 | tf_op jit(solution)/shard_map/ppermute | solution.py:627
  204.4 24.0 %collective-permute-start.9 = (bf16[128,1152]{1,0:T(8,128)(2,1)}, bf16[128,1152]{1,0:T(8,128)(2,1)}, u32[]{:S(2)}, u32[]{:S(2)}) collective-permute-start(bf16[128,1152]{1,0:T(8,128)(2,1)} %get-tuple-element.446), channel_id=1, source_target_pairs={{0,8},{8,0},{16,24},{24,16},{1,9},{9,1},{17,25},{25,17},{2,10},{10... | collective-permute-start | bytes 884744 | tf_op jit(solution)/shard_map/ppermute | solution.py:627
  207.2 21.2 %collective-permute-start.10 = (bf16[4,128,288]{1,2,0:T(8,128)(2,1)}, bf16[4,128,288]{1,2,0:T(8,128)(2,1)}, u32[]{:S(2)}, u32[]{:S(2)}) collective-permute-start(bf16[4,128,288]{1,2,0:T(8,128)(2,1)} %copy-done.128), channel_id=1, source_target_pairs={{0,8},{8,0},{16,24},{24,16},{1,9},{9,1},{17,25},{25,17},{2,10},{10... | collective-permute-start | bytes 884744 | tf_op jit(solution)/shard_map/ppermute | solution.py:627
  263.8 15.6 %collective-permute-start.13 = (bf16[128,1152]{1,0:T(8,128)(2,1)}, bf16[128,1152]{1,0:T(8,128)(2,1)}, u32[]{:S(2)}, u32[]{:S(2)}) collective-permute-start(bf16[128,1152]{1,0:T(8,128)(2,1)} %copy-done.74), channel_id=1, source_target_pairs={{0,8},{8,0},{16,24},{24,16},{1,9},{9,1},{17,25},{25,17},{2,10},{10... | collective-permute-start | bytes 884744 | tf_op jit(solution)/shard_map/ppermute | solution.py:627
  275.6 35.0 %collective-permute-start.15 = (bf16[4,144,2176]{2,1,0:T(8,128)(2,1)}, bf16[4,144,2176]{2,1,0:T(8,128)(2,1)}, u32[]{:S(2)}, u32[]{:S(2)}) collective-permute-start(bf16[4,144,2176]{2,1,0:T(8,128)(2,1)} %get-tuple-element.236), channel_id=1, source_target_pairs={{0,1},{1,0},{2,3},{3,2},{4,5},{5,4},{6,7},{7,6},{8,9},{9,8},{10,11... | collective-permute-start | bytes 7520264 | tf_op jit(solution)/shard_map/ppermute | solution.py:633
  293.5 27.2 %all-to-all-start.2 = ((bf16[4,128,288]{1,2,0:T(8,128)(2,1)}), bf16[4,128,288]{1,2,0:T(8,128)(2,1)}, u32[]{:S(2)}, u32[]{:S(2)}) async-start(bf16[4,128,288]{1,2,0:T(8,128)(2,1)} %copy.73), calls=%async_computation.2 | async-start | bytes 589824 | tf_op jit(solution)/shard_map/all_to_all | solution.py:636
  299.7 21.0 %collective-permute-start.14 = (bf16[128,576]{1,0:T(8,128)(2,1)S(1)}, bf16[128,576]{1,0:T(8,128)(2,1)}, u32[]{:S(2)}, u32[]{:S(2)}) collective-permute-start(bf16[128,576]{1,0:T(8,128)(2,1)S(1)} %copy-done.76), channel_id=1, source_target_pairs={{0,8},{8,0},{16,24},{24,16},{1,9},{9,1},{17,25},{25,17},{2,10},{10... | collective-permute-start | bytes 442376 | tf_op jit(solution)/shard_map/ppermute | solution.py:627
  306.4 129.2 %collective-permute-start.11 = (bf16[128,1152]{1,0:T(8,128)(2,1)}, bf16[128,1152]{1,0:T(8,128)(2,1)}, u32[]{:S(2)}, u32[]{:S(2)}) collective-permute-start(bf16[128,1152]{1,0:T(8,128)(2,1)} %slice.352), channel_id=1, source_target_pairs={{0,8},{8,0},{16,24},{24,16},{1,9},{9,1},{17,25},{25,17},{2,10},{10... | collective-permute-start | bytes 884744 | tf_op jit(solution)/shard_map/ppermute | solution.py:627
  317.2 55.4 %collective-permute-start.17 = (bf16[144,2176]{1,0:T(8,128)(2,1)}, bf16[144,2176]{1,0:T(8,128)(2,1)}, u32[]{:S(2)}, u32[]{:S(2)}) collective-permute-start(bf16[144,2176]{1,0:T(8,128)(2,1)} %get-tuple-element.242), channel_id=1, source_target_pairs={{0,2},{1,3},{2,0},{3,1},{4,6},{5,7},{6,4},{7,5},{8,10},{9,11},{10,... | collective-permute-start | bytes 1880072 | tf_op jit(solution)/shard_map/ppermute | solution.py:633
  318.7 53.8 %collective-permute-start.18 = (bf16[144,2176]{1,0:T(8,128)(2,1)}, bf16[144,2176]{1,0:T(8,128)(2,1)}, u32[]{:S(2)}, u32[]{:S(2)}) collective-permute-start(bf16[144,2176]{1,0:T(8,128)(2,1)} %get-tuple-element.243), channel_id=1, source_target_pairs={{0,4},{1,5},{2,6},{3,7},{4,0},{5,1},{6,2},{7,3},{8,12},{9,13},{10,... | collective-permute-start | bytes 1880072 | tf_op jit(solution)/shard_map/ppermute | solution.py:633
  319.2 53.4 %collective-permute-start.19 = (bf16[144,2176]{1,0:T(8,128)(2,1)}, bf16[144,2176]{1,0:T(8,128)(2,1)}, u32[]{:S(2)}, u32[]{:S(2)}) collective-permute-start(bf16[144,2176]{1,0:T(8,128)(2,1)} %get-tuple-element.244), channel_id=1, source_target_pairs={{0,6},{1,7},{2,4},{3,5},{4,2},{5,3},{6,0},{7,1},{8,14},{9,15},{10,... | collective-permute-start | bytes 1880072 | tf_op jit(solution)/shard_map/ppermute | solution.py:633
  335.1 32.8 %all-to-all-start.3 = ((bf16[4,128,1152]{2,1,0:T(8,128)(2,1)}), bf16[4,128,1152]{2,1,0:T(8,128)(2,1)}, u32[]{:S(2)}, u32[]{:S(2)}) async-start(bf16[4,128,1152]{2,1,0:T(8,128)(2,1)} %copy-done.24), calls=%async_computation.3 | async-start | bytes 2359296 | tf_op jit(solution)/shard_map/all_to_all | solution.py:636
  340.3 128.4 %reduce-scatter.6.cloned.1.call-start = ((), (), s32[]{:S(2)}) async-start(), calls=%async_computation.11 | async-start | bytes 3981312 | tf_op jit(solution)/shard_map/reduce_scatter | solution.py:689
  347.6 20.4 %copy-start.43 = (f32[128,1]{1,0:T(8,128)S(1)}, f32[128,1]{1,0:T(8,128)}, u32[]{:S(2)}) copy-start(f32[128,1]{1,0:T(8,128)} %copy.76.inverse_ref) | copy-start | bytes 1540
  347.6 20.4 %copy-start.44 = (f32[1,1152]{1,0:T(1,128)S(1)}, f32[1,1152]{1,0:T(1,128)}, u32[]{:S(2)}) copy-start(f32[1,1152]{1,0:T(1,128)} %get-tuple-element.472.gain_ref) | copy-start | bytes 13828
  372.6 9.8 %collective-permute-start.16 = (bf16[128,1152]{1,0:T(8,128)(2,1)}, bf16[128,1152]{1,0:T(8,128)(2,1)S(1)}, u32[]{:S(2)}, u32[]{:S(2)}) collective-permute-start(bf16[128,1152]{1,0:T(8,128)(2,1)} %get-tuple-element.255.mine_ref), channel_id=1, source_target_pairs={{0,8},{8,0},{16,24},{24,16},{1,9},{9,1},{17,25},{25,17},{2,10},{10... | collective-permute-start | bytes 884744 | tf_op jit(solution)/shard_map/ppermute | solution.py:627
  375.2 44.7 %collective-permute-start.21 = (bf16[144,2176]{1,0:T(8,128)(2,1)}, bf16[144,2176]{1,0:T(8,128)(2,1)}, u32[]{:S(2)}, u32[]{:S(2)}) collective-permute-start(bf16[144,2176]{1,0:T(8,128)(2,1)} %add_all.9.refs_0_), channel_id=1, source_target_pairs={{0,16},{8,24},{16,0},{24,8},{1,17},{9,25},{17,1},{25,9},{2,18},{10... | collective-permute-start | bytes 1880072 | tf_op jit(solution)/shard_map/ppermute | solution.py:630
  377.0 71.9 %collective-permute-start.24 = (bf16[272,1152]{1,0:T(8,128)(2,1)}, bf16[272,1152]{1,0:T(8,128)(2,1)}, u32[]{:S(2)}, u32[]{:S(2)}) collective-permute-start(bf16[272,1152]{1,0:T(8,128)(2,1)} %reduce-scatter.4.cloned.1.call-done.refs_0_), channel_id=1, source_target_pairs={{0,16},{8,24},{16,0},{24,8},{1,17},{9,25},{17,1},{25,9},{2,18},{10... | collective-permute-start | bytes 1880072 | tf_op jit(solution)/shard_map/ppermute | solution.py:630
  395.5 16.2 %collective-permute-start.20 = (bf16[128,1152]{1,0:T(8,128)(2,1)}, bf16[128,1152]{1,0:T(8,128)(2,1)}, u32[]{:S(2)}, u32[]{:S(2)}) collective-permute-start(bf16[128,1152]{1,0:T(8,128)(2,1)} %get-tuple-element.263), channel_id=1, source_target_pairs={{0,8},{8,0},{16,24},{24,16},{1,9},{9,1},{17,25},{25,17},{2,10},{10... | collective-permute-start | bytes 884744 | tf_op jit(solution)/shard_map/ppermute | solution.py:627
  408.6 30.1 %collective-permute-start.23 = (bf16[4,144,2176]{2,1,0:T(8,128)(2,1)}, bf16[4,144,2176]{2,1,0:T(8,128)(2,1)}, u32[]{:S(2)}, u32[]{:S(2)}) collective-permute-start(bf16[4,144,2176]{2,1,0:T(8,128)(2,1)} %get-tuple-element.268), channel_id=1, source_target_pairs={{0,1},{1,0},{2,3},{3,2},{4,5},{5,4},{6,7},{7,6},{8,9},{9,8},{10,11... | collective-permute-start | bytes 7520264 | tf_op jit(solution)/shard_map/ppermute | solution.py:633
  429.6 19.3 %all-to-all-start.4 = ((bf16[4,128,288]{1,2,0:T(8,128)(2,1)}), bf16[4,128,288]{1,2,0:T(8,128)(2,1)}, u32[]{:S(2)}, u32[]{:S(2)}) async-start(bf16[4,128,288]{1,2,0:T(8,128)(2,1)} %copy.78), calls=%async_computation.5 | async-start | bytes 589824 | tf_op jit(solution)/shard_map/all_to_all | solution.py:636
  433.7 94.8 %reduce-scatter.8.cloned.1.call-start = ((), (), s32[]{:S(2)}) async-start(), calls=%async_computation.12 | async-start | bytes 5640192 | tf_op jit(solution)/shard_map/reduce_scatter | solution.py:689
  433.7 12.8 %collective-permute-start.22 = (bf16[128,576]{1,0:T(8,128)(2,1)S(1)}, bf16[128,576]{1,0:T(8,128)(2,1)S(1)}, u32[]{:S(2)}, u32[]{:S(2)}) collective-permute-start(bf16[128,576]{1,0:T(8,128)(2,1)S(1)} %get-tuple-element.274), channel_id=1, source_target_pairs={{0,8},{8,0},{16,24},{24,16},{1,9},{9,1},{17,25},{25,17},{2,10},{10... | collective-permute-start | bytes 442376 | tf_op jit(solution)/shard_map/ppermute | solution.py:627
  438.2 50.2 %collective-permute-start.28 = (bf16[144,2176]{1,0:T(8,128)(2,1)}, bf16[144,2176]{1,0:T(8,128)(2,1)}, u32[]{:S(2)}, u32[]{:S(2)}) collective-permute-start(bf16[144,2176]{1,0:T(8,128)(2,1)} %add_all.10.own_ref), channel_id=1, source_target_pairs={{0,8},{8,0},{16,24},{24,16},{1,9},{9,1},{17,25},{25,17},{2,10},{10... | collective-permute-start | bytes 1880072 | tf_op jit(solution)/shard_map/ppermute | solution.py:627
  444.7 37.8 %collective-permute-start.29 = (bf16[144,2176]{1,0:T(8,128)(2,1)}, bf16[144,2176]{1,0:T(8,128)(2,1)}, u32[]{:S(2)}, u32[]{:S(2)}) collective-permute-start(bf16[144,2176]{1,0:T(8,128)(2,1)} %get-tuple-element.277), channel_id=1, source_target_pairs={{0,2},{1,3},{2,0},{3,1},{4,6},{5,7},{6,4},{7,5},{8,10},{9,11},{10,... | collective-permute-start | bytes 1880072 | tf_op jit(solution)/shard_map/ppermute | solution.py:633
  446.2 38.1 %collective-permute-start.30 = (bf16[144,2176]{1,0:T(8,128)(2,1)}, bf16[144,2176]{1,0:T(8,128)(2,1)}, u32[]{:S(2)}, u32[]{:S(2)}) collective-permute-start(bf16[144,2176]{1,0:T(8,128)(2,1)} %get-tuple-element.278), channel_id=1, source_target_pairs={{0,4},{1,5},{2,6},{3,7},{4,0},{5,1},{6,2},{7,3},{8,12},{9,13},{10,... | collective-permute-start | bytes 1880072 | tf_op jit(solution)/shard_map/ppermute | solution.py:633
  447.2 37.1 %collective-permute-start.31 = (bf16[144,2176]{1,0:T(8,128)(2,1)}, bf16[144,2176]{1,0:T(8,128)(2,1)}, u32[]{:S(2)}, u32[]{:S(2)}) collective-permute-start(bf16[144,2176]{1,0:T(8,128)(2,1)} %get-tuple-element.279), channel_id=1, source_target_pairs={{0,6},{1,7},{2,4},{3,5},{4,2},{5,3},{6,0},{7,1},{8,14},{9,15},{10,... | collective-permute-start | bytes 1880072 | tf_op jit(solution)/shard_map/ppermute | solution.py:633
  464.2 59.3 %all-to-all-start.5 = ((bf16[4,128,1152]{2,1,0:T(8,128)(2,1)}), bf16[4,128,1152]{2,1,0:T(8,128)(2,1)}, u32[]{:S(2)}, u32[]{:S(2)}) async-start(bf16[4,128,1152]{2,1,0:T(8,128)(2,1)} %copy-done.23), calls=%async_computation.6 | async-start | bytes 2359296 | tf_op jit(solution)/shard_map/all_to_all | solution.py:636
  478.2 34.7 %collective-permute-start.26 = (bf16[144,1472]{1,0:T(8,128)(2,1)}, bf16[144,1472]{1,0:T(8,128)(2,1)S(1)}, u32[]{:S(2)}, u32[]{:S(2)}) collective-permute-start(bf16[144,1472]{1,0:T(8,128)(2,1)} %reduce-scatter.6.cloned.1.call-done), channel_id=1, source_target_pairs={{0,16},{8,24},{16,0},{24,8},{1,17},{9,25},{17,1},{25,9},{2,18},{10... | collective-permute-start | bytes 1271816 | tf_op jit(solution)/shard_map/ppermute | solution.py:630
  482.5 30.1 %collective-permute-start.27 = (bf16[272,1152]{1,0:T(8,128)(2,1)}, bf16[272,1152]{1,0:T(8,128)(2,1)S(1)}, u32[]{:S(2)}, u32[]{:S(2)}) collective-permute-start(bf16[272,1152]{1,0:T(8,128)(2,1)} %copy-done.62), channel_id=1, source_target_pairs={{0,8},{8,0},{16,24},{24,16},{1,9},{9,1},{17,25},{25,17},{2,10},{10... | collective-permute-start | bytes 1880072 | tf_op jit(solution)/shard_map/ppermute | solution.py:627
  484.3 33.8 %collective-permute-start.25 = (bf16[4,144,1472]{2,1,0:T(8,128)(2,1)}, bf16[4,144,1472]{2,1,0:T(8,128)(2,1)S(1)}, u32[]{:S(2)}, u32[]{:S(2)}) collective-permute-start(bf16[4,144,1472]{2,1,0:T(8,128)(2,1)} %get-tuple-element.292), channel_id=1, source_target_pairs={{0,1},{1,0},{2,3},{3,2},{4,5},{5,4},{6,7},{7,6},{8,9},{9,8},{10,11... | collective-permute-start | bytes 5087240 | tf_op jit(solution)/shard_map/ppermute | solution.py:633
  484.3 58.3 %collective-permute-start.36 = (bf16[144,864]{1,0:T(8,128)(2,1)S(1)}, bf16[144,864]{1,0:T(8,128)(2,1)}, u32[]{:S(2)}, u32[]{:S(2)}) collective-permute-start(bf16[144,864]{1,0:T(8,128)(2,1)S(1)} %slice.267.refs_0_), channel_id=1, source_target_pairs={{0,8},{8,0},{16,24},{24,16},{1,9},{9,1},{17,25},{25,17},{2,10},{10... | collective-permute-start | bytes 746504 | tf_op jit(solution)/shard_map/ppermute | solution.py:627
  513.0 27.2 %collective-permute-start.38 = (bf16[144,2176]{1,0:T(8,128)(2,1)}, bf16[144,2176]{1,0:T(8,128)(2,1)}, u32[]{:S(2)}, u32[]{:S(2)}) collective-permute-start(bf16[144,2176]{1,0:T(8,128)(2,1)} %add_all.12.refs_0_), channel_id=1, source_target_pairs={{0,16},{8,24},{16,0},{24,8},{1,17},{9,25},{17,1},{25,9},{2,18},{10... | collective-permute-start | bytes 1880072 | tf_op jit(solution)/shard_map/ppermute | solution.py:630
  516.4 26.3 %collective-permute-start.37 = (bf16[144,1472]{1,0:T(8,128)(2,1)S(1)}, bf16[144,1472]{1,0:T(8,128)(2,1)S(1)}, u32[]{:S(2)}, u32[]{:S(2)}) collective-permute-start(bf16[144,1472]{1,0:T(8,128)(2,1)S(1)} %pad_maximum_fusion.8.sums_ref), channel_id=1, source_target_pairs={{0,8},{8,0},{16,24},{24,16},{1,9},{9,1},{17,25},{25,17},{2,10},{10... | collective-permute-start | bytes 1271816 | tf_op jit(solution)/shard_map/ppermute | solution.py:627
  521.1 24.5 %collective-permute-start.33 = (bf16[144,1472]{1,0:T(8,128)(2,1)}, bf16[144,1472]{1,0:T(8,128)(2,1)S(1)}, u32[]{:S(2)}, u32[]{:S(2)}) collective-permute-start(bf16[144,1472]{1,0:T(8,128)(2,1)} %get-tuple-element.294), channel_id=1, source_target_pairs={{0,2},{1,3},{2,0},{3,1},{4,6},{5,7},{6,4},{7,5},{8,10},{9,11},{10,... | collective-permute-start | bytes 1271816 | tf_op jit(solution)/shard_map/ppermute | solution.py:633
  522.9 22.7 %collective-permute-start.34 = (bf16[144,1472]{1,0:T(8,128)(2,1)}, bf16[144,1472]{1,0:T(8,128)(2,1)}, u32[]{:S(2)}, u32[]{:S(2)}) collective-permute-start(bf16[144,1472]{1,0:T(8,128)(2,1)} %get-tuple-element.295), channel_id=1, source_target_pairs={{0,4},{1,5},{2,6},{3,7},{4,0},{5,1},{6,2},{7,3},{8,12},{9,13},{10,... | collective-permute-start | bytes 1271816 | tf_op jit(solution)/shard_map/ppermute | solution.py:633
  529.8 25.2 %all-to-all-start.6 = ((f32[8,1,3456]{2,1,0:T(1,128)}), f32[8,1,3456]{2,1,0:T(1,128)S(1)}, u32[]{:S(2)}, u32[]{:S(2)}) async-start(f32[8,1,3456]{2,1,0:T(1,128)} %copy.82), calls=%async_computation.9 | async-start | bytes 221184 | tf_op jit(solution)/shard_map/all_to_all | solution.py:993
  540.2 11.2 %collective-permute-start.35 = (bf16[144,1472]{1,0:T(8,128)(2,1)S(1)}, bf16[144,1472]{1,0:T(8,128)(2,1)S(1)}, u32[]{:S(2)}, u32[]{:S(2)}) collective-permute-start(bf16[144,1472]{1,0:T(8,128)(2,1)S(1)} %copy-done.73), channel_id=1, source_target_pairs={{0,6},{1,7},{2,4},{3,5},{4,2},{5,3},{6,0},{7,1},{8,14},{9,15},{10,... | collective-permute-start | bytes 1271816 | tf_op jit(solution)/shard_map/ppermute | solution.py:633
  542.7 36.8 %collective-permute-start.32 = (bf16[272,1152]{1,0:T(8,128)(2,1)}, bf16[272,1152]{1,0:T(8,128)(2,1)}, u32[]{:S(2)}, u32[]{:S(2)}) collective-permute-start(bf16[272,1152]{1,0:T(8,128)(2,1)} %reduce-scatter.8.cloned.1.call-done.refs_0_), channel_id=1, source_target_pairs={{0,16},{8,24},{16,0},{24,8},{1,17},{9,25},{17,1},{25,9},{2,18},{10... | collective-permute-start | bytes 1880072 | tf_op jit(solution)/shard_map/ppermute | solution.py:630
  552.7 41.6 %collective-permute-start.40 = (bf16[144,1472]{1,0:T(8,128)(2,1)S(1)}, bf16[144,1472]{1,0:T(8,128)(2,1)S(1)}, u32[]{:S(2)}, u32[]{:S(2)}) collective-permute-start(bf16[144,1472]{1,0:T(8,128)(2,1)S(1)} %add_all.15), channel_id=1, source_target_pairs={{0,16},{8,24},{16,0},{24,8},{1,17},{9,25},{17,1},{25,9},{2,18},{10... | collective-permute-start | bytes 1271816 | tf_op jit(solution)/shard_map/ppermute | solution.py:630
  552.8 39.6 %collective-permute-start.41 = (bf16[144,2176]{1,0:T(8,128)(2,1)S(1)}, bf16[144,2176]{1,0:T(8,128)(2,1)S(1)}, u32[]{:S(2)}, u32[]{:S(2)}) collective-permute-start(bf16[144,2176]{1,0:T(8,128)(2,1)S(1)} %add_all.14.own_ref), channel_id=1, source_target_pairs={{0,8},{8,0},{16,24},{24,16},{1,9},{9,1},{17,25},{25,17},{2,10},{10... | collective-permute-start | bytes 1880072 | tf_op jit(solution)/shard_map/ppermute | solution.py:627
  554.3 64.4 %collective-permute-start.44 = (bf16[144,864]{1,0:T(8,128)(2,1)S(1)}, bf16[144,864]{1,0:T(8,128)(2,1)S(1)}, u32[]{:S(2)}, u32[]{:S(2)}) collective-permute-start(bf16[144,864]{1,0:T(8,128)(2,1)S(1)} %slice.306.refs_0_), channel_id=1, source_target_pairs={{0,8},{8,0},{16,24},{24,16},{1,9},{9,1},{17,25},{25,17},{2,10},{10... | collective-permute-start | bytes 746504 | tf_op jit(solution)/shard_map/ppermute | solution.py:627
  581.8 14.8 %collective-permute-start.39 = (f32[1,3456]{1,0:T(1,128)S(1)}, f32[1,3456]{1,0:T(1,128)S(1)}, u32[]{:S(2)}, u32[]{:S(2)}) collective-permute-start(f32[1,3456]{1,0:T(1,128)S(1)} %broadcast_in_dim.8), channel_id=1, source_target_pairs={{0,16},{8,24},{16,0},{24,8},{1,17},{9,25},{17,1},{25,9},{2,18},{10... | collective-permute-start | bytes 41480 | tf_op jit(solution)/shard_map/ppermute | solution.py:630
  594.4 17.1 %collective-permute-start.43 = (bf16[272,1152]{1,0:T(8,128)(2,1)S(1)}, bf16[272,1152]{1,0:T(8,128)(2,1)S(1)}, u32[]{:S(2)}, u32[]{:S(2)}) collective-permute-start(bf16[272,1152]{1,0:T(8,128)(2,1)S(1)} %add_all.16.refs_0_), channel_id=1, source_target_pairs={{0,8},{8,0},{16,24},{24,16},{1,9},{9,1},{17,25},{25,17},{2,10},{10... | collective-permute-start | bytes 1880072 | tf_op jit(solution)/shard_map/ppermute | solution.py:627
  594.6 24.2 %collective-permute-start.45 = (bf16[144,1472]{1,0:T(8,128)(2,1)S(1)}, bf16[144,1472]{1,0:T(8,128)(2,1)S(1)}, u32[]{:S(2)}, u32[]{:S(2)}) collective-permute-start(bf16[144,1472]{1,0:T(8,128)(2,1)S(1)} %pad_maximum_fusion.9.sums_ref), channel_id=1, source_target_pairs={{0,8},{8,0},{16,24},{24,16},{1,9},{9,1},{17,25},{25,17},{2,10},{10... | collective-permute-start | bytes 1271816 | tf_op jit(solution)/shard_map/ppermute | solution.py:627
  596.7 21.4 %collective-permute-start.42 = (f32[1,3456]{1,0:T(1,128)S(1)}, f32[1,3456]{1,0:T(1,128)S(1)}, u32[]{:S(2)}, u32[]{:S(2)}) collective-permute-start(f32[1,3456]{1,0:T(1,128)S(1)} %reshape_add_fusion.first_ref), channel_id=1, source_target_pairs={{0,8},{8,0},{16,24},{24,16},{1,9},{9,1},{17,25},{25,17},{2,10},{10... | collective-permute-start | bytes 41480 | tf_op jit(solution)/shard_map/ppermute | solution.py:627
  (147 other events, 548.3 us)
Sparse Core Ops, SparseCore 0:
  12.2 42.7 all-gather.8
  57.5 63.8 all-gather.10
  123.3 38.9 all-gather.12
  164.5 63.8 all-gather.14
  260.8 56.0 reduce-scatter.3
  347.7 48.5 reduce-scatter.5
  438.4 63.1 reduce-scatter.7

commit v3 on v2

--- a/solution.py
+++ b/solution.py
@@ -12,6 +12,8 @@
 EPSILON = 1e-06
 LOW = jnp.bfloat16
 FULL = jnp.float32
+HEAVY = pl.CostEstimate(flops=20_000_000_000, transcendentals=0, bytes_accessed=1)
+LIGHT = pl.CostEstimate(flops=1, transcendentals=0, bytes_accessed=1)
 
 
 def normalize(hidden):
@@ -67,7 +69,7 @@
 
 
 def attend_forward_kernel(qkv_ref, o_ref, lse_ref, acc_ref):
-    tokens, width = o_ref.shape
+    tokens, width = acc_ref.shape
     rows = min(256, tokens)
     scaling = HEAD_DIM ** (-0.5)
     acc_ref[...] = jnp.zeros_like(acc_ref)
@@ -85,35 +87,36 @@
             probability = jnp.exp(scores - lse).astype(LOW)
             acc_ref[start : start + rows, low:high] += mm(probability, values)
             lse_ref[start : start + rows, head : head + 1] = lse
-    o_ref[...] = acc_ref[...].astype(LOW)
-
-
-def attend_forward(qkv):
+    ranks, _, block = o_ref.shape
+    for rank in range(ranks):
+        o_ref[rank] = acc_ref[rank * block : (rank + 1) * block].astype(LOW).T
+
+
+def attend_forward(qkv, ranks):
     _, tokens, width = qkv.shape
     heads = width // HEAD_DIM
     return pl.pallas_call(
         attend_forward_kernel,
         out_shape=(
-            jax.ShapeDtypeStruct((tokens, width), LOW),
+            jax.ShapeDtypeStruct((ranks, width, tokens // ranks), LOW),
             jax.ShapeDtypeStruct((tokens, heads), FULL),
         ),
         in_specs=[pl.BlockSpec(memory_space=pltpu.VMEM)],
         out_specs=(pl.BlockSpec(memory_space=pltpu.VMEM),) * 2,
         scratch_shapes=[pltpu.VMEM((tokens, width), FULL)],
-        compiler_params=pltpu.CompilerParams(vmem_limit_bytes=40 << 20),
-        cost_estimate=pl.CostEstimate(
-            flops=4 * heads * tokens * tokens * 128,
-            transcendentals=2 * heads * tokens * tokens,
-            bytes_accessed=8 * tokens * width,
-        ),
+        compiler_params=pltpu.CompilerParams(vmem_limit_bytes=24 << 20),
+        cost_estimate=LIGHT,
         name="attend_forward",
     )(qkv)
 
 
 def attend_backward_kernel(
-    qkv_ref, do_ref, lse_ref, proj_ref, grad_ref, leave_ref, q_bias_ref, v_bias_ref, dq_ref, dk_ref, dv_ref
+    qkv_ref, got_ref, lse_ref, proj_ref, grad_ref, leave_ref, q_bias_ref, v_bias_ref, dq_ref, dk_ref, dv_ref, do_ref
 ):
     tokens, width = do_ref.shape
+    ranks, _, block = got_ref.shape
+    for rank in range(ranks):
+        do_ref[rank * block : (rank + 1) * block] = got_ref[rank].T
     rows = min(256, tokens)
     scaling = HEAD_DIM ** (-0.5)
     for ref in (dq_ref, dk_ref, dv_ref):
@@ -144,7 +147,6 @@
     grad_ref[:, 2 * width :] = dv
     q_bias_ref[...] = jnp.sum(dq.astype(FULL), axis=0, keepdims=True)
     v_bias_ref[...] = jnp.sum(dv.astype(FULL), axis=0, keepdims=True)
-    ranks, block, _ = leave_ref.shape
     for rank in range(ranks):
         leave_ref[rank] = mm_cols(grad_ref[rank * block : (rank + 1) * block], proj_ref[...]).astype(LOW)
 
@@ -163,9 +165,9 @@
         ),
         in_specs=[pl.BlockSpec(memory_space=pltpu.VMEM)] * 4,
         out_specs=(pl.BlockSpec(memory_space=pltpu.VMEM),) * 4,
-        scratch_shapes=[pltpu.VMEM((tokens, width), FULL)] * 3,
-        compiler_params=pltpu.CompilerParams(vmem_limit_bytes=48 << 20),
-        cost_estimate=pl.CostEstimate(flops=0, transcendentals=0, bytes_accessed=24 << 20),
+        scratch_shapes=[pltpu.VMEM((tokens, width), FULL)] * 3 + [pltpu.VMEM((tokens, width), LOW)],
+        compiler_params=pltpu.CompilerParams(vmem_limit_bytes=24 << 20),
+        cost_estimate=HEAVY,
         name="attend_backward",
     )(qkv, upstream, lse, proj)
 
@@ -205,8 +207,8 @@
         in_specs=[pl.BlockSpec(memory_space=pltpu.SMEM)]
         + [pl.BlockSpec(memory_space=pltpu.VMEM)] * (2 + len(small)),
         out_specs=pl.BlockSpec(memory_space=pltpu.VMEM),
-        compiler_params=pltpu.CompilerParams(vmem_limit_bytes=24 << 20),
-        cost_estimate=pl.CostEstimate(flops=1, transcendentals=0, bytes_accessed=1),
+        compiler_params=pltpu.CompilerParams(vmem_limit_bytes=16 << 20),
+        cost_estimate=LIGHT,
         name="attn_share",
     )(me.reshape(1), out_w, qkv_w, *small)
 
@@ -238,14 +240,13 @@
         out_shape=jax.ShapeDtypeStruct((max(2 * part, half), lanes), LOW),
         in_specs=[pl.BlockSpec(memory_space=pltpu.SMEM)] + [pl.BlockSpec(memory_space=pltpu.VMEM)] * 2,
         out_specs=pl.BlockSpec(memory_space=pltpu.VMEM),
-        compiler_params=pltpu.CompilerParams(vmem_limit_bytes=24 << 20),
-        cost_estimate=pl.CostEstimate(flops=1, transcendentals=0, bytes_accessed=1),
+        compiler_params=pltpu.CompilerParams(vmem_limit_bytes=16 << 20),
+        cost_estimate=LIGHT,
         name="feed_share",
     )(side.reshape(1), up, down)
 
 
-def local_call(kernel, name, out_shape, *operands, scalars=(), scratch=()):
-    moved = sum(math.prod(a.shape) * a.dtype.itemsize for a in (*operands, *jax.tree.leaves(out_shape)))
+def local_call(kernel, name, out_shape, *operands, scalars=(), scratch=(), cost=HEAVY):
     return pl.pallas_call(
         kernel,
         out_shape=out_shape,
@@ -253,28 +254,42 @@
         + [pl.BlockSpec(memory_space=pltpu.VMEM)] * len(operands),
         out_specs=jax.tree.map(lambda _: pl.BlockSpec(memory_space=pltpu.VMEM), out_shape),
         scratch_shapes=list(scratch),
-        compiler_params=pltpu.CompilerParams(vmem_limit_bytes=48 << 20),
-        cost_estimate=pl.CostEstimate(flops=20000000000, transcendentals=0, bytes_accessed=moved),
+        compiler_params=pltpu.CompilerParams(vmem_limit_bytes=24 << 20),
+        cost_estimate=cost,
         name=name,
     )(*[s.reshape(1) for s in scalars], *operands)
 
 
-def grad_kernel(*refs, owners, columns, total, split):
-    core_ref, refs = (refs[0], refs[1:]) if split else (None, refs)
-    count = len(columns)
-    lefts, rights = refs[:count], refs[count : 2 * count]
-    outs, flips = refs[2 * count : len(refs) - count], refs[len(refs) - count :]
-    rows = lefts[0].shape[1] // owners
-    for target, width in columns:
-        gap = slice(target + width, min([t for t, _ in columns if t > target], default=total))
-        if gap.stop > gap.start:
+def grad_kernel(*refs, owners, pieces, total, split):
+    refs = list(refs)
+    core_ref = refs.pop(0) if split else None
+    operands = []
+    for lefts, rights, turned, target in pieces:
+        operands.append(([refs.pop(0) for _ in range(lefts)], [refs.pop(0) for _ in range(rights)], turned, target))
+    outs = [refs.pop(0) for _ in range(2 if split else 1)]
+    filled = []
+    for lefts, rights, turned, target in operands:
+        left_ref, right_ref = refs.pop(0), refs.pop(0)
+        start = 0
+        for ref in lefts:
+            count = ref.shape[1 if turned else 0]
+            left_ref[:, start : start + count] = ref[...] if turned else ref[...].T
+            start += count
+        start = 0
+        for ref in rights:
+            right_ref[start : start + ref.shape[0]] = ref[...]
+            start += ref.shape[0]
+        filled.append((left_ref, right_ref, target, target + right_ref.shape[1]))
+    ends = [f[2] for f in filled[1:]] + [total]
+    for (left_ref, right_ref, target, stop), end in zip(filled, ends, strict=True):
+        if end > stop:
             for out in outs:
-                out[..., gap] = jnp.zeros(out.shape[:-1] + (gap.stop - gap.start,), LOW)
-    for left, right, flip, (target, width) in zip(lefts, rights, flips, columns, strict=True):
-        flip[...] = left[...].T
+                out[..., stop:end] = jnp.zeros(out.shape[:-1] + (end - stop,), LOW)
+        rows = left_ref.shape[0] // owners
+        width = right_ref.shape[1]
         for start in range(0, width, 256):
             size = min(256, width - start)
-            value = mm(flip[...], right[:, start : start + size]).astype(LOW)
+            value = mm(left_ref[...], right_ref[:, start : start + size]).astype(LOW)
             if not split:
                 outs[0][:, target + start : target + start + size] = value
                 continue
@@ -289,58 +304,173 @@
                         ]
 
 
-def weight_grad(pieces, owners, total, core=None):
-    lefts, rights = [p[0] for p in pieces], [p[1] for p in pieces]
-    rows = lefts[0].shape[1]
+def weight_grad(pieces, owners, total, core=None, cost=HEAVY):
     split = core is not None
-    shape = (owners // 2, rows // owners, total) if split else (rows, total)
-    out = jax.ShapeDtypeStruct(shape, LOW)
+    operands, shapes, scratch = [], [], []
+    for lefts, rights, turned, target in pieces:
+        operands += [*lefts, *rights]
+        shapes.append((len(lefts), len(rights), turned, target))
+        rows = lefts[0].shape[0 if turned else 1]
+        tokens = sum(r.shape[0] for r in rights)
+        scratch += [pltpu.VMEM((rows, tokens), LOW), pltpu.VMEM((tokens, rights[0].shape[1]), LOW)]
+    out = jax.ShapeDtypeStruct((owners // 2, rows // owners, total) if split else (rows, total), LOW)
     return local_call(
-        functools.partial(
-            grad_kernel,
-            owners=owners,
-            columns=[(p[2], p[1].shape[1]) for p in pieces],
-            total=total,
-            split=split,
-        ),
+        functools.partial(grad_kernel, owners=owners, pieces=shapes, total=total, split=split),
         "weight_grad",
         (out, out) if split else out,
-        *lefts,
-        *rights,
+        *operands,
         scalars=(core,) if split else (),
-        scratch=[pltpu.VMEM((left.shape[1], left.shape[0]), LOW) for left in lefts],
+        scratch=scratch,
+        cost=cost,
     )
 
 
+def spread_kernel(all_ref, out_ref, qkv_ref, *small):
+    owners, _, _ = all_ref.shape
+    width = out_ref.shape[1]
+    part = out_ref.shape[0] // owners
+    for owner in range(owners):
+        rows = slice(owner * part, (owner + 1) * part)
+        out_ref[rows] = all_ref[owner, :part, :width]
+        qkv_ref[rows] = all_ref[owner, :part, width:]
+        for ref in small:
+            ref[owner] = all_ref[owner, part:, :]
+
+
+def spread(gathered, part, width):
+    owners, rows, columns = gathered.shape
+    return local_call(
+        spread_kernel,
+        "spread",
+        [
+            jax.ShapeDtypeStruct((owners * part, width), LOW),
+            jax.ShapeDtypeStruct((owners * part, columns - width), LOW),
+        ]
+        + [jax.ShapeDtypeStruct((owners, rows - part, columns), LOW)] * (rows > part),
+        gathered,
+        cost=LIGHT,
+    )
+
+
+def unit_tiles(owners, half):
+    flank = owners // 2 * half
+    return [
+        (side * flank + start, min(512, flank - start), side, start)
+        for side in range(2)
+        for start in range(0, flank, 512)
+    ]
+
+
+def up_tile(feed_ref, tile, part, width):
+    _, count, side, start = tile
+    lanes = slice(width + start, width + start + count)
+    rows = slice(side * part, (side + 1) * part)
+    return jnp.concatenate([feed_ref[owner, rows, lanes] for owner in range(feed_ref.shape[0])], axis=0)
+
+
+def down_tile(feed_ref, tile, half, width):
+    first, count, _, _ = tile
+    pieces = []
+    while count:
+        owner, row = divmod(first, half)
+        size = min(count, half - row)
+        pieces.append(feed_ref[owner, row : row + size, :width])
+        first, count = first + size, count - size
+    return jnp.concatenate(pieces, axis=0)
+
+
+GELU_SCALE = (2 / math.pi) ** 0.5
+
+
+def feed_forward_kernel(mine_ref, other_ref, feed_ref, bias_ref, pre_ref, act_ref, *refs, half):
+    tokens, width = mine_ref.shape
+    owners = feed_ref.shape[0]
+    part = width // owners
+    both = jnp.concatenate([mine_ref[...], other_ref[...]], axis=0)
+    if refs:
+        keep_ref, leave_ref, acc_ref = refs
+        acc_ref[...] = jnp.zeros_like(acc_ref)
+    for tile in unit_tiles(owners, half):
+        span = slice(tile[0], tile[0] + tile[1])
+        pre = mm(both, up_tile(feed_ref, tile, part, width)) + bias_ref[:, span]
+        pre_ref[:, span] = pre
+        act = (0.5 * pre * (1 + jnp.tanh(GELU_SCALE * (pre + 0.044715 * (pre * pre * pre))))).astype(LOW)
+        act_ref[:, span] = act
+        if refs:
+            acc_ref[...] += mm(act, down_tile(feed_ref, tile, half, width))
+    if refs:
+        keep_ref[...] = acc_ref[:tokens]
+        leave_ref[...] = acc_ref[tokens:].astype(LOW)
+
+
+def feed_forward(mine, other, feed, bias, half, mixed):
+    tokens, width = mine.shape
+    units = feed.shape[0] * half
+    shapes = [jax.ShapeDtypeStruct((2 * tokens, units), FULL), jax.ShapeDtypeStruct((2 * tokens, units), LOW)]
+    if mixed:
+        shapes += [jax.ShapeDtypeStruct((tokens, width), FULL), jax.ShapeDtypeStruct((tokens, width), LOW)]
+    return local_call(
+        functools.partial(feed_forward_kernel, half=half),
+        "feed_forward",
+        shapes,
+        mine,
+        other,
+        feed,
+        bias,
+        scratch=[pltpu.VMEM((2 * tokens, width), FULL)] * mixed,
+    )
+
+
+def feed_out_kernel(act_ref, feed_ref, keep_ref, leave_ref, acc_ref, *, half):
+    tokens, width = keep_ref.shape
+    acc_ref[...] = jnp.zeros_like(acc_ref)
+    for tile in unit_tiles(feed_ref.shape[0], half):
+        acc_ref[...] += mm(act_ref[:, tile[0] : tile[0] + tile[1]], down_tile(feed_ref, tile, half, width))
+    keep_ref[...] = acc_ref[:tokens]
+    leave_ref[...] = acc_ref[tokens:].astype(LOW)
+
+
+def feed_out(act, feed, width, half):
+    tokens = act.shape[0] // 2
+    return local_call(
+        functools.partial(feed_out_kernel, half=half),
+        "feed_out",
+        (jax.ShapeDtypeStruct((tokens, width), FULL), jax.ShapeDtypeStruct((tokens, width), LOW)),
+        act,
+        feed,
+        scratch=[pltpu.VMEM((2 * tokens, width), FULL)],
+    )
+
+
 def feed_backward_kernel(
-    mine_ref, other_ref, pre_ref, up_ref, down_ref, low_ref, grad_ref, keep_ref, leave_ref, bias_ref, acc_ref
+    mine_ref, other_ref, pre_ref, feed_ref, low_ref, grad_ref, keep_ref, leave_ref, bias_ref, acc_ref, *, half
 ):
-    tokens = mine_ref.shape[0]
+    tokens, width = mine_ref.shape
+    owners = feed_ref.shape[0]
+    part = width // owners
     low_ref[:tokens] = mine_ref[...]
     low_ref[tokens:] = other_ref[...]
     acc_ref[...] = jnp.zeros_like(acc_ref)
-    scale = (2 / math.pi) ** 0.5
-    units = pre_ref.shape[1]
-    for start in range(0, units, 512):
-        span = slice(start, min(start + 512, units))
+    for tile in unit_tiles(owners, half):
+        span = slice(tile[0], tile[0] + tile[1])
         pre = pre_ref[:, span]
         square = pre * pre
-        bend = jnp.tanh(scale * (pre + 0.044715 * pre * square))
-        slope = 0.5 * (1 + bend) + 0.5 * pre * (1 - bend * bend) * (scale * (1 + 3 * 0.044715 * square))
-        grad = mm_cols(low_ref[...], down_ref[span, :]) * slope
+        bend = jnp.tanh(GELU_SCALE * (pre + 0.044715 * pre * square))
+        slope = 0.5 * (1 + bend) + 0.5 * pre * (1 - bend * bend) * (GELU_SCALE * (1 + 3 * 0.044715 * square))
+        grad = mm_cols(low_ref[...], down_tile(feed_ref, tile, half, width)) * slope
         bias_ref[:, span] = jnp.sum(grad, axis=0, keepdims=True)
         grad = grad.astype(LOW)
         grad_ref[:, span] = grad
-        acc_ref[...] += mm_cols(grad, up_ref[:, span])
+        acc_ref[...] += mm_cols(grad, up_tile(feed_ref, tile, part, width))
     keep_ref[...] = acc_ref[:tokens]
     leave_ref[...] = acc_ref[tokens:].astype(LOW)
 
 
-def feed_backward(mine, other, pre_act, up, down):
+def feed_backward(mine, other, pre_act, feed, half):
     tokens, width = mine.shape
     units = pre_act.shape[1]
     return local_call(
-        feed_backward_kernel,
+        functools.partial(feed_backward_kernel, half=half),
         "feed_backward",
         (
             jax.ShapeDtypeStruct((2 * tokens, width), LOW),
@@ -352,8 +482,7 @@
         mine,
         other,
         pre_act,
-        up,
-        down,
+        feed,
         scratch=[pltpu.VMEM((2 * tokens, width), FULL)],
     )
 
@@ -380,9 +509,9 @@
             mine_ref[...] = low[:, side * flank : (side + 1) * flank]
             other_ref[...] = low[:, (1 - side) * flank : (2 - side) * flank]
 
-    ranks, _, slab = send_ref.shape
+    ranks, slab, _ = send_ref.shape
     for rank in range(ranks):
-        send_ref[rank] = mm_cols(low, proj_ref[rank * slab : (rank + 1) * slab, :]).astype(LOW)
+        send_ref[rank] = mm_cols(proj_ref[rank * slab : (rank + 1) * slab, :], low).astype(LOW)
 
 
 def mid_backward(side, keep, got, normed, inverse, gain, grad, proj, ranks):
@@ -394,7 +523,7 @@
         "mid_backward",
         (
             jax.ShapeDtypeStruct((tokens, width), FULL),
-            jax.ShapeDtypeStruct((ranks, tokens, width // ranks), LOW),
+            jax.ShapeDtypeStruct((ranks, width // ranks, tokens), LOW),
             half,
             half,
             row,
@@ -467,7 +596,7 @@
         ),
         out_shape=[jax.ShapeDtypeStruct((rows, columns), LOW)] * chips,
         compiler_params=pltpu.CompilerParams(vmem_limit_bytes=24 << 20),
-        cost_estimate=pl.CostEstimate(flops=0, transcendentals=0, bytes_accessed=6 * chips * rows * columns),
+        cost_estimate=LIGHT,
         name="meet_cores",
     )(chip.reshape(1), keep, got)
 
@@ -480,7 +609,7 @@
 
 
 def add_all(*values):
-    return local_call(add_kernel, "add_all", jax.ShapeDtypeStruct(values[0].shape, LOW), *values)
+    return local_call(add_kernel, "add_all", jax.ShapeDtypeStruct(values[0].shape, LOW), *values, cost=LIGHT)
 
 
 def up_kernel(side_ref, own_ref, across_ref, *refs, owners, half):
@@ -500,8 +629,8 @@
                     out_ref[0, :, target : target + count] = ref[:, source : source + count].astype(FULL)
 
 
-def mixed_kernel(me_ref, sums_ref, others_ref, *refs, ranks, layers_seen, offset):
-    shares, (qkv_out, out_out) = refs[:ranks], refs[-2:]
+def mixed_kernel(me_ref, own_ref, across_ref, *refs, ranks, offset):
+    qkv_out, out_out = refs[-2:]
     width = out_out.shape[2]
     slab, flank, pairs = width // ranks, width // 2, ranks // 2
     for me in range(ranks):
@@ -509,16 +638,15 @@
         @pl.when(me_ref[0] == me)
         def _():
             side, pair = me % 2, me // 2
-            for j in range(pairs):
-                for flip in range(2):
+            for flip, ref in enumerate((own_ref, across_ref)):
+                for j in range(pairs):
                     rank = (pair - j) % pairs * 2 + (side ^ flip)
-                    ref = shares[2 * j + flip]
                     for i in range(3):
                         target = (i * ranks + rank) * slab
-                        qkv_out[0, :, target : target + slab] = ref[:, i * slab : (i + 1) * slab].astype(FULL)
-            for flip, ref in enumerate((sums_ref, others_ref)):
+                        source = j * offset + i * slab
+                        qkv_out[0, :, target : target + slab] = ref[:, source : source + slab].astype(FULL)
                 target = (side ^ flip) * flank
-                out_out[0, :, target : target + flank] = ref[:, offset : offset + flank].astype(FULL)
+                out_out[0, :, target : target + flank] = ref[:, pairs * offset :].astype(FULL)
 
 
 def write_layer(kernel, name, layer, layers, shapes, earlier, scalar, *values):
@@ -532,7 +660,7 @@
         out_specs=tuple(pl.BlockSpec((1,) + s, lambda i: (layer, 0, 0)) for s in shapes),
         input_output_aliases={1 + len(values) + i: i for i in range(len(earlier))},
         compiler_params=pltpu.CompilerParams(vmem_limit_bytes=40 << 20),
-        cost_estimate=pl.CostEstimate(flops=0, transcendentals=0, bytes_accessed=8 << 20),
+        cost_estimate=LIGHT,
         name=name,
     )(scalar.reshape(1), *values, *earlier)
 
@@ -702,22 +830,17 @@
 
         def mixed_steps(value):
             order.leave(value)
-            share = value[:, : 3 * slab]
             got = [pair_shift(value, j) for j in range(1, pairs)]
-            across = [swap(share)]
             yield
             got = order.enter(*got)
             total = add_all(*[v[:, offset:] for v in (value, *got)])
-            sends = [g[:, : 3 * slab] for g in got]
-            sends[0] = jnp.concatenate([got[0][:, :offset], total], axis=1)
-            order.leave(*sends)
-            across += [swap(send) for send in sends]
+            shares = [v[:, :offset] for v in (value, *got)]
+            send = jnp.concatenate([*shares, total], axis=1)
+            order.leave(send)
+            across = swap(send)
             yield
-            across = list(order.enter(*across))
-            shares = [share, across[0]]
-            for piece, flipped in zip(got, across[1:], strict=True):
-                shares += [piece, flipped]
-            return sends[0], across[1], *shares
+            (across,) = order.enter(across)
+            return send, across
 
         def written(steps, stage, write):
             value = yield from steps
@@ -730,13 +853,7 @@
         offset = -(-3 * slab // 128) * 128
 
         def gather_tokens(mine):
-            return [mine] + [shift(mine, j) for j in range(1, ranks)]
-
-        def in_order(blocks):
-            result = jnp.zeros((ranks,) + blocks[0].shape, LOW)
-            for j, block in enumerate(blocks):
-                result = put(result, block, rank_at(-j))
-            return result.reshape(ranks * tokens, width)
+            return exchange(jnp.broadcast_to(mine, (ranks,) + mine.shape))
 
         all_input = gather_tokens(block_input[0])
         small = (
@@ -750,7 +867,8 @@
             up_bias,
         )
         down_turned = down_weight.transpose(1, 0, 2)
-        attn_shares, feed_shares = [], []
+
+        attn_shares, feeds = [], []
         for layer in range(layers):
             share = attn_share(
                 me, out_weight[layer], *order.enter(qkv_weight[layer]), small if layer == 0 else (), layers, ranks
@@ -759,8 +877,12 @@
             attn_shares.append(lax.all_gather(share, "fsdp", axis=0))
             share = feed_share(side, *order.enter(up_weight[layer]), down_turned, layer, owners, half)
             order.leave(share)
-            feed_shares.append(lax.all_gather(share, "fsdp", axis=0))
-        small_all, *all_input = order.enter(attn_shares[0][:, part:], *all_input)
+            feeds.append(lax.all_gather(share, "fsdp", axis=0))
+        (all_input,) = order.enter(all_input)
+        normed_all, _ = normalize(all_input.reshape(ranks * tokens, width).astype(FULL))
+        order.leave(normed_all)
+        *weights, small_all = spread(*order.enter(attn_shares[0]), part, width)
+        order.leave(*weights, small_all)
         rows_all = small_all[:, :layers, : 8 * part].reshape(owners, layers, 8, part)
         rows_all = rows_all.transpose(1, 2, 0, 3).reshape(layers, 8, width).astype(FULL)
         up_all = small_all[:, :layers, 8 * part : 8 * part + hidden_part].astype(FULL)
@@ -789,62 +911,49 @@
         stored = []
         for layer in range(layers):
             v = vectors[layer]
+            last_layer = layer == layers - 1
             normed_one, inverse_one = normalize(hidden)
             if layer == 0:
-                normed_all, _ = normalize(in_order(all_input).astype(FULL))
                 attn_in = (normed_all * v["gain_one"] + v["bias_one"]).astype(LOW)
             else:
                 attn_mine = (normed_one * v["gain_one"] + v["bias_one"]).astype(LOW)
                 order.leave(attn_mine)
-                attn_in = in_order(order.enter(*gather_tokens(attn_mine)))
-            attn = order.enter(attn_shares[layer])[0][:, :part].reshape(width, columns)
-            proj_out, proj_qkv = lax.optimization_barrier((attn[:, :width], attn[:, width:]))
+                attn_in = gather_tokens(attn_mine)
+                weights = spread(*order.enter(attn_shares[layer]), part, width)
+                order.leave(*weights)
+                attn_in = order.enter(attn_in)[0].reshape(ranks * tokens, width)
+            proj_out, proj_qkv = weights
             bias_row = jnp.concatenate([v["bias_q"], jnp.zeros((slab,), FULL), v["bias_v"]])
             projected = (mm(attn_in, proj_qkv) + bias_row).astype(LOW)
             qkv = jnp.stack([projected[:, i * slab : (i + 1) * slab] for i in range(3)])
-            out_heads, lse = attend_forward(qkv)
-            out_heads = out_heads.reshape(ranks, tokens, slab)
+            out_heads, lse = attend_forward(qkv, ranks)
             order.leave(out_heads)
-            (attended,) = order.enter(exchange(out_heads))
-            after_attn = (
-                hidden
-                + lax.dot_general(
-                    attended,
-                    proj_out.reshape(ranks, slab, width),
-                    (((0, 2), (0, 1)), ((), ())),
-                    preferred_element_type=FULL,
-                )
-                + v["bias_out"]
-            )
+            attended = order.enter(exchange(out_heads))[0].reshape(width, tokens)
+            after_attn = hidden + mm_rows(attended, proj_out) + v["bias_out"]
             normed_two, inverse_two = normalize(after_attn)
             mlp_mine = (normed_two * v["gain_two"] + v["bias_two"]).astype(LOW)
             order.leave(mlp_mine)
+            mlp_other = swap(mlp_mine)
             attended_other = swap(order.enter(attended)[0])
-            mlp_other, attended_other, feed = order.enter(swap(mlp_mine), attended_other, feed_shares[layer])
-            attended_pair = jnp.concatenate([attended, attended_other], axis=1)
-            proj_up = jnp.concatenate(
-                [feed[:, i * part : (i + 1) * part, width : width + owners // 2 * half] for i in range(2)], axis=2
-            ).reshape(width, owners * half)
-            proj_down = feed[:, :half, :width].reshape(owners * half, width)
-            proj_up, proj_down = lax.optimization_barrier((proj_up, proj_down))
-            mlp_in = jnp.concatenate([mlp_mine, mlp_other], axis=0)
-            pre_act = mm(mlp_in, proj_up) + v["bias_up"]
-            activated = tangent_gelu(pre_act).astype(LOW)
-            mixed = mm(activated, proj_down)
-            leaving = mixed[tokens:].astype(LOW)
-            order.leave(leaving)
-            other = swap(leaving)
-            if layer < layers - 1:
-                (other,) = order.enter(other)
-            hidden = after_attn + mixed[:tokens] + other.astype(FULL) + v["bias_down"]
+            mlp_other, attended_other = order.enter(mlp_other, attended_other)
+            (feed,) = order.enter(feeds[layer])
+            pre_act, activated, *mixed = feed_forward(
+                mlp_mine, mlp_other, feed, v["bias_up"].reshape(1, owners * half), half, not last_layer
+            )
+            if last_layer:
+                order.leave(pre_act, activated)
+            else:
+                mixed, leaving = mixed
+                order.leave(leaving)
+                (other,) = order.enter(swap(leaving))
+                hidden = after_attn + mixed + other.astype(FULL) + v["bias_down"]
             stored.append(
                 (
-                    (proj_qkv, proj_out, proj_up, proj_down),
-                    (normed_one, inverse_one, attn_in, qkv, lse, attended_pair),
-                    (normed_two, inverse_two, mlp_in, pre_act, activated),
+                    (proj_qkv, proj_out, feed),
+                    (normed_one, inverse_one, attn_in, qkv, lse, attended, attended_other),
+                    (normed_two, inverse_two, mlp_mine, mlp_other, pre_act, activated),
                 )
             )
-        block_output = hidden.astype(LOW)[None]
 
         def writer(key, kernel, layer, scalar, *shapes):
             def write(*values):
@@ -868,22 +977,28 @@
         before = None
         for layer in reversed(range(layers)):
             v = vectors[layer]
-            proj_qkv, proj_out, proj_up, proj_down = stored[layer][0]
-            normed_one, inverse_one, attn_in, qkv, lse, attended_pair = stored[layer][1]
-            normed_two, inverse_two, mlp_in, pre_act, activated = stored[layer][2]
+            proj_qkv, proj_out, feed = stored[layer][0]
+            normed_one, inverse_one, attn_in, qkv, lse, attended, attended_other = stored[layer][1]
+            normed_two, inverse_two, mlp_mine, mlp_other, pre_act, activated = stored[layer][2]
             grad_other = swap(grad_mine)
             if before:
                 before["down"].step()
             (grad_other,) = order.enter(grad_other)
             grad_low, grad_pre_low, mixed, leaving, g_up_bias = feed_backward(
-                grad_mine, grad_other, pre_act, proj_up, proj_down
+                grad_mine, grad_other, pre_act, feed, half
             )
             order.leave(leaving)
             other = swap(leaving)
-            g_down = weight_grad([(activated, order.enter(grad_low)[0], 0)], owners, width)
+            g_down = weight_grad([((activated,), order.enter(grad_low), False, 0)], owners, width)
             order.leave(g_down)
             down_chain = Chain(written(queue_steps(g_down), pair_steps, held))
-            keep, send = weight_grad([(mlp_in, order.enter(grad_pre_low)[0], 0)], owners, half * owners, core)
+            keep, send = weight_grad(
+                [((mlp_mine, mlp_other), order.enter(grad_pre_low), False, 0)],
+                owners,
+                half * owners,
+                core,
+                LIGHT,
+            )
             order.leave(send)
             up_chain = Chain(
                 written(
@@ -921,18 +1036,20 @@
             order.leave(grad_heads)
             if before:
                 before["down"].step()
+                before["mixed"].step()
             grad_proj, leaving, g_q_bias, g_v_bias = attend_backward(
-                qkv, order.enter(grad_heads)[0].reshape(ranks * tokens, slab), lse, proj_qkv, ranks
+                qkv, *order.enter(grad_heads), lse, proj_qkv, ranks
             )
             order.leave(leaving)
             arrived = exchange(leaving)
             if before:
-                before["mixed"].step()
+                before["up"].step()
             (grad_proj,) = order.enter(grad_proj)
-            after_pair = jnp.concatenate([after_mine, after_other], axis=0)
-            attended_flat = attended_pair.transpose(1, 0, 2).reshape(2 * tokens, width)
             g_mixed = weight_grad(
-                [(attn_in, grad_proj, 0), (attended_flat, after_pair, offset)],
+                [
+                    ((attn_in,), (grad_proj,), False, 0),
+                    ((attended, attended_other), (after_mine, after_other), True, offset),
+                ],
                 owners,
                 offset + flank,
                 core if before else None,
@@ -944,7 +1061,7 @@
                     mixed_steps,
                     writer(
                         "mixed",
-                        functools.partial(mixed_kernel, ranks=ranks, layers_seen=layers, offset=offset),
+                        functools.partial(mixed_kernel, ranks=ranks, offset=offset),
                         layer,
                         me,
                         (part, 3 * width),
@@ -953,18 +1070,23 @@
                 )
             )
             if before:
+                up_chain.step()
+                down_chain.step()
                 mixed_chain.step()
+            else:
+                final, leaving = feed_out(*order.enter(activated), feed, width, half)
+                order.leave(leaving)
+                final_other = swap(leaving)
             (arrived,) = order.enter(arrived)
             grad_hidden, grad_mine, g_gain_one, g_bias_one = end_backward(
                 arrived, normed_one, inverse_one, v["gain_one"].reshape(1, width), grad_after
             )
-            order.leave(grad_mine)
-            up_chain.step()
+            order.leave(grad_hidden)
             if before:
-                before["up"].step()
+                before["mixed"].step()
                 before["down"].step()
-                before["mixed"].step()
-                down_chain.step()
+            else:
+                up_chain.step()
             last, before = before, dict(up=up_chain, down=down_chain, mixed=mixed_chain)
             downs[layer] = down_chain
 
@@ -982,19 +1104,21 @@
             )
 
         each = 8 * part + 2 * half
+        v = vectors[layers - 1]
         small_sum = local_call(
             functools.partial(pack_kernel, owners=owners, layers=layers, half=half),
             "pack_small",
             jax.ShapeDtypeStruct((owners, -(-layers * each // 128) * 128), FULL),
             *order.enter(*[row for grads in small_grads for row in grads]),
             scalars=(side,),
+            cost=LIGHT,
         )
         order.leave(small_sum)
         small_sum = lax.all_to_all(small_sum, "fsdp", split_axis=0, concat_axis=0, tiled=True)
         before["up"].step()
+        before["down"].step()
         last["mixed"].step()
         before["mixed"].step()
-        before["down"].step()
         small_sum = sum_rows(order.enter(small_sum)[0])
         order.leave(small_sum)
         total = small_sum
@@ -1002,10 +1126,10 @@
             total = total + pair_shift(small_sum, j)
         before["up"].step()
         before["mixed"].step()
+        before["down"].step()
         (total,) = order.enter(total)
         order.leave(total)
         total_other = swap(total)
-        before["down"].step()
         down_out = local_call(
             down_kernel,
             "write_down",
@@ -1014,6 +1138,9 @@
             scalars=(side,),
         )
         order.leave(down_out)
+        (final_other,) = order.enter(final_other)
+        block_output = (after_attn + final + final_other.astype(FULL) + v["bias_down"]).astype(LOW)[None]
+        order.leave(block_output)
         s = local_call(
             functools.partial(unpack_kernel, layers=layers, half=half),
             "unpack_small",

time: 639 us -> 614 us (0.961)
  local copies, waits for them, and re-layouts: 135 us -> 113 us
  waiting for transfers between devices: 215 us -> 235 us
  blocking collectives: 0 us -> 19.5 us
  other arithmetic: 30 us -> 13.5 us
  starting transfers between devices: 91.3 us -> 76.1 us
  matrix products: 18.9 us -> 5.49 us
    slice x16 -> x4, local copies, waits for them, and re-layouts: 28.4 us -> 3.64 us  [mixed_steps(): shares = [v[:, :offset] for v in (value, *got)]]
    all_to_all x6 -> x7, waiting for transfers between devices: 33.4 us -> 57.3 us  [exchange(): lax.all_to_all(blocks, 'seq', split_axis=0, concat_axis=0, tiled=True)]
    unnamed x304 -> x276, local copies, waits for them, and re-layouts: 67.9 us -> 89.5 us
    all_to_all x0 -> x2, blocking collectives: none -> 19.5 us  [the longest x1 11.6 us: exchange(): lax.all_to_all(blocks, 'seq', split_axis=0, concat_axis=0, tiled=True)]
    all_gather x2, waiting for transfers between devices: 29.8 us -> 15.3 us  [body(): attn_shares.append(lax.all_gather(share, 'fsdp', axis=0))]
    ppermute x6 -> x0, starting transfers between devices: 12.6 us -> none  [shift(): lax.ppermute(value, 'seq', [(i, (i + step) % ranks) for i in range(ranks)])]
    ppermute x12, waiting for transfers between devices: 5.85 us -> 17.5 us  [owner_xor(): return lax.ppermute(value, 'fsdp', [(i, i ^ bits) for i in range(owners)])]
    dot_general x6 -> x2, matrix products: 14.4 us -> 2.95 us  [mm(): return jnp.dot(left, right, preferred_element_type=FULL)]
  transfers between devices with their start and end apart: 60 -> 52, of which waited for: 22 -> 21; matrix products, arithmetic and copies ran while one was open for 18% -> 6% of each run, Pallas kernels for 17% -> 19%
where the time goes in v3:
time: 614 us; the launch traced here: 603 us
  waiting for transfers between devices  235 us (38%)
  Pallas kernels  125 us (20%)
  local copies, waits for them, and re-layouts  113 us (18%)
  starting transfers between devices  76.1 us (12%)
  blocking collectives  19.5 us (3%)
  between operations  15.9 us (3%)
  other arithmetic  13.5 us (2%)
    unnamed x276, local copies, waits for them, and re-layouts  89.5 us
    pallas_call x29, Pallas kernels, local_call(): pl.pallas_call(kernel, out_shape=out_shape, in_specs=[pl.BlockSpec(memory...  75.2 us
    ppermute x19, waiting for transfers between devices, swap(): return lax.ppermute(value, 'seq', [(i, i ^ 1) for i in range(ranks)])  65.3 us
    all_to_all x7, waiting for transfers between devices, exchange(): lax.all_to_all(blocks, 'seq', split_axis=0, concat_axis=0, tiled=True)  57.3 us
    all_gather x2, waiting for transfers between devices, body(): feeds.append(lax.all_gather(share, 'fsdp', axis=0))  41.1 us
    ppermute x7, waiting for transfers between devices, pair_shift(): lax.ppermute(value, 'seq', [(i, (i + 2 * step) % ranks) for i in range(ra...  38.6 us
    all_to_all x7, starting transfers between devices, exchange(): lax.all_to_all(blocks, 'seq', split_axis=0, concat_axis=0, tiled=True)  30.5 us
    ppermute x19, starting transfers between devices, swap(): return lax.ppermute(value, 'seq', [(i, i ^ 1) for i in range(ranks)])  20.1 us
  transfers between devices with their start and end apart: 52, of which 21 were waited for; matrix products, arithmetic and copies ran while one was open for 6% of the time, Pallas kernels for 19%

profile of v3, /device:TPU:0, one launch (start us, length us, event | category | flops | bytes accessed | tf_op | source)
XLA Modules:
  0.0 603.4 jit_solution(6499388174177304781)
XLA Ops:
  12.8 3.4 slice_bitcast_fusion
  28.3 6.6 %all-to-all-start = ((bf16[4,128,1152]{2,1,0:T(8,128)(2,1)}), bf16[4,128,1152]{2,1,0:T(8,128)(2,1)S(1)}, u32[]{:S(2)}, u32[]{:S(2)}) async-start(bf16[4,128,1152]{2,1,0:T(8,128)(2,1)} %broadcast_in_dim.10), calls=%async_computation | async-start | bytes 2359296 | tf_op jit(solution)/shard_map/all_to_all | solution.py:764
  34.9 28.6 %all-to-all-done = bf16[4,128,1152]{2,1,0:T(8,128)(2,1)S(1)} async-done(((bf16[4,128,1152]{2,1,0:T(8,128)(2,1)}), bf16[4,128,1152]{2,1,0:T(8,128)(2,1)S(1)}, u32[]{:S(2)}, u32[]{:S(2)}) %all-to-all-start) | async-done | bytes 1179680 | tf_op jit(solution)/shard_map/all_to_all | solution.py:764
  64.5 3.1 copy-done.7
  75.8 4.2 attend_forward.2
  81.6 3.9 all-to-all-start.1
  86.1 8.3 %all-to-all-done.1 = bf16[4,288,128]{2,1,0:T(8,128)(2,1)S(1)} async-done(((bf16[4,288,128]{2,1,0:T(8,128)(2,1)}), bf16[4,288,128]{2,1,0:T(8,128)(2,1)S(1)}, u32[]{:S(2)}, u32[]{:S(2)}) %all-to-all-start.1) | async-done | bytes 294944 | tf_op jit(solution)/shard_map/all_to_all | solution.py:764
  100.9 10.2 %collective-permute-done.1.refs_4_ = bf16[1152,128]{1,0:T(8,128)(2,1)S(1)} collective-permute-done((bf16[1152,128]{1,0:T(8,128)(2,1)S(1)}, bf16[1152,128]{1,0:T(8,128)(2,1)S(1)}, u32[]{:S(2)}, u32[]{:S(2)}) %collective-permute-start.1) | collective-permute-done | bytes 294944 | tf_op jit(solution)/shard_map/ppermute | solution.py:755
  111.1 10.9 %all-gather.11.cloned.1.call-done = bf16[2304,2304]{1,0:T(8,128)(2,1)} async-done(((bf16[288,2304]{1,0:T(8,128)(2,1)}), bf16[2304,2304]{1,0:T(8,128)(2,1)}) %all-gather.11.cloned.1.call-update) | async-done | bytes 10616848 | tf_op jit(solution)/shard_map/all_gather | solution.py:880
  122.0 4.0 copy-done.71
  126.1 4.4 feed_forward.2
  132.1 7.7 %collective-permute-done.2 = bf16[128,1152]{1,0:T(8,128)(2,1)S(1)} collective-permute-done((bf16[128,1152]{1,0:T(8,128)(2,1)S(1)}, bf16[128,1152]{1,0:T(8,128)(2,1)S(1)}, u32[]{:S(2)}, u32[]{:S(2)}) %collective-permute-start.2) | collective-permute-done | bytes 294944 | tf_op jit(solution)/shard_map/ppermute | solution.py:755
  143.0 4.6 all-to-all-start.2
  147.6 15.3 %all-gather.13.cloned.1.call-done = bf16[1152,2016]{1,0:T(8,128)(2,1)} async-done(((bf16[144,2016]{1,0:T(8,128)(2,1)}), bf16[1152,2016]{1,0:T(8,128)(2,1)}) %all-gather.13.cloned.1.call-update) | async-done | bytes 4644880 | tf_op jit(solution)/shard_map/all_gather | solution.py:877
  162.9 2.3 copy-done.8
  167.1 8.8 %all-to-all-done.2 = bf16[4,128,1152]{2,1,0:T(8,128)(2,1)S(1)} async-done(((bf16[4,128,1152]{2,1,0:T(8,128)(2,1)}), bf16[4,128,1152]{2,1,0:T(8,128)(2,1)S(1)}, u32[]{:S(2)}, u32[]{:S(2)}) %all-to-all-start.2) | async-done | bytes 1179680 | tf_op jit(solution)/shard_map/all_to_all | solution.py:764
  178.0 3.5 attend_forward.3
  181.5 11.6 %all_to_all.52 = bf16[4,288,128]{2,1,0:T(8,128)(2,1)S(1)} all-to-all(bf16[4,288,128]{2,1,0:T(8,128)(2,1)S(1)} %get-tuple-element.214), channel_id=1, replica_groups=mesh['seq'=4,'fsdp'=8] {'seq'}, dimensions={0} | all-to-all | bytes 589824 | tf_op jit(solution)/shard_map/all_to_all | solution.py:764
  198.9 30.2 %all-gather.15.cloned.1.call-done = bf16[2304,2304]{1,0:T(8,128)(2,1)} async-done(((bf16[288,2304]{1,0:T(8,128)(2,1)}), bf16[2304,2304]{1,0:T(8,128)(2,1)}) %all-gather.15.cloned.1.call-update) | async-done | bytes 10616848 | tf_op jit(solution)/shard_map/all_gather | solution.py:880
  229.0 4.0 copy-done.73
  233.1 3.2 feed_forward.3
  236.3 6.2 %feed_backward.2 = (bf16[256,1152]{1,0:T(8,128)(2,1)S(1)}, bf16[256,2176]{1,0:T(8,128)(2,1)S(1)}, f32[128,1152]{1,0:T(8,128)S(1)}, bf16[128,1152]{1,0:T(8,128)(2,1)S(1)}, f32[1,2176]{1,0:T(1,128)S(1)}) custom-call(bf16[128,1152]{1,0:T(8,128)(2,1)} %bitcast.27.mine_ref, bf16[128,1152]{1,0:T(8,128)(2,1)} %collective-permute-done.5.other_ref, ...), custom_call_target="tpu_custom_call" | custom-call | flops 20000000000 | bytes 1 | tf_op jit(solution)/shard_map/feed_backward/pallas_call | solution.py:250
  246.7 2.3 copy-done.5
  251.8 7.2 %weight_grad.7 = (bf16[4,144,2176]{2,1,0:T(8,128)(2,1)S(1)}, bf16[4,144,2176]{2,1,0:T(8,128)(2,1)}) custom-call(s32[1]{0:T(128)} %bitcast.28.refs_0_, bf16[128,1152]{1,0:T(8,128)(2,1)S(1)} %get-tuple-element.428.mine_ref.refs_1_, bf16[128,1152]{1,0:T(8,128)(2,1)} %collective-permute-done.3.other_ref.refs_2_, bf16[256,2176]{1,0:T(8,128)(2,1)S(1)} %copy-done.32), custom_call_target="tpu_custom_call" | custom-call | flops 1 | bytes 1 | tf_op jit(solution)/shard_map/weight_grad/pallas_call | solution.py:250
  267.2 3.1 mid_backward.2
  274.1 4.1 all-to-all-start.4
  282.0 4.0 meet_cores.3
  292.9 8.1 %attend_backward.2 = (bf16[512,864]{1,0:T(8,128)(2,1)S(1)}, bf16[4,128,1152]{2,1,0:T(8,128)(2,1)S(1)}, f32[1,288]{1,0:T(1,128)S(1)}, f32[1,288]{1,0:T(1,128)S(1)}) custom-call(bf16[3,512,288]{2,1,0:T(8,128)(2,1)S(1)} %pad_maximum_fusion.1.qkv_ref, bf16[4,288,128]{2,1,0:T(8,128)(2,1)} %all-to-all-done.4.got_ref, f32[512,4]{1,0:T(8,128)S(1)} %copy-done.86, ...), custom_call_target="tpu_custom_call" | custom-call | flops 20000000000 | bytes 1 | tf_op jit(solution)/shard_map/attend_backward/pallas_call | solution.py:158
  303.0 3.7 all-to-all-start.5
  309.7 4.7 weight_grad.8
  314.9 4.1 copy-done.74
  320.2 2.5 feed_out.1
  323.7 11.6 %all-to-all-done.5.got_ref = bf16[4,128,1152]{2,1,0:T(8,128)(2,1)S(1)} async-done(((bf16[4,128,1152]{2,1,0:T(8,128)(2,1)}), bf16[4,128,1152]{2,1,0:T(8,128)(2,1)S(1)}, u32[]{:S(2)}, u32[]{:S(2)}) %all-to-all-start.5) | async-done | bytes 1179680 | tf_op jit(solution)/shard_map/all_to_all | solution.py:764
  339.6 2.1 collective-permute-start.16
  341.7 6.7 %collective-permute-done.10.other_ref = bf16[128,1152]{1,0:T(8,128)(2,1)S(1)} collective-permute-done((bf16[128,1152]{1,0:T(8,128)(2,1)S(1)}, bf16[128,1152]{1,0:T(8,128)(2,1)S(1)}, u32[]{:S(2)}, u32[]{:S(2)}) %collective-permute-start.10) | collective-permute-done | bytes 294944 | tf_op jit(solution)/shard_map/ppermute | solution.py:755
  348.4 4.5 copy-done.72
  354.5 5.4 feed_backward.3
  361.7 2.2 copy-done.6
  364.0 6.2 %weight_grad.10 = (bf16[4,144,2176]{2,1,0:T(8,128)(2,1)S(1)}, bf16[4,144,2176]{2,1,0:T(8,128)(2,1)}) custom-call(s32[1]{0:T(128)} %bitcast.28.refs_0_, bf16[128,1152]{1,0:T(8,128)(2,1)S(1)} %copy-done.30, bf16[128,1152]{1,0:T(8,128)(2,1)S(1)} %copy-done.51, bf16[256,2176]{1,0:T(8,128)(2,1)S(1)} %get-tuple-element.264.refs_3_), custom_call_target="tpu_custom_call" | custom-call | flops 1 | bytes 1 | tf_op jit(solution)/shard_map/weight_grad/pallas_call | solution.py:250
  371.7 3.1 collective-permute-start.21
  378.3 2.4 mid_backward.3
  383.7 3.5 all-to-all-start.6
  391.2 4.2 meet_cores.4
  396.2 15.2 %collective-permute-done.20.refs_6_ = bf16[128,576]{1,0:T(8,128)(2,1)S(1)} collective-permute-done((bf16[128,576]{1,0:T(8,128)(2,1)}, bf16[128,576]{1,0:T(8,128)(2,1)S(1)}, u32[]{:S(2)}, u32[]{:S(2)}) %collective-permute-start.20) | collective-permute-done | bytes 147488 | tf_op jit(solution)/shard_map/ppermute | solution.py:755
  417.7 8.3 %attend_backward.3 = (bf16[512,864]{1,0:T(8,128)(2,1)S(1)}, bf16[4,128,1152]{2,1,0:T(8,128)(2,1)}, f32[1,288]{1,0:T(1,128)S(1)}, f32[1,288]{1,0:T(1,128)S(1)}) custom-call(bf16[3,512,288]{2,1,0:T(8,128)(2,1)S(1)} %copy-done.10, bf16[4,288,128]{2,1,0:T(8,128)(2,1)S(1)} %copy-done.48, f32[512,4]{1,0:T(8,128)S(1)} %copy-done.84, bf16[1152,864]{1,0:T(8,128)(2,1)S(1)} %copy-done.77), custom_call_target="tpu_custom_call" | custom-call | flops 20000000000 | bytes 1 | tf_op jit(solution)/shard_map/attend_backward/pallas_call | solution.py:158
  426.9 4.3 all-to-all-start.7
  433.8 6.2 %weight_grad.11 = (bf16[4,144,1472]{2,1,0:T(8,128)(2,1)S(1)}, bf16[4,144,1472]{2,1,0:T(8,128)(2,1)}) custom-call(s32[1]{0:T(128)} %bitcast.28.refs_0_, bf16[512,1152]{1,0:T(8,128)(2,1)S(1)} %copy-done.27, bf16[512,864]{1,0:T(8,128)(2,1)S(1)} %copy-done.101, bf16[1152,128]{1,0:T(8,128)(2,1)S(1)} %bitcast.98, bf16[1152,128]{1,0:T(8,128)(2,1)S(1)} %copy-done.81, ...), custom_call_target="tpu_custom_call" | custom-call | flops 20000000000 | bytes 1 | tf_op jit(solution)/shard_map/weight_grad/pallas_call | solution.py:250
  448.6 3.0 collective-permute-start.27
  451.7 5.9 collective-permute-done.17.refs_1_
  458.4 2.1 collective-permute-start.26
  460.5 11.5 %collective-permute-done.18.refs_2_ = bf16[144,2176]{1,0:T(8,128)(2,1)} collective-permute-done((bf16[144,2176]{1,0:T(8,128)(2,1)}, bf16[144,2176]{1,0:T(8,128)(2,1)}, u32[]{:S(2)}, u32[]{:S(2)}) %collective-permute-start.18) | collective-permute-done | bytes 626720 | tf_op jit(solution)/shard_map/ppermute | solution.py:761
  475.8 3.1 collective-permute-start.24
  478.9 3.5 meet_cores.5
  485.4 2.7 end_backward.3
  494.1 26.8 %collective-permute-done.24.refs_1_ = bf16[144,2176]{1,0:T(8,128)(2,1)} collective-permute-done((bf16[144,2176]{1,0:T(8,128)(2,1)S(1)}, bf16[144,2176]{1,0:T(8,128)(2,1)}, u32[]{:S(2)}, u32[]{:S(2)}) %collective-permute-start.24) | collective-permute-done | bytes 626720 | tf_op jit(solution)/shard_map/ppermute | solution.py:758
  524.4 8.7 %collective-permute-done.23.refs_1_ = bf16[272,1152]{1,0:T(8,128)(2,1)} collective-permute-done((bf16[272,1152]{1,0:T(8,128)(2,1)}, bf16[272,1152]{1,0:T(8,128)(2,1)}, u32[]{:S(2)}, u32[]{:S(2)}) %collective-permute-start.23) | collective-permute-done | bytes 626720 | tf_op jit(solution)/shard_map/ppermute | solution.py:758
  539.5 3.5 collective-permute-start.33
  543.1 7.9 %all_to_all.53 = f32[8,1,3456]{2,1,0:T(1,128)S(1)} all-to-all(f32[8,1,3456]{2,1,0:T(1,128)S(1)} %copy.53), channel_id=1, replica_groups=mesh['seq'=4,'fsdp'=8] {'fsdp'}, dimensions={0} | all-to-all | bytes 221184 | tf_op jit(solution)/shard_map/all_to_all | solution.py:1117
  553.2 3.8 collective-permute-done.34.across_ref
  557.0 3.0 write_up.3
  560.1 3.1 collective-permute-done.33
  565.4 13.7 %collective-permute-done.28.refs_1_ = bf16[272,1152]{1,0:T(8,128)(2,1)S(1)} collective-permute-done((bf16[272,1152]{1,0:T(8,128)(2,1)S(1)}, bf16[272,1152]{1,0:T(8,128)(2,1)S(1)}, u32[]{:S(2)}, u32[]{:S(2)}) %collective-permute-start.28) | collective-permute-done | bytes 626720 | tf_op jit(solution)/shard_map/ppermute | solution.py:755
  580.3 4.7 write_down.1
  585.9 7.0 %collective-permute-done.36.second_ref = f32[1,3456]{1,0:T(1,128)S(1)} collective-permute-done((f32[1,3456]{1,0:T(1,128)S(1)}, f32[1,3456]{1,0:T(1,128)S(1)}, u32[]{:S(2)}, u32[]{:S(2)}) %collective-permute-start.36) | collective-permute-done | bytes 13856 | tf_op jit(solution)/shard_map/ppermute | solution.py:755
  (452 shorter events, 158.9 us)
Async XLA Ops:
  7.2 57.0 %all-gather.9.cloned.1.call-start = ((), (), s32[]{:S(2)}) async-start(), calls=%async_computation.15 | async-start | bytes 5603328 | tf_op jit(solution)/shard_map/all_gather | solution.py:877
  12.8 109.3 %all-gather.11.cloned.1.call-start = ((), (), s32[]{:S(2)}) async-start(), calls=%async_computation.16 | async-start | bytes 11943936 | tf_op jit(solution)/shard_map/all_gather | solution.py:880
  20.6 142.2 %all-gather.13.cloned.1.call-start = ((), (), s32[]{:S(2)}) async-start(), calls=%async_computation.17 | async-start | bytes 5308416 | tf_op jit(solution)/shard_map/all_gather | solution.py:877
  22.7 206.3 %all-gather.15.cloned.1.call-start = ((), (), s32[]{:S(2)}) async-start(), calls=%async_computation.18 | async-start | bytes 11943936 | tf_op jit(solution)/shard_map/all_gather | solution.py:880
  28.3 35.2 %all-to-all-start = ((bf16[4,128,1152]{2,1,0:T(8,128)(2,1)}), bf16[4,128,1152]{2,1,0:T(8,128)(2,1)S(1)}, u32[]{:S(2)}, u32[]{:S(2)}) async-start(bf16[4,128,1152]{2,1,0:T(8,128)(2,1)} %broadcast_in_dim.10), calls=%async_computation | async-start | bytes 2359296 | tf_op jit(solution)/shard_map/all_to_all | solution.py:764
  69.3 25.2 %copy-start.11 = (bf16[1152,1152]{1,0:T(8,128)(2,1)}, bf16[1152,1152]{1,0:T(8,128)(2,1)S(1)}, u32[]{:S(2)}) copy-start(bf16[1152,1152]{1,0:T(8,128)(2,1)S(1)} %get-tuple-element.203.proj_ref) | copy-start | bytes 7962628
  81.6 12.8 %all-to-all-start.1 = ((bf16[4,288,128]{2,1,0:T(8,128)(2,1)}), bf16[4,288,128]{2,1,0:T(8,128)(2,1)S(1)}, u32[]{:S(2)}, u32[]{:S(2)}) async-start(bf16[4,288,128]{2,1,0:T(8,128)(2,1)} %get-tuple-element.201), calls=%async_computation.1 | async-start | bytes 589824 | tf_op jit(solution)/shard_map/all_to_all | solution.py:764
  98.0 32.5 %copy-start.29 = (bf16[128,1152]{1,0:T(8,128)(2,1)}, bf16[128,1152]{1,0:T(8,128)(2,1)S(1)}, u32[]{:S(2)}) copy-start(bf16[128,1152]{1,0:T(8,128)(2,1)S(1)} %get-tuple-element.434.mine_ref.refs_1_) | copy-start | bytes 884740
  98.0 13.1 %collective-permute-start = (bf16[128,1152]{1,0:T(8,128)(2,1)S(1)}, bf16[128,1152]{1,0:T(8,128)(2,1)S(1)}, u32[]{:S(2)}, u32[]{:S(2)}) collective-permute-start(bf16[128,1152]{1,0:T(8,128)(2,1)S(1)} %get-tuple-element.434.mine_ref.refs_1_), channel_id=1, source_target_pairs={{0,8},{8,0},{16,24},{24,16},{1,9},{9,1},{17,25},{25,17},{2,10},{10... | collective-permute-start | bytes 884744 | tf_op jit(solution)/shard_map/ppermute | solution.py:755
  98.0 13.1 %collective-permute-start.1 = (bf16[1152,128]{1,0:T(8,128)(2,1)S(1)}, bf16[1152,128]{1,0:T(8,128)(2,1)S(1)}, u32[]{:S(2)}, u32[]{:S(2)}) collective-permute-start(bf16[1152,128]{1,0:T(8,128)(2,1)S(1)} %bitcast.97), channel_id=1, source_target_pairs={{0,8},{8,0},{16,24},{24,16},{1,9},{9,1},{17,25},{25,17},{2,10},{10... | collective-permute-start | bytes 884744 | tf_op jit(solution)/shard_map/ppermute | solution.py:755
  130.6 9.2 %collective-permute-start.2 = (bf16[128,1152]{1,0:T(8,128)(2,1)S(1)}, bf16[128,1152]{1,0:T(8,128)(2,1)S(1)}, u32[]{:S(2)}, u32[]{:S(2)}) collective-permute-start(bf16[128,1152]{1,0:T(8,128)(2,1)S(1)} %get-tuple-element.208), channel_id=1, source_target_pairs={{0,8},{8,0},{16,24},{24,16},{1,9},{9,1},{17,25},{25,17},{2,10},{10... | collective-permute-start | bytes 884744 | tf_op jit(solution)/shard_map/ppermute | solution.py:755
  143.0 32.9 %all-to-all-start.2 = ((bf16[4,128,1152]{2,1,0:T(8,128)(2,1)}), bf16[4,128,1152]{2,1,0:T(8,128)(2,1)S(1)}, u32[]{:S(2)}, u32[]{:S(2)}) async-start(bf16[4,128,1152]{2,1,0:T(8,128)(2,1)} %broadcast_in_dim.11), calls=%async_computation.2 | async-start | bytes 2359296 | tf_op jit(solution)/shard_map/all_to_all | solution.py:764
  147.6 194.1 %reduce-scatter.4.cloned.1.call-start = ((), (), s32[]{:S(2)}) async-start(), calls=%async_computation.12 | async-start | bytes 5640192 | tf_op jit(solution)/shard_map/reduce_scatter | solution.py:817
  194.8 34.3 %collective-permute-start.4 = (bf16[1152,128]{1,0:T(8,128)(2,1)S(1)}, bf16[1152,128]{1,0:T(8,128)(2,1)}, u32[]{:S(2)}, u32[]{:S(2)}) collective-permute-start(bf16[1152,128]{1,0:T(8,128)(2,1)S(1)} %bitcast.100), channel_id=1, source_target_pairs={{0,8},{8,0},{16,24},{24,16},{1,9},{9,1},{17,25},{25,17},{2,10},{10... | collective-permute-start | bytes 884744 | tf_op jit(solution)/shard_map/ppermute | solution.py:755
  195.3 33.7 %collective-permute-start.3 = (bf16[128,1152]{1,0:T(8,128)(2,1)S(1)}, bf16[128,1152]{1,0:T(8,128)(2,1)}, u32[]{:S(2)}, u32[]{:S(2)}) collective-permute-start(bf16[128,1152]{1,0:T(8,128)(2,1)S(1)} %get-tuple-element.428.mine_ref.refs_1_), channel_id=1, source_target_pairs={{0,8},{8,0},{16,24},{24,16},{1,9},{9,1},{17,25},{25,17},{2,10},{10... | collective-permute-start | bytes 884744 | tf_op jit(solution)/shard_map/ppermute | solution.py:755
  196.9 39.4 %collective-permute-start.5 = (bf16[128,1152]{1,0:T(8,128)(2,1)}, bf16[128,1152]{1,0:T(8,128)(2,1)}, u32[]{:S(2)}, u32[]{:S(2)}) collective-permute-start(bf16[128,1152]{1,0:T(8,128)(2,1)} %bitcast.27.mine_ref), channel_id=1, source_target_pairs={{0,8},{8,0},{16,24},{24,16},{1,9},{9,1},{17,25},{25,17},{2,10},{10... | collective-permute-start | bytes 884744 | tf_op jit(solution)/shard_map/ppermute | solution.py:755
  249.0 13.5 %collective-permute-start.6 = (bf16[128,1152]{1,0:T(8,128)(2,1)}, bf16[128,1152]{1,0:T(8,128)(2,1)}, u32[]{:S(2)}, u32[]{:S(2)}) collective-permute-start(bf16[128,1152]{1,0:T(8,128)(2,1)} %copy-done.82), channel_id=1, source_target_pairs={{0,8},{8,0},{16,24},{24,16},{1,9},{9,1},{17,25},{25,17},{2,10},{10... | collective-permute-start | bytes 884744 | tf_op jit(solution)/shard_map/ppermute | solution.py:755
  260.5 19.8 %collective-permute-start.8 = (bf16[4,144,2176]{2,1,0:T(8,128)(2,1)}, bf16[4,144,2176]{2,1,0:T(8,128)(2,1)}, u32[]{:S(2)}, u32[]{:S(2)}) collective-permute-start(bf16[4,144,2176]{2,1,0:T(8,128)(2,1)} %get-tuple-element.228), channel_id=1, source_target_pairs={{0,1},{1,0},{2,3},{3,2},{4,5},{5,4},{6,7},{7,6},{8,9},{9,8},{10,11... | collective-permute-start | bytes 7520264 | tf_op jit(solution)/shard_map/ppermute | solution.py:761
  274.1 16.2 %all-to-all-start.4 = ((bf16[4,288,128]{2,1,0:T(8,128)(2,1)}), bf16[4,288,128]{2,1,0:T(8,128)(2,1)}, u32[]{:S(2)}, u32[]{:S(2)}) async-start(bf16[4,288,128]{2,1,0:T(8,128)(2,1)} %get-tuple-element.230), calls=%async_computation.4 | async-start | bytes 589824 | tf_op jit(solution)/shard_map/all_to_all | solution.py:764
  278.2 11.5 %collective-permute-start.7 = (bf16[128,576]{1,0:T(8,128)(2,1)}, bf16[128,576]{1,0:T(8,128)(2,1)S(1)}, u32[]{:S(2)}, u32[]{:S(2)}) collective-permute-start(bf16[128,576]{1,0:T(8,128)(2,1)} %get-tuple-element.231), channel_id=1, source_target_pairs={{0,8},{8,0},{16,24},{24,16},{1,9},{9,1},{17,25},{25,17},{2,10},{10... | collective-permute-start | bytes 442376 | tf_op jit(solution)/shard_map/ppermute | solution.py:755
  286.0 51.6 %collective-permute-start.11 = (bf16[144,2176]{1,0:T(8,128)(2,1)}, bf16[144,2176]{1,0:T(8,128)(2,1)}, u32[]{:S(2)}, u32[]{:S(2)}) collective-permute-start(bf16[144,2176]{1,0:T(8,128)(2,1)} %get-tuple-element.234), channel_id=1, source_target_pairs={{0,2},{1,3},{2,0},{3,1},{4,6},{5,7},{6,4},{7,5},{8,10},{9,11},{10,... | collective-permute-start | bytes 1880072 | tf_op jit(solution)/shard_map/ppermute | solution.py:761
  287.5 50.2 %collective-permute-start.12 = (bf16[144,2176]{1,0:T(8,128)(2,1)}, bf16[144,2176]{1,0:T(8,128)(2,1)}, u32[]{:S(2)}, u32[]{:S(2)}) collective-permute-start(bf16[144,2176]{1,0:T(8,128)(2,1)} %get-tuple-element.235), channel_id=1, source_target_pairs={{0,4},{1,5},{2,6},{3,7},{4,0},{5,1},{6,2},{7,3},{8,12},{9,13},{10,... | collective-permute-start | bytes 1880072 | tf_op jit(solution)/shard_map/ppermute | solution.py:761
  288.2 49.5 %collective-permute-start.13 = (bf16[144,2176]{1,0:T(8,128)(2,1)}, bf16[144,2176]{1,0:T(8,128)(2,1)}, u32[]{:S(2)}, u32[]{:S(2)}) collective-permute-start(bf16[144,2176]{1,0:T(8,128)(2,1)} %get-tuple-element.236), channel_id=1, source_target_pairs={{0,6},{1,7},{2,4},{3,5},{4,2},{5,3},{6,0},{7,1},{8,14},{9,15},{10,... | collective-permute-start | bytes 1880072 | tf_op jit(solution)/shard_map/ppermute | solution.py:761
  303.0 32.3 %all-to-all-start.5 = ((bf16[4,128,1152]{2,1,0:T(8,128)(2,1)}), bf16[4,128,1152]{2,1,0:T(8,128)(2,1)S(1)}, u32[]{:S(2)}, u32[]{:S(2)}) async-start(bf16[4,128,1152]{2,1,0:T(8,128)(2,1)} %copy-done.28), calls=%async_computation.5 | async-start | bytes 2359296 | tf_op jit(solution)/shard_map/all_to_all | solution.py:764
  306.7 107.5 %reduce-scatter.8.cloned.1.call-start = ((), (), s32[]{:S(2)}) async-start(), calls=%async_computation.14 | async-start | bytes 3981312 | tf_op jit(solution)/shard_map/reduce_scatter | solution.py:817
  314.4 20.9 %copy-start.42 = (f32[128,1152]{1,0:T(8,128)S(1)}, f32[128,1152]{1,0:T(8,128)}, u32[]{:S(2)}) copy-start(f32[128,1152]{1,0:T(8,128)} %get-tuple-element.431.normed_ref) | copy-start | bytes 1769476
  314.4 20.8 %copy-start.62 = (f32[1,1152]{1,0:T(1,128)S(1)}, f32[1,1152]{1,0:T(1,128)}, u32[]{:S(2)}) copy-start(f32[1,1152]{1,0:T(1,128)} %get-tuple-element.450.gain_ref) | copy-start | bytes 13828
  314.4 164.5 %reduce-scatter.6.cloned.1.call-start = ((), (), s32[]{:S(2)}) async-start(), calls=%async_computation.13 | async-start | bytes 5640192 | tf_op jit(solution)/shard_map/reduce_scatter | solution.py:817
  337.6 10.8 %collective-permute-start.10 = (bf16[128,1152]{1,0:T(8,128)(2,1)S(1)}, bf16[128,1152]{1,0:T(8,128)(2,1)S(1)}, u32[]{:S(2)}, u32[]{:S(2)}) collective-permute-start(bf16[128,1152]{1,0:T(8,128)(2,1)S(1)} %get-tuple-element.251.mine_ref), channel_id=1, source_target_pairs={{0,8},{8,0},{16,24},{24,16},{1,9},{9,1},{17,25},{25,17},{2,10},{10... | collective-permute-start | bytes 884744 | tf_op jit(solution)/shard_map/ppermute | solution.py:755
  339.6 20.4 %copy-start.16 = (bf16[144,2176]{1,0:T(8,128)(2,1)}, bf16[144,2176]{1,0:T(8,128)(2,1)S(1)}, u32[]{:S(2)}) copy-start(bf16[144,2176]{1,0:T(8,128)(2,1)S(1)} %add_all.9.refs_0_) | copy-start | bytes 1880068
  339.6 36.0 %collective-permute-start.16 = (bf16[144,2176]{1,0:T(8,128)(2,1)S(1)}, bf16[144,2176]{1,0:T(8,128)(2,1)}, u32[]{:S(2)}, u32[]{:S(2)}) collective-permute-start(bf16[144,2176]{1,0:T(8,128)(2,1)S(1)} %add_all.9.refs_0_), channel_id=1, source_target_pairs={{0,16},{8,24},{16,0},{24,8},{1,17},{9,25},{17,1},{25,9},{2,18},{10... | collective-permute-start | bytes 1880072 | tf_op jit(solution)/shard_map/ppermute | solution.py:758
  360.0 15.7 %collective-permute-start.15 = (bf16[128,1152]{1,0:T(8,128)(2,1)}, bf16[128,1152]{1,0:T(8,128)(2,1)}, u32[]{:S(2)}, u32[]{:S(2)}) collective-permute-start(bf16[128,1152]{1,0:T(8,128)(2,1)} %get-tuple-element.261), channel_id=1, source_target_pairs={{0,8},{8,0},{16,24},{24,16},{1,9},{9,1},{17,25},{25,17},{2,10},{10... | collective-permute-start | bytes 884744 | tf_op jit(solution)/shard_map/ppermute | solution.py:755
  371.6 17.6 %collective-permute-start.14 = (bf16[4,144,2176]{2,1,0:T(8,128)(2,1)}, bf16[4,144,2176]{2,1,0:T(8,128)(2,1)}, u32[]{:S(2)}, u32[]{:S(2)}) collective-permute-start(bf16[4,144,2176]{2,1,0:T(8,128)(2,1)} %get-tuple-element.266), channel_id=1, source_target_pairs={{0,1},{1,0},{2,3},{3,2},{4,5},{5,4},{6,7},{7,6},{8,9},{9,8},{10,11... | collective-permute-start | bytes 7520264 | tf_op jit(solution)/shard_map/ppermute | solution.py:761
  371.7 41.0 %collective-permute-start.21 = (bf16[272,1152]{1,0:T(8,128)(2,1)}, bf16[272,1152]{1,0:T(8,128)(2,1)}, u32[]{:S(2)}, u32[]{:S(2)}) collective-permute-start(bf16[272,1152]{1,0:T(8,128)(2,1)} %reduce-scatter.4.cloned.1.call-done.refs_0_), channel_id=1, source_target_pairs={{0,16},{8,24},{16,0},{24,8},{1,17},{9,25},{17,1},{25,9},{2,18},{10... | collective-permute-start | bytes 1880072 | tf_op jit(solution)/shard_map/ppermute | solution.py:758
  383.7 28.4 %all-to-all-start.6 = ((bf16[4,288,128]{2,1,0:T(8,128)(2,1)}), bf16[4,288,128]{2,1,0:T(8,128)(2,1)S(1)}, u32[]{:S(2)}, u32[]{:S(2)}) async-start(bf16[4,288,128]{2,1,0:T(8,128)(2,1)} %copy-done.49), calls=%async_computation.8 | async-start | bytes 589824 | tf_op jit(solution)/shard_map/all_to_all | solution.py:764
  387.1 24.2 %collective-permute-start.20 = (bf16[128,576]{1,0:T(8,128)(2,1)}, bf16[128,576]{1,0:T(8,128)(2,1)S(1)}, u32[]{:S(2)}, u32[]{:S(2)}) collective-permute-start(bf16[128,576]{1,0:T(8,128)(2,1)} %copy-done.91), channel_id=1, source_target_pairs={{0,8},{8,0},{16,24},{24,16},{1,9},{9,1},{17,25},{25,17},{2,10},{10... | collective-permute-start | bytes 442376 | tf_op jit(solution)/shard_map/ppermute | solution.py:755
  389.1 42.2 %collective-permute-start.22 = (bf16[144,2176]{1,0:T(8,128)(2,1)S(1)}, bf16[144,2176]{1,0:T(8,128)(2,1)S(1)}, u32[]{:S(2)}, u32[]{:S(2)}) collective-permute-start(bf16[144,2176]{1,0:T(8,128)(2,1)S(1)} %add_all.10.own_ref), channel_id=1, source_target_pairs={{0,8},{8,0},{16,24},{24,16},{1,9},{9,1},{17,25},{25,17},{2,10},{10... | collective-permute-start | bytes 1880072 | tf_op jit(solution)/shard_map/ppermute | solution.py:755
  426.9 56.3 %all-to-all-start.7 = ((bf16[4,128,1152]{2,1,0:T(8,128)(2,1)}), bf16[4,128,1152]{2,1,0:T(8,128)(2,1)}, u32[]{:S(2)}, u32[]{:S(2)}) async-start(bf16[4,128,1152]{2,1,0:T(8,128)(2,1)} %get-tuple-element.284), calls=%async_computation.10 | async-start | bytes 2359296 | tf_op jit(solution)/shard_map/all_to_all | solution.py:764
  440.0 38.9 %collective-permute-start.25 = (bf16[4,144,1472]{2,1,0:T(8,128)(2,1)}, bf16[4,144,1472]{2,1,0:T(8,128)(2,1)}, u32[]{:S(2)}, u32[]{:S(2)}) collective-permute-start(bf16[4,144,1472]{2,1,0:T(8,128)(2,1)} %get-tuple-element.291), channel_id=1, source_target_pairs={{0,1},{1,0},{2,3},{3,2},{4,5},{5,4},{6,7},{7,6},{8,9},{9,8},{10,11... | collective-permute-start | bytes 5087240 | tf_op jit(solution)/shard_map/ppermute | solution.py:761
  440.4 17.2 %collective-permute-start.17 = (bf16[144,2176]{1,0:T(8,128)(2,1)}, bf16[144,2176]{1,0:T(8,128)(2,1)S(1)}, u32[]{:S(2)}, u32[]{:S(2)}) collective-permute-start(bf16[144,2176]{1,0:T(8,128)(2,1)} %get-tuple-element.274), channel_id=1, source_target_pairs={{0,2},{1,3},{2,0},{3,1},{4,6},{5,7},{6,4},{7,5},{8,10},{9,11},{10,... | collective-permute-start | bytes 1880072 | tf_op jit(solution)/shard_map/ppermute | solution.py:761
  442.0 30.0 %collective-permute-start.18 = (bf16[144,2176]{1,0:T(8,128)(2,1)}, bf16[144,2176]{1,0:T(8,128)(2,1)}, u32[]{:S(2)}, u32[]{:S(2)}) collective-permute-start(bf16[144,2176]{1,0:T(8,128)(2,1)} %get-tuple-element.275), channel_id=1, source_target_pairs={{0,4},{1,5},{2,6},{3,7},{4,0},{5,1},{6,2},{7,3},{8,12},{9,13},{10,... | collective-permute-start | bytes 1880072 | tf_op jit(solution)/shard_map/ppermute | solution.py:761
  442.1 30.0 %collective-permute-start.19 = (bf16[144,2176]{1,0:T(8,128)(2,1)}, bf16[144,2176]{1,0:T(8,128)(2,1)}, u32[]{:S(2)}, u32[]{:S(2)}) collective-permute-start(bf16[144,2176]{1,0:T(8,128)(2,1)} %get-tuple-element.276), channel_id=1, source_target_pairs={{0,6},{1,7},{2,4},{3,5},{4,2},{5,3},{6,0},{7,1},{8,14},{9,15},{10,... | collective-permute-start | bytes 1880072 | tf_op jit(solution)/shard_map/ppermute | solution.py:761
  448.6 39.4 %collective-permute-start.27 = (bf16[144,1472]{1,0:T(8,128)(2,1)}, bf16[144,1472]{1,0:T(8,128)(2,1)}, u32[]{:S(2)}, u32[]{:S(2)}) collective-permute-start(bf16[144,1472]{1,0:T(8,128)(2,1)} %reduce-scatter.8.cloned.1.call-done), channel_id=1, source_target_pairs={{0,16},{8,24},{16,0},{24,8},{1,17},{9,25},{17,1},{25,9},{2,18},{10... | collective-permute-start | bytes 1271816 | tf_op jit(solution)/shard_map/ppermute | solution.py:758
  458.4 34.3 %collective-permute-start.26 = (bf16[272,1152]{1,0:T(8,128)(2,1)S(1)}, bf16[272,1152]{1,0:T(8,128)(2,1)}, u32[]{:S(2)}, u32[]{:S(2)}) collective-permute-start(bf16[272,1152]{1,0:T(8,128)(2,1)S(1)} %add_all.11.refs_2_), channel_id=1, source_target_pairs={{0,8},{8,0},{16,24},{24,16},{1,9},{9,1},{17,25},{25,17},{2,10},{10... | collective-permute-start | bytes 1880072 | tf_op jit(solution)/shard_map/ppermute | solution.py:755
  475.8 45.1 %collective-permute-start.24 = (bf16[144,2176]{1,0:T(8,128)(2,1)S(1)}, bf16[144,2176]{1,0:T(8,128)(2,1)}, u32[]{:S(2)}, u32[]{:S(2)}) collective-permute-start(bf16[144,2176]{1,0:T(8,128)(2,1)S(1)} %add_all.12.refs_0_), channel_id=1, source_target_pairs={{0,16},{8,24},{16,0},{24,8},{1,17},{9,25},{17,1},{25,9},{2,18},{10... | collective-permute-start | bytes 1880072 | tf_op jit(solution)/shard_map/ppermute | solution.py:758
  488.0 34.7 %copy-start.55 = (f32[1,1152]{1,0:T(1,128)S(1)}, f32[1,1152]{1,0:T(1,128)}, u32[]{:S(2)}) copy-start(f32[1,1152]{1,0:T(1,128)} %copy-done.54) | copy-start | bytes 13828
  488.0 34.7 %copy-start.57 = (f32[1,1152]{1,0:T(1,128)S(1)}, f32[1,1152]{1,0:T(1,128)}, u32[]{:S(2)}) copy-start(f32[1,1152]{1,0:T(1,128)} %copy-done.56) | copy-start | bytes 13828
  488.1 34.7 %copy-start.59 = (f32[1,1152]{1,0:T(1,128)S(1)}, f32[1,1152]{1,0:T(1,128)}, u32[]{:S(2)}) copy-start(f32[1,1152]{1,0:T(1,128)} %copy-done.58) | copy-start | bytes 13828
  488.1 34.7 %copy-start.61 = (f32[1,1152]{1,0:T(1,128)S(1)}, f32[1,1152]{1,0:T(1,128)}, u32[]{:S(2)}) copy-start(f32[1,1152]{1,0:T(1,128)} %copy-done.60) | copy-start | bytes 13828
  489.1 44.0 %collective-permute-start.23 = (bf16[272,1152]{1,0:T(8,128)(2,1)}, bf16[272,1152]{1,0:T(8,128)(2,1)}, u32[]{:S(2)}, u32[]{:S(2)}) collective-permute-start(bf16[272,1152]{1,0:T(8,128)(2,1)} %reduce-scatter.6.cloned.1.call-done.refs_0_), channel_id=1, source_target_pairs={{0,16},{8,24},{16,0},{24,8},{1,17},{9,25},{17,1},{25,9},{2,18},{10... | collective-permute-start | bytes 1880072 | tf_op jit(solution)/shard_map/ppermute | solution.py:758
  490.3 45.7 %collective-permute-start.32 = (bf16[144,2368]{1,0:T(8,128)(2,1)S(1)}, bf16[144,2368]{1,0:T(8,128)(2,1)S(1)}, u32[]{:S(2)}, u32[]{:S(2)}) collective-permute-start(bf16[144,2368]{1,0:T(8,128)(2,1)S(1)} %pad_maximum_fusion.2.own_ref), channel_id=1, source_target_pairs={{0,8},{8,0},{16,24},{24,16},{1,9},{9,1},{17,25},{25,17},{2,10},{10... | collective-permute-start | bytes 2045960 | tf_op jit(solution)/shard_map/ppermute | solution.py:755
  492.3 45.6 %collective-permute-start.29 = (bf16[144,1472]{1,0:T(8,128)(2,1)}, bf16[144,1472]{1,0:T(8,128)(2,1)}, u32[]{:S(2)}, u32[]{:S(2)}) collective-permute-start(bf16[144,1472]{1,0:T(8,128)(2,1)} %get-tuple-element.297), channel_id=1, source_target_pairs={{0,2},{1,3},{2,0},{3,1},{4,6},{5,7},{6,4},{7,5},{8,10},{9,11},{10,... | collective-permute-start | bytes 1271816 | tf_op jit(solution)/shard_map/ppermute | solution.py:761
  492.7 45.2 %collective-permute-start.30 = (bf16[144,1472]{1,0:T(8,128)(2,1)}, bf16[144,1472]{1,0:T(8,128)(2,1)}, u32[]{:S(2)}, u32[]{:S(2)}) collective-permute-start(bf16[144,1472]{1,0:T(8,128)(2,1)} %get-tuple-element.298), channel_id=1, source_target_pairs={{0,4},{1,5},{2,6},{3,7},{4,0},{5,1},{6,2},{7,3},{8,12},{9,13},{10,... | collective-permute-start | bytes 1271816 | tf_op jit(solution)/shard_map/ppermute | solution.py:761
  520.9 17.0 %collective-permute-start.31 = (bf16[144,1472]{1,0:T(8,128)(2,1)}, bf16[144,1472]{1,0:T(8,128)(2,1)}, u32[]{:S(2)}, u32[]{:S(2)}) collective-permute-start(bf16[144,1472]{1,0:T(8,128)(2,1)} %get-tuple-element.299), channel_id=1, source_target_pairs={{0,6},{1,7},{2,4},{3,5},{4,2},{5,3},{6,0},{7,1},{8,14},{9,15},{10,... | collective-permute-start | bytes 1271816 | tf_op jit(solution)/shard_map/ppermute | solution.py:761
  533.1 24.0 %collective-permute-start.34 = (bf16[144,2176]{1,0:T(8,128)(2,1)S(1)}, bf16[144,2176]{1,0:T(8,128)(2,1)}, u32[]{:S(2)}, u32[]{:S(2)}) collective-permute-start(bf16[144,2176]{1,0:T(8,128)(2,1)S(1)} %add_all.14.own_ref), channel_id=1, source_target_pairs={{0,8},{8,0},{16,24},{24,16},{1,9},{9,1},{17,25},{25,17},{2,10},{10... | collective-permute-start | bytes 1880072 | tf_op jit(solution)/shard_map/ppermute | solution.py:755
  539.5 23.7 %collective-permute-start.33 = (bf16[144,1472]{1,0:T(8,128)(2,1)S(1)}, bf16[144,1472]{1,0:T(8,128)(2,1)}, u32[]{:S(2)}, u32[]{:S(2)}) collective-permute-start(bf16[144,1472]{1,0:T(8,128)(2,1)S(1)} %add_all.16), channel_id=1, source_target_pairs={{0,16},{8,24},{16,0},{24,8},{1,17},{9,25},{17,1},{25,9},{2,18},{10... | collective-permute-start | bytes 1271816 | tf_op jit(solution)/shard_map/ppermute | solution.py:758
  551.1 13.1 %collective-permute-start.35 = (f32[1,3456]{1,0:T(1,128)S(1)}, f32[1,3456]{1,0:T(1,128)S(1)}, u32[]{:S(2)}, u32[]{:S(2)}) collective-permute-start(f32[1,3456]{1,0:T(1,128)S(1)} %broadcast_in_dim.12), channel_id=1, source_target_pairs={{0,16},{8,24},{16,0},{24,8},{1,17},{9,25},{17,1},{25,9},{2,18},{10... | collective-permute-start | bytes 41480 | tf_op jit(solution)/shard_map/ppermute | solution.py:758
  551.2 33.9 %collective-permute-start.9 = (bf16[128,1152]{1,0:T(8,128)(2,1)}, bf16[128,1152]{1,0:T(8,128)(2,1)S(1)}, u32[]{:S(2)}, u32[]{:S(2)}) collective-permute-start(bf16[128,1152]{1,0:T(8,128)(2,1)} %get-tuple-element.247), channel_id=1, source_target_pairs={{0,8},{8,0},{16,24},{24,16},{1,9},{9,1},{17,25},{25,17},{2,10},{10... | collective-permute-start | bytes 884744 | tf_op jit(solution)/shard_map/ppermute | solution.py:755
  551.9 27.1 %collective-permute-start.28 = (bf16[272,1152]{1,0:T(8,128)(2,1)S(1)}, bf16[272,1152]{1,0:T(8,128)(2,1)S(1)}, u32[]{:S(2)}, u32[]{:S(2)}) collective-permute-start(bf16[272,1152]{1,0:T(8,128)(2,1)S(1)} %copy-done.36), channel_id=1, source_target_pairs={{0,8},{8,0},{16,24},{24,16},{1,9},{9,1},{17,25},{25,17},{2,10},{10... | collective-permute-start | bytes 1880072 | tf_op jit(solution)/shard_map/ppermute | solution.py:755
  565.3 19.8 %copy-start.40 = (f32[128,1152]{1,0:T(8,128)S(1)}, f32[128,1152]{1,0:T(8,128)}, u32[]{:S(2)}) copy-start(f32[128,1152]{1,0:T(8,128)} %copy-done.39) | copy-start | bytes 1769476
  565.3 19.8 %copy-start.118 = (f32[128,1152]{1,0:T(8,128)S(1)}, f32[128,1152]{1,0:T(8,128)}, u32[]{:S(2)}) copy-start(f32[128,1152]{1,0:T(8,128)} %copy-done.117) | copy-start | bytes 1769476
  565.3 19.7 %copy-start.126 = (f32[1152]{0:T(1024)S(1)}, f32[1152]{0:T(1024)}, u32[]{:S(2)}) copy-start(f32[1152]{0:T(1024)} %get-tuple-element.416) | copy-start | bytes 13828
  565.3 28.9 %collective-permute-start.37 = (bf16[144,2368]{1,0:T(8,128)(2,1)S(1)}, bf16[144,2368]{1,0:T(8,128)(2,1)S(1)}, u32[]{:S(2)}, u32[]{:S(2)}) collective-permute-start(bf16[144,2368]{1,0:T(8,128)(2,1)S(1)} %pad_maximum_fusion.3.own_ref), channel_id=1, source_target_pairs={{0,8},{8,0},{16,24},{24,16},{1,9},{9,1},{17,25},{25,17},{2,10},{10... | collective-permute-start | bytes 2045960 | tf_op jit(solution)/shard_map/ppermute | solution.py:755
  579.0 13.9 %collective-permute-start.36 = (f32[1,3456]{1,0:T(1,128)S(1)}, f32[1,3456]{1,0:T(1,128)S(1)}, u32[]{:S(2)}, u32[]{:S(2)}) collective-permute-start(f32[1,3456]{1,0:T(1,128)S(1)} %reshape_add_fusion.first_ref), channel_id=1, source_target_pairs={{0,8},{8,0},{16,24},{24,16},{1,9},{9,1},{17,25},{25,17},{2,10},{10... | collective-permute-start | bytes 41480 | tf_op jit(solution)/shard_map/ppermute | solution.py:755
  (125 other events, 458.9 us)
Sparse Core Ops, SparseCore 0:
  12.9 42.7 all-gather.8
  58.1 63.8 all-gather.10
  123.9 38.9 all-gather.12
  165.2 63.8 all-gather.14
  249.1 68.8 reduce-scatter.3
  322.3 52.9 reduce-scatter.7
  379.2 55.7 reduce-scatter.5

commit v4 on v3

--- a/solution.py
+++ b/solution.py
@@ -14,6 +14,11 @@
 FULL = jnp.float32
 HEAVY = pl.CostEstimate(flops=20_000_000_000, transcendentals=0, bytes_accessed=1)
 LIGHT = pl.CostEstimate(flops=1, transcendentals=0, bytes_accessed=1)
+PLAN = {"final_early": 1, "other_late": 0, "sum_up_late": 1, "add_up_early": 1, "add_mixed_early": 1}
+
+
+def cost_of(name):
+    return HEAVY if PLAN.get(name, 0) else LIGHT
 
 
 def normalize(hidden):
@@ -608,8 +613,8 @@
     refs[-1][...] = total.astype(LOW)
 
 
-def add_all(*values):
-    return local_call(add_kernel, "add_all", jax.ShapeDtypeStruct(values[0].shape, LOW), *values, cost=LIGHT)
+def add_all(*values, cost=LIGHT):
+    return local_call(add_kernel, "add_all", jax.ShapeDtypeStruct(values[0].shape, LOW), *values, cost=cost)
 
 
 def up_kernel(side_ref, own_ref, across_ref, *refs, owners, half):
@@ -660,7 +665,7 @@
         out_specs=tuple(pl.BlockSpec((1,) + s, lambda i: (layer, 0, 0)) for s in shapes),
         input_output_aliases={1 + len(values) + i: i for i in range(len(earlier))},
         compiler_params=pltpu.CompilerParams(vmem_limit_bytes=40 << 20),
-        cost_estimate=LIGHT,
+        cost_estimate=cost_of(name + str(layer)),
         name=name,
     )(scalar.reshape(1), *values, *earlier)
 
@@ -803,7 +808,7 @@
 
         order = Order()
 
-        def owner_steps(keep, send):
+        def owner_steps(keep, send, tag):
             got = owner_xor(send, 1)
             yield
             (got,) = order.enter(got)
@@ -811,29 +816,29 @@
             order.leave(*sends)
             got = [owner_xor(send, 2 * j) for j, send in enumerate(sends, 1)]
             yield
-            return add_all(mine, *order.enter(*got))
+            return add_all(mine, *order.enter(*got), cost=cost_of("sum_" + tag))
 
         def queue_steps(value):
             value = lax.psum_scatter(value, "fsdp", scatter_dimension=0, tiled=True)
             yield
             return order.enter(value)[0]
 
-        def pair_steps(value):
+        def pair_steps(value, tag):
             order.leave(value)
             got = [pair_shift(value, j) for j in range(1, pairs)]
             yield
-            own = add_all(value, *order.enter(*got))
+            own = add_all(value, *order.enter(*got), cost=cost_of("add_" + tag))
             order.leave(own)
             across = swap(own)
             yield
             return own, order.enter(across)[0]
 
-        def mixed_steps(value):
+        def mixed_steps(value, tag):
             order.leave(value)
             got = [pair_shift(value, j) for j in range(1, pairs)]
             yield
             got = order.enter(*got)
-            total = add_all(*[v[:, offset:] for v in (value, *got)])
+            total = add_all(*[v[:, offset:] for v in (value, *got)], cost=cost_of("add_" + tag))
             shares = [v[:, :offset] for v in (value, *got)]
             send = jnp.concatenate([*shares, total], axis=1)
             order.leave(send)
@@ -842,9 +847,9 @@
             (across,) = order.enter(across)
             return send, across
 
-        def written(steps, stage, write):
+        def written(steps, stage, write, tag):
             value = yield from steps
-            value = yield from stage(value)
+            value = yield from stage(value, tag)
             value = write(*value)
             order.leave(*value)
             return value
@@ -977,12 +982,15 @@
         before = None
         for layer in reversed(range(layers)):
             v = vectors[layer]
+            tag = "_late" if before else "_early"
             proj_qkv, proj_out, feed = stored[layer][0]
             normed_one, inverse_one, attn_in, qkv, lse, attended, attended_other = stored[layer][1]
             normed_two, inverse_two, mlp_mine, mlp_other, pre_act, activated = stored[layer][2]
             grad_other = swap(grad_mine)
             if before:
                 before["down"].step()
+                if PLAN.get("final_early", 0):
+                    grad_other, final_other = order.enter(grad_other, final_other)
             (grad_other,) = order.enter(grad_other)
             grad_low, grad_pre_low, mixed, leaving, g_up_bias = feed_backward(
                 grad_mine, grad_other, pre_act, feed, half
@@ -991,18 +999,18 @@
             other = swap(leaving)
             g_down = weight_grad([((activated,), order.enter(grad_low), False, 0)], owners, width)
             order.leave(g_down)
-            down_chain = Chain(written(queue_steps(g_down), pair_steps, held))
+            down_chain = Chain(written(queue_steps(g_down), pair_steps, held, "down" + tag))
             keep, send = weight_grad(
                 [((mlp_mine, mlp_other), order.enter(grad_pre_low), False, 0)],
                 owners,
                 half * owners,
                 core,
-                LIGHT,
+                cost_of("wgu" + tag),
             )
             order.leave(send)
             up_chain = Chain(
                 written(
-                    owner_steps(keep, send),
+                    owner_steps(keep, send, "up" + tag),
                     pair_steps,
                     writer(
                         "up",
@@ -1011,6 +1019,7 @@
                         side,
                         (part, owners * hidden_part),
                     ),
+                    "up" + tag,
                 )
             )
             (other,) = order.enter(other)
@@ -1032,7 +1041,10 @@
             grad_heads = exchange(sends)
             after_other = swap(after_send)
             up_chain.step()
-            grad_heads, after_other = order.enter(grad_heads, after_other)
+            if PLAN.get("other" + tag, 1):
+                grad_heads, after_other = order.enter(grad_heads, after_other)
+            else:
+                (grad_heads,) = order.enter(grad_heads)
             order.leave(grad_heads)
             if before:
                 before["down"].step()
@@ -1044,7 +1056,7 @@
             arrived = exchange(leaving)
             if before:
                 before["up"].step()
-            (grad_proj,) = order.enter(grad_proj)
+            grad_proj, after_other = order.enter(grad_proj, after_other)
             g_mixed = weight_grad(
                 [
                     ((attn_in,), (grad_proj,), False, 0),
@@ -1057,7 +1069,7 @@
             order.leave(*(g_mixed if before else (g_mixed,)))
             mixed_chain = Chain(
                 written(
-                    owner_steps(*g_mixed) if before else queue_steps(g_mixed),
+                    owner_steps(*g_mixed, "mixed" + tag) if before else queue_steps(g_mixed),
                     mixed_steps,
                     writer(
                         "mixed",
@@ -1067,11 +1079,14 @@
                         (part, 3 * width),
                         (part, width),
                     ),
+                    "mixed" + tag,
                 )
             )
             if before:
-                up_chain.step()
-                down_chain.step()
+                if PLAN.get("sum_in", 1):
+                    up_chain.step()
+                if PLAN.get("down_in", 1):
+                    down_chain.step()
                 mixed_chain.step()
             else:
                 final, leaving = feed_out(*order.enter(activated), feed, width, half)
@@ -1083,6 +1098,10 @@
             )
             order.leave(grad_hidden)
             if before:
+                if not PLAN.get("sum_in", 1):
+                    up_chain.step()
+                if not PLAN.get("down_in", 1):
+                    down_chain.step()
                 before["mixed"].step()
                 before["down"].step()
             else:
@@ -1115,10 +1134,9 @@
         )
         order.leave(small_sum)
         small_sum = lax.all_to_all(small_sum, "fsdp", split_axis=0, concat_axis=0, tiled=True)
-        before["up"].step()
-        before["down"].step()
-        last["mixed"].step()
-        before["mixed"].step()
+        steps = dict(d=before["down"], m=before["mixed"], u=before["up"], w=last["mixed"])
+        for key in PLAN.get("tail", "udwm"):
+            steps[key].step()
         small_sum = sum_rows(order.enter(small_sum)[0])
         order.leave(small_sum)
         total = small_sum

time: 614 us -> 596 us (0.971)
  waiting for transfers between devices: 235 us -> 211 us
    ppermute x19, waiting for transfers between devices: 65.3 us -> 46.3 us  [swap(): return lax.ppermute(value, 'seq', [(i, i ^ 1) for i in range(ranks)])]
    unnamed x276 -> x316, local copies, waits for them, and re-layouts: 89.5 us -> 91.1 us
  transfers between devices with their start and end apart: 52 -> 52, of which waited for: 21 -> 18; matrix products, arithmetic and copies ran while one was open for 6% -> 7% of each run, Pallas kernels for 19% -> 20%
where the time goes in v4:
time: 596 us; the launch traced here: 586 us
  waiting for transfers between devices  211 us (35%)
  Pallas kernels  128 us (21%)
  local copies, waits for them, and re-layouts  115 us (19%)
  starting transfers between devices  73.5 us (12%)
  blocking collectives  20.5 us (3%)
  between operations  16.1 us (3%)
  other arithmetic  15.5 us (3%)
  matrix products  6.66 us (1%)
    unnamed x316, local copies, waits for them, and re-layouts  91.1 us
    pallas_call x29, Pallas kernels, local_call(): pl.pallas_call(kernel, out_shape=out_shape, in_specs=[pl.BlockSpec(memory...  79.9 us
    all_to_all x7, waiting for transfers between devices, exchange(): lax.all_to_all(blocks, 'seq', split_axis=0, concat_axis=0, tiled=True)  56 us
    ppermute x19, waiting for transfers between devices, swap(): return lax.ppermute(value, 'seq', [(i, i ^ 1) for i in range(ranks)])  46.3 us
    ppermute x7, waiting for transfers between devices, pair_shift(): lax.ppermute(value, 'seq', [(i, (i + 2 * step) % ranks) for i in range(ra...  41.1 us
    all_gather x2, waiting for transfers between devices, body(): feeds.append(lax.all_gather(share, 'fsdp', axis=0))  38.2 us
    all_to_all x7, starting transfers between devices, exchange(): lax.all_to_all(blocks, 'seq', split_axis=0, concat_axis=0, tiled=True)  30.7 us
    ppermute x19, starting transfers between devices, swap(): return lax.ppermute(value, 'seq', [(i, i ^ 1) for i in range(ranks)])  18.9 us
  transfers between devices with their start and end apart: 52, of which 18 were waited for; matrix products, arithmetic and copies ran while one was open for 7% of the time, Pallas kernels for 20%

profile of v4, /device:TPU:0, one launch (start us, length us, event | category | flops | bytes accessed | tf_op | source)
XLA Modules:
  0.0 586.3 jit_solution(4771960290878848529)
XLA Ops:
  12.8 3.4 slice_bitcast_fusion
  28.3 6.6 %all-to-all-start = ((bf16[4,128,1152]{2,1,0:T(8,128)(2,1)}), bf16[4,128,1152]{2,1,0:T(8,128)(2,1)S(1)}, u32[]{:S(2)}, u32[]{:S(2)}) async-start(bf16[4,128,1152]{2,1,0:T(8,128)(2,1)} %broadcast_in_dim.10), calls=%async_computation | async-start | bytes 2359296 | tf_op jit(solution)/shard_map/all_to_all | solution.py:769
  34.9 28.6 %all-to-all-done = bf16[4,128,1152]{2,1,0:T(8,128)(2,1)S(1)} async-done(((bf16[4,128,1152]{2,1,0:T(8,128)(2,1)}), bf16[4,128,1152]{2,1,0:T(8,128)(2,1)S(1)}, u32[]{:S(2)}, u32[]{:S(2)}) %all-to-all-start) | async-done | bytes 1179680 | tf_op jit(solution)/shard_map/all_to_all | solution.py:769
  64.5 3.0 copy-done.7
  75.8 4.2 attend_forward.2
  81.7 3.9 all-to-all-start.1
  85.6 8.9 %all-to-all-done.1 = bf16[4,288,128]{2,1,0:T(8,128)(2,1)S(1)} async-done(((bf16[4,288,128]{2,1,0:T(8,128)(2,1)}), bf16[4,288,128]{2,1,0:T(8,128)(2,1)S(1)}, u32[]{:S(2)}, u32[]{:S(2)}) %all-to-all-start.1) | async-done | bytes 294944 | tf_op jit(solution)/shard_map/all_to_all | solution.py:769
  100.6 10.2 %collective-permute-done.1.refs_4_ = bf16[1152,128]{1,0:T(8,128)(2,1)S(1)} collective-permute-done((bf16[1152,128]{1,0:T(8,128)(2,1)S(1)}, bf16[1152,128]{1,0:T(8,128)(2,1)S(1)}, u32[]{:S(2)}, u32[]{:S(2)}) %collective-permute-start.1) | collective-permute-done | bytes 294944 | tf_op jit(solution)/shard_map/ppermute | solution.py:760
  110.8 11.2 %all-gather.11.cloned.1.call-done = bf16[2304,2304]{1,0:T(8,128)(2,1)} async-done(((bf16[288,2304]{1,0:T(8,128)(2,1)}), bf16[2304,2304]{1,0:T(8,128)(2,1)}) %all-gather.11.cloned.1.call-update) | async-done | bytes 10616848 | tf_op jit(solution)/shard_map/all_gather | solution.py:885
  122.0 4.0 copy-done.89
  126.0 4.4 feed_forward.2
  132.1 7.7 %collective-permute-done.2 = bf16[128,1152]{1,0:T(8,128)(2,1)S(1)} collective-permute-done((bf16[128,1152]{1,0:T(8,128)(2,1)S(1)}, bf16[128,1152]{1,0:T(8,128)(2,1)S(1)}, u32[]{:S(2)}, u32[]{:S(2)}) %collective-permute-start.2) | collective-permute-done | bytes 294944 | tf_op jit(solution)/shard_map/ppermute | solution.py:760
  142.8 4.6 all-to-all-start.2
  147.4 15.4 %all-gather.13.cloned.1.call-done = bf16[1152,2016]{1,0:T(8,128)(2,1)} async-done(((bf16[144,2016]{1,0:T(8,128)(2,1)}), bf16[1152,2016]{1,0:T(8,128)(2,1)}) %all-gather.13.cloned.1.call-update) | async-done | bytes 4644880 | tf_op jit(solution)/shard_map/all_gather | solution.py:882
  162.8 2.3 copy-done.8
  168.3 7.4 %all-to-all-done.2 = bf16[4,128,1152]{2,1,0:T(8,128)(2,1)S(1)} async-done(((bf16[4,128,1152]{2,1,0:T(8,128)(2,1)}), bf16[4,128,1152]{2,1,0:T(8,128)(2,1)S(1)}, u32[]{:S(2)}, u32[]{:S(2)}) %all-to-all-start.2) | async-done | bytes 1179680 | tf_op jit(solution)/shard_map/all_to_all | solution.py:769
  175.7 3.0 add_convert_fusion.1
  179.4 3.5 attend_forward.3
  183.6 11.9 %all_to_all.52 = bf16[4,288,128]{2,1,0:T(8,128)(2,1)S(1)} all-to-all(bf16[4,288,128]{2,1,0:T(8,128)(2,1)S(1)} %get-tuple-element.217), channel_id=1, replica_groups=mesh['seq'=4,'fsdp'=8] {'seq'}, dimensions={0} | all-to-all | bytes 589824 | tf_op jit(solution)/shard_map/all_to_all | solution.py:769
  202.0 27.0 %all-gather.15.cloned.1.call-done = bf16[2304,2304]{1,0:T(8,128)(2,1)} async-done(((bf16[288,2304]{1,0:T(8,128)(2,1)}), bf16[2304,2304]{1,0:T(8,128)(2,1)}) %all-gather.15.cloned.1.call-update) | async-done | bytes 10616848 | tf_op jit(solution)/shard_map/all_gather | solution.py:885
  229.0 4.0 copy-done.91
  233.0 3.2 feed_forward.3
  236.2 6.6 %feed_backward.2 = (bf16[256,1152]{1,0:T(8,128)(2,1)S(1)}, bf16[256,2176]{1,0:T(8,128)(2,1)S(1)}, f32[128,1152]{1,0:T(8,128)S(1)}, bf16[128,1152]{1,0:T(8,128)(2,1)}, f32[1,2176]{1,0:T(1,128)S(1)}) custom-call(bf16[128,1152]{1,0:T(8,128)(2,1)S(1)} %bitcast.106, bf16[128,1152]{1,0:T(8,128)(2,1)} %collective-permute-done.5.other_ref, ...), custom_call_target="tpu_custom_call" | custom-call | flops 20000000000 | bytes 1 | tf_op jit(solution)/shard_map/feed_backward/pallas_call | solution.py:255
  246.3 2.3 copy-done.5
  251.5 7.2 %weight_grad.7 = (bf16[4,144,2176]{2,1,0:T(8,128)(2,1)S(1)}, bf16[4,144,2176]{2,1,0:T(8,128)(2,1)}) custom-call(s32[1]{0:T(128)} %bitcast.28.refs_0_, bf16[128,1152]{1,0:T(8,128)(2,1)S(1)} %get-tuple-element.434.mine_ref.refs_1_, bf16[128,1152]{1,0:T(8,128)(2,1)} %collective-permute-done.3.other_ref.refs_2_, bf16[256,2176]{1,0:T(8,128)(2,1)S(1)} %copy-done.26), custom_call_target="tpu_custom_call" | custom-call | flops 1 | bytes 1 | tf_op jit(solution)/shard_map/weight_grad/pallas_call | solution.py:255
  267.5 2.4 mid_backward.2
  275.2 3.9 all-to-all-start.4
  280.1 2.1 collective-permute-start.7
  284.2 4.0 meet_cores.3
  295.0 7.2 %attend_backward.2 = (bf16[512,864]{1,0:T(8,128)(2,1)S(1)}, bf16[4,128,1152]{2,1,0:T(8,128)(2,1)S(1)}, f32[1,288]{1,0:T(1,128)S(1)}, f32[1,288]{1,0:T(1,128)S(1)}) custom-call(bf16[3,512,288]{2,1,0:T(8,128)(2,1)S(1)} %pad_maximum_fusion.1.qkv_ref, bf16[4,288,128]{2,1,0:T(8,128)(2,1)S(1)} %all-to-all-done.4.got_ref, f32[512,4]{1,0:T(8,128)S(1)} %copy-done.109, ...), custom_call_target="tpu_custom_call" | custom-call | flops 20000000000 | bytes 1 | tf_op jit(solution)/shard_map/attend_backward/pallas_call | solution.py:163
  304.1 3.8 all-to-all-start.5
  309.5 4.7 weight_grad.8
  314.3 4.1 copy-done.92
  324.4 11.1 %all-to-all-done.5.got_ref = bf16[4,128,1152]{2,1,0:T(8,128)(2,1)S(1)} async-done(((bf16[4,128,1152]{2,1,0:T(8,128)(2,1)}), bf16[4,128,1152]{2,1,0:T(8,128)(2,1)S(1)}, u32[]{:S(2)}, u32[]{:S(2)}) %all-to-all-start.5) | async-done | bytes 1179680 | tf_op jit(solution)/shard_map/all_to_all | solution.py:769
  340.4 2.7 add_all.9.refs_0_
  346.1 2.6 collective-permute-done.9.other_ref
  348.7 4.6 copy-done.90
  354.9 6.5 %feed_backward.3 = (bf16[256,1152]{1,0:T(8,128)(2,1)S(1)}, bf16[256,2176]{1,0:T(8,128)(2,1)S(1)}, f32[128,1152]{1,0:T(8,128)S(1)}, bf16[128,1152]{1,0:T(8,128)(2,1)}, f32[1,2176]{1,0:T(1,128)S(1)}) custom-call(bf16[128,1152]{1,0:T(8,128)(2,1)} %get-tuple-element.254.mine_ref, bf16[128,1152]{1,0:T(8,128)(2,1)S(1)} %collective-permute-done.9.other_ref, ...), custom_call_target="tpu_custom_call" | custom-call | flops 20000000000 | bytes 1 | tf_op jit(solution)/shard_map/feed_backward/pallas_call | solution.py:255
  365.2 2.2 copy-done.6
  369.7 6.2 %weight_grad.10 = (bf16[4,144,2176]{2,1,0:T(8,128)(2,1)S(1)}, bf16[4,144,2176]{2,1,0:T(8,128)(2,1)}) custom-call(s32[1]{0:T(128)} %bitcast.28.refs_0_, bf16[128,1152]{1,0:T(8,128)(2,1)S(1)} %copy-done.24, bf16[128,1152]{1,0:T(8,128)(2,1)S(1)} %copy-done.46, bf16[256,2176]{1,0:T(8,128)(2,1)S(1)} %copy-done.28), custom_call_target="tpu_custom_call" | custom-call | flops 1 | bytes 1 | tf_op jit(solution)/shard_map/weight_grad/pallas_call | solution.py:255
  376.0 2.6 collective-permute-done.15.got_ref
  378.6 9.1 %collective-permute-done.16.refs_1_ = bf16[144,2176]{1,0:T(8,128)(2,1)} collective-permute-done((bf16[144,2176]{1,0:T(8,128)(2,1)}, bf16[144,2176]{1,0:T(8,128)(2,1)}, u32[]{:S(2)}, u32[]{:S(2)}) %collective-permute-start.16) | collective-permute-done | bytes 626720 | tf_op jit(solution)/shard_map/ppermute | solution.py:763
  389.2 3.4 mid_backward.3
  396.4 3.5 all-to-all-start.6
  403.9 3.9 meet_cores.4
  411.6 2.2 add_all.11.refs_2_
  417.0 2.9 collective-permute-start.27
  424.4 8.2 %attend_backward.3 = (bf16[512,864]{1,0:T(8,128)(2,1)S(1)}, bf16[4,128,1152]{2,1,0:T(8,128)(2,1)}, f32[1,288]{1,0:T(1,128)S(1)}, f32[1,288]{1,0:T(1,128)S(1)}) custom-call(bf16[3,512,288]{2,1,0:T(8,128)(2,1)S(1)} %copy-done.10, bf16[4,288,128]{2,1,0:T(8,128)(2,1)S(1)} %all-to-all-done.6.got_ref, f32[512,4]{1,0:T(8,128)S(1)} %copy-done.107, ...), custom_call_target="tpu_custom_call" | custom-call | flops 20000000000 | bytes 1 | tf_op jit(solution)/shard_map/attend_backward/pallas_call | solution.py:163
  434.7 4.6 all-to-all-start.7
  440.2 3.1 write_up.2.refs_0_
  444.5 7.0 %weight_grad.11 = (bf16[4,144,1472]{2,1,0:T(8,128)(2,1)S(1)}, bf16[4,144,1472]{2,1,0:T(8,128)(2,1)}) custom-call(s32[1]{0:T(128)} %bitcast.28.refs_0_, bf16[512,1152]{1,0:T(8,128)(2,1)S(1)} %copy-done.21, bf16[512,864]{1,0:T(8,128)(2,1)S(1)} %copy-done.120, bf16[1152,128]{1,0:T(8,128)(2,1)S(1)} %bitcast.98, bf16[1152,128]{1,0:T(8,128)(2,1)S(1)} %copy-done.105, ...), custom_call_target="tpu_custom_call" | custom-call | flops 20000000000 | bytes 1 | tf_op jit(solution)/shard_map/weight_grad/pallas_call | solution.py:255
  451.6 14.0 %collective-permute-done.18.refs_2_ = bf16[144,2176]{1,0:T(8,128)(2,1)S(1)} collective-permute-done((bf16[144,2176]{1,0:T(8,128)(2,1)}, bf16[144,2176]{1,0:T(8,128)(2,1)S(1)}, u32[]{:S(2)}, u32[]{:S(2)}) %collective-permute-start.18) | collective-permute-done | bytes 626720 | tf_op jit(solution)/shard_map/ppermute | solution.py:766
  465.6 2.2 add_all.12.refs_0_
  467.8 2.4 collective-permute-start.24
  476.8 2.7 end_backward.3
  485.4 24.0 %collective-permute-done.24.refs_1_ = bf16[144,2176]{1,0:T(8,128)(2,1)} collective-permute-done((bf16[144,2176]{1,0:T(8,128)(2,1)}, bf16[144,2176]{1,0:T(8,128)(2,1)}, u32[]{:S(2)}, u32[]{:S(2)}) %collective-permute-start.24) | collective-permute-done | bytes 626720 | tf_op jit(solution)/shard_map/ppermute | solution.py:763
  513.9 8.1 %collective-permute-done.23.refs_1_ = bf16[272,1152]{1,0:T(8,128)(2,1)} collective-permute-done((bf16[272,1152]{1,0:T(8,128)(2,1)}, bf16[272,1152]{1,0:T(8,128)(2,1)}, u32[]{:S(2)}, u32[]{:S(2)}) %collective-permute-start.23) | collective-permute-done | bytes 626720 | tf_op jit(solution)/shard_map/ppermute | solution.py:763
  527.0 3.5 collective-permute-start.33
  530.6 8.7 %all_to_all.53 = f32[8,1,3456]{2,1,0:T(1,128)S(1)} all-to-all(f32[8,1,3456]{2,1,0:T(1,128)S(1)} %copy.53), channel_id=1, replica_groups=mesh['seq'=4,'fsdp'=8] {'fsdp'}, dimensions={0} | all-to-all | bytes 221184 | tf_op jit(solution)/shard_map/all_to_all | solution.py:1136
  540.6 7.0 %collective-permute-done.34.across_ref = bf16[144,2176]{1,0:T(8,128)(2,1)} collective-permute-done((bf16[144,2176]{1,0:T(8,128)(2,1)S(1)}, bf16[144,2176]{1,0:T(8,128)(2,1)}, u32[]{:S(2)}, u32[]{:S(2)}) %collective-permute-start.34) | collective-permute-done | bytes 626720 | tf_op jit(solution)/shard_map/ppermute | solution.py:760
  547.6 3.3 write_up.3
  552.9 9.3 %collective-permute-done.28.refs_1_ = bf16[272,1152]{1,0:T(8,128)(2,1)S(1)} collective-permute-done((bf16[272,1152]{1,0:T(8,128)(2,1)S(1)}, bf16[272,1152]{1,0:T(8,128)(2,1)S(1)}, u32[]{:S(2)}, u32[]{:S(2)}) %collective-permute-start.28) | collective-permute-done | bytes 626720 | tf_op jit(solution)/shard_map/ppermute | solution.py:760
  562.5 4.6 write_down.1
  569.0 6.8 %collective-permute-done.36.second_ref = f32[1,3456]{1,0:T(1,128)S(1)} collective-permute-done((f32[1,3456]{1,0:T(1,128)S(1)}, f32[1,3456]{1,0:T(1,128)S(1)}, u32[]{:S(2)}, u32[]{:S(2)}) %collective-permute-start.36) | collective-permute-done | bytes 13856 | tf_op jit(solution)/shard_map/ppermute | solution.py:760
  (492 shorter events, 160.5 us)
Async XLA Ops:
  7.2 57.0 %all-gather.9.cloned.1.call-start = ((), (), s32[]{:S(2)}) async-start(), calls=%async_computation.15 | async-start | bytes 5603328 | tf_op jit(solution)/shard_map/all_gather | solution.py:882
  12.8 109.2 %all-gather.11.cloned.1.call-start = ((), (), s32[]{:S(2)}) async-start(), calls=%async_computation.16 | async-start | bytes 11943936 | tf_op jit(solution)/shard_map/all_gather | solution.py:885
  20.6 142.2 %all-gather.13.cloned.1.call-start = ((), (), s32[]{:S(2)}) async-start(), calls=%async_computation.17 | async-start | bytes 5308416 | tf_op jit(solution)/shard_map/all_gather | solution.py:882
  22.7 206.3 %all-gather.15.cloned.1.call-start = ((), (), s32[]{:S(2)}) async-start(), calls=%async_computation.18 | async-start | bytes 11943936 | tf_op jit(solution)/shard_map/all_gather | solution.py:885
  28.3 35.2 %all-to-all-start = ((bf16[4,128,1152]{2,1,0:T(8,128)(2,1)}), bf16[4,128,1152]{2,1,0:T(8,128)(2,1)S(1)}, u32[]{:S(2)}, u32[]{:S(2)}) async-start(bf16[4,128,1152]{2,1,0:T(8,128)(2,1)} %broadcast_in_dim.10), calls=%async_computation | async-start | bytes 2359296 | tf_op jit(solution)/shard_map/all_to_all | solution.py:769
  81.7 12.8 %all-to-all-start.1 = ((bf16[4,288,128]{2,1,0:T(8,128)(2,1)}), bf16[4,288,128]{2,1,0:T(8,128)(2,1)S(1)}, u32[]{:S(2)}, u32[]{:S(2)}) async-start(bf16[4,288,128]{2,1,0:T(8,128)(2,1)} %get-tuple-element.204), calls=%async_computation.1 | async-start | bytes 589824 | tf_op jit(solution)/shard_map/all_to_all | solution.py:769
  97.7 32.8 %copy-start.23 = (bf16[128,1152]{1,0:T(8,128)(2,1)}, bf16[128,1152]{1,0:T(8,128)(2,1)S(1)}, u32[]{:S(2)}) copy-start(bf16[128,1152]{1,0:T(8,128)(2,1)S(1)} %get-tuple-element.440.mine_ref.refs_1_) | copy-start | bytes 884740
  97.7 13.1 %collective-permute-start = (bf16[128,1152]{1,0:T(8,128)(2,1)S(1)}, bf16[128,1152]{1,0:T(8,128)(2,1)S(1)}, u32[]{:S(2)}, u32[]{:S(2)}) collective-permute-start(bf16[128,1152]{1,0:T(8,128)(2,1)S(1)} %get-tuple-element.440.mine_ref.refs_1_), channel_id=1, source_target_pairs={{0,8},{8,0},{16,24},{24,16},{1,9},{9,1},{17,25},{25,17},{2,10},{10... | collective-permute-start | bytes 884744 | tf_op jit(solution)/shard_map/ppermute | solution.py:760
  97.7 13.1 %collective-permute-start.1 = (bf16[1152,128]{1,0:T(8,128)(2,1)S(1)}, bf16[1152,128]{1,0:T(8,128)(2,1)S(1)}, u32[]{:S(2)}, u32[]{:S(2)}) collective-permute-start(bf16[1152,128]{1,0:T(8,128)(2,1)S(1)} %bitcast.97), channel_id=1, source_target_pairs={{0,8},{8,0},{16,24},{24,16},{1,9},{9,1},{17,25},{25,17},{2,10},{10... | collective-permute-start | bytes 884744 | tf_op jit(solution)/shard_map/ppermute | solution.py:760
  130.5 9.2 %collective-permute-start.2 = (bf16[128,1152]{1,0:T(8,128)(2,1)S(1)}, bf16[128,1152]{1,0:T(8,128)(2,1)S(1)}, u32[]{:S(2)}, u32[]{:S(2)}) collective-permute-start(bf16[128,1152]{1,0:T(8,128)(2,1)S(1)} %get-tuple-element.211), channel_id=1, source_target_pairs={{0,8},{8,0},{16,24},{24,16},{1,9},{9,1},{17,25},{25,17},{2,10},{10... | collective-permute-start | bytes 884744 | tf_op jit(solution)/shard_map/ppermute | solution.py:760
  142.8 32.9 %all-to-all-start.2 = ((bf16[4,128,1152]{2,1,0:T(8,128)(2,1)}), bf16[4,128,1152]{2,1,0:T(8,128)(2,1)S(1)}, u32[]{:S(2)}, u32[]{:S(2)}) async-start(bf16[4,128,1152]{2,1,0:T(8,128)(2,1)} %broadcast_in_dim.11), calls=%async_computation.2 | async-start | bytes 2359296 | tf_op jit(solution)/shard_map/all_to_all | solution.py:769
  147.4 197.8 %reduce-scatter.4.cloned.1.call-start = ((), (), s32[]{:S(2)}) async-start(), calls=%async_computation.12 | async-start | bytes 5640192 | tf_op jit(solution)/shard_map/reduce_scatter | solution.py:822
  197.9 31.1 %collective-permute-start.4 = (bf16[1152,128]{1,0:T(8,128)(2,1)S(1)}, bf16[1152,128]{1,0:T(8,128)(2,1)}, u32[]{:S(2)}, u32[]{:S(2)}) collective-permute-start(bf16[1152,128]{1,0:T(8,128)(2,1)S(1)} %bitcast.100), channel_id=1, source_target_pairs={{0,8},{8,0},{16,24},{24,16},{1,9},{9,1},{17,25},{25,17},{2,10},{10... | collective-permute-start | bytes 884744 | tf_op jit(solution)/shard_map/ppermute | solution.py:760
  198.4 30.6 %collective-permute-start.3 = (bf16[128,1152]{1,0:T(8,128)(2,1)S(1)}, bf16[128,1152]{1,0:T(8,128)(2,1)}, u32[]{:S(2)}, u32[]{:S(2)}) collective-permute-start(bf16[128,1152]{1,0:T(8,128)(2,1)S(1)} %get-tuple-element.434.mine_ref.refs_1_), channel_id=1, source_target_pairs={{0,8},{8,0},{16,24},{24,16},{1,9},{9,1},{17,25},{25,17},{2,10},{10... | collective-permute-start | bytes 884744 | tf_op jit(solution)/shard_map/ppermute | solution.py:760
  200.0 36.3 %collective-permute-start.5 = (bf16[128,1152]{1,0:T(8,128)(2,1)S(1)}, bf16[128,1152]{1,0:T(8,128)(2,1)}, u32[]{:S(2)}, u32[]{:S(2)}) collective-permute-start(bf16[128,1152]{1,0:T(8,128)(2,1)S(1)} %bitcast.105), channel_id=1, source_target_pairs={{0,8},{8,0},{16,24},{24,16},{1,9},{9,1},{17,25},{25,17},{2,10},{10... | collective-permute-start | bytes 884744 | tf_op jit(solution)/shard_map/ppermute | solution.py:760
  248.7 13.4 %collective-permute-start.6 = (bf16[128,1152]{1,0:T(8,128)(2,1)}, bf16[128,1152]{1,0:T(8,128)(2,1)}, u32[]{:S(2)}, u32[]{:S(2)}) collective-permute-start(bf16[128,1152]{1,0:T(8,128)(2,1)} %get-tuple-element.226), channel_id=1, source_target_pairs={{0,8},{8,0},{16,24},{24,16},{1,9},{9,1},{17,25},{25,17},{2,10},{10... | collective-permute-start | bytes 884744 | tf_op jit(solution)/shard_map/ppermute | solution.py:760
  260.2 22.2 %collective-permute-start.8 = (bf16[4,144,2176]{2,1,0:T(8,128)(2,1)}, bf16[4,144,2176]{2,1,0:T(8,128)(2,1)}, u32[]{:S(2)}, u32[]{:S(2)}) collective-permute-start(bf16[4,144,2176]{2,1,0:T(8,128)(2,1)} %get-tuple-element.231), channel_id=1, source_target_pairs={{0,1},{1,0},{2,3},{3,2},{4,5},{5,4},{6,7},{7,6},{8,9},{9,8},{10,11... | collective-permute-start | bytes 7520264 | tf_op jit(solution)/shard_map/ppermute | solution.py:766
  275.2 17.3 %all-to-all-start.4 = ((bf16[4,288,128]{2,1,0:T(8,128)(2,1)}), bf16[4,288,128]{2,1,0:T(8,128)(2,1)S(1)}, u32[]{:S(2)}, u32[]{:S(2)}) async-start(bf16[4,288,128]{2,1,0:T(8,128)(2,1)} %copy-done.44), calls=%async_computation.4 | async-start | bytes 589824 | tf_op jit(solution)/shard_map/all_to_all | solution.py:769
  280.1 12.3 %collective-permute-start.7 = (bf16[128,576]{1,0:T(8,128)(2,1)}, bf16[128,576]{1,0:T(8,128)(2,1)S(1)}, u32[]{:S(2)}, u32[]{:S(2)}) collective-permute-start(bf16[128,576]{1,0:T(8,128)(2,1)} %copy-done.110), channel_id=1, source_target_pairs={{0,8},{8,0},{16,24},{24,16},{1,9},{9,1},{17,25},{25,17},{2,10},{10... | collective-permute-start | bytes 442376 | tf_op jit(solution)/shard_map/ppermute | solution.py:760
  282.2 57.1 %copy-start.152 = (f32[128]{0:T(128)}, f32[128]{0:T(128)S(1)}, u32[]{:S(2)}) copy-start(f32[128]{0:T(128)S(1)} %broadcast_multiply_fusion.1) | copy-start | bytes 1540
  289.0 51.4 %collective-permute-start.11 = (bf16[144,2176]{1,0:T(8,128)(2,1)}, bf16[144,2176]{1,0:T(8,128)(2,1)}, u32[]{:S(2)}, u32[]{:S(2)}) collective-permute-start(bf16[144,2176]{1,0:T(8,128)(2,1)} %get-tuple-element.237), channel_id=1, source_target_pairs={{0,2},{1,3},{2,0},{3,1},{4,6},{5,7},{6,4},{7,5},{8,10},{9,11},{10,... | collective-permute-start | bytes 1880072 | tf_op jit(solution)/shard_map/ppermute | solution.py:766
  290.3 50.1 %collective-permute-start.12 = (bf16[144,2176]{1,0:T(8,128)(2,1)}, bf16[144,2176]{1,0:T(8,128)(2,1)}, u32[]{:S(2)}, u32[]{:S(2)}) collective-permute-start(bf16[144,2176]{1,0:T(8,128)(2,1)} %get-tuple-element.238), channel_id=1, source_target_pairs={{0,4},{1,5},{2,6},{3,7},{4,0},{5,1},{6,2},{7,3},{8,12},{9,13},{10,... | collective-permute-start | bytes 1880072 | tf_op jit(solution)/shard_map/ppermute | solution.py:766
  291.0 49.4 %collective-permute-start.13 = (bf16[144,2176]{1,0:T(8,128)(2,1)}, bf16[144,2176]{1,0:T(8,128)(2,1)}, u32[]{:S(2)}, u32[]{:S(2)}) collective-permute-start(bf16[144,2176]{1,0:T(8,128)(2,1)} %get-tuple-element.239), channel_id=1, source_target_pairs={{0,6},{1,7},{2,4},{3,5},{4,2},{5,3},{6,0},{7,1},{8,14},{9,15},{10,... | collective-permute-start | bytes 1880072 | tf_op jit(solution)/shard_map/ppermute | solution.py:766
  304.1 31.4 %all-to-all-start.5 = ((bf16[4,128,1152]{2,1,0:T(8,128)(2,1)}), bf16[4,128,1152]{2,1,0:T(8,128)(2,1)S(1)}, u32[]{:S(2)}, u32[]{:S(2)}) async-start(bf16[4,128,1152]{2,1,0:T(8,128)(2,1)} %copy-done.22), calls=%async_computation.5 | async-start | bytes 2359296 | tf_op jit(solution)/shard_map/all_to_all | solution.py:769
  307.9 105.8 %reduce-scatter.8.cloned.1.call-start = ((), (), s32[]{:S(2)}) async-start(), calls=%async_computation.14 | async-start | bytes 3981312 | tf_op jit(solution)/shard_map/reduce_scatter | solution.py:822
  314.3 156.0 %reduce-scatter.6.cloned.1.call-start = ((), (), s32[]{:S(2)}) async-start(), calls=%async_computation.13 | async-start | bytes 5640192 | tf_op jit(solution)/shard_map/reduce_scatter | solution.py:822
  322.3 23.8 %collective-permute-start.10 = (bf16[128,1152]{1,0:T(8,128)(2,1)S(1)}, bf16[128,1152]{1,0:T(8,128)(2,1)}, u32[]{:S(2)}, u32[]{:S(2)}) collective-permute-start(bf16[128,1152]{1,0:T(8,128)(2,1)S(1)} %get-tuple-element.251), channel_id=1, source_target_pairs={{0,8},{8,0},{16,24},{24,16},{1,9},{9,1},{17,25},{25,17},{2,10},{10... | collective-permute-start | bytes 884744 | tf_op jit(solution)/shard_map/ppermute | solution.py:760
  339.3 9.4 %collective-permute-start.9 = (bf16[128,1152]{1,0:T(8,128)(2,1)}, bf16[128,1152]{1,0:T(8,128)(2,1)S(1)}, u32[]{:S(2)}, u32[]{:S(2)}) collective-permute-start(bf16[128,1152]{1,0:T(8,128)(2,1)} %get-tuple-element.254.mine_ref), channel_id=1, source_target_pairs={{0,8},{8,0},{16,24},{24,16},{1,9},{9,1},{17,25},{25,17},{2,10},{10... | collective-permute-start | bytes 884744 | tf_op jit(solution)/shard_map/ppermute | solution.py:760
  343.2 44.5 %collective-permute-start.16 = (bf16[144,2176]{1,0:T(8,128)(2,1)}, bf16[144,2176]{1,0:T(8,128)(2,1)}, u32[]{:S(2)}, u32[]{:S(2)}) collective-permute-start(bf16[144,2176]{1,0:T(8,128)(2,1)} %add_all.9.refs_0_), channel_id=1, source_target_pairs={{0,16},{8,24},{16,0},{24,8},{1,17},{9,25},{17,1},{25,9},{2,18},{10... | collective-permute-start | bytes 1880072 | tf_op jit(solution)/shard_map/ppermute | solution.py:763
  345.2 65.2 %collective-permute-start.20 = (bf16[272,1152]{1,0:T(8,128)(2,1)}, bf16[272,1152]{1,0:T(8,128)(2,1)}, u32[]{:S(2)}, u32[]{:S(2)}) collective-permute-start(bf16[272,1152]{1,0:T(8,128)(2,1)} %reduce-scatter.4.cloned.1.call-done.refs_0_), channel_id=1, source_target_pairs={{0,16},{8,24},{16,0},{24,8},{1,17},{9,25},{17,1},{25,9},{2,18},{10... | collective-permute-start | bytes 1880072 | tf_op jit(solution)/shard_map/ppermute | solution.py:763
  363.3 15.3 %collective-permute-start.15 = (bf16[128,1152]{1,0:T(8,128)(2,1)}, bf16[128,1152]{1,0:T(8,128)(2,1)}, u32[]{:S(2)}, u32[]{:S(2)}) collective-permute-start(bf16[128,1152]{1,0:T(8,128)(2,1)} %get-tuple-element.267), channel_id=1, source_target_pairs={{0,8},{8,0},{16,24},{24,16},{1,9},{9,1},{17,25},{25,17},{2,10},{10... | collective-permute-start | bytes 884744 | tf_op jit(solution)/shard_map/ppermute | solution.py:760
  375.9 28.0 %collective-permute-start.14 = (bf16[4,144,2176]{2,1,0:T(8,128)(2,1)}, bf16[4,144,2176]{2,1,0:T(8,128)(2,1)}, u32[]{:S(2)}, u32[]{:S(2)}) collective-permute-start(bf16[4,144,2176]{2,1,0:T(8,128)(2,1)} %get-tuple-element.272), channel_id=1, source_target_pairs={{0,1},{1,0},{2,3},{3,2},{4,5},{5,4},{6,7},{7,6},{8,9},{9,8},{10,11... | collective-permute-start | bytes 7520264 | tf_op jit(solution)/shard_map/ppermute | solution.py:766
  396.4 13.9 %all-to-all-start.6 = ((bf16[4,288,128]{2,1,0:T(8,128)(2,1)}), bf16[4,288,128]{2,1,0:T(8,128)(2,1)S(1)}, u32[]{:S(2)}, u32[]{:S(2)}) async-start(bf16[4,288,128]{2,1,0:T(8,128)(2,1)} %get-tuple-element.277), calls=%async_computation.8 | async-start | bytes 589824 | tf_op jit(solution)/shard_map/all_to_all | solution.py:769
  401.9 37.5 %collective-permute-start.22 = (bf16[144,2176]{1,0:T(8,128)(2,1)}, bf16[144,2176]{1,0:T(8,128)(2,1)}, u32[]{:S(2)}, u32[]{:S(2)}) collective-permute-start(bf16[144,2176]{1,0:T(8,128)(2,1)} %copy-done.33), channel_id=1, source_target_pairs={{0,8},{8,0},{16,24},{24,16},{1,9},{9,1},{17,25},{25,17},{2,10},{10... | collective-permute-start | bytes 1880072 | tf_op jit(solution)/shard_map/ppermute | solution.py:760
  403.9 39.5 %collective-permute-start.21 = (bf16[128,576]{1,0:T(8,128)(2,1)}, bf16[128,576]{1,0:T(8,128)(2,1)}, u32[]{:S(2)}, u32[]{:S(2)}) collective-permute-start(bf16[128,576]{1,0:T(8,128)(2,1)} %get-tuple-element.289), channel_id=1, source_target_pairs={{0,8},{8,0},{16,24},{24,16},{1,9},{9,1},{17,25},{25,17},{2,10},{10... | collective-permute-start | bytes 442376 | tf_op jit(solution)/shard_map/ppermute | solution.py:760
  417.0 62.5 %collective-permute-start.27 = (bf16[144,1472]{1,0:T(8,128)(2,1)}, bf16[144,1472]{1,0:T(8,128)(2,1)}, u32[]{:S(2)}, u32[]{:S(2)}) collective-permute-start(bf16[144,1472]{1,0:T(8,128)(2,1)} %reduce-scatter.8.cloned.1.call-done), channel_id=1, source_target_pairs={{0,16},{8,24},{16,0},{24,8},{1,17},{9,25},{17,1},{25,9},{2,18},{10... | collective-permute-start | bytes 1271816 | tf_op jit(solution)/shard_map/ppermute | solution.py:763
  419.9 65.0 %collective-permute-start.26 = (bf16[272,1152]{1,0:T(8,128)(2,1)}, bf16[272,1152]{1,0:T(8,128)(2,1)}, u32[]{:S(2)}, u32[]{:S(2)}) collective-permute-start(bf16[272,1152]{1,0:T(8,128)(2,1)} %add_all.11.refs_2_), channel_id=1, source_target_pairs={{0,8},{8,0},{16,24},{24,16},{1,9},{9,1},{17,25},{25,17},{2,10},{10... | collective-permute-start | bytes 1880072 | tf_op jit(solution)/shard_map/ppermute | solution.py:760
  421.4 30.2 %collective-permute-start.17 = (bf16[144,2176]{1,0:T(8,128)(2,1)S(1)}, bf16[144,2176]{1,0:T(8,128)(2,1)}, u32[]{:S(2)}, u32[]{:S(2)}) collective-permute-start(bf16[144,2176]{1,0:T(8,128)(2,1)S(1)} %copy-done.103), channel_id=1, source_target_pairs={{0,2},{1,3},{2,0},{3,1},{4,6},{5,7},{6,4},{7,5},{8,10},{9,11},{10,... | collective-permute-start | bytes 1880072 | tf_op jit(solution)/shard_map/ppermute | solution.py:766
  434.7 38.5 %all-to-all-start.7 = ((bf16[4,128,1152]{2,1,0:T(8,128)(2,1)}), bf16[4,128,1152]{2,1,0:T(8,128)(2,1)}, u32[]{:S(2)}, u32[]{:S(2)}) async-start(bf16[4,128,1152]{2,1,0:T(8,128)(2,1)} %get-tuple-element.290), calls=%async_computation.10 | async-start | bytes 2359296 | tf_op jit(solution)/shard_map/all_to_all | solution.py:769
  439.4 26.2 %collective-permute-start.18 = (bf16[144,2176]{1,0:T(8,128)(2,1)}, bf16[144,2176]{1,0:T(8,128)(2,1)S(1)}, u32[]{:S(2)}, u32[]{:S(2)}) collective-permute-start(bf16[144,2176]{1,0:T(8,128)(2,1)} %get-tuple-element.281), channel_id=1, source_target_pairs={{0,4},{1,5},{2,6},{3,7},{4,0},{5,1},{6,2},{7,3},{8,12},{9,13},{10,... | collective-permute-start | bytes 1880072 | tf_op jit(solution)/shard_map/ppermute | solution.py:766
  443.3 22.2 %collective-permute-start.19 = (bf16[144,2176]{1,0:T(8,128)(2,1)S(1)}, bf16[144,2176]{1,0:T(8,128)(2,1)S(1)}, u32[]{:S(2)}, u32[]{:S(2)}) collective-permute-start(bf16[144,2176]{1,0:T(8,128)(2,1)S(1)} %copy-done.101), channel_id=1, source_target_pairs={{0,6},{1,7},{2,4},{3,5},{4,2},{5,3},{6,0},{7,1},{8,14},{9,15},{10,... | collective-permute-start | bytes 1880072 | tf_op jit(solution)/shard_map/ppermute | solution.py:766
  451.6 19.2 %collective-permute-start.25 = (bf16[4,144,1472]{2,1,0:T(8,128)(2,1)}, bf16[4,144,1472]{2,1,0:T(8,128)(2,1)S(1)}, u32[]{:S(2)}, u32[]{:S(2)}) collective-permute-start(bf16[4,144,1472]{2,1,0:T(8,128)(2,1)} %get-tuple-element.297), channel_id=1, source_target_pairs={{0,1},{1,0},{2,3},{3,2},{4,5},{5,4},{6,7},{7,6},{8,9},{9,8},{10,11... | collective-permute-start | bytes 5087240 | tf_op jit(solution)/shard_map/ppermute | solution.py:766
  467.8 41.6 %collective-permute-start.24 = (bf16[144,2176]{1,0:T(8,128)(2,1)}, bf16[144,2176]{1,0:T(8,128)(2,1)}, u32[]{:S(2)}, u32[]{:S(2)}) collective-permute-start(bf16[144,2176]{1,0:T(8,128)(2,1)} %add_all.12.refs_0_), channel_id=1, source_target_pairs={{0,16},{8,24},{16,0},{24,8},{1,17},{9,25},{17,1},{25,9},{2,18},{10... | collective-permute-start | bytes 1880072 | tf_op jit(solution)/shard_map/ppermute | solution.py:763
  470.2 51.8 %collective-permute-start.23 = (bf16[272,1152]{1,0:T(8,128)(2,1)}, bf16[272,1152]{1,0:T(8,128)(2,1)}, u32[]{:S(2)}, u32[]{:S(2)}) collective-permute-start(bf16[272,1152]{1,0:T(8,128)(2,1)} %reduce-scatter.6.cloned.1.call-done.refs_0_), channel_id=1, source_target_pairs={{0,16},{8,24},{16,0},{24,8},{1,17},{9,25},{17,1},{25,9},{2,18},{10... | collective-permute-start | bytes 1880072 | tf_op jit(solution)/shard_map/ppermute | solution.py:763
  480.6 31.4 %copy-start.51 = (f32[1,2176]{1,0:T(1,128)S(1)}, f32[1,2176]{1,0:T(1,128)}, u32[]{:S(2)}) copy-start(f32[1,2176]{1,0:T(1,128)} %copy-done.50) | copy-start | bytes 26116
  480.6 31.4 %copy-start.55 = (f32[1,1152]{1,0:T(1,128)S(1)}, f32[1,1152]{1,0:T(1,128)}, u32[]{:S(2)}) copy-start(f32[1,1152]{1,0:T(1,128)} %copy-done.54) | copy-start | bytes 13828
  480.6 31.4 %copy-start.57 = (f32[1,1152]{1,0:T(1,128)S(1)}, f32[1,1152]{1,0:T(1,128)}, u32[]{:S(2)}) copy-start(f32[1,1152]{1,0:T(1,128)} %copy-done.56) | copy-start | bytes 13828
  480.6 31.4 %copy-start.59 = (f32[1,1152]{1,0:T(1,128)S(1)}, f32[1,1152]{1,0:T(1,128)}, u32[]{:S(2)}) copy-start(f32[1,1152]{1,0:T(1,128)} %copy-done.58) | copy-start | bytes 13828
  480.6 31.4 %copy-start.61 = (f32[1,1152]{1,0:T(1,128)S(1)}, f32[1,1152]{1,0:T(1,128)}, u32[]{:S(2)}) copy-start(f32[1,1152]{1,0:T(1,128)} %copy-done.60) | copy-start | bytes 13828
  480.6 31.4 %copy-start.64 = (f32[1,1152]{1,0:T(1,128)S(1)}, f32[1,1152]{1,0:T(1,128)}, u32[]{:S(2)}) copy-start(f32[1,1152]{1,0:T(1,128)} %copy-done.63) | copy-start | bytes 13828
  480.6 31.4 %copy-start.66 = (f32[1,1152]{1,0:T(1,128)S(1)}, f32[1,1152]{1,0:T(1,128)}, u32[]{:S(2)}) copy-start(f32[1,1152]{1,0:T(1,128)} %copy-done.65) | copy-start | bytes 13828
  480.6 31.4 %copy-start.69 = (f32[1,1152]{1,0:T(1,128)S(1)}, f32[1,1152]{1,0:T(1,128)}, u32[]{:S(2)}) copy-start(f32[1,1152]{1,0:T(1,128)} %copy-done.68) | copy-start | bytes 13828
  480.7 31.4 %copy-start.71 = (f32[1,1152]{1,0:T(1,128)S(1)}, f32[1,1152]{1,0:T(1,128)}, u32[]{:S(2)}) copy-start(f32[1,1152]{1,0:T(1,128)} %copy-done.70) | copy-start | bytes 13828
  481.8 40.5 %copy-start.30 = (bf16[272,1152]{1,0:T(8,128)(2,1)S(1)}, bf16[272,1152]{1,0:T(8,128)(2,1)}, u32[]{:S(2)}) copy-start(bf16[272,1152]{1,0:T(8,128)(2,1)} %reduce-scatter.6.cloned.1.call-done.refs_0_) | copy-start | bytes 1880068
  481.8 41.7 %collective-permute-start.32 = (bf16[144,2368]{1,0:T(8,128)(2,1)S(1)}, bf16[144,2368]{1,0:T(8,128)(2,1)S(1)}, u32[]{:S(2)}, u32[]{:S(2)}) collective-permute-start(bf16[144,2368]{1,0:T(8,128)(2,1)S(1)} %pad_maximum_fusion.2.own_ref), channel_id=1, source_target_pairs={{0,8},{8,0},{16,24},{24,16},{1,9},{9,1},{17,25},{25,17},{2,10},{10... | collective-permute-start | bytes 2045960 | tf_op jit(solution)/shard_map/ppermute | solution.py:760
  483.4 42.1 %collective-permute-start.29 = (bf16[144,1472]{1,0:T(8,128)(2,1)}, bf16[144,1472]{1,0:T(8,128)(2,1)}, u32[]{:S(2)}, u32[]{:S(2)}) collective-permute-start(bf16[144,1472]{1,0:T(8,128)(2,1)} %get-tuple-element.303), channel_id=1, source_target_pairs={{0,2},{1,3},{2,0},{3,1},{4,6},{5,7},{6,4},{7,5},{8,10},{9,11},{10,... | collective-permute-start | bytes 1271816 | tf_op jit(solution)/shard_map/ppermute | solution.py:766
  484.9 40.6 %collective-permute-start.30 = (bf16[144,1472]{1,0:T(8,128)(2,1)}, bf16[144,1472]{1,0:T(8,128)(2,1)}, u32[]{:S(2)}, u32[]{:S(2)}) collective-permute-start(bf16[144,1472]{1,0:T(8,128)(2,1)} %get-tuple-element.304), channel_id=1, source_target_pairs={{0,4},{1,5},{2,6},{3,7},{4,0},{5,1},{6,2},{7,3},{8,12},{9,13},{10,... | collective-permute-start | bytes 1271816 | tf_op jit(solution)/shard_map/ppermute | solution.py:766
  509.4 16.1 %collective-permute-start.31 = (bf16[144,1472]{1,0:T(8,128)(2,1)}, bf16[144,1472]{1,0:T(8,128)(2,1)}, u32[]{:S(2)}, u32[]{:S(2)}) collective-permute-start(bf16[144,1472]{1,0:T(8,128)(2,1)} %get-tuple-element.305), channel_id=1, source_target_pairs={{0,6},{1,7},{2,4},{3,5},{4,2},{5,3},{6,0},{7,1},{8,14},{9,15},{10,... | collective-permute-start | bytes 1271816 | tf_op jit(solution)/shard_map/ppermute | solution.py:766
  522.0 25.6 %collective-permute-start.34 = (bf16[144,2176]{1,0:T(8,128)(2,1)S(1)}, bf16[144,2176]{1,0:T(8,128)(2,1)}, u32[]{:S(2)}, u32[]{:S(2)}) collective-permute-start(bf16[144,2176]{1,0:T(8,128)(2,1)S(1)} %add_all.14.own_ref), channel_id=1, source_target_pairs={{0,8},{8,0},{16,24},{24,16},{1,9},{9,1},{17,25},{25,17},{2,10},{10... | collective-permute-start | bytes 1880072 | tf_op jit(solution)/shard_map/ppermute | solution.py:760
  527.0 23.9 %collective-permute-start.33 = (bf16[144,1472]{1,0:T(8,128)(2,1)S(1)}, bf16[144,1472]{1,0:T(8,128)(2,1)S(1)}, u32[]{:S(2)}, u32[]{:S(2)}) collective-permute-start(bf16[144,1472]{1,0:T(8,128)(2,1)S(1)} %add_all.16), channel_id=1, source_target_pairs={{0,16},{8,24},{16,0},{24,8},{1,17},{9,25},{17,1},{25,9},{2,18},{10... | collective-permute-start | bytes 1271816 | tf_op jit(solution)/shard_map/ppermute | solution.py:763
  539.4 11.6 %collective-permute-start.35 = (f32[1,3456]{1,0:T(1,128)S(1)}, f32[1,3456]{1,0:T(1,128)S(1)}, u32[]{:S(2)}, u32[]{:S(2)}) collective-permute-start(f32[1,3456]{1,0:T(1,128)S(1)} %broadcast_in_dim.12), channel_id=1, source_target_pairs={{0,16},{8,24},{16,0},{24,8},{1,17},{9,25},{17,1},{25,9},{2,18},{10... | collective-permute-start | bytes 41480 | tf_op jit(solution)/shard_map/ppermute | solution.py:763
  539.5 22.8 %collective-permute-start.28 = (bf16[272,1152]{1,0:T(8,128)(2,1)S(1)}, bf16[272,1152]{1,0:T(8,128)(2,1)S(1)}, u32[]{:S(2)}, u32[]{:S(2)}) collective-permute-start(bf16[272,1152]{1,0:T(8,128)(2,1)S(1)} %add_all.15.refs_0_), channel_id=1, source_target_pairs={{0,8},{8,0},{16,24},{24,16},{1,9},{9,1},{17,25},{25,17},{2,10},{10... | collective-permute-start | bytes 1880072 | tf_op jit(solution)/shard_map/ppermute | solution.py:760
  552.8 24.2 %collective-permute-start.37 = (bf16[144,2368]{1,0:T(8,128)(2,1)S(1)}, bf16[144,2368]{1,0:T(8,128)(2,1)S(1)}, u32[]{:S(2)}, u32[]{:S(2)}) collective-permute-start(bf16[144,2368]{1,0:T(8,128)(2,1)S(1)} %pad_maximum_fusion.3.own_ref), channel_id=1, source_target_pairs={{0,8},{8,0},{16,24},{24,16},{1,9},{9,1},{17,25},{25,17},{2,10},{10... | collective-permute-start | bytes 2045960 | tf_op jit(solution)/shard_map/ppermute | solution.py:760
  562.3 13.5 %collective-permute-start.36 = (f32[1,3456]{1,0:T(1,128)S(1)}, f32[1,3456]{1,0:T(1,128)S(1)}, u32[]{:S(2)}, u32[]{:S(2)}) collective-permute-start(f32[1,3456]{1,0:T(1,128)S(1)} %reshape_add_fusion.first_ref), channel_id=1, source_target_pairs={{0,8},{8,0},{16,24},{24,16},{1,9},{9,1},{17,25},{25,17},{2,10},{10... | collective-permute-start | bytes 41480 | tf_op jit(solution)/shard_map/ppermute | solution.py:760
  (145 other events, 837.4 us)
Sparse Core Ops, SparseCore 0:
  12.9 42.7 all-gather.8
  58.1 63.8 all-gather.10
  123.9 38.9 all-gather.12
  165.1 63.8 all-gather.14
  248.8 78.1 reduce-scatter.3
  331.2 46.6 reduce-scatter.7
  381.8 59.7 reduce-scatter.5

commit v5 on v4

--- a/solution.py
+++ b/solution.py
@@ -13,6 +13,7 @@
 LOW = jnp.bfloat16
 FULL = jnp.float32
 HEAVY = pl.CostEstimate(flops=20_000_000_000, transcendentals=0, bytes_accessed=1)
+MEDIUM = pl.CostEstimate(flops=2_300_000_000, transcendentals=0, bytes_accessed=1)
 LIGHT = pl.CostEstimate(flops=1, transcendentals=0, bytes_accessed=1)
 PLAN = {"final_early": 1, "other_late": 0, "sum_up_late": 1, "add_up_early": 1, "add_mixed_early": 1}
 
@@ -493,12 +494,12 @@
 
 
 def mid_backward_kernel(
-    side_ref, keep_ref, got_ref, normed_ref, inverse_ref, gain_ref, grad_ref, proj_ref, *outs
+    side_ref, keep_ref, got_ref, hidden_ref, gain_ref, grad_ref, proj_ref, *outs
 ):
     after_ref, send_ref, mine_ref, other_ref, g_gain_ref, g_bias_ref, g_out_ref, g_down_ref = outs
     upstream = keep_ref[...] + got_ref[...].astype(FULL)
-    grad = grad_ref[...]
-    back, g_gain, g_bias = normalize_back(upstream, normed_ref[...], inverse_ref[...], gain_ref[...])
+    grad = grad_ref[...].astype(FULL)
+    back, g_gain, g_bias = normalize_back(upstream, *normalize(hidden_ref[...]), gain_ref[...])
     after = grad + back
     after_ref[...] = after
     g_gain_ref[...] = g_gain
@@ -519,7 +520,7 @@
         send_ref[rank] = mm_cols(proj_ref[rank * slab : (rank + 1) * slab, :], low).astype(LOW)
 
 
-def mid_backward(side, keep, got, normed, inverse, gain, grad, proj, ranks):
+def mid_backward(side, keep, got, hidden, gain, grad, proj, ranks):
     tokens, width = keep.shape
     row = jax.ShapeDtypeStruct((1, width), FULL)
     half = jax.ShapeDtypeStruct((tokens, width // 2), LOW)
@@ -538,8 +539,7 @@
         ),
         keep,
         got,
-        normed,
-        inverse,
+        hidden,
         gain,
         grad,
         proj,
@@ -547,11 +547,11 @@
     )
 
 
-def end_backward_kernel(got_ref, normed_ref, inverse_ref, gain_ref, after_ref, out_ref, low_ref, g_gain_ref, g_bias_ref):
+def end_backward_kernel(got_ref, hidden_ref, gain_ref, after_ref, out_ref, low_ref, g_gain_ref, g_bias_ref):
     upstream = got_ref[0].astype(FULL)
     for rank in range(1, got_ref.shape[0]):
         upstream += got_ref[rank].astype(FULL)
-    back, g_gain, g_bias = normalize_back(upstream, normed_ref[...], inverse_ref[...], gain_ref[...])
+    back, g_gain, g_bias = normalize_back(upstream, *normalize(hidden_ref[...].astype(FULL)), gain_ref[...])
     total = after_ref[...] + back
     out_ref[...] = total
     low_ref[...] = total.astype(LOW)
@@ -559,7 +559,7 @@
     g_bias_ref[...] = g_bias
 
 
-def end_backward(got, normed, inverse, gain, after):
+def end_backward(got, hidden, gain, after):
     tokens, width = after.shape
     row = jax.ShapeDtypeStruct((1, width), FULL)
     return local_call(
@@ -572,8 +572,7 @@
             row,
         ),
         got,
-        normed,
-        inverse,
+        hidden,
         gain,
         after,
     )
@@ -917,7 +916,8 @@
         for layer in range(layers):
             v = vectors[layer]
             last_layer = layer == layers - 1
-            normed_one, inverse_one = normalize(hidden)
+            hidden_in = hidden
+            normed_one, _ = normalize(hidden)
             if layer == 0:
                 attn_in = (normed_all * v["gain_one"] + v["bias_one"]).astype(LOW)
             else:
@@ -935,7 +935,7 @@
             order.leave(out_heads)
             attended = order.enter(exchange(out_heads))[0].reshape(width, tokens)
             after_attn = hidden + mm_rows(attended, proj_out) + v["bias_out"]
-            normed_two, inverse_two = normalize(after_attn)
+            normed_two, _ = normalize(after_attn)
             mlp_mine = (normed_two * v["gain_two"] + v["bias_two"]).astype(LOW)
             order.leave(mlp_mine)
             mlp_other = swap(mlp_mine)
@@ -955,8 +955,8 @@
             stored.append(
                 (
                     (proj_qkv, proj_out, feed),
-                    (normed_one, inverse_one, attn_in, qkv, lse, attended, attended_other),
-                    (normed_two, inverse_two, mlp_mine, mlp_other, pre_act, activated),
+                    (block_input[0] if layer == 0 else hidden_in, attn_in, qkv, lse, attended, attended_other),
+                    (after_attn, mlp_mine, mlp_other, pre_act, activated),
                 )
             )
 
@@ -975,7 +975,7 @@
         def sum_rows(value):
             return jnp.sum(value, axis=0, keepdims=True)
 
-        grad_hidden, grad_mine = grad_output[0].astype(FULL), grad_output[0]
+        grad_hidden = grad_mine = grad_output[0]
         small_grads = [None] * layers
         downs = [None] * layers
         outs = dict(up=(), mixed=())
@@ -984,8 +984,8 @@
             v = vectors[layer]
             tag = "_late" if before else "_early"
             proj_qkv, proj_out, feed = stored[layer][0]
-            normed_one, inverse_one, attn_in, qkv, lse, attended, attended_other = stored[layer][1]
-            normed_two, inverse_two, mlp_mine, mlp_other, pre_act, activated = stored[layer][2]
+            hidden_in, attn_in, qkv, lse, attended, attended_other = stored[layer][1]
+            mid_hidden, mlp_mine, mlp_other, pre_act, activated = stored[layer][2]
             grad_other = swap(grad_mine)
             if before:
                 before["down"].step()
@@ -997,7 +997,9 @@
             )
             order.leave(leaving)
             other = swap(leaving)
-            g_down = weight_grad([((activated,), order.enter(grad_low), False, 0)], owners, width)
+            g_down = weight_grad(
+                [((activated,), order.enter(grad_low), False, 0)], owners, width
+            )
             order.leave(g_down)
             down_chain = Chain(written(queue_steps(g_down), pair_steps, held, "down" + tag))
             keep, send = weight_grad(
@@ -1030,8 +1032,7 @@
                 side,
                 mixed,
                 *order.enter(other),
-                normed_two,
-                inverse_two,
+                mid_hidden,
                 v["gain_two"].reshape(1, width),
                 grad_hidden,
                 proj_out,
@@ -1094,7 +1095,7 @@
                 final_other = swap(leaving)
             (arrived,) = order.enter(arrived)
             grad_hidden, grad_mine, g_gain_one, g_bias_one = end_backward(
-                arrived, normed_one, inverse_one, v["gain_one"].reshape(1, width), grad_after
+                arrived, hidden_in, v["gain_one"].reshape(1, width), grad_after
             )
             order.leave(grad_hidden)
             if before:

time: 596 us -> 592 us (level)
  other arithmetic: 15.5 us -> 6.99 us
  waiting for transfers between devices: 211 us -> 219 us
  local copies, waits for them, and re-layouts: 115 us -> 109 us
    unnamed x316 -> x296, local copies, waits for them, and re-layouts: 91.1 us -> 87.3 us
  transfers between devices with their start and end apart: 52 -> 52, of which waited for: 18 -> 20; matrix products, arithmetic and copies ran while one was open for 7% -> 6% of each run, Pallas kernels for 20% -> 20%
where the time goes in v5:
time: 592 us; the launch traced here: 582 us
  waiting for transfers between devices  219 us (37%)
  Pallas kernels  128 us (22%)
  local copies, waits for them, and re-layouts  109 us (18%)
  starting transfers between devices  75 us (13%)
  blocking collectives  20.3 us (3%)
  between operations  16.2 us (3%)
  matrix products  7.39 us (1%)
  other arithmetic  6.99 us (1%)
    unnamed x296, local copies, waits for them, and re-layouts  87.3 us
    pallas_call x29, Pallas kernels, local_call(): pl.pallas_call(kernel, out_shape=out_shape, in_specs=[pl.BlockSpec(memory...  76.5 us
    all_to_all x7, waiting for transfers between devices, exchange(): lax.all_to_all(blocks, 'seq', split_axis=0, concat_axis=0, tiled=True)  53.9 us
    ppermute x7, waiting for transfers between devices, pair_shift(): lax.ppermute(value, 'seq', [(i, (i + 2 * step) % ranks) for i in range(ra...  43.9 us
    ppermute x19, waiting for transfers between devices, swap(): return lax.ppermute(value, 'seq', [(i, i ^ 1) for i in range(ranks)])  43.9 us
    all_gather x2, waiting for transfers between devices, body(): feeds.append(lax.all_gather(share, 'fsdp', axis=0))  41.8 us
    all_to_all x7, starting transfers between devices, exchange(): lax.all_to_all(blocks, 'seq', split_axis=0, concat_axis=0, tiled=True)  31.9 us
    ppermute x19, starting transfers between devices, swap(): return lax.ppermute(value, 'seq', [(i, i ^ 1) for i in range(ranks)])  20.9 us
  transfers between devices with their start and end apart: 52, of which 20 were waited for; matrix products, arithmetic and copies ran while one was open for 6% of the time, Pallas kernels for 20%

profile of v5, /device:TPU:0, one launch (start us, length us, event | category | flops | bytes accessed | tf_op | source)
XLA Modules:
  0.0 582.4 jit_solution(9731552583212131849)
XLA Ops:
  9.1 2.6 slice_bitcast_fusion.3
  13.1 3.4 slice_bitcast_fusion
  28.7 6.7 %all-to-all-start = ((bf16[4,128,1152]{2,1,0:T(8,128)(2,1)}), bf16[4,128,1152]{2,1,0:T(8,128)(2,1)S(1)}, u32[]{:S(2)}, u32[]{:S(2)}) async-start(bf16[4,128,1152]{2,1,0:T(8,128)(2,1)} %broadcast_in_dim.10), calls=%async_computation | async-start | bytes 2359296 | tf_op jit(solution)/shard_map/all_to_all | solution.py:768
  35.4 28.5 %all-to-all-done = bf16[4,128,1152]{2,1,0:T(8,128)(2,1)S(1)} async-done(((bf16[4,128,1152]{2,1,0:T(8,128)(2,1)}), bf16[4,128,1152]{2,1,0:T(8,128)(2,1)S(1)}, u32[]{:S(2)}, u32[]{:S(2)}) %all-to-all-start) | async-done | bytes 1179680 | tf_op jit(solution)/shard_map/all_to_all | solution.py:768
  64.9 3.0 copy-done.9
  76.2 4.2 attend_forward.2
  81.4 3.9 all-to-all-start.1
  86.7 7.5 %all-to-all-done.1 = bf16[4,288,128]{2,1,0:T(8,128)(2,1)S(1)} async-done(((bf16[4,288,128]{2,1,0:T(8,128)(2,1)}), bf16[4,288,128]{2,1,0:T(8,128)(2,1)S(1)}, u32[]{:S(2)}, u32[]{:S(2)}) %all-to-all-start.1) | async-done | bytes 294944 | tf_op jit(solution)/shard_map/all_to_all | solution.py:768
  99.4 10.2 %collective-permute-done.1.refs_4_ = bf16[1152,128]{1,0:T(8,128)(2,1)S(1)} collective-permute-done((bf16[1152,128]{1,0:T(8,128)(2,1)S(1)}, bf16[1152,128]{1,0:T(8,128)(2,1)S(1)}, u32[]{:S(2)}, u32[]{:S(2)}) %collective-permute-start.1) | collective-permute-done | bytes 294944 | tf_op jit(solution)/shard_map/ppermute | solution.py:759
  109.7 12.5 %all-gather.11.cloned.1.call-done = bf16[2304,2304]{1,0:T(8,128)(2,1)} async-done(((bf16[288,2304]{1,0:T(8,128)(2,1)}), bf16[2304,2304]{1,0:T(8,128)(2,1)}) %all-gather.11.cloned.1.call-update) | async-done | bytes 10616848 | tf_op jit(solution)/shard_map/all_gather | solution.py:884
  122.2 4.0 copy-done.90
  126.2 4.4 feed_forward.2
  133.5 7.7 %collective-permute-done.2 = bf16[128,1152]{1,0:T(8,128)(2,1)S(1)} collective-permute-done((bf16[128,1152]{1,0:T(8,128)(2,1)S(1)}, bf16[128,1152]{1,0:T(8,128)(2,1)S(1)}, u32[]{:S(2)}, u32[]{:S(2)}) %collective-permute-start.2) | collective-permute-done | bytes 294944 | tf_op jit(solution)/shard_map/ppermute | solution.py:759
  142.9 4.6 all-to-all-start.2
  147.6 16.1 %all-gather.13.cloned.1.call-done = bf16[1152,2016]{1,0:T(8,128)(2,1)} async-done(((bf16[144,2016]{1,0:T(8,128)(2,1)}), bf16[1152,2016]{1,0:T(8,128)(2,1)}) %all-gather.13.cloned.1.call-update) | async-done | bytes 4644880 | tf_op jit(solution)/shard_map/all_gather | solution.py:881
  163.7 2.3 copy-done.10
  169.2 6.6 %all-to-all-done.2 = bf16[4,128,1152]{2,1,0:T(8,128)(2,1)S(1)} async-done(((bf16[4,128,1152]{2,1,0:T(8,128)(2,1)}), bf16[4,128,1152]{2,1,0:T(8,128)(2,1)S(1)}, u32[]{:S(2)}, u32[]{:S(2)}) %all-to-all-start.2) | async-done | bytes 1179680 | tf_op jit(solution)/shard_map/all_to_all | solution.py:768
  175.8 3.5 add_convert_fusion.1
  180.0 3.5 attend_forward.3
  183.4 11.9 %all_to_all.52 = bf16[4,288,128]{2,1,0:T(8,128)(2,1)S(1)} all-to-all(bf16[4,288,128]{2,1,0:T(8,128)(2,1)S(1)} %get-tuple-element.217), channel_id=1, replica_groups=mesh['seq'=4,'fsdp'=8] {'seq'}, dimensions={0} | all-to-all | bytes 589824 | tf_op jit(solution)/shard_map/all_to_all | solution.py:768
  200.6 29.2 %all-gather.15.cloned.1.call-done = bf16[2304,2304]{1,0:T(8,128)(2,1)} async-done(((bf16[288,2304]{1,0:T(8,128)(2,1)}), bf16[2304,2304]{1,0:T(8,128)(2,1)}) %all-gather.15.cloned.1.call-update) | async-done | bytes 10616848 | tf_op jit(solution)/shard_map/all_gather | solution.py:884
  229.8 4.0 copy-done.92
  236.1 6.2 %feed_backward.2 = (bf16[256,1152]{1,0:T(8,128)(2,1)S(1)}, bf16[256,2176]{1,0:T(8,128)(2,1)S(1)}, f32[128,1152]{1,0:T(8,128)S(1)}, bf16[128,1152]{1,0:T(8,128)(2,1)S(1)}, f32[1,2176]{1,0:T(1,128)S(1)}) custom-call(bf16[128,1152]{1,0:T(8,128)(2,1)} %bitcast.27.mine_ref.grad_ref, bf16[128,1152]{1,0:T(8,128)(2,1)} %collective-permute-done.5.other_ref, ...), custom_call_target="tpu_custom_call" | custom-call | flops 20000000000 | bytes 1 | tf_op jit(solution)/shard_map/feed_backward/pallas_call | solution.py:256
  246.5 2.3 copy-done.7
  251.6 6.2 %weight_grad.7 = (bf16[4,144,2176]{2,1,0:T(8,128)(2,1)S(1)}, bf16[4,144,2176]{2,1,0:T(8,128)(2,1)}) custom-call(s32[1]{0:T(128)} %bitcast.28.refs_0_, bf16[128,1152]{1,0:T(8,128)(2,1)S(1)} %add_convert_fusion.4.mine_ref.refs_1_, bf16[128,1152]{1,0:T(8,128)(2,1)S(1)} %collective-permute-done.3.other_ref.refs_2_, bf16[256,2176]{1,0:T(8,128)(2,1)S(1)} %copy-done.32), custom_call_target="tpu_custom_call" | custom-call | flops 1 | bytes 1 | tf_op jit(solution)/shard_map/weight_grad/pallas_call | solution.py:256
  263.0 3.3 mid_backward.2
  270.2 3.8 all-to-all-start.4
  277.8 4.0 meet_cores.3
  287.7 7.2 %attend_backward.2 = (bf16[512,864]{1,0:T(8,128)(2,1)S(1)}, bf16[4,128,1152]{2,1,0:T(8,128)(2,1)S(1)}, f32[1,288]{1,0:T(1,128)S(1)}, f32[1,288]{1,0:T(1,128)S(1)}) custom-call(bf16[3,512,288]{2,1,0:T(8,128)(2,1)S(1)} %pad_maximum_fusion.1.qkv_ref, bf16[4,288,128]{2,1,0:T(8,128)(2,1)S(1)} %all-to-all-done.4.got_ref, f32[512,4]{1,0:T(8,128)S(1)} %copy-done.109, ...), custom_call_target="tpu_custom_call" | custom-call | flops 20000000000 | bytes 1 | tf_op jit(solution)/shard_map/attend_backward/pallas_call | solution.py:164
  297.4 4.4 all-to-all-start.5
  303.3 2.9 weight_grad.8
  308.6 4.1 copy-done.93
  318.6 11.2 %all-to-all-done.5.got_ref = bf16[4,128,1152]{2,1,0:T(8,128)(2,1)} async-done(((bf16[4,128,1152]{2,1,0:T(8,128)(2,1)}), bf16[4,128,1152]{2,1,0:T(8,128)(2,1)}, u32[]{:S(2)}, u32[]{:S(2)}) %all-to-all-start.5) | async-done | bytes 1179680 | tf_op jit(solution)/shard_map/all_to_all | solution.py:768
  333.7 3.0 add_all.9.refs_0_
  339.6 3.0 collective-permute-done.9.other_ref
  342.6 4.0 copy-done.91
  348.2 5.4 feed_backward.3
  358.0 2.2 copy-done.8
  363.4 6.2 %weight_grad.10 = (bf16[4,144,2176]{2,1,0:T(8,128)(2,1)S(1)}, bf16[4,144,2176]{2,1,0:T(8,128)(2,1)}) custom-call(s32[1]{0:T(128)} %bitcast.28.refs_0_, bf16[128,1152]{1,0:T(8,128)(2,1)S(1)} %copy-done.30, bf16[128,1152]{1,0:T(8,128)(2,1)S(1)} %copy-done.49, bf16[256,2176]{1,0:T(8,128)(2,1)S(1)} %copy-done.34), custom_call_target="tpu_custom_call" | custom-call | flops 1 | bytes 1 | tf_op jit(solution)/shard_map/weight_grad/pallas_call | solution.py:256
  369.7 2.7 collective-permute-done.15.got_ref
  372.4 8.3 %collective-permute-done.16.refs_1_ = bf16[144,2176]{1,0:T(8,128)(2,1)} collective-permute-done((bf16[144,2176]{1,0:T(8,128)(2,1)}, bf16[144,2176]{1,0:T(8,128)(2,1)}, u32[]{:S(2)}, u32[]{:S(2)}) %collective-permute-start.16) | collective-permute-done | bytes 626720 | tf_op jit(solution)/shard_map/ppermute | solution.py:762
  382.2 2.7 mid_backward.3
  390.2 4.1 all-to-all-start.6
  396.4 3.8 meet_cores.4
  407.7 2.8 collective-permute-start.27
  416.2 9.2 %attend_backward.3 = (bf16[512,864]{1,0:T(8,128)(2,1)S(1)}, bf16[4,128,1152]{2,1,0:T(8,128)(2,1)}, f32[1,288]{1,0:T(1,128)S(1)}, f32[1,288]{1,0:T(1,128)S(1)}) custom-call(bf16[3,512,288]{2,1,0:T(8,128)(2,1)S(1)} %copy-done.12, bf16[4,288,128]{2,1,0:T(8,128)(2,1)} %all-to-all-done.6.got_ref, f32[512,4]{1,0:T(8,128)S(1)} %copy-done.107, ...), custom_call_target="tpu_custom_call" | custom-call | flops 20000000000 | bytes 1 | tf_op jit(solution)/shard_map/attend_backward/pallas_call | solution.py:164
  426.9 4.4 all-to-all-start.7
  432.4 3.2 write_up.2.refs_0_
  436.8 7.0 %weight_grad.11 = (bf16[4,144,1472]{2,1,0:T(8,128)(2,1)S(1)}, bf16[4,144,1472]{2,1,0:T(8,128)(2,1)}) custom-call(s32[1]{0:T(128)} %bitcast.28.refs_0_, bf16[512,1152]{1,0:T(8,128)(2,1)S(1)} %copy-done.25, bf16[512,864]{1,0:T(8,128)(2,1)S(1)} %copy-done.120, bf16[1152,128]{1,0:T(8,128)(2,1)S(1)} %bitcast.86, bf16[1152,128]{1,0:T(8,128)(2,1)S(1)} %copy-done.104, ...), custom_call_target="tpu_custom_call" | custom-call | flops 20000000000 | bytes 1 | tf_op jit(solution)/shard_map/weight_grad/pallas_call | solution.py:256
  443.8 19.6 %collective-permute-done.18.refs_2_ = bf16[144,2176]{1,0:T(8,128)(2,1)S(1)} collective-permute-done((bf16[144,2176]{1,0:T(8,128)(2,1)}, bf16[144,2176]{1,0:T(8,128)(2,1)S(1)}, u32[]{:S(2)}, u32[]{:S(2)}) %collective-permute-start.18) | collective-permute-done | bytes 626720 | tf_op jit(solution)/shard_map/ppermute | solution.py:765
  463.4 2.2 add_all.12.refs_0_
  465.7 2.6 collective-permute-start.24
  468.6 3.5 meet_cores.5
  474.0 2.8 end_backward.3
  482.5 23.9 %collective-permute-done.24.refs_1_ = bf16[144,2176]{1,0:T(8,128)(2,1)} collective-permute-done((bf16[144,2176]{1,0:T(8,128)(2,1)}, bf16[144,2176]{1,0:T(8,128)(2,1)}, u32[]{:S(2)}, u32[]{:S(2)}) %collective-permute-start.24) | collective-permute-done | bytes 626720 | tf_op jit(solution)/shard_map/ppermute | solution.py:762
  509.4 9.1 %collective-permute-done.23.refs_1_ = bf16[272,1152]{1,0:T(8,128)(2,1)} collective-permute-done((bf16[272,1152]{1,0:T(8,128)(2,1)}, bf16[272,1152]{1,0:T(8,128)(2,1)}, u32[]{:S(2)}, u32[]{:S(2)}) %collective-permute-start.23) | collective-permute-done | bytes 626720 | tf_op jit(solution)/shard_map/ppermute | solution.py:762
  524.8 3.4 collective-permute-start.33
  528.3 8.4 %all_to_all.53 = f32[8,1,3456]{2,1,0:T(1,128)S(1)} all-to-all(f32[8,1,3456]{2,1,0:T(1,128)S(1)} %copy.41), channel_id=1, replica_groups=mesh['seq'=4,'fsdp'=8] {'fsdp'}, dimensions={0} | all-to-all | bytes 221184 | tf_op jit(solution)/shard_map/all_to_all | solution.py:1137
  537.9 4.8 collective-permute-done.34.across_ref
  542.7 3.0 write_up.3
  545.8 2.5 collective-permute-done.33
  548.7 9.5 %collective-permute-done.28.refs_1_ = bf16[272,1152]{1,0:T(8,128)(2,1)S(1)} collective-permute-done((bf16[272,1152]{1,0:T(8,128)(2,1)S(1)}, bf16[272,1152]{1,0:T(8,128)(2,1)S(1)}, u32[]{:S(2)}, u32[]{:S(2)}) %collective-permute-start.28) | collective-permute-done | bytes 626720 | tf_op jit(solution)/shard_map/ppermute | solution.py:759
  559.4 4.9 write_down.1
  566.1 5.9 %collective-permute-done.36.second_ref = f32[1,3456]{1,0:T(1,128)S(1)} collective-permute-done((f32[1,3456]{1,0:T(1,128)S(1)}, f32[1,3456]{1,0:T(1,128)S(1)}, u32[]{:S(2)}, u32[]{:S(2)}) %collective-permute-start.36) | collective-permute-done | bytes 13856 | tf_op jit(solution)/shard_map/ppermute | solution.py:759
  (462 shorter events, 151.9 us)
Async XLA Ops:
  7.2 57.4 %all-gather.9.cloned.1.call-start = ((), (), s32[]{:S(2)}) async-start(), calls=%async_computation.15 | async-start | bytes 5603328 | tf_op jit(solution)/shard_map/all_gather | solution.py:881
  13.0 109.2 %all-gather.11.cloned.1.call-start = ((), (), s32[]{:S(2)}) async-start(), calls=%async_computation.16 | async-start | bytes 11943936 | tf_op jit(solution)/shard_map/all_gather | solution.py:884
  20.9 142.8 %all-gather.13.cloned.1.call-start = ((), (), s32[]{:S(2)}) async-start(), calls=%async_computation.17 | async-start | bytes 5308416 | tf_op jit(solution)/shard_map/all_gather | solution.py:881
  23.1 206.7 %all-gather.15.cloned.1.call-start = ((), (), s32[]{:S(2)}) async-start(), calls=%async_computation.18 | async-start | bytes 11943936 | tf_op jit(solution)/shard_map/all_gather | solution.py:884
  28.7 35.2 %all-to-all-start = ((bf16[4,128,1152]{2,1,0:T(8,128)(2,1)}), bf16[4,128,1152]{2,1,0:T(8,128)(2,1)S(1)}, u32[]{:S(2)}, u32[]{:S(2)}) async-start(bf16[4,128,1152]{2,1,0:T(8,128)(2,1)} %broadcast_in_dim.10), calls=%async_computation | async-start | bytes 2359296 | tf_op jit(solution)/shard_map/all_to_all | solution.py:768
  81.4 12.9 %all-to-all-start.1 = ((bf16[4,288,128]{2,1,0:T(8,128)(2,1)}), bf16[4,288,128]{2,1,0:T(8,128)(2,1)S(1)}, u32[]{:S(2)}, u32[]{:S(2)}) async-start(bf16[4,288,128]{2,1,0:T(8,128)(2,1)} %get-tuple-element.204), calls=%async_computation.1 | async-start | bytes 589824 | tf_op jit(solution)/shard_map/all_to_all | solution.py:768
  96.0 45.2 %copy-start.1 = (f32[128,1152]{1,0:T(8,128)}, f32[128,1152]{1,0:T(8,128)S(1)}, u32[]{:S(2)}) copy-start(f32[128,1152]{1,0:T(8,128)S(1)} %get-tuple-element.462.hidden_ref) | copy-start | bytes 1769476
  96.5 34.2 %copy-start.29 = (bf16[128,1152]{1,0:T(8,128)(2,1)}, bf16[128,1152]{1,0:T(8,128)(2,1)S(1)}, u32[]{:S(2)}) copy-start(bf16[128,1152]{1,0:T(8,128)(2,1)S(1)} %add_convert_fusion.6.mine_ref.refs_1_) | copy-start | bytes 884740
  96.5 13.2 %collective-permute-start = (bf16[128,1152]{1,0:T(8,128)(2,1)S(1)}, bf16[128,1152]{1,0:T(8,128)(2,1)S(1)}, u32[]{:S(2)}, u32[]{:S(2)}) collective-permute-start(bf16[128,1152]{1,0:T(8,128)(2,1)S(1)} %add_convert_fusion.6.mine_ref.refs_1_), channel_id=1, source_target_pairs={{0,8},{8,0},{16,24},{24,16},{1,9},{9,1},{17,25},{25,17},{2,10},{10... | collective-permute-start | bytes 884744 | tf_op jit(solution)/shard_map/ppermute | solution.py:759
  96.6 13.1 %collective-permute-start.1 = (bf16[1152,128]{1,0:T(8,128)(2,1)S(1)}, bf16[1152,128]{1,0:T(8,128)(2,1)S(1)}, u32[]{:S(2)}, u32[]{:S(2)}) collective-permute-start(bf16[1152,128]{1,0:T(8,128)(2,1)S(1)} %bitcast.85), channel_id=1, source_target_pairs={{0,8},{8,0},{16,24},{24,16},{1,9},{9,1},{17,25},{25,17},{2,10},{10... | collective-permute-start | bytes 884744 | tf_op jit(solution)/shard_map/ppermute | solution.py:759
  132.1 9.2 %collective-permute-start.2 = (bf16[128,1152]{1,0:T(8,128)(2,1)S(1)}, bf16[128,1152]{1,0:T(8,128)(2,1)S(1)}, u32[]{:S(2)}, u32[]{:S(2)}) collective-permute-start(bf16[128,1152]{1,0:T(8,128)(2,1)S(1)} %get-tuple-element.211), channel_id=1, source_target_pairs={{0,8},{8,0},{16,24},{24,16},{1,9},{9,1},{17,25},{25,17},{2,10},{10... | collective-permute-start | bytes 884744 | tf_op jit(solution)/shard_map/ppermute | solution.py:759
  142.9 32.9 %all-to-all-start.2 = ((bf16[4,128,1152]{2,1,0:T(8,128)(2,1)}), bf16[4,128,1152]{2,1,0:T(8,128)(2,1)S(1)}, u32[]{:S(2)}, u32[]{:S(2)}) async-start(bf16[4,128,1152]{2,1,0:T(8,128)(2,1)} %broadcast_in_dim.11), calls=%async_computation.2 | async-start | bytes 2359296 | tf_op jit(solution)/shard_map/all_to_all | solution.py:768
  147.5 190.7 %reduce-scatter.4.cloned.1.call-start = ((), (), s32[]{:S(2)}) async-start(), calls=%async_computation.12 | async-start | bytes 5640192 | tf_op jit(solution)/shard_map/reduce_scatter | solution.py:821
  196.5 33.3 %collective-permute-start.4 = (bf16[1152,128]{1,0:T(8,128)(2,1)S(1)}, bf16[1152,128]{1,0:T(8,128)(2,1)}, u32[]{:S(2)}, u32[]{:S(2)}) collective-permute-start(bf16[1152,128]{1,0:T(8,128)(2,1)S(1)} %bitcast.88), channel_id=1, source_target_pairs={{0,8},{8,0},{16,24},{24,16},{1,9},{9,1},{17,25},{25,17},{2,10},{10... | collective-permute-start | bytes 884744 | tf_op jit(solution)/shard_map/ppermute | solution.py:759
  197.1 32.8 %collective-permute-start.3 = (bf16[128,1152]{1,0:T(8,128)(2,1)S(1)}, bf16[128,1152]{1,0:T(8,128)(2,1)S(1)}, u32[]{:S(2)}, u32[]{:S(2)}) collective-permute-start(bf16[128,1152]{1,0:T(8,128)(2,1)S(1)} %add_convert_fusion.4.mine_ref.refs_1_), channel_id=1, source_target_pairs={{0,8},{8,0},{16,24},{24,16},{1,9},{9,1},{17,25},{25,17},{2,10},{10... | collective-permute-start | bytes 884744 | tf_op jit(solution)/shard_map/ppermute | solution.py:759
  198.6 37.5 %collective-permute-start.5 = (bf16[128,1152]{1,0:T(8,128)(2,1)}, bf16[128,1152]{1,0:T(8,128)(2,1)}, u32[]{:S(2)}, u32[]{:S(2)}) collective-permute-start(bf16[128,1152]{1,0:T(8,128)(2,1)} %bitcast.27.mine_ref.grad_ref), channel_id=1, source_target_pairs={{0,8},{8,0},{16,24},{24,16},{1,9},{9,1},{17,25},{25,17},{2,10},{10... | collective-permute-start | bytes 884744 | tf_op jit(solution)/shard_map/ppermute | solution.py:759
  248.8 10.5 %collective-permute-start.6 = (bf16[128,1152]{1,0:T(8,128)(2,1)}, bf16[128,1152]{1,0:T(8,128)(2,1)}, u32[]{:S(2)}, u32[]{:S(2)}) collective-permute-start(bf16[128,1152]{1,0:T(8,128)(2,1)} %copy-done.105), channel_id=1, source_target_pairs={{0,8},{8,0},{16,24},{24,16},{1,9},{9,1},{17,25},{25,17},{2,10},{10... | collective-permute-start | bytes 884744 | tf_op jit(solution)/shard_map/ppermute | solution.py:759
  259.3 16.8 %collective-permute-start.8 = (bf16[4,144,2176]{2,1,0:T(8,128)(2,1)}, bf16[4,144,2176]{2,1,0:T(8,128)(2,1)}, u32[]{:S(2)}, u32[]{:S(2)}) collective-permute-start(bf16[4,144,2176]{2,1,0:T(8,128)(2,1)} %get-tuple-element.231), channel_id=1, source_target_pairs={{0,1},{1,0},{2,3},{3,2},{4,5},{5,4},{6,7},{7,6},{8,9},{9,8},{10,11... | collective-permute-start | bytes 7520264 | tf_op jit(solution)/shard_map/ppermute | solution.py:765
  270.2 15.9 %all-to-all-start.4 = ((bf16[4,288,128]{2,1,0:T(8,128)(2,1)}), bf16[4,288,128]{2,1,0:T(8,128)(2,1)S(1)}, u32[]{:S(2)}, u32[]{:S(2)}) async-start(bf16[4,288,128]{2,1,0:T(8,128)(2,1)} %get-tuple-element.233), calls=%async_computation.4 | async-start | bytes 589824 | tf_op jit(solution)/shard_map/all_to_all | solution.py:768
  274.1 12.1 %collective-permute-start.7 = (bf16[128,576]{1,0:T(8,128)(2,1)}, bf16[128,576]{1,0:T(8,128)(2,1)}, u32[]{:S(2)}, u32[]{:S(2)}) collective-permute-start(bf16[128,576]{1,0:T(8,128)(2,1)} %get-tuple-element.234), channel_id=1, source_target_pairs={{0,8},{8,0},{16,24},{24,16},{1,9},{9,1},{17,25},{25,17},{2,10},{10... | collective-permute-start | bytes 442376 | tf_op jit(solution)/shard_map/ppermute | solution.py:759
  282.6 51.0 %collective-permute-start.11 = (bf16[144,2176]{1,0:T(8,128)(2,1)}, bf16[144,2176]{1,0:T(8,128)(2,1)}, u32[]{:S(2)}, u32[]{:S(2)}) collective-permute-start(bf16[144,2176]{1,0:T(8,128)(2,1)} %get-tuple-element.237), channel_id=1, source_target_pairs={{0,2},{1,3},{2,0},{3,1},{4,6},{5,7},{6,4},{7,5},{8,10},{9,11},{10,... | collective-permute-start | bytes 1880072 | tf_op jit(solution)/shard_map/ppermute | solution.py:765
  284.1 49.6 %collective-permute-start.12 = (bf16[144,2176]{1,0:T(8,128)(2,1)}, bf16[144,2176]{1,0:T(8,128)(2,1)}, u32[]{:S(2)}, u32[]{:S(2)}) collective-permute-start(bf16[144,2176]{1,0:T(8,128)(2,1)} %get-tuple-element.238), channel_id=1, source_target_pairs={{0,4},{1,5},{2,6},{3,7},{4,0},{5,1},{6,2},{7,3},{8,12},{9,13},{10,... | collective-permute-start | bytes 1880072 | tf_op jit(solution)/shard_map/ppermute | solution.py:765
  284.8 48.9 %collective-permute-start.13 = (bf16[144,2176]{1,0:T(8,128)(2,1)}, bf16[144,2176]{1,0:T(8,128)(2,1)}, u32[]{:S(2)}, u32[]{:S(2)}) collective-permute-start(bf16[144,2176]{1,0:T(8,128)(2,1)} %get-tuple-element.239), channel_id=1, source_target_pairs={{0,6},{1,7},{2,4},{3,5},{4,2},{5,3},{6,0},{7,1},{8,14},{9,15},{10,... | collective-permute-start | bytes 1880072 | tf_op jit(solution)/shard_map/ppermute | solution.py:765
  297.4 32.4 %all-to-all-start.5 = ((bf16[4,128,1152]{2,1,0:T(8,128)(2,1)}), bf16[4,128,1152]{2,1,0:T(8,128)(2,1)}, u32[]{:S(2)}, u32[]{:S(2)}) async-start(bf16[4,128,1152]{2,1,0:T(8,128)(2,1)} %copy-done.28), calls=%async_computation.5 | async-start | bytes 2359296 | tf_op jit(solution)/shard_map/all_to_all | solution.py:768
  301.8 103.3 %reduce-scatter.8.cloned.1.call-start = ((), (), s32[]{:S(2)}) async-start(), calls=%async_computation.14 | async-start | bytes 3981312 | tf_op jit(solution)/shard_map/reduce_scatter | solution.py:821
  308.1 160.1 %reduce-scatter.6.cloned.1.call-start = ((), (), s32[]{:S(2)}) async-start(), calls=%async_computation.13 | async-start | bytes 5640192 | tf_op jit(solution)/shard_map/reduce_scatter | solution.py:821
  316.6 23.0 %collective-permute-start.10 = (bf16[128,1152]{1,0:T(8,128)(2,1)S(1)}, bf16[128,1152]{1,0:T(8,128)(2,1)}, u32[]{:S(2)}, u32[]{:S(2)}) collective-permute-start(bf16[128,1152]{1,0:T(8,128)(2,1)S(1)} %get-tuple-element.251), channel_id=1, source_target_pairs={{0,8},{8,0},{16,24},{24,16},{1,9},{9,1},{17,25},{25,17},{2,10},{10... | collective-permute-start | bytes 884744 | tf_op jit(solution)/shard_map/ppermute | solution.py:759
  333.6 8.9 %collective-permute-start.9 = (bf16[128,1152]{1,0:T(8,128)(2,1)S(1)}, bf16[128,1152]{1,0:T(8,128)(2,1)S(1)}, u32[]{:S(2)}, u32[]{:S(2)}) collective-permute-start(bf16[128,1152]{1,0:T(8,128)(2,1)S(1)} %get-tuple-element.254.mine_ref), channel_id=1, source_target_pairs={{0,8},{8,0},{16,24},{24,16},{1,9},{9,1},{17,25},{25,17},{2,10},{10... | collective-permute-start | bytes 884744 | tf_op jit(solution)/shard_map/ppermute | solution.py:759
  336.7 44.1 %collective-permute-start.16 = (bf16[144,2176]{1,0:T(8,128)(2,1)}, bf16[144,2176]{1,0:T(8,128)(2,1)}, u32[]{:S(2)}, u32[]{:S(2)}) collective-permute-start(bf16[144,2176]{1,0:T(8,128)(2,1)} %add_all.9.refs_0_), channel_id=1, source_target_pairs={{0,16},{8,24},{16,0},{24,8},{1,17},{9,25},{17,1},{25,9},{2,18},{10... | collective-permute-start | bytes 1880072 | tf_op jit(solution)/shard_map/ppermute | solution.py:762
  338.2 63.6 %collective-permute-start.20 = (bf16[272,1152]{1,0:T(8,128)(2,1)}, bf16[272,1152]{1,0:T(8,128)(2,1)}, u32[]{:S(2)}, u32[]{:S(2)}) collective-permute-start(bf16[272,1152]{1,0:T(8,128)(2,1)} %reduce-scatter.4.cloned.1.call-done.refs_0_), channel_id=1, source_target_pairs={{0,16},{8,24},{16,0},{24,8},{1,17},{9,25},{17,1},{25,9},{2,18},{10... | collective-permute-start | bytes 1880072 | tf_op jit(solution)/shard_map/ppermute | solution.py:762
  355.3 17.2 %collective-permute-start.15 = (bf16[128,1152]{1,0:T(8,128)(2,1)}, bf16[128,1152]{1,0:T(8,128)(2,1)}, u32[]{:S(2)}, u32[]{:S(2)}) collective-permute-start(bf16[128,1152]{1,0:T(8,128)(2,1)} %get-tuple-element.267), channel_id=1, source_target_pairs={{0,8},{8,0},{16,24},{24,16},{1,9},{9,1},{17,25},{25,17},{2,10},{10... | collective-permute-start | bytes 884744 | tf_op jit(solution)/shard_map/ppermute | solution.py:759
  369.6 26.7 %collective-permute-start.14 = (bf16[4,144,2176]{2,1,0:T(8,128)(2,1)}, bf16[4,144,2176]{2,1,0:T(8,128)(2,1)}, u32[]{:S(2)}, u32[]{:S(2)}) collective-permute-start(bf16[4,144,2176]{2,1,0:T(8,128)(2,1)} %get-tuple-element.272), channel_id=1, source_target_pairs={{0,1},{1,0},{2,3},{3,2},{4,5},{5,4},{6,7},{7,6},{8,9},{9,8},{10,11... | collective-permute-start | bytes 7520264 | tf_op jit(solution)/shard_map/ppermute | solution.py:765
  390.2 11.7 %all-to-all-start.6 = ((bf16[4,288,128]{2,1,0:T(8,128)(2,1)}), bf16[4,288,128]{2,1,0:T(8,128)(2,1)}, u32[]{:S(2)}, u32[]{:S(2)}) async-start(bf16[4,288,128]{2,1,0:T(8,128)(2,1)} %copy-done.47), calls=%async_computation.8 | async-start | bytes 589824 | tf_op jit(solution)/shard_map/all_to_all | solution.py:768
  394.3 37.1 %collective-permute-start.22 = (bf16[144,2176]{1,0:T(8,128)(2,1)}, bf16[144,2176]{1,0:T(8,128)(2,1)}, u32[]{:S(2)}, u32[]{:S(2)}) collective-permute-start(bf16[144,2176]{1,0:T(8,128)(2,1)} %copy-done.41), channel_id=1, source_target_pairs={{0,8},{8,0},{16,24},{24,16},{1,9},{9,1},{17,25},{25,17},{2,10},{10... | collective-permute-start | bytes 1880072 | tf_op jit(solution)/shard_map/ppermute | solution.py:759
  396.3 39.4 %collective-permute-start.21 = (bf16[128,576]{1,0:T(8,128)(2,1)}, bf16[128,576]{1,0:T(8,128)(2,1)}, u32[]{:S(2)}, u32[]{:S(2)}) collective-permute-start(bf16[128,576]{1,0:T(8,128)(2,1)} %copy-done.110), channel_id=1, source_target_pairs={{0,8},{8,0},{16,24},{24,16},{1,9},{9,1},{17,25},{25,17},{2,10},{10... | collective-permute-start | bytes 442376 | tf_op jit(solution)/shard_map/ppermute | solution.py:759
  407.7 69.1 %collective-permute-start.27 = (bf16[144,1472]{1,0:T(8,128)(2,1)}, bf16[144,1472]{1,0:T(8,128)(2,1)}, u32[]{:S(2)}, u32[]{:S(2)}) collective-permute-start(bf16[144,1472]{1,0:T(8,128)(2,1)} %reduce-scatter.8.cloned.1.call-done), channel_id=1, source_target_pairs={{0,16},{8,24},{16,0},{24,8},{1,17},{9,25},{17,1},{25,9},{2,18},{10... | collective-permute-start | bytes 1271816 | tf_op jit(solution)/shard_map/ppermute | solution.py:762
  410.5 71.0 %collective-permute-start.26 = (bf16[272,1152]{1,0:T(8,128)(2,1)}, bf16[272,1152]{1,0:T(8,128)(2,1)}, u32[]{:S(2)}, u32[]{:S(2)}) collective-permute-start(bf16[272,1152]{1,0:T(8,128)(2,1)} %add_all.11.refs_2_), channel_id=1, source_target_pairs={{0,8},{8,0},{16,24},{24,16},{1,9},{9,1},{17,25},{25,17},{2,10},{10... | collective-permute-start | bytes 1880072 | tf_op jit(solution)/shard_map/ppermute | solution.py:759
  412.0 31.8 %collective-permute-start.17 = (bf16[144,2176]{1,0:T(8,128)(2,1)}, bf16[144,2176]{1,0:T(8,128)(2,1)}, u32[]{:S(2)}, u32[]{:S(2)}) collective-permute-start(bf16[144,2176]{1,0:T(8,128)(2,1)} %get-tuple-element.280), channel_id=1, source_target_pairs={{0,2},{1,3},{2,0},{3,1},{4,6},{5,7},{6,4},{7,5},{8,10},{9,11},{10,... | collective-permute-start | bytes 1880072 | tf_op jit(solution)/shard_map/ppermute | solution.py:765
  426.9 46.0 %all-to-all-start.7 = ((bf16[4,128,1152]{2,1,0:T(8,128)(2,1)}), bf16[4,128,1152]{2,1,0:T(8,128)(2,1)}, u32[]{:S(2)}, u32[]{:S(2)}) async-start(bf16[4,128,1152]{2,1,0:T(8,128)(2,1)} %get-tuple-element.290), calls=%async_computation.10 | async-start | bytes 2359296 | tf_op jit(solution)/shard_map/all_to_all | solution.py:768
  431.3 32.1 %collective-permute-start.18 = (bf16[144,2176]{1,0:T(8,128)(2,1)}, bf16[144,2176]{1,0:T(8,128)(2,1)S(1)}, u32[]{:S(2)}, u32[]{:S(2)}) collective-permute-start(bf16[144,2176]{1,0:T(8,128)(2,1)} %get-tuple-element.281), channel_id=1, source_target_pairs={{0,4},{1,5},{2,6},{3,7},{4,0},{5,1},{6,2},{7,3},{8,12},{9,13},{10,... | collective-permute-start | bytes 1880072 | tf_op jit(solution)/shard_map/ppermute | solution.py:765
  435.7 27.7 %collective-permute-start.19 = (bf16[144,2176]{1,0:T(8,128)(2,1)S(1)}, bf16[144,2176]{1,0:T(8,128)(2,1)S(1)}, u32[]{:S(2)}, u32[]{:S(2)}) collective-permute-start(bf16[144,2176]{1,0:T(8,128)(2,1)S(1)} %copy-done.102), channel_id=1, source_target_pairs={{0,6},{1,7},{2,4},{3,5},{4,2},{5,3},{6,0},{7,1},{8,14},{9,15},{10,... | collective-permute-start | bytes 1880072 | tf_op jit(solution)/shard_map/ppermute | solution.py:765
  443.8 24.8 %collective-permute-start.25 = (bf16[4,144,1472]{2,1,0:T(8,128)(2,1)}, bf16[4,144,1472]{2,1,0:T(8,128)(2,1)}, u32[]{:S(2)}, u32[]{:S(2)}) collective-permute-start(bf16[4,144,1472]{2,1,0:T(8,128)(2,1)} %get-tuple-element.297), channel_id=1, source_target_pairs={{0,1},{1,0},{2,3},{3,2},{4,5},{5,4},{6,7},{7,6},{8,9},{9,8},{10,11... | collective-permute-start | bytes 5087240 | tf_op jit(solution)/shard_map/ppermute | solution.py:765
  465.7 40.8 %collective-permute-start.24 = (bf16[144,2176]{1,0:T(8,128)(2,1)}, bf16[144,2176]{1,0:T(8,128)(2,1)}, u32[]{:S(2)}, u32[]{:S(2)}) collective-permute-start(bf16[144,2176]{1,0:T(8,128)(2,1)} %add_all.12.refs_0_), channel_id=1, source_target_pairs={{0,16},{8,24},{16,0},{24,8},{1,17},{9,25},{17,1},{25,9},{2,18},{10... | collective-permute-start | bytes 1880072 | tf_op jit(solution)/shard_map/ppermute | solution.py:762
  468.2 50.3 %collective-permute-start.23 = (bf16[272,1152]{1,0:T(8,128)(2,1)}, bf16[272,1152]{1,0:T(8,128)(2,1)}, u32[]{:S(2)}, u32[]{:S(2)}) collective-permute-start(bf16[272,1152]{1,0:T(8,128)(2,1)} %reduce-scatter.6.cloned.1.call-done.refs_0_), channel_id=1, source_target_pairs={{0,16},{8,24},{16,0},{24,8},{1,17},{9,25},{17,1},{25,9},{2,18},{10... | collective-permute-start | bytes 1880072 | tf_op jit(solution)/shard_map/ppermute | solution.py:762
  477.8 29.7 %copy-start.52 = (f32[1,2176]{1,0:T(1,128)S(1)}, f32[1,2176]{1,0:T(1,128)}, u32[]{:S(2)}) copy-start(f32[1,2176]{1,0:T(1,128)} %copy-done.51) | copy-start | bytes 26116
  477.8 29.7 %copy-start.56 = (f32[1,1152]{1,0:T(1,128)S(1)}, f32[1,1152]{1,0:T(1,128)}, u32[]{:S(2)}) copy-start(f32[1,1152]{1,0:T(1,128)} %copy-done.55) | copy-start | bytes 13828
  477.9 29.7 %copy-start.58 = (f32[1,1152]{1,0:T(1,128)S(1)}, f32[1,1152]{1,0:T(1,128)}, u32[]{:S(2)}) copy-start(f32[1,1152]{1,0:T(1,128)} %copy-done.57) | copy-start | bytes 13828
  477.9 29.7 %copy-start.60 = (f32[1,1152]{1,0:T(1,128)S(1)}, f32[1,1152]{1,0:T(1,128)}, u32[]{:S(2)}) copy-start(f32[1,1152]{1,0:T(1,128)} %copy-done.59) | copy-start | bytes 13828
  477.9 29.7 %copy-start.62 = (f32[1,1152]{1,0:T(1,128)S(1)}, f32[1,1152]{1,0:T(1,128)}, u32[]{:S(2)}) copy-start(f32[1,1152]{1,0:T(1,128)} %copy-done.61) | copy-start | bytes 13828
  477.9 29.7 %copy-start.65 = (f32[1,1152]{1,0:T(1,128)S(1)}, f32[1,1152]{1,0:T(1,128)}, u32[]{:S(2)}) copy-start(f32[1,1152]{1,0:T(1,128)} %copy-done.64) | copy-start | bytes 13828
  477.9 29.7 %copy-start.67 = (f32[1,1152]{1,0:T(1,128)S(1)}, f32[1,1152]{1,0:T(1,128)}, u32[]{:S(2)}) copy-start(f32[1,1152]{1,0:T(1,128)} %copy-done.66) | copy-start | bytes 13828
  477.9 29.7 %copy-start.70 = (f32[1,1152]{1,0:T(1,128)S(1)}, f32[1,1152]{1,0:T(1,128)}, u32[]{:S(2)}) copy-start(f32[1,1152]{1,0:T(1,128)} %copy-done.69) | copy-start | bytes 13828
  477.9 29.7 %copy-start.72 = (f32[1,1152]{1,0:T(1,128)S(1)}, f32[1,1152]{1,0:T(1,128)}, u32[]{:S(2)}) copy-start(f32[1,1152]{1,0:T(1,128)} %copy-done.71) | copy-start | bytes 13828
  479.0 40.2 %copy-start.36 = (bf16[272,1152]{1,0:T(8,128)(2,1)S(1)}, bf16[272,1152]{1,0:T(8,128)(2,1)}, u32[]{:S(2)}) copy-start(bf16[272,1152]{1,0:T(8,128)(2,1)} %reduce-scatter.6.cloned.1.call-done.refs_0_) | copy-start | bytes 1880068
  479.1 42.2 %collective-permute-start.32 = (bf16[144,2368]{1,0:T(8,128)(2,1)S(1)}, bf16[144,2368]{1,0:T(8,128)(2,1)S(1)}, u32[]{:S(2)}, u32[]{:S(2)}) collective-permute-start(bf16[144,2368]{1,0:T(8,128)(2,1)S(1)} %pad_maximum_fusion.2.own_ref), channel_id=1, source_target_pairs={{0,8},{8,0},{16,24},{24,16},{1,9},{9,1},{17,25},{25,17},{2,10},{10... | collective-permute-start | bytes 2045960 | tf_op jit(solution)/shard_map/ppermute | solution.py:759
  480.8 42.3 %collective-permute-start.29 = (bf16[144,1472]{1,0:T(8,128)(2,1)}, bf16[144,1472]{1,0:T(8,128)(2,1)}, u32[]{:S(2)}, u32[]{:S(2)}) collective-permute-start(bf16[144,1472]{1,0:T(8,128)(2,1)} %get-tuple-element.303), channel_id=1, source_target_pairs={{0,2},{1,3},{2,0},{3,1},{4,6},{5,7},{6,4},{7,5},{8,10},{9,11},{10,... | collective-permute-start | bytes 1271816 | tf_op jit(solution)/shard_map/ppermute | solution.py:765
  481.6 41.6 %collective-permute-start.30 = (bf16[144,1472]{1,0:T(8,128)(2,1)}, bf16[144,1472]{1,0:T(8,128)(2,1)}, u32[]{:S(2)}, u32[]{:S(2)}) collective-permute-start(bf16[144,1472]{1,0:T(8,128)(2,1)} %get-tuple-element.304), channel_id=1, source_target_pairs={{0,4},{1,5},{2,6},{3,7},{4,0},{5,1},{6,2},{7,3},{8,12},{9,13},{10,... | collective-permute-start | bytes 1271816 | tf_op jit(solution)/shard_map/ppermute | solution.py:765
  506.5 16.7 %collective-permute-start.31 = (bf16[144,1472]{1,0:T(8,128)(2,1)}, bf16[144,1472]{1,0:T(8,128)(2,1)}, u32[]{:S(2)}, u32[]{:S(2)}) collective-permute-start(bf16[144,1472]{1,0:T(8,128)(2,1)} %get-tuple-element.305), channel_id=1, source_target_pairs={{0,6},{1,7},{2,4},{3,5},{4,2},{5,3},{6,0},{7,1},{8,14},{9,15},{10,... | collective-permute-start | bytes 1271816 | tf_op jit(solution)/shard_map/ppermute | solution.py:765
  518.5 24.2 %collective-permute-start.34 = (bf16[144,2176]{1,0:T(8,128)(2,1)S(1)}, bf16[144,2176]{1,0:T(8,128)(2,1)}, u32[]{:S(2)}, u32[]{:S(2)}) collective-permute-start(bf16[144,2176]{1,0:T(8,128)(2,1)S(1)} %add_all.14.own_ref), channel_id=1, source_target_pairs={{0,8},{8,0},{16,24},{24,16},{1,9},{9,1},{17,25},{25,17},{2,10},{10... | collective-permute-start | bytes 1880072 | tf_op jit(solution)/shard_map/ppermute | solution.py:759
  524.8 23.5 %collective-permute-start.33 = (bf16[144,1472]{1,0:T(8,128)(2,1)S(1)}, bf16[144,1472]{1,0:T(8,128)(2,1)S(1)}, u32[]{:S(2)}, u32[]{:S(2)}) collective-permute-start(bf16[144,1472]{1,0:T(8,128)(2,1)S(1)} %add_all.16), channel_id=1, source_target_pairs={{0,16},{8,24},{16,0},{24,8},{1,17},{9,25},{17,1},{25,9},{2,18},{10... | collective-permute-start | bytes 1271816 | tf_op jit(solution)/shard_map/ppermute | solution.py:762
  536.7 11.7 %collective-permute-start.35 = (f32[1,3456]{1,0:T(1,128)S(1)}, f32[1,3456]{1,0:T(1,128)S(1)}, u32[]{:S(2)}, u32[]{:S(2)}) collective-permute-start(f32[1,3456]{1,0:T(1,128)S(1)} %broadcast_in_dim.12), channel_id=1, source_target_pairs={{0,16},{8,24},{16,0},{24,8},{1,17},{9,25},{17,1},{25,9},{2,18},{10... | collective-permute-start | bytes 41480 | tf_op jit(solution)/shard_map/ppermute | solution.py:762
  536.8 21.4 %collective-permute-start.28 = (bf16[272,1152]{1,0:T(8,128)(2,1)S(1)}, bf16[272,1152]{1,0:T(8,128)(2,1)S(1)}, u32[]{:S(2)}, u32[]{:S(2)}) collective-permute-start(bf16[272,1152]{1,0:T(8,128)(2,1)S(1)} %copy-done.40), channel_id=1, source_target_pairs={{0,8},{8,0},{16,24},{24,16},{1,9},{9,1},{17,25},{25,17},{2,10},{10... | collective-permute-start | bytes 1880072 | tf_op jit(solution)/shard_map/ppermute | solution.py:759
  548.6 24.6 %collective-permute-start.37 = (bf16[144,2368]{1,0:T(8,128)(2,1)S(1)}, bf16[144,2368]{1,0:T(8,128)(2,1)S(1)}, u32[]{:S(2)}, u32[]{:S(2)}) collective-permute-start(bf16[144,2368]{1,0:T(8,128)(2,1)S(1)} %pad_maximum_fusion.3.own_ref), channel_id=1, source_target_pairs={{0,8},{8,0},{16,24},{24,16},{1,9},{9,1},{17,25},{25,17},{2,10},{10... | collective-permute-start | bytes 2045960 | tf_op jit(solution)/shard_map/ppermute | solution.py:759
  558.2 13.7 %collective-permute-start.36 = (f32[1,3456]{1,0:T(1,128)S(1)}, f32[1,3456]{1,0:T(1,128)S(1)}, u32[]{:S(2)}, u32[]{:S(2)}) collective-permute-start(f32[1,3456]{1,0:T(1,128)S(1)} %reshape_add_fusion.first_ref), channel_id=1, source_target_pairs={{0,8},{8,0},{16,24},{24,16},{1,9},{9,1},{17,25},{25,17},{2,10},{10... | collective-permute-start | bytes 41480 | tf_op jit(solution)/shard_map/ppermute | solution.py:759
  (135 other events, 772.2 us)
Sparse Core Ops, SparseCore 0:
  13.1 42.7 all-gather.8
  58.4 63.8 all-gather.10
  124.7 38.9 all-gather.12
  166.0 63.8 all-gather.14
  248.9 71.6 reduce-scatter.3
  324.9 49.7 reduce-scatter.7
  378.6 82.4 reduce-scatter.5
